TPU v7x, 32 devices: a whole 2x2x4 slice. The times are simulated.
32 devices in a mesh: expert: 4 (over y, core), context: 4 (over z), dp: 2 (over x).
Axes of the slice: x: 2, y: 2, z: 4, core: 2. Of those that a mesh axis runs over, the one named last changes fastest.
Arguments:
- inputs: bfloat16 [8, 2, 1024, 768], P(('expert', 'dp'), None, 'context'), may hold values from -6 to 6
- keep_flags: int32 [8, 2, 1024], P(('expert', 'dp'), None, 'context'), may hold values 0 or 1
- block_ids: int32 [8, 2, 1024], P(('expert', 'dp'), None, 'context'), may hold values from 0 to 7, never falling along the last dimension, each value on 1 to 256 neighbouring positions
- expert_ids: int32 [8, 2, 1024, 2], P(('expert', 'dp'), None, 'context'), may hold values from 0 to 3, all different within a row; in each aligned block of 256 rows (0 to 255, 256 to 511, ..., all dimensions but the last counted through in order) at most 256 rows name the same one
- gate_weights: float32 [8, 2, 1024, 2], P(('expert', 'dp'), None, 'context'), may hold values from 0.2 to 0.8
- norm_attn: bfloat16 [768], P('dp'), may hold values from 0.5 to 1.5
- w_qkv: bfloat16 [768, 2304], P('dp'), may hold values from -0.21875 to 0.21875
- w_attn_out: bfloat16 [768, 768], P('dp'), may hold values from -4 to 4
- norm_ffn: bfloat16 [768], P('dp'), may hold values from 0.5 to 1.5
- w_shared_in: bfloat16 [768, 4096], P('dp'), may hold values from -0.21875 to 0.21875
- w_shared_out: bfloat16 [2048, 768], P('dp'), may hold values from -0.125 to 0.125
- w_expert_in: bfloat16 [4, 768, 4096], P('expert', 'dp'), may hold values from -0.21875 to 0.21875
- w_expert_out: bfloat16 [4, 2048, 768], P('expert', 'dp'), may hold values from -0.125 to 0.125
- cotangent: bfloat16 [8, 2, 1024, 768], P(('expert', 'dp'), None, 'context'), may hold values from -6 to 6
Outputs:
- output: bfloat16 [8, 2, 1024, 768], P(('expert', 'dp'), None, 'context')
- grad_input: float32 [8, 2, 1024, 768], P(('expert', 'dp'), None, 'context')
- grad_norm_attn: float32 [768], P('dp')
- grad_w_qkv: float32 [768, 2304], P('dp')
- grad_w_attn_out: float32 [768, 768], P('dp')
- grad_norm_ffn: float32 [768], P('dp')
- grad_w_shared_in: float32 [768, 4096], P('dp')
- grad_w_shared_out: float32 [2048, 768], P('dp')
- grad_w_expert_in: float32 [4, 768, 4096], P('expert', 'dp')
- grad_w_expert_out: float32 [4, 2048, 768], P('expert', 'dp')
Inputs may be any that keep to these rules, and one draw needn't show every extreme that they name: `expert_ids`: in each aligned block of 256 rows (one device's positions of one micro-batch) no expert is named more than 256 times; some expert is named exactly 256 times in some block. `block_ids`: never falling along a micro-batch; each block holds 1 to 256 positions and one holds exactly 256.
All inputs are finite; a program needn't handle non-finite values. No bound on the sum of `keep_flags` on one device may be relied on, other than what follows from the above.
Results may differ from a plain program's by a relative error of at most 0.02.
Values may be sent and summed in bfloat16 or wider, within the bound.
A program may use at most 320 MiB of HBM per device.

v0:
```python
import math

import jax
import jax.numpy as jnp
from jax import lax
from jax.sharding import PartitionSpec as P

HEAD = 64
TOP = 2
MICRO = 2


EPSILON = 1e-05
ROPE_BASE = 10000.0
MASKED = -3e30
NEG_START = -1e30


def rms_scale(values):
    return lax.rsqrt(jnp.mean(values * values, -1, keepdims=True) + EPSILON)


def rotary_tables(positions, head):
    half = head // 2
    freq = jnp.exp(-math.log(ROPE_BASE) * jnp.arange(half, dtype=jnp.float32) * 2.0 / head)
    angle = positions.astype(jnp.float32)[:, None] * freq[None, :]
    return (jnp.cos(angle), jnp.sin(angle))


def rotate(values, cosines, sines, head):
    rows = values.shape[0]
    shaped = values.reshape(rows, -1, head)
    first = shaped[..., : head // 2]
    second = shaped[..., head // 2 :]
    cos_b = cosines[:, None, :]
    sin_b = sines[:, None, :]
    turned = jnp.concatenate([first * cos_b - second * sin_b, second * cos_b + first * sin_b], -1)
    return turned.reshape(rows, -1)


def silu_glu(joined):
    half = joined.shape[-1] // 2
    return jax.nn.silu(joined[..., :half]) * joined[..., half:]


def glu_grad(joined, grad_hidden):
    half = joined.shape[-1] // 2
    gate_part = joined[..., :half]
    up_part = joined[..., half:]
    sigma = jax.nn.sigmoid(gate_part)
    activated = gate_part * sigma
    slope = sigma * (1.0 + gate_part * (1.0 - sigma))
    return jnp.concatenate([grad_hidden * up_part * slope, grad_hidden * activated], -1)


def tdot(left, right):
    return lax.dot_general(
        left, right, (((0,), (0,)), ((), ())), preferred_element_type=jnp.float32
    )


def dott(left, right):
    return lax.dot_general(
        left, right, (((1,), (1,)), ((), ())), preferred_element_type=jnp.float32
    )


def norm_backward(values, scale, gain, grad_out):
    gain_grad = jnp.sum(grad_out * values * scale, 0)
    scaled = gain * grad_out
    grad_in = scale * scaled - values * scale * scale * scale * jnp.mean(
        scaled * values, -1, keepdims=True
    )
    return (grad_in, gain_grad)


def route_slots(ids, capacity, experts):
    flat = ids.reshape(-1)
    onehot = (flat[:, None] == jnp.arange(experts, dtype=jnp.int32)[None, :]).astype(jnp.int32)
    before = jnp.cumsum(onehot, 0) - onehot
    return flat * capacity + jnp.sum(before * onehot, 1)


def visibility(start, count, tags, held, tok_rows, seq_rows, query_pos, query_block, micro_now):
    index_all = start + jnp.arange(count, dtype=jnp.int32)
    owner = index_all // held
    within = index_all % held
    key_micro = within // tok_rows
    key_pos = key_micro * seq_rows + owner * tok_rows + within % tok_rows
    key_block = tags // 2
    key_keep = tags % 2
    earlier = key_micro[None, :] < micro_now
    same = (key_micro[None, :] == micro_now) & (key_block[None, :] <= query_block[:, None])
    usable = (key_keep[None, :] == 1) | (key_pos[None, :] == query_pos[:, None])
    return (earlier | same) & usable


def add_into(total, value):
    return value if total is None else total + value


def body(
    inputs,
    keep_flags,
    block_ids,
    expert_ids,
    gate_weights,
    norm_attn,
    w_qkv,
    w_attn_out,
    norm_ffn,
    w_shared_in,
    w_shared_out,
    w_expert_in,
    w_expert_out,
    cotangent,
):
    width = w_qkv.shape[1] // 3
    heads = width // HEAD
    tok_rows = inputs.shape[2]
    contexts = lax.axis_size("context")
    context_idx = lax.axis_index("context")
    local_experts = w_expert_in.shape[0]
    experts = lax.axis_size("expert") * local_experts
    capacity = 4 * tok_rows // experts
    seq_rows = tok_rows * contexts
    assigns = tok_rows * TOP
    source_rows = jnp.arange(assigns, dtype=jnp.int32) // TOP
    local_pos = jnp.arange(tok_rows, dtype=jnp.int32)
    shards = (
        norm_attn,
        w_qkv,
        w_attn_out,
        norm_ffn,
        w_shared_in,
        w_shared_out,
        w_expert_in,
        w_expert_out,
    )

    def fetch_all():
        return (
            lax.all_gather(shards[0], "dp", axis=0, tiled=True),
            lax.all_gather(shards[1], "dp", axis=0, tiled=True),
            lax.all_gather(shards[2], "dp", axis=0, tiled=True),
            lax.all_gather(shards[3], "dp", axis=0, tiled=True),
            lax.all_gather(shards[4], "dp", axis=0, tiled=True),
            lax.all_gather(shards[5], "dp", axis=0, tiled=True),
            lax.all_gather(shards[6], "dp", axis=1, tiled=True),
            lax.all_gather(shards[7], "dp", axis=1, tiled=True),
        )

    key_cache = []
    value_cache = []
    tag_cache = []
    saved = []
    outputs = []
    for micro_idx in range(MICRO):
        gain_attn, mat_qkv, mat_out, gain_ffn, mat_sin, mat_sout, mat_ein, mat_eout = fetch_all()
        tokens = inputs[0, micro_idx].astype(jnp.float32)
        positions = micro_idx * seq_rows + context_idx * tok_rows + local_pos
        cosines, sines = rotary_tables(positions, HEAD)
        scale_one = rms_scale(tokens)
        normed = (tokens * scale_one * gain_attn.astype(jnp.float32)).astype(jnp.bfloat16)
        joined = jnp.dot(normed, mat_qkv, preferred_element_type=jnp.float32)
        queries = (rotate(joined[:, :width], cosines, sines, HEAD) * 0.125).astype(jnp.bfloat16)
        key_cache.append(
            rotate(joined[:, width : 2 * width], cosines, sines, HEAD).astype(jnp.bfloat16)
        )
        value_cache.append(joined[:, 2 * width :].astype(jnp.bfloat16))
        own_blocks = block_ids[0, micro_idx]
        tag_cache.append(own_blocks * 2 + keep_flags[0, micro_idx])
        keys_sofar = jnp.concatenate(key_cache, 0)
        values_sofar = jnp.concatenate(value_cache, 0)
        tags_sofar = jnp.concatenate(tag_cache, 0)
        held = keys_sofar.shape[0]
        query_heads = queries.reshape(tok_rows, heads, HEAD)

        def accumulate(
            carry,
            piece,
            start,
            query_heads=query_heads,
            positions=positions,
            own_blocks=own_blocks,
            micro_idx=micro_idx,
            held=held,
        ):
            totals, maxima, sums = carry
            key_piece, value_piece, tag_piece = piece
            count = key_piece.shape[0]
            visible = visibility(
                start, count, tag_piece, held, tok_rows, seq_rows, positions, own_blocks, micro_idx
            )
            scores = jnp.einsum(
                "qhd,khd->hqk",
                query_heads,
                key_piece.reshape(count, heads, HEAD),
                preferred_element_type=jnp.float32,
            )
            scores = jnp.where(visible[None], scores, MASKED)
            new_max = jnp.maximum(maxima, jnp.max(scores, -1))
            expo = jnp.exp(scores - new_max[..., None])
            sums = jnp.sum(expo, -1)
            totals = jnp.einsum(
                "hqk,khd->hqd",
                expo.astype(jnp.bfloat16),
                value_piece.reshape(count, heads, HEAD),
                preferred_element_type=jnp.float32,
            )
            return (totals, new_max, sums)

        start_state = (
            jnp.zeros((heads, tok_rows, HEAD), jnp.float32),
            jnp.full((heads, tok_rows), NEG_START, jnp.float32),
            jnp.zeros((heads, tok_rows), jnp.float32),
        )
        totals, maxima, sums = accumulate(
            start_state,
            (
                lax.all_gather(keys_sofar, "context", axis=0, tiled=True),
                lax.all_gather(values_sofar, "context", axis=0, tiled=True),
                lax.all_gather(tags_sofar, "context", axis=0, tiled=True),
            ),
            jnp.int32(0),
        )
        mixed = (totals / sums[..., None]).transpose(1, 0, 2).reshape(tok_rows, width)
        log_sums = maxima + jnp.log(sums)
        residual = tokens + jnp.dot(
            mixed.astype(jnp.bfloat16), mat_out, preferred_element_type=jnp.float32
        )
        normed_ffn = (residual * rms_scale(residual) * gain_ffn.astype(jnp.float32)).astype(
            jnp.bfloat16
        )
        shared_hidden = silu_glu(
            jnp.dot(normed_ffn, mat_sin, preferred_element_type=jnp.float32)
        ).astype(jnp.bfloat16)
        shared = jnp.dot(shared_hidden, mat_sout, preferred_element_type=jnp.float32)
        dest = route_slots(expert_ids[0, micro_idx], capacity, experts)
        send = (
            jnp.zeros((experts * capacity, width), jnp.bfloat16)
            .at[dest]
            .set(normed_ffn[source_rows])
            .reshape(experts, capacity, width)
        )

        def experts_forward(received, mat_ein=mat_ein, mat_eout=mat_eout):
            items = received.shape[1]
            grouped = received.reshape(-1, local_experts, items, width)
            expert_joined = jnp.einsum(
                "necd,edf->necf", grouped, mat_ein, preferred_element_type=jnp.float32
            )
            expert_hidden = silu_glu(expert_joined).astype(jnp.bfloat16)
            produced = (
                jnp.einsum(
                    "necf,efd->necd", expert_hidden, mat_eout, preferred_element_type=jnp.float32
                )
                .astype(jnp.bfloat16)
                .reshape(received.shape)
            )
            returned = lax.all_to_all(produced, "expert", split_axis=0, concat_axis=0, tiled=True)
            return (returned, received)

        returned, arrived = experts_forward(
            lax.all_to_all(send, "expert", split_axis=0, concat_axis=0, tiled=True)
        )
        picked = returned.reshape(experts * capacity, width)[dest].astype(jnp.float32)
        gates_now = gate_weights[0, micro_idx].reshape(assigns)
        routed = jnp.sum((picked * gates_now[:, None]).reshape(tok_rows, TOP, width), 1)
        outputs.append((residual + shared + routed).astype(jnp.bfloat16))
        saved.append((residual, mixed, log_sums, queries, dest, arrived))
    key_acc = [jnp.zeros((tok_rows, width), jnp.float32) for index_m in range(MICRO)]
    value_acc = [jnp.zeros((tok_rows, width), jnp.float32) for index_m in range(MICRO)]
    grad_g1 = None
    grad_qkv = None
    grad_out = None
    grad_g2 = None
    grad_sin = None
    grad_sout = None
    grad_ein = None
    grad_eout = None
    input_grads = [None] * MICRO
    for micro_idx in reversed(range(MICRO)):
        gain_attn, mat_qkv, mat_out, gain_ffn, mat_sin, mat_sout, mat_ein, mat_eout = fetch_all()
        residual, mixed, log_sums, queries, dest, arrived = saved[micro_idx]
        grad_bf = cotangent[0, micro_idx]
        grad_top = grad_bf.astype(jnp.float32)
        scale_two = rms_scale(residual)
        gain_two = gain_ffn.astype(jnp.float32)
        normed_ffn = (residual * scale_two * gain_two).astype(jnp.bfloat16)
        shared_joined = jnp.dot(normed_ffn, mat_sin, preferred_element_type=jnp.float32)
        shared_hidden = silu_glu(shared_joined).astype(jnp.bfloat16)
        grad_sout = add_into(grad_sout, tdot(shared_hidden, grad_bf))
        grad_shidden = dott(grad_bf, mat_sout)
        grad_sjoined = glu_grad(shared_joined, grad_shidden).astype(jnp.bfloat16)
        grad_sin = add_into(grad_sin, tdot(normed_ffn, grad_sjoined))
        grad_normed = dott(grad_sjoined, mat_sin)
        gates_now = gate_weights[0, micro_idx].reshape(assigns)
        slot_grads = (gates_now[:, None] * grad_top[source_rows]).astype(jnp.bfloat16)
        grad_buffer = (
            jnp.zeros((experts * capacity, width), jnp.bfloat16)
            .at[dest]
            .set(slot_grads)
            .reshape(experts, capacity, width)
        )
        arrived_grads = lax.all_to_all(
            grad_buffer, "expert", split_axis=0, concat_axis=0, tiled=True
        )
        grouped = arrived.reshape(-1, local_experts, capacity, width)
        grouped_grads = arrived_grads.reshape(-1, local_experts, capacity, width)
        expert_joined = jnp.einsum(
            "necd,edf->necf", grouped, mat_ein, preferred_element_type=jnp.float32
        )
        expert_hidden = silu_glu(expert_joined).astype(jnp.bfloat16)
        grad_eout = add_into(
            grad_eout,
            jnp.einsum(
                "necf,necd->efd", expert_hidden, grouped_grads, preferred_element_type=jnp.float32
            ),
        )
        grad_ehidden = jnp.einsum(
            "necd,efd->necf", grouped_grads, mat_eout, preferred_element_type=jnp.float32
        )
        grad_ejoined = glu_grad(expert_joined, grad_ehidden).astype(jnp.bfloat16)
        grad_ein = add_into(
            grad_ein,
            jnp.einsum("necd,necf->edf", grouped, grad_ejoined, preferred_element_type=jnp.float32),
        )
        grad_rows = (
            jnp.einsum("necf,edf->necd", grad_ejoined, mat_ein, preferred_element_type=jnp.float32)
            .astype(jnp.bfloat16)
            .reshape(arrived.shape)
        )
        grad_back = lax.all_to_all(grad_rows, "expert", split_axis=0, concat_axis=0, tiled=True)
        grad_picked = grad_back.reshape(experts * capacity, width)[dest].astype(jnp.float32)
        grad_normed = grad_normed + jnp.sum(grad_picked.reshape(tok_rows, TOP, width), 1)
        grad_mid, gain_two_grad = norm_backward(residual, scale_two, gain_two, grad_normed)
        grad_g2 = add_into(grad_g2, gain_two_grad)
        grad_res = grad_top + grad_mid
        grad_res_bf = grad_res.astype(jnp.bfloat16)
        grad_out = add_into(grad_out, tdot(mixed.astype(jnp.bfloat16), grad_res_bf))
        grad_mixed = dott(grad_res_bf, mat_out).astype(jnp.bfloat16)
        grad_heads = grad_mixed.reshape(tok_rows, heads, HEAD)
        delta = jnp.sum(
            (grad_mixed.astype(jnp.float32) * mixed).reshape(tok_rows, heads, HEAD), -1
        ).T
        keys_sofar = jnp.concatenate(key_cache[: micro_idx + 1], 0)
        values_sofar = jnp.concatenate(value_cache[: micro_idx + 1], 0)
        tags_sofar = jnp.concatenate(tag_cache[: micro_idx + 1], 0)
        held = keys_sofar.shape[0]
        all_keys, all_values, all_tags = (
            lax.all_gather(keys_sofar, "context", axis=0, tiled=True),
            lax.all_gather(values_sofar, "context", axis=0, tiled=True),
            lax.all_gather(tags_sofar, "context", axis=0, tiled=True),
        )
        count = all_keys.shape[0]
        positions = micro_idx * seq_rows + context_idx * tok_rows + local_pos
        own_blocks = block_ids[0, micro_idx]
        visible = visibility(
            0, count, all_tags, held, tok_rows, seq_rows, positions, own_blocks, micro_idx
        )
        query_heads = queries.reshape(tok_rows, heads, HEAD)
        key_heads = all_keys.reshape(count, heads, HEAD)
        value_heads = all_values.reshape(count, heads, HEAD)
        scores = jnp.einsum(
            "qhd,khd->hqk", query_heads, key_heads, preferred_element_type=jnp.float32
        )
        scores = jnp.where(visible[None], scores, MASKED)
        probs = jnp.exp(scores - log_sums[..., None])
        value_grads = jnp.einsum(
            "hqk,qhd->khd",
            probs.astype(jnp.bfloat16),
            grad_heads,
            preferred_element_type=jnp.float32,
        )
        prob_grads = jnp.einsum(
            "qhd,khd->hqk", grad_heads, value_heads, preferred_element_type=jnp.float32
        )
        score_grads = (probs * (prob_grads - delta[..., None])).astype(jnp.bfloat16)
        query_grads = jnp.einsum(
            "hqk,khd->qhd", score_grads, key_heads, preferred_element_type=jnp.float32
        ).reshape(tok_rows, width)
        key_grads = jnp.einsum(
            "hqk,qhd->khd", score_grads, query_heads, preferred_element_type=jnp.float32
        ).reshape(count, width)
        own_key_grads, own_value_grads = (
            lax.psum_scatter(
                key_grads.astype(jnp.bfloat16), "context", scatter_dimension=0, tiled=True
            ).astype(jnp.float32),
            lax.psum_scatter(
                value_grads.reshape(count, width).astype(jnp.bfloat16),
                "context",
                scatter_dimension=0,
                tiled=True,
            ).astype(jnp.float32),
        )
        for earlier in range(micro_idx + 1):
            key_acc[earlier] = (
                key_acc[earlier] + own_key_grads[earlier * tok_rows : (earlier + 1) * tok_rows]
            )
            value_acc[earlier] = (
                value_acc[earlier] + own_value_grads[earlier * tok_rows : (earlier + 1) * tok_rows]
            )
        cosines, sines = rotary_tables(positions, HEAD)
        grad_joined = jnp.concatenate(
            [
                rotate(query_grads * 0.125, cosines, -sines, HEAD),
                rotate(key_acc[micro_idx], cosines, -sines, HEAD),
                value_acc[micro_idx],
            ],
            -1,
        ).astype(jnp.bfloat16)
        tokens = inputs[0, micro_idx].astype(jnp.float32)
        scale_one = rms_scale(tokens)
        gain_one = gain_attn.astype(jnp.float32)
        normed = (tokens * scale_one * gain_one).astype(jnp.bfloat16)
        grad_qkv = add_into(grad_qkv, tdot(normed, grad_joined))
        grad_first = dott(grad_joined, mat_qkv)
        grad_tokens, gain_one_grad = norm_backward(tokens, scale_one, gain_one, grad_first)
        grad_g1 = add_into(grad_g1, gain_one_grad)
        input_grads[micro_idx] = grad_res + grad_tokens
    red_g1, red_qkv, red_out, red_g2, red_sin, red_sout, red_ein, red_eout = (
        lax.psum_scatter(
            grad_g1.astype(jnp.bfloat16), "dp", scatter_dimension=0, tiled=True
        ).astype(jnp.float32),
        lax.psum_scatter(
            grad_qkv.astype(jnp.bfloat16), "dp", scatter_dimension=0, tiled=True
        ).astype(jnp.float32),
        lax.psum_scatter(
            grad_out.astype(jnp.bfloat16), "dp", scatter_dimension=0, tiled=True
        ).astype(jnp.float32),
        lax.psum_scatter(
            grad_g2.astype(jnp.bfloat16), "dp", scatter_dimension=0, tiled=True
        ).astype(jnp.float32),
        lax.psum_scatter(
            grad_sin.astype(jnp.bfloat16), "dp", scatter_dimension=0, tiled=True
        ).astype(jnp.float32),
        lax.psum_scatter(
            grad_sout.astype(jnp.bfloat16), "dp", scatter_dimension=0, tiled=True
        ).astype(jnp.float32),
        lax.psum_scatter(
            grad_ein.astype(jnp.bfloat16), "dp", scatter_dimension=1, tiled=True
        ).astype(jnp.float32),
        lax.psum_scatter(
            grad_eout.astype(jnp.bfloat16), "dp", scatter_dimension=1, tiled=True
        ).astype(jnp.float32),
    )
    sum_g1, sum_qkv, sum_out, sum_g2, sum_sin, sum_sout = lax.psum(
        (red_g1, red_qkv, red_out, red_g2, red_sin, red_sout), ("expert", "context")
    )
    sum_ein, sum_eout = (
        lax.psum(red_ein.astype(jnp.bfloat16), "context").astype(jnp.float32),
        lax.psum(red_eout.astype(jnp.bfloat16), "context").astype(jnp.float32),
    )
    output = jnp.stack(outputs, 0)[None]
    grad_input = jnp.stack(input_grads, 0)[None]
    return (
        output,
        grad_input,
        sum_g1,
        sum_qkv,
        sum_out,
        sum_g2,
        sum_sin,
        sum_sout,
        sum_ein,
        sum_eout,
    )


def solution(mesh):
    placed = (
        P(("expert", "dp"), None, "context", None),
        P(("expert", "dp"), None, "context"),
        P(("expert", "dp"), None, "context"),
        P(("expert", "dp"), None, "context", None),
        P(("expert", "dp"), None, "context", None),
        P("dp"),
        P("dp", None),
        P("dp", None),
        P("dp"),
        P("dp", None),
        P("dp", None),
        P("expert", "dp", None),
        P("expert", "dp", None),
        P(("expert", "dp"), None, "context", None),
    )
    return jax.shard_map(
        body,
        mesh=mesh,
        in_specs=placed,
        out_specs=(
            P(("expert", "dp"), None, "context", None),
            P(("expert", "dp"), None, "context", None),
            P("dp"),
            P("dp", None),
            P("dp", None),
            P("dp"),
            P("dp", None),
            P("dp", None),
            P("expert", "dp", None),
            P("expert", "dp", None),
        ),
        check_vma=False,
    )
```

profile of v0, /device:TPU:0, one launch (start us, length us, event | category | flops | bytes accessed | tf_op | source)
XLA Modules:
  0.0 2003.6 jit_solution(7188637147787042870)
XLA Ops:
  8.6 5.2 all-gather.1
  15.3 46.4 %all-gather.15.cloned.1.call-done = bf16[768,2304]{1,0:T(8,128)(2,1)} async-done(((bf16[384,2304]{1,0:T(8,128)(2,1)}), bf16[768,2304]{1,0:T(8,128)(2,1)}) %all-gather.15.cloned.1.call-update) | async-done | bytes 3538960 | tf_op jit(solution)/shard_map/all_gather | solution.py:144
  77.6 11.0 all-gather
  88.6 4.3 all-gather.2
  107.6 34.3 %all-gather.17.cloned.1.call-done = bf16[1024,768]{0,1:T(8,128)(2,1)} async-done(((bf16[256,768]{0,1:T(8,128)(2,1)}), bf16[1024,768]{0,1:T(8,128)(2,1)}) %all-gather.17.cloned.1.call-update) | async-done | bytes 1572880 | tf_op jit(solution)/shard_map/all_gather | solution.py:221
  150.3 4.9 fusion.99
  155.2 9.0 all-gather.21.cloned.1.call-done
  167.5 6.7 scatter_custom_fusion
  178.6 8.3 scatter_custom_fusion.2
  186.9 12.0 all-gather.3
  201.9 4.9 all-to-all-start.4
  206.8 39.2 %all-gather.27.cloned.1.call-done = bf16[1,768,4096]{2,1,0:T(8,128)(2,1)} async-done(((bf16[1,384,4096]{2,1,0:T(8,128)(2,1)}), bf16[1,768,4096]{2,1,0:T(8,128)(2,1)}) %all-gather.27.cloned.1.call-update) | async-done | bytes 6291472 | tf_op jit(solution)/shard_map/all_gather | solution.py:149
  246.0 13.3 convolution_bitcast_fusion.1
  259.4 33.0 %all-gather.29.cloned.1.call-done = bf16[1,2048,768]{2,1,0:T(8,128)(2,1)} async-done(((bf16[1,1024,768]{2,1,0:T(8,128)(2,1)}), bf16[1,2048,768]{2,1,0:T(8,128)(2,1)}) %all-gather.29.cloned.1.call-update) | async-done | bytes 3145744 | tf_op jit(solution)/shard_map/all_gather | solution.py:150
  292.4 13.3 fusion.46
  309.2 10.7 fusion.62
  323.7 50.6 %all-gather.23.cloned.1.call-done = bf16[768,4096]{1,0:T(8,128)(2,1)} async-done(((bf16[384,4096]{1,0:T(8,128)(2,1)}), bf16[768,4096]{1,0:T(8,128)(2,1)}) %all-gather.23.cloned.1.call-update) | async-done | bytes 6291472 | tf_op jit(solution)/shard_map/all_gather | solution.py:147
  374.4 6.6 fusion.251
  381.0 39.9 %all-gather.25.cloned.1.call-done = bf16[2048,768]{1,0:T(8,128)(2,1)} async-done(((bf16[1024,768]{1,0:T(8,128)(2,1)}), bf16[2048,768]{1,0:T(8,128)(2,1)}) %all-gather.25.cloned.1.call-update) | async-done | bytes 3145744 | tf_op jit(solution)/shard_map/all_gather | solution.py:148
  420.9 6.4 multiply_convert_fusion.7
  435.2 51.3 %all-gather.31.cloned.1.call-done = bf16[2048,768]{0,1:T(8,128)(2,1)} async-done(((bf16[512,768]{0,1:T(8,128)(2,1)}), bf16[2048,768]{0,1:T(8,128)(2,1)}) %all-gather.31.cloned.1.call-update) | async-done | bytes 3145744 | tf_op jit(solution)/shard_map/all_gather | solution.py:221
  486.5 14.9 select_reduce_fusion
  501.4 11.3 fusion
  512.7 38.0 %all-gather.33.cloned.1.call-done = bf16[2048,768]{1,0:T(8,128)(2,1)} async-done(((bf16[512,768]{1,0:T(8,128)(2,1)}), bf16[2048,768]{1,0:T(8,128)(2,1)}) %all-gather.33.cloned.1.call-update) | async-done | bytes 3145744 | tf_op jit(solution)/shard_map/all_gather | solution.py:222
  550.8 5.2 copy.81
  556.0 11.9 fusion.96
  570.3 5.0 multiply_reduce_fusion.2
  575.3 7.7 scatter_custom_fusion.1
  583.0 4.5 all-to-all-start.2
  587.8 5.9 scatter_custom_fusion.3
  594.9 12.8 all-to-all-done.2
  611.4 12.4 convolution_bitcast_fusion
  623.8 7.6 all-to-all-done.6
  631.4 12.4 fusion.47
  647.2 10.6 fusion.65
  661.6 4.7 fusion.252
  669.6 11.9 all-to-all-done.7
  689.6 6.3 multiply_reduce_fusion.3
  704.3 17.1 multiply_convert_fusion
  721.4 8.8 convolution_convert_fusion
  730.3 12.9 fusion.48
  749.8 7.8 multiply_convert_fusion.1
  761.0 7.7 fusion.74
  768.8 6.2 fusion.253
  775.0 6.7 fusion.59
  781.7 13.6 fusion.41
  795.4 13.5 fusion.40
  821.3 4.6 add_convert_fusion
  826.0 6.4 fusion.84
  832.4 9.4 fusion.83
  845.1 6.4 reduce-scatter.15.cloned.1.call-done
  852.5 37.2 %reduce-scatter.13.cloned.1.call-done = bf16[256,768]{0,1:T(8,128)(2,1)} async-done(((bf16[1024,768]{0,1:T(8,128)(2,1)}), bf16[256,768]{0,1:T(8,128)(2,1)}) %reduce-scatter.13.cloned.1.call-update) | async-done | bytes 393232 | tf_op jit(solution)/shard_map/reduce_scatter | solution.py:387
  892.4 34.3 %reduce-scatter.17.cloned.1.call-done = bf16[256,768]{0,1:T(8,128)(2,1)} async-done(((bf16[1024,768]{0,1:T(8,128)(2,1)}), bf16[256,768]{0,1:T(8,128)(2,1)}) %reduce-scatter.17.cloned.1.call-update) | async-done | bytes 393232 | tf_op jit(solution)/shard_map/reduce_scatter | solution.py:390
  935.0 6.7 fusion.68
  945.5 25.6 %reduce-scatter.29.cloned.1.call-done = bf16[1,1024,768]{2,1,0:T(8,128)(2,1)} async-done(((bf16[1,2048,768]{2,1,0:T(8,128)(2,1)}), bf16[1,1024,768]{2,1,0:T(8,128)(2,1)}) %reduce-scatter.29.cloned.1.call-update) | async-done | bytes 1572880 | tf_op jit(solution)/shard_map/reduce_scatter | solution.py:444
  971.1 79.4 %reduce-scatter.27.cloned.1.call-done = bf16[1,384,4096]{2,1,0:T(8,128)(2,1)} async-done(((bf16[1,768,4096]{2,1,0:T(8,128)(2,1)}), bf16[1,384,4096]{2,1,0:T(8,128)(2,1)}) %reduce-scatter.27.cloned.1.call-update) | async-done | bytes 3145744 | tf_op jit(solution)/shard_map/reduce_scatter | solution.py:441
  1050.5 7.7 fusion.71
  1076.6 5.4 all-to-all-done.3
  1093.2 27.3 %reduce-scatter.25.cloned.1.call-done = bf16[1024,768]{1,0:T(8,128)(2,1)} async-done(((bf16[2048,768]{1,0:T(8,128)(2,1)}), bf16[1024,768]{1,0:T(8,128)(2,1)}) %reduce-scatter.25.cloned.1.call-update) | async-done | bytes 1572880 | tf_op jit(solution)/shard_map/reduce_scatter | solution.py:438
  1126.8 4.9 all-reduce.4
  1136.5 64.1 %reduce-scatter.23.cloned.1.call-done = bf16[384,4096]{1,0:T(8,128)(2,1)} async-done(((bf16[768,4096]{1,0:T(8,128)(2,1)}), bf16[384,4096]{1,0:T(8,128)(2,1)}) %reduce-scatter.23.cloned.1.call-update) | async-done | bytes 3145744 | tf_op jit(solution)/shard_map/reduce_scatter | solution.py:435
  1200.5 50.5 %reduce-scatter.19.cloned.1.call-done = bf16[384,2304]{1,0:T(8,128)(2,1)} async-done(((bf16[768,2304]{1,0:T(8,128)(2,1)}), bf16[384,2304]{1,0:T(8,128)(2,1)}) %reduce-scatter.19.cloned.1.call-update) | async-done | bytes 1769488 | tf_op jit(solution)/shard_map/reduce_scatter | solution.py:426
  1251.0 738.2 %all-reduce.9 = (f32[384]{0:T(512)}, f32[384,2304]{1,0:T(8,128)}, f32[384,768]{1,0:T(8,128)}, f32[384]{0:T(512)}, f32[384,4096]{1,0:T(8,128)}, /*index=5*/f32[1024,768]{1,0:T(8,128)}) all-reduce(f32[384]{0:T(512)S(1)} %dynamic-slice_convert_fusion.1, ...), channel_id=1, replica_groups=mesh['expert'=4,'context'=4,'dp'=2] {'expert','context'}, use_global_device_ids=true, to_apply=%region_35.36 | all-reduce | flops 3539712 | bytes 21239808 | tf_op jit(solution)/shard_map/psum | solution.py:448
  1989.2 5.5 convert_element_type.423
  (433 shorter events, 184.2 us)
Async XLA Ops:
  7.2 54.5 %all-gather.15.cloned.1.call-start = ((), (), s32[]{:S(2)}) async-start(), calls=%async_computation.18 | async-start | bytes 5308416 | tf_op jit(solution)/shard_map/all_gather | solution.py:144
  7.9 97.1 %all-gather.19.cloned.1.call-start = ((), (), s32[]{:S(2)}) async-start(), calls=%async_computation.20 | async-start | bytes 1966080 | tf_op jit(solution)/shard_map/all_gather | solution.py:222
  13.9 83.7 %copy-start.77 = (f32[768]{0:T(1024)}, f32[768]{0:T(1024)S(1)}, u32[]{:S(2)}) copy-start(f32[768]{0:T(1024)S(1)} %reshape.1102) | copy-start | bytes 9220
  15.3 49.7 %copy-start.89 = (f32[256]{0:T(256)}, f32[256]{0:T(256)S(1)}, u32[]{:S(2)}) copy-start(f32[256]{0:T(256)S(1)} %get-tuple-element.116) | copy-start | bytes 3076
  15.3 82.3 %copy-start.87 = (f32[256]{0:T(256)}, f32[256]{0:T(256)S(1)}, u32[]{:S(2)}) copy-start(f32[256]{0:T(256)S(1)} %get-tuple-element.115) | copy-start | bytes 3076
  65.7 76.1 %all-gather.17.cloned.1.call-start = ((), (), s32[]{:S(2)}) async-start(), calls=%async_computation.19 | async-start | bytes 1966080 | tf_op jit(solution)/shard_map/all_gather | solution.py:221
  66.7 36.0 %copy-start.79 = (f32[256,32]{0,1:T(8,128)}, f32[256,32]{0,1:T(8,128)S(1)}, u32[]{:S(2)}) copy-start(f32[256,32]{0,1:T(8,128)S(1)} %get-tuple-element.98) | copy-start | bytes 98308
  71.3 92.9 %all-gather.21.cloned.1.call-start = ((), (), s32[]{:S(2)}) async-start(), calls=%async_computation.21 | async-start | bytes 1769472 | tf_op jit(solution)/shard_map/all_gather | solution.py:145
  71.9 174.1 %all-gather.27.cloned.1.call-start = ((), (), s32[]{:S(2)}) async-start(), calls=%async_computation.24 | async-start | bytes 9437184 | tf_op jit(solution)/shard_map/all_gather | solution.py:149
  72.5 219.9 %all-gather.29.cloned.1.call-start = ((), (), s32[]{:S(2)}) async-start(), calls=%async_computation.25 | async-start | bytes 4718592 | tf_op jit(solution)/shard_map/all_gather | solution.py:150
  73.1 22.1 %copy-start.98 = (f32[1,2,256,2]{2,3,1,0:T(2,128)S(1)}, f32[1,2,256,2]{2,3,1,0:T(2,128)}, u32[]{:S(2)}) copy-start(f32[1,2,256,2]{2,3,1,0:T(2,128)} %param.18) | copy-start | bytes 12292
  73.1 23.1 %copy-start.16 = (bf16[1,2,256,768]{3,2,1,0:T(8,128)(2,1)S(1)}, bf16[1,2,256,768]{3,2,1,0:T(8,128)(2,1)}, u32[]{:S(2)}) copy-start(bf16[1,2,256,768]{3,2,1,0:T(8,128)(2,1)} %param.27) | copy-start | bytes 2359300
  73.1 301.2 %all-gather.23.cloned.1.call-start = ((), (), s32[]{:S(2)}) async-start(), calls=%async_computation.22 | async-start | bytes 9437184 | tf_op jit(solution)/shard_map/all_gather | solution.py:147
  73.9 23.7 %copy-start.3 = (bf16[1,2,256,768]{3,2,1,0:T(8,128)(2,1)S(1)}, bf16[1,2,256,768]{3,2,1,0:T(8,128)(2,1)}, u32[]{:S(2)}) copy-start(bf16[1,2,256,768]{3,2,1,0:T(8,128)(2,1)} %param.14) | copy-start | bytes 2359300
  73.9 347.0 %all-gather.25.cloned.1.call-start = ((), (), s32[]{:S(2)}) async-start(), calls=%async_computation.23 | async-start | bytes 4718592 | tf_op jit(solution)/shard_map/all_gather | solution.py:148
  74.7 411.9 %all-gather.31.cloned.1.call-start = ((), (), s32[]{:S(2)}) async-start(), calls=%async_computation.26 | async-start | bytes 3932160 | tf_op jit(solution)/shard_map/all_gather | solution.py:221
  95.0 332.3 %copy-start.91 = (s32[1024]{0:T(1024)}, s32[1024]{0:T(1024)S(1)}, u32[]{:S(2)}) copy-start(s32[1024]{0:T(1024)S(1)} %pad_clamp_fusion.1) | copy-start | bytes 12292
  96.2 52.8 %copy-start.26 = (pred[256,1024]{1,0:T(8,128)(4,1)}, pred[256,1024]{1,0:T(8,128)(4,1)S(1)}, u32[]{:S(2)}) copy-start(pred[256,1024]{1,0:T(8,128)(4,1)S(1)} %or_and_fusion.1) | copy-start | bytes 786436
  167.5 206.9 %copy-start.30 = (bf16[256,768]{1,0:T(8,128)(2,1)}, bf16[256,768]{1,0:T(8,128)(2,1)S(1)}, u32[]{:S(2)}) copy-start(bf16[256,768]{1,0:T(8,128)(2,1)S(1)} %multiply_convert_fusion.15) | copy-start | bytes 1179652
  174.2 26.8 %copy-start.38 = (bf16[256,768]{1,0:T(8,128)(2,1)S(1)}, bf16[256,768]{1,0:T(8,128)(2,1)}, u32[]{:S(2)}) copy-start(bf16[256,768]{1,0:T(8,128)(2,1)} %slice.419) | copy-start | bytes 1179652
  174.2 27.7 %all-to-all-start = ((bf16[4,256,768]{2,1,0:T(8,128)(2,1)}), bf16[4,256,768]{2,1,0:T(8,128)(2,1)S(1)}, u32[]{:S(2)}, u32[]{:S(2)}) async-start(bf16[4,256,768]{2,1,0:T(8,128)(2,1)} %bitcast.18), calls=%async_computation | async-start | bytes 3145728 | tf_op jit(solution)/shard_map/all_to_all | solution.py:265
  177.9 372.8 %all-gather.33.cloned.1.call-start = ((), (), s32[]{:S(2)}) async-start(), calls=%async_computation.27 | async-start | bytes 3932160 | tf_op jit(solution)/shard_map/all_gather | solution.py:222
  201.9 57.5 %copy-start.28 = (bf16[4,256,768]{2,1,0:T(8,128)(2,1)}, bf16[4,256,768]{2,1,0:T(8,128)(2,1)S(1)}, u32[]{:S(2)}) copy-start(bf16[4,256,768]{2,1,0:T(8,128)(2,1)S(1)} %all-to-all-done) | copy-start | bytes 4718596
  201.9 57.4 %all-to-all-start.4 = ((bf16[4,256,768]{2,1,0:T(8,128)(2,1)}), bf16[4,256,768]{2,1,0:T(8,128)(2,1)}, u32[]{:S(2)}, u32[]{:S(2)}) async-start(bf16[4,256,768]{2,1,0:T(8,128)(2,1)} %bitcast.368), calls=%async_computation.4 | async-start | bytes 3145728 | tf_op jit(solution)/shard_map/all_to_all | solution.py:306
  320.0 107.3 %all-to-all-start.5 = ((bf16[4,256,768]{2,1,0:T(8,128)(2,1)}), bf16[4,256,768]{2,1,0:T(8,128)(2,1)S(1)}, u32[]{:S(2)}, u32[]{:S(2)}) async-start(bf16[4,256,768]{2,1,0:T(8,128)(2,1)} %fusion.62), calls=%async_computation.5 | async-start | bytes 3145728 | tf_op jit(solution)/shard_map/all_to_all | solution.py:334
  323.7 97.2 %copy-start.17 = (bf16[1,2,256,768]{3,2,1,0:T(8,128)(2,1)S(1)}, bf16[1,2,256,768]{3,2,1,0:T(8,128)(2,1)}, u32[]{:S(2)}) copy-start(bf16[1,2,256,768]{3,2,1,0:T(8,128)(2,1)} %param.27) | copy-start | bytes 2359300
  430.0 56.5 %copy-start.35 = (f32[256,12,32]{0,2,1:T(8,128)S(1)}, f32[256,12,32]{0,2,1:T(8,128)}, u32[]{:S(2)}) copy-start(f32[256,12,32]{0,2,1:T(8,128)} %get-tuple-element.58) | copy-start | bytes 1179652
  583.0 24.7 %all-to-all-start.2 = ((bf16[4,256,768]{2,1,0:T(8,128)(2,1)}), bf16[4,256,768]{2,1,0:T(8,128)(2,1)}, u32[]{:S(2)}, u32[]{:S(2)}) async-start(bf16[4,256,768]{2,1,0:T(8,128)(2,1)} %bitcast.369), calls=%async_computation.2 | async-start | bytes 3145728 | tf_op jit(solution)/shard_map/all_to_all | solution.py:265
  593.7 87.9 %copy-start.93 = (s32[1024]{0:T(1024)}, s32[1024]{0:T(1024)S(1)}, u32[]{:S(2)}) copy-start(s32[1024]{0:T(1024)S(1)} %pad_clamp_fusion) | copy-start | bytes 12292
  607.6 23.8 %all-to-all-start.6 = ((bf16[4,256,768]{2,1,0:T(8,128)(2,1)}), bf16[4,256,768]{2,1,0:T(8,128)(2,1)S(1)}, u32[]{:S(2)}, u32[]{:S(2)}) async-start(bf16[4,256,768]{2,1,0:T(8,128)(2,1)} %bitcast.370), calls=%async_computation.6 | async-start | bytes 3145728 | tf_op jit(solution)/shard_map/all_to_all | solution.py:306
  657.8 23.7 %all-to-all-start.7 = ((bf16[4,256,768]{2,1,0:T(8,128)(2,1)}), bf16[4,256,768]{2,1,0:T(8,128)(2,1)S(1)}, u32[]{:S(2)}, u32[]{:S(2)}) async-start(bf16[4,256,768]{2,1,0:T(8,128)(2,1)} %fusion.65), calls=%async_computation.7 | async-start | bytes 3145728 | tf_op jit(solution)/shard_map/all_to_all | solution.py:334
  661.5 180.2 %reduce-scatter.11.cloned.1.call-start = ((), (), s32[]{:S(2)}) async-start(), calls=%async_computation.28 | async-start | bytes 3932160 | tf_op jit(solution)/shard_map/reduce_scatter | solution.py:387
  696.5 112.4 %copy-start.12 = (f32[256,768]{1,0:T(8,128)}, f32[256,768]{1,0:T(8,128)S(1)}, u32[]{:S(2)}) copy-start(f32[256,768]{1,0:T(8,128)S(1)} %get-tuple-element.67) | copy-start | bytes 2359300
  696.5 114.1 %copy-start.10 = (f32[256,768]{1,0:T(8,128)}, f32[256,768]{1,0:T(8,128)S(1)}, u32[]{:S(2)}) copy-start(f32[256,768]{1,0:T(8,128)S(1)} %get-tuple-element.66) | copy-start | bytes 2359300
  730.2 121.2 %reduce-scatter.15.cloned.1.call-start = ((), (), s32[]{:S(2)}) async-start(), calls=%async_computation.30 | async-start | bytes 3932160 | tf_op jit(solution)/shard_map/reduce_scatter | solution.py:390
  743.2 146.5 %reduce-scatter.13.cloned.1.call-start = ((), (), s32[]{:S(2)}) async-start(), calls=%async_computation.29 | async-start | bytes 1966080 | tf_op jit(solution)/shard_map/reduce_scatter | solution.py:387
  760.9 165.8 %reduce-scatter.17.cloned.1.call-start = ((), (), s32[]{:S(2)}) async-start(), calls=%async_computation.31 | async-start | bytes 1966080 | tf_op jit(solution)/shard_map/reduce_scatter | solution.py:390
  768.7 202.4 %reduce-scatter.29.cloned.1.call-start = ((), (), s32[]{:S(2)}) async-start(), calls=%async_computation.37 | async-start | bytes 4718592 | tf_op jit(solution)/shard_map/reduce_scatter | solution.py:444
  781.7 268.8 %reduce-scatter.27.cloned.1.call-start = ((), (), s32[]{:S(2)}) async-start(), calls=%async_computation.36 | async-start | bytes 9437184 | tf_op jit(solution)/shard_map/reduce_scatter | solution.py:441
  808.9 284.3 %reduce-scatter.21.cloned.1.call-start = ((), (), s32[]{:S(2)}) async-start(), calls=%async_computation.33 | async-start | bytes 1769472 | tf_op jit(solution)/shard_map/reduce_scatter | solution.py:429
  812.2 308.3 %reduce-scatter.25.cloned.1.call-start = ((), (), s32[]{:S(2)}) async-start(), calls=%async_computation.35 | async-start | bytes 4718592 | tf_op jit(solution)/shard_map/reduce_scatter | solution.py:438
  817.8 382.7 %reduce-scatter.23.cloned.1.call-start = ((), (), s32[]{:S(2)}) async-start(), calls=%async_computation.34 | async-start | bytes 9437184 | tf_op jit(solution)/shard_map/reduce_scatter | solution.py:435
  825.9 425.1 %reduce-scatter.19.cloned.1.call-start = ((), (), s32[]{:S(2)}) async-start(), calls=%async_computation.32 | async-start | bytes 5308416 | tf_op jit(solution)/shard_map/reduce_scatter | solution.py:426
  841.7 49.1 %copy-start.41 = (f32[256,12,64]{0,2,1:T(8,128)S(1)}, f32[256,12,64]{0,2,1:T(8,128)}, u32[]{:S(2)}) copy-start(f32[256,12,64]{0,2,1:T(8,128)} %fusion.84) | copy-start | bytes 2359300
  852.5 75.4 %copy-start.50 = (bf16[256,768]{0,1:T(8,128)(2,1)}, bf16[256,768]{0,1:T(8,128)(2,1)S(1)}, u32[]{:S(2)}) copy-start(bf16[256,768]{0,1:T(8,128)(2,1)S(1)} %slice.280) | copy-start | bytes 1179652
  852.5 39.5 %copy-start.40 = (f32[256,12,64]{0,2,1:T(8,128)S(1)}, f32[256,12,64]{0,2,1:T(8,128)}, u32[]{:S(2)}) copy-start(f32[256,12,64]{0,2,1:T(8,128)} %fusion.83) | copy-start | bytes 2359300
  892.0 37.3 %copy-start.52 = (bf16[256,12,64]{0,2,1:T(8,128)(2,1)}, bf16[256,12,64]{0,2,1:T(8,128)(2,1)S(1)}, u32[]{:S(2)}) copy-start(bf16[256,12,64]{0,2,1:T(8,128)(2,1)S(1)} %pad_maximum_fusion.31) | copy-start | bytes 1179652
  892.0 36.0 %copy-start.5 = (bf16[1,2,256,768]{3,2,1,0:T(8,128)(2,1)S(1)}, bf16[1,2,256,768]{3,2,1,0:T(8,128)(2,1)}, u32[]{:S(2)}) copy-start(bf16[1,2,256,768]{3,2,1,0:T(8,128)(2,1)} %param.14) | copy-start | bytes 2359300
  892.0 36.0 %copy-start.78 = (f32[768]{0:T(1024)S(1)}, f32[768]{0:T(1024)}, u32[]{:S(2)}) copy-start(f32[768]{0:T(1024)} %copy-done.77) | copy-start | bytes 9220
  892.0 36.0 %copy-start.88 = (f32[256]{0:T(256)S(1)}, f32[256]{0:T(256)}, u32[]{:S(2)}) copy-start(f32[256]{0:T(256)} %copy-done.87) | copy-start | bytes 3076
  892.0 37.3 %copy-start.54 = (bf16[256,12,64]{0,2,1:T(8,128)(2,1)}, bf16[256,12,64]{0,2,1:T(8,128)(2,1)S(1)}, u32[]{:S(2)}) copy-start(bf16[256,12,64]{0,2,1:T(8,128)(2,1)S(1)} %pad_maximum_fusion.30) | copy-start | bytes 1179652
  892.4 36.9 %copy-start.56 = (bf16[256,12,64]{0,2,1:T(8,128)(2,1)}, bf16[256,12,64]{0,2,1:T(8,128)(2,1)S(1)}, u32[]{:S(2)}) copy-start(bf16[256,12,64]{0,2,1:T(8,128)(2,1)S(1)} %pad_maximum_fusion.33) | copy-start | bytes 1179652
  892.4 36.9 %copy-start.58 = (bf16[256,12,64]{0,2,1:T(8,128)(2,1)}, bf16[256,12,64]{0,2,1:T(8,128)(2,1)S(1)}, u32[]{:S(2)}) copy-start(bf16[256,12,64]{0,2,1:T(8,128)(2,1)S(1)} %pad_maximum_fusion.32) | copy-start | bytes 1179652
  941.7 116.5 %all-to-all-start.1 = ((bf16[4,256,768]{2,1,0:T(8,128)(2,1)}), bf16[4,256,768]{2,1,0:T(8,128)(2,1)S(1)}, u32[]{:S(2)}, u32[]{:S(2)}) async-start(bf16[4,256,768]{2,1,0:T(8,128)(2,1)} %fusion.68), calls=%async_computation.1 | async-start | bytes 3145728 | tf_op jit(solution)/shard_map/all_to_all | solution.py:261
  945.3 1043.9 %all-reduce.8.cloned.1.call-start = ((), (), s32[]{:S(2)}) async-start(), calls=%async_computation.38 | async-start | bytes 9437184 | tf_op jit(solution)/shard_map/psum | solution.py:452
  1058.3 23.8 %all-to-all-start.3 = ((bf16[4,256,768]{2,1,0:T(8,128)(2,1)}), bf16[4,256,768]{2,1,0:T(8,128)(2,1)S(1)}, u32[]{:S(2)}, u32[]{:S(2)}) async-start(bf16[4,256,768]{2,1,0:T(8,128)(2,1)} %fusion.71), calls=%async_computation.3 | async-start | bytes 3145728 | tf_op jit(solution)/shard_map/all_to_all | solution.py:261
  1089.2 31.3 %copy-start.53 = (bf16[256,12,64]{0,2,1:T(8,128)(2,1)S(1)}, bf16[256,12,64]{0,2,1:T(8,128)(2,1)}, u32[]{:S(2)}) copy-start(bf16[256,12,64]{0,2,1:T(8,128)(2,1)} %copy-done.52) | copy-start | bytes 1179652
  1089.2 31.3 %copy-start.55 = (bf16[256,12,64]{0,2,1:T(8,128)(2,1)S(1)}, bf16[256,12,64]{0,2,1:T(8,128)(2,1)}, u32[]{:S(2)}) copy-start(bf16[256,12,64]{0,2,1:T(8,128)(2,1)} %copy-done.54) | copy-start | bytes 1179652
  1093.2 30.8 %copy-start.6 = (bf16[1,2,256,768]{3,2,1,0:T(8,128)(2,1)S(1)}, bf16[1,2,256,768]{3,2,1,0:T(8,128)(2,1)}, u32[]{:S(2)}) copy-start(bf16[1,2,256,768]{3,2,1,0:T(8,128)(2,1)} %param.14) | copy-start | bytes 2359300
  1093.2 30.8 %copy-start.51 = (bf16[256,768]{0,1:T(8,128)(2,1)S(1)}, bf16[256,768]{0,1:T(8,128)(2,1)}, u32[]{:S(2)}) copy-start(bf16[256,768]{0,1:T(8,128)(2,1)} %copy-done.50) | copy-start | bytes 1179652
  1093.2 30.8 %copy-start.57 = (bf16[256,12,64]{0,2,1:T(8,128)(2,1)S(1)}, bf16[256,12,64]{0,2,1:T(8,128)(2,1)}, u32[]{:S(2)}) copy-start(bf16[256,12,64]{0,2,1:T(8,128)(2,1)} %copy-done.56) | copy-start | bytes 1179652
  1093.2 30.8 %copy-start.59 = (bf16[256,12,64]{0,2,1:T(8,128)(2,1)S(1)}, bf16[256,12,64]{0,2,1:T(8,128)(2,1)}, u32[]{:S(2)}) copy-start(bf16[256,12,64]{0,2,1:T(8,128)(2,1)} %copy-done.58) | copy-start | bytes 1179652
  1133.3 117.7 %copy-start.75 = (bf16[384,768]{1,0:T(8,128)(2,1)S(1)}, bf16[384,768]{1,0:T(8,128)(2,1)}, u32[]{:S(2)}) copy-start(bf16[384,768]{1,0:T(8,128)(2,1)} %reduce-scatter.21.cloned.1.call-done) | copy-start | bytes 1769476
  1135.2 115.8 %copy-start.62 = (bf16[1024,768]{1,0:T(8,128)(2,1)S(1)}, bf16[1024,768]{1,0:T(8,128)(2,1)}, u32[]{:S(2)}) copy-start(bf16[1024,768]{1,0:T(8,128)(2,1)} %reduce-scatter.25.cloned.1.call-done) | copy-start | bytes 4718596
  (77 other events, 390.8 us)
Sparse Core Ops, SparseCore 0:
  9.6 52.0 all-gather.14
  65.9 37.1 all-gather.18
  105.2 36.5 all-gather.16
  143.2 20.9 all-gather.20
  165.6 80.3 all-gather.26
  247.4 44.9 all-gather.28
  294.0 80.3 all-gather.22
  375.9 44.9 all-gather.24
  423.0 63.4 all-gather.30
  488.5 62.1 all-gather.32
  730.4 57.9 reduce-scatter.10
  791.1 60.2 reduce-scatter.14
  854.3 35.3 reduce-scatter.12
  892.4 34.2 reduce-scatter.16
  928.8 42.2 reduce-scatter.28
  973.4 77.0 reduce-scatter.26
  1053.2 21.7 reduce-scatter.20
  1077.1 43.3 reduce-scatter.24
  1123.4 77.0 reduce-scatter.22
  1203.3 47.6 reduce-scatter.18
  1253.4 324.0 all-reduce.7
where the time goes:
time: 2020 us; the launch traced here: 2000 us
  blocking collectives  776 us (38%)
  waiting for transfers between devices  708 us (35%)
  matrix products  313 us (15%)
  local copies, waits for them, and re-layouts  83 us (4%)
  other arithmetic  73.2 us (4%)
  starting transfers between devices  33.2 us (2%)
    psum x1, blocking collectives, body(): lax.psum((red_g1, red_qkv, red_out, red_g2, red_sin, red_sout), ('expert'...  738 us
    all_gather x2, waiting for transfers between devices, body(): lax.all_gather(keys_sofar, 'context', axis=0, tiled=True)  85.6 us
    reduce_scatter x1, waiting for transfers between devices, body(): lax.psum_scatter(grad_ein.astype(jnp.bfloat16), 'dp', scatter_dimension=1...  79.4 us
    reduce_scatter x1, waiting for transfers between devices, body(): lax.psum_scatter(grad_sin.astype(jnp.bfloat16), 'dp', scatter_dimension=0...  64.1 us
    all_gather x1, waiting for transfers between devices, fetch_all(): lax.all_gather(shards[4], 'dp', axis=0, tiled=True)  50.6 us
    reduce_scatter x1, waiting for transfers between devices, body(): lax.psum_scatter(grad_qkv.astype(jnp.bfloat16), 'dp', scatter_dimension=0...  50.5 us
    all_gather x1, waiting for transfers between devices, fetch_all(): lax.all_gather(shards[1], 'dp', axis=0, tiled=True)  46.4 us
    reduce_scatter x2, waiting for transfers between devices, body(): lax.psum_scatter(value_grads.reshape(count, width).astype(jnp.bfloat16),...  40.6 us
  transfers between devices with their start and end apart: 29, of which 21 were waited for; matrix products, arithmetic and copies ran while one was open for 17% of the time, Pallas kernels for 0%

commit v1 on v0

v1 whole, which is shorter than its diff:
```python
import functools
import math

import jax
import jax.numpy as jnp
from jax import lax
from jax.experimental import pallas as pl
from jax.experimental.pallas import tpu as pltpu
from jax.sharding import PartitionSpec as P

HEAD = 64
MICRO = 2
TILE = 256
HALF = 128
EPSILON = 1e-05
ROPE_BASE = 10000.0
MASKED = -3e30
HIDDEN = 1 << 20
BF = jnp.bfloat16
F32 = jnp.float32
NT = (((1,), (1,)), ((), ()))
TN = (((0,), (0,)), ((), ()))
VMEM_LIMIT = 60 << 20
FB = 512


def dot(left, right, dims=(((1,), (0,)), ((), ()))):
    return lax.dot_general(left, right, dims, preferred_element_type=F32)


def rms_scale(values):
    return lax.rsqrt(jnp.mean(values * values, -1, keepdims=True) + EPSILON)


def low_lanes(rows):
    return lax.broadcasted_iota(jnp.int32, (rows, HALF), 1) < HEAD


def swap_heads(first, second):
    low = low_lanes(HALF)
    return (
        jnp.where(low, first, pltpu.roll(second, HEAD, 1)),
        jnp.where(low, pltpu.roll(first, HEAD, 1), second),
    )


def rotate(tile, cosines, sines):
    lane = lax.broadcasted_iota(jnp.int32, tile.shape, 1)
    partner = jnp.where(
        lane % HEAD < HEAD // 2,
        pltpu.roll(tile, HALF - HEAD // 2, 1),
        pltpu.roll(tile, HEAD // 2, 1),
    )
    return tile * cosines + partner * sines


def call(kernel, out_shape, *, grid=(), in_specs=None, out_specs=None, scratch=(), us=5):
    return pl.pallas_call(
        kernel,
        out_shape=out_shape,
        grid=grid,
        in_specs=in_specs,
        out_specs=out_specs,
        scratch_shapes=scratch,
        compiler_params=pltpu.CompilerParams(vmem_limit_bytes=VMEM_LIMIT),
        cost_estimate=price(us),
    )


def full_spec(shape):
    return pl.BlockSpec(tuple(shape), lambda *_: (0,) * len(shape))


def struct(shape, dtype):
    return jax.ShapeDtypeStruct(tuple(shape), dtype)


def pre_kernel(x_ref, gain_ref, w_ref, cos_ref, sin_ref, out_ref, *, groups):
    tokens = x_ref[0].astype(F32)
    normed = (tokens * rms_scale(tokens) * gain_ref[...]).astype(BF)
    width = tokens.shape[1]
    per = width // HEAD // groups
    cosines, sines = cos_ref[...], sin_ref[...]
    for kind in range(3):
        joined = dot(normed, w_ref[:, kind * width : (kind + 1) * width])
        for pair in range(width // HALF):
            tile = joined[:, pair * HALF : (pair + 1) * HALF]
            if kind < 2:
                tile = rotate(tile, cosines, sines)
            if kind == 0:
                tile = tile * 0.125
            for side, packed in enumerate(swap_heads(tile[:HALF], tile[HALF:])):
                head = 2 * pair + side
                out_ref[head // per, kind * per + head % per] = packed.astype(BF)


def run_pre(x, micro, gain, w, cosines, sines, groups):
    _, rows, width = x.shape
    per = width // HEAD // groups
    return call(
        functools.partial(pre_kernel, groups=groups),
        struct((groups, 3 * per, HALF, HALF), BF),
        grid=(1,),
        in_specs=[
            pl.BlockSpec((1, rows, width), lambda _: (micro, 0, 0)),
            full_spec(gain.shape),
            full_spec(w.shape),
            pl.BlockSpec((rows, HALF), lambda _: (micro, 0)),
            pl.BlockSpec((rows, HALF), lambda _: (micro, 0)),
        ],
        out_specs=full_spec((groups, 3 * per, HALF, HALF)),
        us=5,
    )(x, gain, w, cosines, sines)


def unpack(ref, index, kind_head):
    tile = ref[index, kind_head]
    return tile, pltpu.roll(tile.astype(F32), HEAD, 1).astype(BF)


def fill_keys(recvs, ks, vs, heads):
    for micro, recv in enumerate(recvs):
        for src in range(recv.shape[0]):
            base = (micro * recv.shape[0] + src) * TILE
            for h in range(heads):
                for store, kind in ((ks, 1), (vs, 2)):
                    first, second = unpack(recv, src, kind * heads + h)
                    store[h, base : base + HALF] = first
                    store[h, base + HALF : base + TILE] = second


def masked_rows(ref, index, kind_head):
    tile = ref[index, kind_head].astype(F32)
    both = jnp.concatenate([tile, pltpu.roll(tile, HEAD, 1)], 0)
    return jnp.where(low_lanes(TILE), both, 0.0)


def pack_rows(values):
    return jnp.where(low_lanes(HALF), values[:HALF], pltpu.roll(values[HALF:], HEAD, 1))


def attend_kernel(*refs, micro, heads, groups):
    recvs = refs[: micro + 1]
    key_tag, query_tag, out_ref, lse_ref, ks, vs, scores = refs[micro + 1 :]
    step = pl.program_id(0)

    @pl.when(step == 0)
    def _():
        fill_keys(recvs, ks, vs, heads)

    count = groups * micro + jnp.minimum(step + 2, groups)
    queries = [masked_rows(recvs[micro], step, h).astype(BF) for h in range(heads)]
    tag = query_tag[...]
    same = lax.broadcasted_iota(jnp.int32, (TILE, TILE), 0) == lax.broadcasted_iota(
        jnp.int32, (TILE, TILE), 1
    )

    def first_pass(j, tops):
        keys = pl.ds(pl.multiple_of(j * TILE, TILE), TILE)
        seen = (key_tag[j] <= tag) | (same & (j == groups * micro + step))
        new = []
        for h in range(heads):
            part = jnp.where(seen, dot(queries[h], ks[h, keys, :], NT), MASKED)
            scores[h, :, keys] = part
            new.append(jnp.maximum(tops[h], jnp.maximum(part[:, :HALF], part[:, HALF:])))
        return tuple(new)

    tops = lax.fori_loop(
        0, count, first_pass, (jnp.full((TILE, HALF), MASKED, F32),) * heads
    )
    tops = [jnp.max(top, 1, keepdims=True) for top in tops]

    def second_pass(j, carry):
        keys = pl.ds(pl.multiple_of(j * TILE, TILE), TILE)
        sums, totals = carry
        new_sums, new_totals = [], []
        for h in range(heads):
            expo = jnp.exp(scores[h, :, keys] - tops[h])
            new_sums.append(sums[h] + (expo[:, :HALF] + expo[:, HALF:]))
            new_totals.append(totals[h] + dot(expo.astype(BF), vs[h, keys, :]))
        return tuple(new_sums), tuple(new_totals)

    zero = (jnp.zeros((TILE, HALF), F32),) * heads
    sums, totals = lax.fori_loop(0, count, second_pass, (zero, zero))
    lane = lax.broadcasted_iota(jnp.int32, (TILE, HALF), 1)
    logs = jnp.zeros((TILE, HALF), F32)
    for h in range(heads):
        total = jnp.sum(sums[h], 1, keepdims=True)
        out_ref[step, h] = pack_rows(totals[h] / total).astype(BF)
        logs = jnp.where(lane == h, tops[h] + jnp.log(total), logs)
    lse_ref[step] = logs.T[:8]


def run_attend(recvs, key_tag, query_tag, groups):
    micro = len(recvs) - 1
    heads = recvs[0].shape[1] // 3
    held = groups * (micro + 1) * TILE
    return call(
        functools.partial(attend_kernel, micro=micro, heads=heads, groups=groups),
        (struct((groups, heads, HALF, HALF), BF), struct((groups, 8, TILE), F32)),
        grid=(groups,),
        in_specs=[full_spec(r.shape) for r in recvs]
        + [full_spec(key_tag.shape), pl.BlockSpec((TILE, 1), lambda s: (micro * groups + s, 0))],
        out_specs=(full_spec((groups, heads, HALF, HALF)), full_spec((groups, 8, TILE))),
        scratch=[
            pltpu.VMEM((heads, held, HALF), BF),
            pltpu.VMEM((heads, held, HALF), BF),
            pltpu.VMEM((heads, TILE, held), F32),
        ],
        us=15 + 11 * micro,
    )(*recvs, key_tag, query_tag)


def attend_back_kernel(*refs, micro, heads, groups):
    recvs = refs[: micro + 1]
    refs = refs[micro + 1 :]
    grad_ref, out_ref, lse_ref, key_tag, query_tag = refs[:5]
    refs = refs[5:]
    if micro == 0:
        pay_ref, early_k, early_v, ks, vs, dk, dv = refs
    else:
        early_k, early_v, pay_ref, pay0_ref, ks, vs, dk, dv = refs
    step = pl.program_id(0)

    @pl.when(step == 0)
    def _():
        fill_keys(recvs, ks, vs, heads)
        dk[...] = jnp.zeros_like(dk)
        dv[...] = jnp.zeros_like(dv)
        if micro > 0:
            dk[:, : groups * TILE] = early_k[...]
            dv[:, : groups * TILE] = early_v[...]

    count = groups * micro + jnp.minimum(step + 2, groups)
    queries = [masked_rows(recvs[micro], step, h).astype(BF) for h in range(heads)]
    grads_f = [masked_rows(grad_ref, step, h) for h in range(heads)]
    grads = [g.astype(BF) for g in grads_f]
    ones = jnp.ones((8, HALF), F32)
    deltas = [
        lax.dot_general(
            ones,
            grads_f[h] * masked_rows(out_ref, step, h),
            NT,
            precision=lax.Precision.HIGHEST,
            preferred_element_type=F32,
        )[:1]
        for h in range(heads)
    ]
    logs = [lse_ref[step, h : h + 1, :] for h in range(heads)]
    tag = query_tag[groups * micro + step]
    same = lax.broadcasted_iota(jnp.int32, (TILE, TILE), 0) == lax.broadcasted_iota(
        jnp.int32, (TILE, TILE), 1
    )

    def tile(j, totals):
        keys = pl.ds(pl.multiple_of(j * TILE, TILE), TILE)
        seen = (key_tag[keys, :] <= tag) | (same & (j == groups * micro + step))
        new = []
        for h in range(heads):
            key, value = ks[h, keys, :], vs[h, keys, :]
            scores = dot(key, queries[h], NT)
            probs = jnp.where(seen, jnp.exp(scores - logs[h]), 0.0)
            dv[h, keys, :] += dot(probs.astype(BF), grads[h])
            slope = (probs * (dot(value, grads[h], NT) - deltas[h])).astype(BF)
            dk[h, keys, :] += dot(slope, queries[h])
            new.append(totals[h] + dot(slope, key, TN))
        return tuple(new)

    totals = lax.fori_loop(0, count, tile, (jnp.zeros((TILE, HALF), F32),) * heads)
    for h in range(heads):
        pay_ref[step, h] = pack_rows(totals[h]).astype(BF)

    @pl.when(step == groups - 1)
    def _():
        if micro == 0:
            early_k[...] = dk[...]
            early_v[...] = dv[...]
        else:
            for src in range(groups):
                for ref, base, first in ((pay0_ref, 0, 0), (pay_ref, groups, heads)):
                    rows = slice((base + src) * TILE, (base + src + 1) * TILE)
                    for h in range(heads):
                        ref[src, first + h] = pack_rows(dk[h, rows]).astype(BF)
                        ref[src, first + heads + h] = pack_rows(dv[h, rows]).astype(BF)


def run_attend_back(recvs, grad, out, lse, key_tag, query_tag, early, groups):
    micro = len(recvs) - 1
    heads = recvs[0].shape[1] // 3
    held = groups * (micro + 1) * TILE
    pay = lambda n: struct((groups, n * heads, HALF, HALF), BF)
    part = struct((heads, groups * TILE, HALF), F32)
    args = [*recvs, grad, out, lse, key_tag, query_tag, *early]
    outs = [pay(1), part, part] if micro == 0 else [pay(3), pay(2)]
    return call(
        functools.partial(attend_back_kernel, micro=micro, heads=heads, groups=groups),
        tuple(outs),
        grid=(groups,),
        in_specs=[full_spec(a.shape) for a in args],
        out_specs=tuple(full_spec(o.shape) for o in outs),
        scratch=[
            pltpu.VMEM((heads, held, HALF), BF),
            pltpu.VMEM((heads, held, HALF), BF),
            pltpu.VMEM((heads, held, HALF), F32),
            pltpu.VMEM((heads, held, HALF), F32),
        ],
        us=23 + 20 * micro,
    )(*args)


def natural(ref, first_kind, pair, per):
    tiles = []
    for head in (2 * pair, 2 * pair + 1):
        tiles.append(ref[head // per, first_kind * per + head % per].astype(F32))
    return jnp.concatenate(swap_heads(*tiles), 0)


def post_kernel(o_ref, x_ref, w_ref, gain_ref, att_ref, res_ref, nf_ref, *, per):
    width = x_ref.shape[2]
    for pair in range(width // HALF):
        att_ref[:, pair * HALF : (pair + 1) * HALF] = natural(o_ref, 0, pair, per).astype(BF)
    residual = x_ref[0].astype(F32) + dot(att_ref[...], w_ref[...])
    res_ref[...] = residual
    nf_ref[...] = (residual * rms_scale(residual) * gain_ref[...]).astype(BF)


def run_post(mixed, x, micro, w, gain):
    _, rows, width = x.shape
    return call(
        functools.partial(post_kernel, per=mixed.shape[1]),
        (struct((rows, width), BF), struct((rows, width), F32), struct((rows, width), BF)),
        grid=(1,),
        in_specs=[
            full_spec(mixed.shape),
            pl.BlockSpec((1, rows, width), lambda _: (micro, 0, 0)),
            full_spec(w.shape),
            full_spec(gain.shape),
        ],
        out_specs=(full_spec((rows, width)),) * 3,
        us=3,
    )(mixed, x, w, gain)


def ffn_kernel(*refs, tr, spans, counts, first, gated, opened, summed, closing, parts):
    offs = refs[0]
    refs = list(refs[1:])
    take = lambda n: [refs.pop(0) for _ in range(n)]
    x_ref, dy_in = take(2)
    gate_ref = take(1)[0] if gated else None
    wg_parts, wu_parts, wo_parts = take(parts), take(parts), take(parts)
    y0, dx0 = take(2) if opened else (None, None)
    g0 = take(3) if summed else None
    y_ref, dx_ref, dwg_ref, dwu_ref, dwo_ref = take(5)
    xt, yacc, dxacc, hs, djg, dju, wg_ref, wu_ref, wo_ref = take(9)
    dy_ref = take(1)[0] if gated else dy_in
    f = pl.program_id(0)
    rows = x_ref.shape[0]

    @pl.when(f == 0)
    def _():
        xt[...] = x_ref[...].T
        if opened:
            yacc[...] = y0[...].astype(F32)
            dxacc[...] = dx0[...].astype(F32)
        else:
            yacc[...] = jnp.zeros_like(yacc)
            dxacc[...] = jnp.zeros_like(dxacc)
        if gated:
            dy_ref[...] = (dy_in[...].astype(F32) * gate_ref[...]).astype(BF)

    for index, span in enumerate(spans):
        place = pl.ds(pl.multiple_of(offs[index], HALF // 2), span)
        wg_ref[place, :] = wg_parts[index][...]
        wu_ref[place, :] = wu_parts[index][...]
        begin = offs[parts + index]

        @pl.when((f + first >= begin) & (f + first < begin + counts[index]))
        def _(index=index):
            wo_ref[...] = wo_parts[index][...]

    wg, wu, wo = wg_ref[...], wu_ref[...], wo_ref[...]

    def tile(i, carry):
        r = pl.ds(pl.multiple_of(i * tr, tr), tr)
        x = x_ref[r, :]
        g = dot(x, wg)
        u = dot(x, wu)
        dh = dot(dy_ref[r, :], wo, NT)
        sig = 1.0 / (1.0 + jnp.exp(-g))
        act = g * sig
        h = (act * u).astype(BF)
        dg = (dh * u * (sig * (1.0 + g * (1.0 - sig)))).astype(BF)
        du = (dh * act).astype(BF)
        hs[r, :] = h
        djg[r, :] = dg
        dju[r, :] = du
        yacc[r, :] += dot(h, wo)
        dxacc[r, :] += dot(dg, wg, NT) + dot(du, wu, NT)
        return carry

    lax.fori_loop(0, rows // tr, tile, 0)
    grads = [dot(xt[...], djg[...]), dot(xt[...], dju[...]), dot(hs[...], dy_ref[...], TN)]
    for k, out in enumerate((dwg_ref, dwu_ref, dwo_ref)):
        value = grads[k]
        if summed:
            value = value + g0[k][...].astype(F32)
        out[...] = value.astype(BF)

    @pl.when(f == pl.num_programs(0) - 1)
    def _():
        made = yacc[...].astype(BF)
        if gated and closing:
            made = (made.astype(F32) * gate_ref[...]).astype(BF)
        y_ref[...] = made
        dx_ref[...] = dxacc[...].astype(BF)


def run_ffn(x, dy, gate, w_in, w_out, offsets, start=None, grads=None, span=None, closing=True, tr=512, fb=FB, us=10):
    rows, d = x.shape
    ff = sum(w.shape[0] for w in w_out)
    nf = ff // fb
    first, last = span or (0, nf)
    steps = last - first
    gated = gate is not None
    parts = len(w_in)
    spans = [w.shape[0] for w in w_in]
    counts = [w.shape[0] // fb for w in w_out]
    whole = lambda a: pl.BlockSpec(
        a.shape, lambda f, o: (0,) * a.ndim, pipeline_mode=pl.Buffered(1)
    )
    args = [x, dy] + ([gate] if gated else [])
    specs = [whole(a) for a in args]
    args += list(w_in) * 2 + list(w_out)
    specs += [pl.BlockSpec((n, fb), lambda f, o: (0, f + first)) for n in spans]
    specs += [pl.BlockSpec((n, fb), lambda f, o: (0, f + first + nf)) for n in spans]
    for i, c in enumerate(counts):
        specs.append(
            pl.BlockSpec(
                (fb, d), lambda f, o, i=i, c=c: (jnp.clip(f + first - o[parts + i], 0, c - 1), 0)
            )
        )
    if start is not None:
        args += list(start)
        specs += [whole(a) for a in start]
    wide = pl.BlockSpec((d, fb), lambda f, o: (0, f))
    tall = pl.BlockSpec((fb, d), lambda f, o: (f, 0))
    if grads is not None:
        args += list(grads)
        specs += [
            pl.BlockSpec((d, fb), lambda f, o: (0, f + first)),
            pl.BlockSpec((d, fb), lambda f, o: (0, f + first)),
            pl.BlockSpec((fb, d), lambda f, o: (f + first, 0)),
        ]
    full = pl.BlockSpec((rows, d), lambda f, o: (0, 0), pipeline_mode=pl.Buffered(1))
    return pl.pallas_call(
        functools.partial(
            ffn_kernel,
            tr=math.gcd(tr, rows),
            spans=spans,
            counts=counts,
            first=first,
            gated=gated,
            opened=start is not None,
            summed=grads is not None,
            closing=closing,
            parts=parts,
        ),
        out_shape=(
            struct((rows, d), BF),
            struct((rows, d), BF),
            struct((d, steps * fb), BF),
            struct((d, steps * fb), BF),
            struct((steps * fb, d), BF),
        ),
        grid_spec=pltpu.PrefetchScalarGridSpec(
            num_scalar_prefetch=1,
            grid=(steps,),
            in_specs=specs,
            out_specs=(full, full, wide, wide, tall),
            scratch_shapes=[
                pltpu.VMEM((d, rows), BF),
                pltpu.VMEM((rows, d), F32),
                pltpu.VMEM((rows, d), F32),
                pltpu.VMEM((rows, fb), BF),
                pltpu.VMEM((rows, fb), BF),
                pltpu.VMEM((rows, fb), BF),
                pltpu.VMEM((d, fb), BF),
                pltpu.VMEM((d, fb), BF),
                pltpu.VMEM((fb, d), BF),
            ]
            + ([pltpu.VMEM((rows, d), BF)] if gated else []),
        ),
        compiler_params=pltpu.CompilerParams(vmem_limit_bytes=VMEM_LIMIT),
        cost_estimate=price(us),
    )(offsets, *args)


def price(us):
    return pl.CostEstimate(flops=int(us * 1.15e9), bytes_accessed=0, transcendentals=0)


def norm_back(values, scale, gain, grad):
    gain_grad = jnp.sum(grad * values * scale, 0, keepdims=True)
    scaled = gain * grad
    grad_in = scale * scaled - values * (scale * scale * scale) * jnp.mean(
        scaled * values, -1, keepdims=True
    )
    return grad_in, gain_grad


def mid_kernel(*refs, per, first):
    dxs, dxr, res_ref, gain_ref, cot_ref, w_ref, att_ref = refs[:7]
    if first:
        gres_ref, pay, gg_ref, gbf = refs[7:]
    else:
        att0, gbf0, gres_ref, pay, gg_ref, gw_ref, gbf = refs[7:]
    residual = res_ref[...]
    grad = dxs[...].astype(F32) + dxr[...].astype(F32)
    back, gain_grad = norm_back(residual, rms_scale(residual), gain_ref[...], grad)
    gg_ref[...] = gain_grad
    total = cot_ref[0].astype(F32) + back
    gres_ref[...] = total
    gbf[...] = total.astype(BF)
    mixed = dot(gbf[...], w_ref[...], NT)
    for pair in range(mixed.shape[1] // HALF):
        tile = mixed[:, pair * HALF : (pair + 1) * HALF]
        for side, packed in enumerate(swap_heads(tile[:HALF], tile[HALF:])):
            head = 2 * pair + side
            pay[head // per, head % per] = packed.astype(BF)
    if not first:
        gw_ref[...] = (dot(att_ref[...], gbf[...], TN) + dot(att0[...], gbf0[...], TN)).astype(BF)


def run_mid(dxs, dxr, residual, gain, cot, w, att, groups, micro, before=()):
    rows, width = residual.shape
    per = width // HEAD // groups
    args = (dxs, dxr, residual, gain, cot, w, att, *before)
    specs = [full_spec(a.shape) for a in args]
    specs[0] = pl.BlockSpec((rows, width), lambda _: (micro, 0))
    specs[4] = pl.BlockSpec((1, rows, width), lambda _: (micro, 0, 0))
    pay = (groups, per, HALF, HALF)
    outs = [struct((rows, width), F32), struct(pay, BF), struct((1, width), F32)]
    if micro == 0:
        outs.append(struct((rows, width), BF))
        scratch = []
    else:
        outs.append(struct((width, width), BF))
        scratch = [pltpu.VMEM((rows, width), BF)]
    return call(
        functools.partial(mid_kernel, per=per, first=micro == 0),
        tuple(outs),
        grid=(1,),
        in_specs=specs,
        out_specs=tuple(full_spec(o.shape) for o in outs),
        scratch=scratch,
        us=4 + micro,
    )(*args)


def fin_kernel(q0, kv0, d1, x_ref, gain_ref, w_ref, cos_ref, sin_ref, res0, res1, gin_ref, gw_ref, gj, *, per):
    width = x_ref.shape[1]
    for micro, sources in enumerate((((q0, 0), (kv0, 0), (kv0, 1)), ((d1, 0), (d1, 1), (d1, 2)))):
        rows = slice(micro * TILE, (micro + 1) * TILE)
        cosines, sines = cos_ref[rows, :], sin_ref[rows, :]
        for kind in range(3):
            for pair in range(width // HALF):
                tile = natural(*sources[kind], pair, per)
                if kind == 0:
                    tile = tile * 0.125
                if kind < 2:
                    tile = rotate(tile, cosines, -sines)
                gj[rows, kind * width + pair * HALF : kind * width + (pair + 1) * HALF] = tile.astype(BF)
    tokens = x_ref[...].astype(F32)
    scale = rms_scale(tokens)
    gain = gain_ref[...]
    normed = (tokens * scale * gain).astype(BF)
    first = dot(gj[...], w_ref[...], NT)
    back, _ = norm_back(tokens, scale, gain, first)
    gin_ref[:TILE] = res0[...] + back[:TILE]
    gin_ref[TILE:] = res1[...] + back[TILE:]
    turned = normed.T
    for kind in range(3):
        cols = slice(kind * width, (kind + 1) * width)
        gw_ref[:, cols] = dot(turned, gj[:, cols]).astype(BF)


def run_fin(parts, x, gain, w, cosines, sines, gres):
    rows, width = x.shape
    args = (*parts, x, gain, w, cosines, sines, *gres)
    outs = (struct((rows, width), F32), struct((width, 3 * width), BF))
    return call(
        functools.partial(fin_kernel, per=parts[0].shape[1]),
        outs,
        grid=(1,),
        in_specs=[full_spec(a.shape) for a in args],
        out_specs=tuple(full_spec(o.shape) for o in outs),
        scratch=[pltpu.VMEM((rows, 3 * width), BF)],
        us=11,
    )(*args)


def exchange(value, axis, mask):
    size = lax.axis_size(axis)
    return lax.ppermute(value, axis, [(i, i ^ mask) for i in range(size)])


def bits_of(size):
    return [1 << b for b in range(size.bit_length() - 1)]


def gather_xor(value, axis):
    for mask in reversed(bits_of(lax.axis_size(axis))):
        value = jnp.concatenate([value, exchange(value, axis, mask)], 0)
    return value


def scatter_xor(value, axis):
    for mask in bits_of(lax.axis_size(axis)):
        half = value.shape[0] // 2
        got = exchange(value[half:], axis, mask)
        value = (value[:half].astype(F32) + got.astype(F32)).astype(value.dtype)
    return value


def ordered(flag, mine, theirs):
    first = jnp.where(flag == 0, mine, theirs)
    second = jnp.where(flag == 0, theirs, mine)
    return jnp.concatenate([first, second], 0)


def pick(value, parts, index):
    size = value.shape[0] // parts
    return lax.dynamic_slice_in_dim(value, index * size, size, 0)


def after(value, token):
    return lax.optimization_barrier((value, token))[0]


def fetch_parts(shard, axis):
    part = exchange(pick(shard, 2, lax.axis_index(axis) % 2), "dp", 1)
    return part, exchange(part, axis, 1)


def fetch_whole(shard):
    part, other = fetch_parts(shard, "expert")
    core = lax.axis_index("expert") % 2
    return part, ordered(lax.axis_index("dp"), shard, ordered(core, part, other))


PIECES = 4


def remote(src, dst, sems, index, target):
    return pltpu.make_async_remote_copy(
        src_ref=src,
        dst_ref=dst,
        send_sem=sems[0].at[index],
        recv_sem=sems[1].at[index],
        device_id=target,
        device_id_type=pl.DeviceIdType.MESH,
    )


def reduce_kernel(*refs, owned, common):
    refs = list(refs)
    take = lambda n: [refs.pop(0) for _ in range(n)]
    own_in, com_in = take(owned), take(common)
    own_out, com_out = take(owned), take(common)
    own_buf = [take(4) for _ in range(owned)]
    com_buf = [take(6) for _ in range(common)]
    own_sems, com_sems = take(10), take(20)
    barrier = pltpu.get_barrier_semaphore()
    e, z, d = lax.axis_index("expert"), lax.axis_index("context"), lax.axis_index("dp")
    core, y = e % 2, e // 2 % 2
    mate = z + 1 - 2 * (z % 2)
    outer = (z == 0) | (z == 3)
    inner = (z == 1) | (z == 2)
    to_x = {"dp": 1 - d}
    to_core = {"expert": e + 1 - 2 * core}
    to_y = {"expert": e + 2 - 4 * y}
    to_mate = {"context": mate}
    to_mid = {"context": 3 - z}
    near = [to_x, to_core, to_y, to_mate]
    for target in near:
        pl.semaphore_signal(barrier, inc=1, device_id=target, device_id_type=pl.DeviceIdType.MESH)

    @pl.when(inner)
    def _():
        pl.semaphore_signal(barrier, inc=1, device_id=to_mid, device_id_type=pl.DeviceIdType.MESH)
        pl.semaphore_wait(barrier, 5)

    @pl.when(outer)
    def _():
        pl.semaphore_wait(barrier, 4)

    o_load, o_store = own_sems[:2]
    o_x, o_1, o_2, o_3 = [own_sems[2 + 2 * k : 4 + 2 * k] for k in range(4)]
    c_load, c_store = com_sems[:2]
    c_core, c_y, c_x, c_1, c_2, c_3, c_back, c_fore, c_last = [
        com_sems[2 + 2 * k : 4 + 2 * k] for k in range(9)
    ]

    chunks = owned * PIECES
    where = lambda c: (c // PIECES, c % PIECES)

    def o_sum(c):
        j, k = where(c)
        return own_buf[j][0].at[k]

    def o_loading(c):
        j, k = where(c)
        return pltpu.make_async_copy(own_in[j].at[d, k], o_sum(c), o_load.at[c])

    def o_storing(c):
        j, k = where(c)
        return pltpu.make_async_copy(own_buf[j][2].at[k], own_out[j].at[k], o_store.at[c])

    def o_wire(stage, c):
        j, k = where(c)
        buf = own_buf[j]
        if stage == "x":
            return remote(own_in[j].at[1 - d, k], buf[1].at[k], o_x, c, to_x)
        if stage == "1":
            return remote(o_sum(c), buf[2].at[k], o_1, c, to_mate)
        if stage == "2":
            return remote(o_sum(c), buf[3].at[k], o_2, c, to_mid)
        return remote(buf[2].at[k], own_out[j].at[k], o_3, c, to_mate)

    def o_first(c):
        j, k = where(c)
        o_loading(c).wait()
        o_wire("x", c).wait_recv()
        if c + 2 < chunks:
            o_wire("x", c + 2).start()
        own_buf[j][0][k] = own_buf[j][0][k] + own_buf[j][1][k]

        @pl.when(outer)
        def _():
            o_wire("1", c).start()

    def o_second(c):
        j, k = where(c)

        @pl.when(inner)
        def _():
            o_wire("1", c).wait_recv()
            own_buf[j][0][k] = own_buf[j][0][k] + own_buf[j][2][k]
            o_wire("2", c).start()

    def o_third(c):
        j, k = where(c)

        @pl.when(inner)
        def _():
            o_wire("2", c).wait_recv()
            own_buf[j][2][k] = own_buf[j][0][k] + own_buf[j][3][k]
            o_wire("3", c).start()
            o_storing(c).start()

    def o_fourth(c):
        @pl.when(outer)
        def _():
            o_wire("3", c).wait_recv()

    def c_loading(i, h):
        return pltpu.make_async_copy(com_in[i].at[h, core], com_buf[i][0].at[h], c_load.at[2 * i + h])

    def c_storing(i):
        return pltpu.make_async_copy(com_buf[i][4], com_out[i].at[core, y], c_store.at[i])

    def c_wire(stage, i, h=0):
        total, r_core, r_y, r_x, r_1, r_2 = com_buf[i]
        if stage == "core":
            return remote(com_in[i].at[h, 1 - core], r_core.at[h], c_core, 2 * i + h, to_core)
        if stage == "y":
            return remote(total.at[h, 1 - y], r_y.at[h], c_y, 2 * i + h, to_y)
        if stage == "x":
            return remote(total.at[1 - d, y], r_x, c_x, i, to_x)
        if stage == "1":
            return remote(total.at[d, y], r_1, c_1, i, to_mate)
        if stage == "2":
            return remote(total.at[d, y], r_2, c_2, i, to_mid)
        if stage == "3":
            return remote(r_1, com_out[i].at[core, y], c_3, i, to_mate)
        if stage == "fore":
            return remote(r_1, com_out[i].at[core, y], c_fore, i, to_y)
        if stage == "back":
            return remote(com_out[i].at[core, y], com_out[i].at[core, y], c_fore, i, to_y)
        return remote(com_out[i].at[core], com_out[i].at[core], c_last, i, to_core)

    def c_a(i):
        for h in range(2):
            c_loading(i, h).wait()
            c_wire("core", i, h).wait_recv()
        com_buf[i][0][...] = com_buf[i][0][...] + com_buf[i][1][...]
        for h in range(2):
            c_wire("y", i, h).start()

    def c_b(i):
        total, r_y = com_buf[i][0], com_buf[i][2]
        for h in range(2):
            c_wire("y", i, h).wait_recv()
            total[h, y] = total[h, y] + r_y[h]
        c_wire("x", i).start()

    def c_c(i):
        total, r_x = com_buf[i][0], com_buf[i][3]
        c_wire("x", i).wait_recv()
        total[d, y] = total[d, y] + r_x[...]

        @pl.when(outer)
        def _():
            c_wire("1", i).start()

    def c_d(i):
        total, r_1 = com_buf[i][0], com_buf[i][4]

        @pl.when(inner)
        def _():
            c_wire("1", i).wait_recv()
            total[d, y] = total[d, y] + r_1[...]
            c_wire("2", i).start()

    def c_e(i):
        total, r_1, r_2 = com_buf[i][0], com_buf[i][4], com_buf[i][5]

        @pl.when(inner)
        def _():
            c_wire("2", i).wait_recv()
            r_1[...] = total[d, y] + r_2[...]
            c_wire("3", i).start()
            c_wire("fore", i).start()
            c_storing(i).start()

    def c_f(i):
        @pl.when(outer)
        def _():
            c_wire("3", i).wait_recv()
            c_wire("back", i).start()

    def c_g(i):
        @pl.when(inner)
        def _():
            c_storing(i).wait()

        c_wire("fore", i).wait_recv()
        c_wire("last", i).start()

    def c_h(i):
        c_wire("last", i).wait_recv()

    for i in range(common):
        for h in range(2):
            c_wire("core", i, h).start()
            c_loading(i, h).start()
    for c in range(chunks):
        o_loading(c).start()
        if c < 2:
            o_wire("x", c).start()
    events = []
    for c in range(chunks):
        for lag, step in ((1, o_first), (2.5, o_second), (3.5, o_third), (4.6, o_fourth)):
            events.append((c + lag, step, c))
    for i in range(common):
        base = 2.0 * i + 0.5
        for lag, step in zip((0, 2.3, 4, 5.5, 6.6, 7.7, 8.9, 9.6), (c_a, c_b, c_c, c_d, c_e, c_f, c_g, c_h)):
            events.append((base + lag, step, i))
    for _, step, index in sorted(events, key=lambda v: v[0]):
        step(index)
    for c in range(chunks):
        o_wire("x", c).wait_send()
    for i in range(common):
        for h in range(2):
            c_wire("core", i, h).wait_send()
            c_wire("y", i, h).wait_send()
        c_wire("x", i).wait_send()
        c_wire("last", i).wait_send()

    @pl.when(outer)
    def _():
        for c in range(chunks):
            o_wire("1", c).wait_send()
        for i in range(common):
            c_wire("1", i).wait_send()
            c_wire("back", i).wait_send()

    @pl.when(inner)
    def _():
        for c in range(chunks):
            o_wire("2", c).wait_send()
            o_wire("3", c).wait_send()
            o_storing(c).wait()
        for i in range(common):
            c_wire("2", i).wait_send()
            c_wire("3", i).wait_send()
            c_wire("fore", i).wait_send()


def run_reduce(expert_grads, shared_grads, collective_id, us):
    own = [g.reshape(2, PIECES, g.shape[0] // (2 * PIECES), g.shape[1]) for g in expert_grads]
    com = []
    for g in shared_grads:
        for mask in bits_of(lax.axis_size("expert"))[2:]:
            g = g + exchange(g, "expert", mask)
        com.append(g.reshape(2, 2, 2, g.shape[0] // 8, g.shape[1]))
    chunks = len(own) * PIECES
    scratch = []
    for g in own:
        scratch += [pltpu.VMEM(g.shape[1:], BF)] * 4
    for g in com:
        small = g.shape[3:]
        scratch += [pltpu.VMEM((2, 2, *small), BF)] * 2 + [pltpu.VMEM((2, *small), BF)]
        scratch += [pltpu.VMEM(small, BF)] * 3
    dma = lambda n: pltpu.SemaphoreType.DMA((max(n, 1),))
    scratch += [dma(chunks)] * 10
    n = len(com)
    scratch += [dma(2 * n), dma(n)] + [dma(2 * n)] * 4 + [dma(n)] * 14
    anywhere = pl.BlockSpec(memory_space=pl.ANY)
    outs = [struct(g.shape[1:], BF) for g in own] + [struct((2, 2, *g.shape[3:]), BF) for g in com]
    got = pl.pallas_call(
        functools.partial(reduce_kernel, owned=len(own), common=n),
        out_shape=tuple(outs),
        in_specs=[anywhere] * (len(own) + n),
        out_specs=(anywhere,) * len(outs),
        scratch_shapes=scratch,
        compiler_params=pltpu.CompilerParams(
            vmem_limit_bytes=VMEM_LIMIT, collective_id=collective_id, has_side_effects=True
        ),
        cost_estimate=price(us),
    )(*own, *com)
    return [g.reshape(-1, g.shape[-1]).astype(F32) for g in got]


def body(
    inputs,
    keep_flags,
    block_ids,
    expert_ids,
    gate_weights,
    norm_attn,
    w_qkv,
    w_attn_out,
    norm_ffn,
    w_shared_in,
    w_shared_out,
    w_expert_in,
    w_expert_out,
    cotangent,
):
    width = w_qkv.shape[1] // 3
    rows = inputs.shape[2]
    groups = lax.axis_size("context")
    experts = lax.axis_size("expert")
    z = lax.axis_index("context")
    seq_rows = rows * groups
    x = inputs[0]
    cot = cotangent[0].reshape(MICRO * rows, width)

    positions = (
        jnp.arange(MICRO, dtype=jnp.int32)[:, None] * seq_rows
        + z * rows
        + jnp.arange(rows, dtype=jnp.int32)[None, :]
    ).reshape(-1)
    half = HEAD // 2
    freq = jnp.exp(-math.log(ROPE_BASE) * jnp.arange(half, dtype=F32) * 2.0 / HEAD)
    angle = positions.astype(F32)[:, None] * freq[None, :]
    cos_t, sin_t = jnp.cos(angle), jnp.sin(angle)
    cosines = jnp.concatenate([cos_t] * 4, -1)
    sines = jnp.concatenate([-sin_t, sin_t, -sin_t, sin_t], -1)

    blocks = block_ids[0] + 8 * jnp.arange(MICRO, dtype=jnp.int32)[:, None]
    key_tags = jnp.where(keep_flags[0] == 1, blocks, HIDDEN)
    tags = jnp.broadcast_to(jnp.stack([blocks, key_tags])[None], (groups, 2, MICRO, rows))
    tags = lax.all_to_all(tags, "context", 0, 0, tiled=True).transpose(1, 2, 0, 3)
    query_row = tags[0].reshape(MICRO * groups, 1, rows)
    key_row = tags[1].reshape(MICRO * groups, 1, rows)
    query_col = tags[0].reshape(-1, 1)
    key_col = tags[1].reshape(-1, 1)

    gains = jnp.stack([norm_attn, norm_ffn])
    both = ordered(lax.axis_index("dp"), gains[None], exchange(gains, "dp", 1)[None]).astype(F32)
    gain_attn = both[:, 0].reshape(1, width)
    gain_ffn = both[:, 1].reshape(1, width)
    qkv_part, mat_qkv = fetch_whole(w_qkv)
    out_part, mat_out = fetch_whole(w_attn_out)

    ids = expert_ids[0].reshape(MICRO * rows, -1)
    gates = gate_weights[0].reshape(MICRO * rows, -1)
    per_expert = jnp.sum(
        jnp.where(
            ids[None] == jnp.arange(experts, dtype=jnp.int32)[:, None, None], gates[None], 0.0
        ),
        -1,
    )
    all_gates = gather_xor(per_expert[None], "expert")
    gate = lax.dynamic_index_in_dim(all_gates, lax.axis_index("expert"), 1, False).reshape(-1, 1)

    core = lax.axis_index("expert") % 2
    dp = lax.axis_index("dp")
    k_half, f_half = width // 2, w_shared_out.shape[0]
    ein_parts = (w_expert_in[0], *fetch_parts(after(w_expert_in[0], qkv_part), "context"))
    eout_parts = (w_expert_out[0], *fetch_parts(after(w_expert_out[0], out_part), "context"))
    sin_parts = (w_shared_in, *fetch_parts(after(w_shared_in, ein_parts[1]), "expert"))
    sout_parts = (w_shared_out, *fetch_parts(after(w_shared_out, eout_parts[1]), "expert"))

    def offsets(bit):
        places = [2 * (1 - dp) + bit, 2 * (1 - dp) + 1 - bit]
        return jnp.stack(
            [dp * k_half]
            + [p * (k_half // 2) for p in places]
            + [dp * f_half // FB]
            + [p * (f_half // 2) // FB for p in places]
        )

    all_cot = [gather_xor(cotangent[0, m], "expert") for m in range(MICRO)]
    gate = [
        lax.dynamic_index_in_dim(
            all_gates.reshape(experts, experts, MICRO, rows)[:, :, m], lax.axis_index("expert"), 1, False
        ).reshape(-1, 1)
        for m in range(MICRO)
    ]

    recvs, mixed, lses, att, res, nf = [], [], [], [], [], []
    for micro in range(MICRO):
        pay = run_pre(x, micro, gain_attn, mat_qkv, cosines, sines, groups)
        recvs.append(lax.all_to_all(pay, "context", 0, 0, tiled=True))
    for micro in range(MICRO):
        out, lse = run_attend(recvs[: micro + 1], key_row, query_col, groups)
        mixed.append(out)
        lses.append(lse)
    for micro in range(MICRO):
        got = lax.all_to_all(mixed[micro], "context", 0, 0, tiled=True)
        a, r, n = run_post(got, x, micro, mat_out, gain_ffn)
        att.append(a)
        res.append(r)
        nf.append(n)

    capacity = 4 * rows // experts

    def expert_pass(m, grads):
        hidden, grad, weight = gather_xor(nf[m], "expert"), all_cot[m], gate[m]
        if capacity < rows:
            chosen = weight.reshape(-1, rows) > 0
            slots = jnp.cumsum(chosen.astype(jnp.int32), 1) - 1
            select = (
                chosen[:, None] & (slots[:, None] == jnp.arange(capacity, dtype=jnp.int32)[:, None])
            ).astype(BF)
            squeeze = lambda v: jnp.einsum("bcr,brd->bcd", select, v.reshape(-1, rows, width)).reshape(-1, width)
            spread = lambda v: jnp.einsum("bcr,bcd->brd", select, v.reshape(-1, capacity, width)).reshape(-1, width)
            hidden, grad = squeeze(hidden), squeeze(grad)
            weight = jnp.sum(select.astype(F32) * weight.reshape(-1, 1, rows), -1).reshape(-1, 1)
        made, dx, *grads = run_ffn(
            hidden, grad, weight, ein_parts, eout_parts, offsets(z % 2), grads=grads, us=38
        )
        if capacity < rows:
            made, dx = spread(made), spread(dx)
        return scatter_xor(dx, "expert"), scatter_xor(made, "expert"), grads

    dx0, routed0, g_expert = expert_pass(0, None)
    shared, dx_shared, *g_shared = run_ffn(
        jnp.concatenate(nf, 0), cot, None, sin_parts, sout_parts, offsets(core), us=21
    )
    dx1, routed1, g_expert = expert_pass(1, g_expert)
    output = jnp.stack(
        [
            (res[m] + shared[m * rows : (m + 1) * rows].astype(F32) + r.astype(F32)).astype(BF)
            for m, r in enumerate((routed0, routed1))
        ]
    )

    gres0, pay0, gg0, gbf0 = run_mid(
        dx_shared, dx0, res[0], gain_ffn, cotangent[0], mat_out, att[0], groups, 0
    )
    grad0 = lax.all_to_all(pay0, "context", 0, 0, tiled=True)
    back_q0, early_k, early_v = run_attend_back(
        recvs[:1], grad0, mixed[0], lses[0], key_col, query_row, (), groups
    )
    q0 = lax.all_to_all(back_q0, "context", 0, 0, tiled=True)
    gres1, pay1, gg1, g_out = run_mid(
        dx_shared, dx1, res[1], gain_ffn, cotangent[0], mat_out, att[1], groups, 1, (att[0], gbf0)
    )
    grad1 = lax.all_to_all(pay1, "context", 0, 0, tiled=True)
    back1, back_kv0 = run_attend_back(
        recvs, grad1, mixed[1], lses[1], key_col, query_row, (early_k, early_v), groups
    )
    kv0 = lax.all_to_all(back_kv0, "context", 0, 0, tiled=True)
    d1 = lax.all_to_all(back1, "context", 0, 0, tiled=True)
    grad_input, g_qkv = run_fin(
        (q0, kv0, d1),
        x.reshape(MICRO * rows, width),
        gain_attn,
        mat_qkv,
        cosines,
        sines,
        (gres0, gres1),
    )

    g_gain_ffn = gg0 + gg1
    total = g_gain_ffn
    for axis in ("expert", "context", "dp"):
        for mask in bits_of(lax.axis_size(axis)):
            total = total + exchange(total, axis, mask)
    r_gain_ffn = pick(total[0], 2, dp)
    e_gate, e_up, r_eout, r_gate, r_up, r_sout, r_out, r_qkv = run_reduce(
        g_expert, [*g_shared, g_out, g_qkv], 1, 160
    )
    r_sin = jnp.concatenate([r_gate, r_up], 1)
    r_gain_attn = jnp.sum(w_qkv.astype(F32) * r_qkv, 1) / norm_attn.astype(F32)
    r_ein = jnp.concatenate([e_gate, e_up], 1)
    return (
        output[None],
        grad_input.reshape(1, MICRO, rows, width),
        r_gain_attn,
        r_qkv,
        r_out,
        r_gain_ffn,
        r_sin,
        r_sout,
        r_ein[None],
        r_eout[None],
    )


def solution(mesh):
    tokens = P(("expert", "dp"), None, "context", None)
    flags = P(("expert", "dp"), None, "context")
    placed = (
        tokens,
        flags,
        flags,
        tokens,
        tokens,
        P("dp"),
        P("dp", None),
        P("dp", None),
        P("dp"),
        P("dp", None),
        P("dp", None),
        P("expert", "dp", None),
        P("expert", "dp", None),
        tokens,
    )
    return jax.shard_map(
        body,
        mesh=mesh,
        in_specs=placed,
        out_specs=(
            tokens,
            tokens,
            P("dp"),
            P("dp", None),
            P("dp", None),
            P("dp"),
            P("dp", None),
            P("dp", None),
            P("expert", "dp", None),
            P("expert", "dp", None),
        ),
        check_vma=False,
    )
```

time: 2020 us -> 761 us (0.38)
  blocking collectives: 776 us -> 0 us
  waiting for transfers between devices: 708 us -> 141 us
  Pallas kernels: 0 us -> 445 us
  matrix products: 313 us -> 0 us
  local copies, waits for them, and re-layouts: 83 us -> 38.2 us
  starting transfers between devices: 33.2 us -> 75.2 us
  other arithmetic: 73.2 us -> 49.9 us
    psum x1 -> x0, blocking collectives: 738 us -> none  [body(): lax.psum((red_g1, red_qkv, red_out, red_g2, red_sin, red_sout), ('expert'...]
    pallas_call x0 -> x15, Pallas kernels: none -> 445 us  [the longest x1 196 us: run_reduce(): pl.pallas_call(functools.partial(reduce_kernel, owned=len(own), common=n)...]
    all_gather x10 -> x0, waiting for transfers between devices: 342 us -> none  [the longest x2 85.6 us: body(): lax.all_gather(keys_sofar, 'context', axis=0, tiled=True)]
    reduce_scatter x10 -> x0, waiting for transfers between devices: 325 us -> none  [the longest x1 79.4 us: body(): lax.psum_scatter(grad_ein.astype(jnp.bfloat16), 'dp', scatter_dimension=1...]
    dot_general x48 -> x0, matrix products: 313 us -> none  [the longest x8 31.3 us: dott(): lax.dot_general(left, right, (((1,), (1,)), ((), ())), preferred_element_...]
    ppermute x0 -> x36, waiting for transfers between devices: none -> 89 us  [exchange(): return lax.ppermute(value, axis, [(i, i ^ mask) for i in range(size)])]
    all_gather x4 -> x0, blocking collectives: 32.6 us -> none  [the longest x2 23 us: body(): lax.all_gather(tags_sofar, 'context', axis=0, tiled=True)]
    ppermute x0 -> x36, starting transfers between devices: none -> 28.9 us  [exchange(): return lax.ppermute(value, axis, [(i, i ^ mask) for i in range(size)])]
  transfers between devices with their start and end apart: 29 -> 46, of which waited for: 21 -> 14; matrix products, arithmetic and copies ran while one was open for 17% -> 9% of each run, Pallas kernels for 0% -> 32%
where the time goes in v1:
time: 761 us; the launch traced here: 751 us
  Pallas kernels  445 us (58%)
  waiting for transfers between devices  141 us (19%)
  starting transfers between devices  75.2 us (10%)
  other arithmetic  49.9 us (7%)
  local copies, waits for them, and re-layouts  38.2 us (5%)
    pallas_call x1, Pallas kernels, run_reduce(): pl.pallas_call(functools.partial(reduce_kernel, owned=len(own), common=n)...  196 us
    pallas_call x3, Pallas kernels, run_ffn(): pl.pallas_call(functools.partial(ffn_kernel, tr=math.gcd(tr, rows), spans...  108 us
    ppermute x36, waiting for transfers between devices, exchange(): return lax.ppermute(value, axis, [(i, i ^ mask) for i in range(size)])  89 us
    pallas_call x2, Pallas kernels, run_attend_back(): call(functools.partial(attend_back_kernel, micro=micro, heads=heads, grou...  65.6 us
    pallas_call x2, Pallas kernels, run_attend(): call(functools.partial(attend_kernel, micro=micro, heads=heads, groups=gr...  39.8 us
    ppermute x36, starting transfers between devices, exchange(): return lax.ppermute(value, axis, [(i, i ^ mask) for i in range(size)])  28.9 us
    all_to_all x2, waiting for transfers between devices, body(): recvs.append(lax.all_to_all(pay, 'context', 0, 0, tiled=True))  24.2 us
    all_to_all x1, waiting for transfers between devices, body(): kv0 = lax.all_to_all(back_kv0, 'context', 0, 0, tiled=True)  17 us
  transfers between devices with their start and end apart: 46, of which 14 were waited for; matrix products, arithmetic and copies ran while one was open for 9% of the time, Pallas kernels for 32%

profile of v1, /device:TPU:0, one launch (start us, length us, event | category | flops | bytes accessed | tf_op | source)
XLA Modules:
  0.0 750.5 jit_solution(14350475467464326872)
XLA Ops:
  1.9 3.0 collective-permute-start.1
  5.8 5.4 all-to-all-start.1
  11.2 13.4 %collective-permute-done.1 = bf16[192,2304]{1,0:T(8,128)(2,1)S(1)} collective-permute-done((bf16[192,2304]{1,0:T(8,128)(2,1)S(1)}, bf16[192,2304]{1,0:T(8,128)(2,1)S(1)}, u32[]{:S(2)}, u32[]{:S(2)}) %collective-permute-start.1) | collective-permute-done | bytes 884768 | tf_op jit(solution)/shard_map/ppermute | solution.py:604
  29.7 2.0 pad_maximum_fusion.w_ref
  31.7 5.0 shard_map.216
  36.7 5.1 all-to-all-start.3
  41.8 5.0 shard_map.213
  46.8 24.2 %all-to-all-done.3.refs_1_ = bf16[4,9,128,128]{3,2,1,0:T(8,128)(2,1)S(1)} async-done(((bf16[4,9,128,128]{3,2,1,0:T(8,128)(2,1)}), bf16[4,9,128,128]{3,2,1,0:T(8,128)(2,1)S(1)}, u32[]{:S(2)}, u32[]{:S(2)}) %all-to-all-start.3) | async-done | bytes 1179680 | tf_op jit(solution)/shard_map/all_to_all | solution.py:1027
  71.0 4.3 all-to-all-start
  75.3 1.6 constant_dynamic-slice_fusion.7
  79.2 1.6 collective-permute-start.13
  83.5 35.7 %collective-permute-done.3 = bf16[192,768]{1,0:T(8,128)(2,1)} collective-permute-done((bf16[192,768]{1,0:T(8,128)(2,1)S(1)}, bf16[192,768]{1,0:T(8,128)(2,1)}, u32[]{:S(2)}, u32[]{:S(2)}) %collective-permute-start.3) | collective-permute-done | bytes 294944 | tf_op jit(solution)/shard_map/ppermute | solution.py:604
  119.2 1.9 reshape_squeeze.32.refs_2_.refs_3_
  121.7 2.1 constant_dynamic-slice_fusion.5
  128.7 25.4 %shard_map.217 = (bf16[4,3,128,128]{3,2,1,0:T(8,128)(2,1)}, f32[4,8,256]{2,1,0:T(8,128)}) custom-call(bf16[4,9,128,128]{3,2,1,0:T(8,128)(2,1)} %all-to-all-done.refs_0_, bf16[4,9,128,128]{3,2,1,0:T(8,128)(2,1)} %copy-done.17, s32[8,1,256]{2,1,0:T(1,128)} %bitcast.97, s32[2048,1]{1,0:T(8,128)} %reshape_squeeze.32.refs_2_.refs_3_), custom_call_target="tpu_custom_call" | custom-call | flops 29899999232 | tf_op jit(solution)/shard_map/pallas_call | solution.py:198
  154.2 4.7 all-to-all-start.4
  158.9 14.4 %shard_map.214 = (bf16[4,3,128,128]{3,2,1,0:T(8,128)(2,1)}, f32[4,8,256]{2,1,0:T(8,128)}) custom-call(bf16[4,9,128,128]{3,2,1,0:T(8,128)(2,1)} %all-to-all-done.refs_0_, s32[8,1,256]{2,1,0:T(1,128)} %bitcast.98, s32[2048,1]{1,0:T(8,128)} %reshape_squeeze.32.refs_2_.refs_3_), custom_call_target="tpu_custom_call" | custom-call | flops 17250000896 | tf_op jit(solution)/shard_map/pallas_call | solution.py:198
  174.1 5.3 all-to-all-start.2
  181.5 3.1 shard_map.218
  186.1 4.8 all-to-all-done.2.o_ref
  191.6 3.1 shard_map.215
  204.1 2.1 constant_dynamic-slice_fusion.4
  206.1 2.6 pad_maximum_fusion.8
  208.7 2.3 collective-permute-start.9
  216.0 1.7 copy.61.refs_3_
  217.7 1.7 copy.62.refs_3_
  220.6 2.6 reshape_squeeze.33.refs_4_.refs_5_
  223.2 2.4 pad_maximum_fusion.3.refs_2_
  225.6 2.4 pad_maximum_fusion.5.refs_2_
  228.0 5.6 collective-permute-done.9.refs_10_
  234.2 2.5 pad_maximum_fusion.2.refs_1_
  236.7 14.5 %collective-permute-done.18.refs_12_ = bf16[512,768]{1,0:T(8,128)(2,1)} collective-permute-done((bf16[512,768]{1,0:T(8,128)(2,1)}, bf16[512,768]{1,0:T(8,128)(2,1)}, u32[]{:S(2)}, u32[]{:S(2)}) %collective-permute-start.18) | collective-permute-done | bytes 786464 | tf_op jit(solution)/shard_map/ppermute | solution.py:604
  251.2 41.7 %shard_map.220 = (bf16[1024,768]{1,0:T(8,128)(2,1)}, bf16[1024,768]{1,0:T(8,128)(2,1)}, bf16[768,2048]{1,0:T(8,128)(2,1)}, bf16[768,2048]{1,0:T(8,128)(2,1)}, bf16[2048,768]{1,0:T(8,128)(2,1)}) custom-call(s32[6]{0:T(128)} %stack.83.refs_0_, bf16[1024,768]{1,0:T(8,128)(2,1)} %pad_maximum_fusion.2.refs_1_, bf16[1024,768]{1,0:T(8,128)(2,1)} %pad_maximum_fusion.3.refs_2_, ...), custom_call_target="tpu_custom_call" | custom-call | flops 43699998720 | tf_op jit(solution)/shard_map/pallas_call | solution.py:455
  294.1 2.2 pad_maximum_fusion.4.refs_1_
  296.4 42.9 %shard_map.221 = (bf16[1024,768]{1,0:T(8,128)(2,1)}, bf16[1024,768]{1,0:T(8,128)(2,1)}, bf16[768,2048]{1,0:T(8,128)(2,1)}, bf16[768,2048]{1,0:T(8,128)(2,1)}, bf16[2048,768]{1,0:T(8,128)(2,1)}) custom-call(s32[6]{0:T(128)} %stack.83.refs_0_, bf16[1024,768]{1,0:T(8,128)(2,1)} %pad_maximum_fusion.4.refs_1_, bf16[1024,768]{1,0:T(8,128)(2,1)} %pad_maximum_fusion.5.refs_2_, ...), custom_call_target="tpu_custom_call" | custom-call | flops 43699998720 | tf_op jit(solution)/shard_map/pallas_call | solution.py:455
  341.9 23.6 %shard_map.219 = (bf16[512,768]{1,0:T(8,128)(2,1)}, bf16[512,768]{1,0:T(8,128)(2,1)}, bf16[768,2048]{1,0:T(8,128)(2,1)}, bf16[768,2048]{1,0:T(8,128)(2,1)}, bf16[2048,768]{1,0:T(8,128)(2,1)}) custom-call(s32[6]{0:T(128)} %stack.78.refs_0_, bf16[512,768]{1,0:T(8,128)(2,1)} %get-tuple-element.130.refs_1_, bf16[512,768]{1,0:T(8,128)(2,1)} %bitcast.80, ...), custom_call_target="tpu_custom_call" | custom-call | flops 24149999616 | tf_op jit(solution)/shard_map/pallas_call | solution.py:455
  366.9 1.6 collective-permute-start.30
  368.5 1.8 add_convert_fusion.5.refs_1_
  370.3 3.6 shard_map.222
  373.9 3.5 all-to-all-start.5
  378.8 4.6 shard_map.224
  383.4 5.8 all-to-all-done.5.refs_1_
  389.2 3.5 all-to-all-start.7
  392.7 22.5 %shard_map.223 = (bf16[4,3,128,128]{3,2,1,0:T(8,128)(2,1)}, f32[3,1024,128]{2,1,0:T(8,128)}, f32[3,1024,128]{2,1,0:T(8,128)}) custom-call(bf16[4,9,128,128]{3,2,1,0:T(8,128)(2,1)} %all-to-all-done.refs_0_, bf16[4,3,128,128]{3,2,1,0:T(8,128)(2,1)} %copy-done.21, bf16[4,3,128,128]{3,2,1,0:T(8,128)(2,1)} %get-tuple-element.62.refs_2_, ...), custom_call_target="tpu_custom_call" | custom-call | flops 26449999872 | tf_op jit(solution)/shard_map/pallas_call | solution.py:295
  415.1 5.0 all-to-all-start.6
  420.2 43.1 %shard_map.225 = (bf16[4,9,128,128]{3,2,1,0:T(8,128)(2,1)}, bf16[4,6,128,128]{3,2,1,0:T(8,128)(2,1)}) custom-call(bf16[4,9,128,128]{3,2,1,0:T(8,128)(2,1)} %all-to-all-done.refs_0_, bf16[4,9,128,128]{3,2,1,0:T(8,128)(2,1)} %copy-done.17, bf16[4,3,128,128]{3,2,1,0:T(8,128)(2,1)} %copy-done.22, bf16[4,3,128,128]{3,2,1,0:T(8,128)(2,1)} %get-tuple-element.65.refs_3_, ...), custom_call_target="tpu_custom_call" | custom-call | flops 49450000384 | tf_op jit(solution)/shard_map/pallas_call | solution.py:295
  464.1 5.2 all-to-all-start.8
  470.8 17.0 %all-to-all-done.8.kv0 = bf16[4,6,128,128]{3,2,1,0:T(8,128)(2,1)} async-done(((bf16[4,6,128,128]{3,2,1,0:T(8,128)(2,1)}), bf16[4,6,128,128]{3,2,1,0:T(8,128)(2,1)}, u32[]{:S(2)}, u32[]{:S(2)}) %all-to-all-start.8) | async-done | bytes 786464 | tf_op jit(solution)/shard_map/all_to_all | solution.py:1087
  487.9 4.4 all-to-all-start.9
  492.3 1.6 add_convert_fusion.2
  496.5 1.6 collective-permute-start.20
  499.9 13.6 %collective-permute-done.32 = f32[1,768]{1,0:T(1,128)S(1)} collective-permute-done((f32[1,768]{1,0:T(1,128)S(1)}, f32[1,768]{1,0:T(1,128)S(1)}, u32[]{:S(2)}, u32[]{:S(2)}) %collective-permute-start.32) | collective-permute-done | bytes 3104 | tf_op jit(solution)/shard_map/ppermute | solution.py:604
  513.4 1.7 collective-permute-start.33
  515.2 2.2 collective-permute-done.33
  517.4 2.3 collective-permute-start.34
  519.7 1.9 fusion.1
  523.4 2.1 collective-permute-done.35
  526.1 10.9 %shard_map.226 = (f32[512,768]{1,0:T(8,128)}, bf16[768,2304]{1,0:T(8,128)(2,1)}) custom-call(bf16[4,3,128,128]{3,2,1,0:T(8,128)(2,1)} %copy-done.20, bf16[4,6,128,128]{3,2,1,0:T(8,128)(2,1)} %all-to-all-done.8.kv0, bf16[4,9,128,128]{3,2,1,0:T(8,128)(2,1)} %all-to-all-done.9.d1, bf16[512,768]{1,0:T(8,128)(2,1)} %bitcast.112, f32[1,768]{1,0:T(1,128)} %bitcast.103, ...), custom_call_target="tpu_custom_call" | custom-call | flops 12650000384 | tf_op jit(solution)/shard_map/pallas_call | solution.py:591
  536.9 196.1 %shard_map.227 = (bf16[4,96,2048]{2,1,0:T(8,128)(2,1)}, bf16[4,96,2048]{2,1,0:T(8,128)(2,1)}, bf16[4,256,768]{2,1,0:T(8,128)(2,1)}, bf16[2,2,96,2048]{3,2,1,0:T(...) custom-call(bf16[2,4,96,2048]{3,2,1,0:T(8,128)(2,1)} %bitcast.114, ...), custom_call_target="tpu_custom_call" | custom-call | flops 184000004096 | tf_op jit(solution)/shard_map/pallas_call | solution.py:921
  733.0 3.8 multiply_reduce_fusion
  737.5 1.9 bitcast_convert_fusion.1
  739.4 2.0 bitcast_convert_fusion.2
  743.3 3.5 fusion
  746.8 3.5 maximum_convert_fusion
  (199 shorter events, 57.1 us)
Async XLA Ops:
  0.6 4.3 copy-start.26
  0.7 4.3 copy-start.34
  0.7 4.4 copy-start.32
  0.7 4.4 copy-start.33
  1.9 22.7 %collective-permute-start.1 = (bf16[192,2304]{1,0:T(8,128)(2,1)S(1)}, bf16[192,2304]{1,0:T(8,128)(2,1)S(1)}, u32[]{:S(2)}, u32[]{:S(2)}) collective-permute-start(bf16[192,2304]{1,0:T(8,128)(2,1)S(1)} %constant_dynamic-slice_fusion.9), channel_id=1, source_target_pairs={{0,1},{1,0},{2,3},{3,2},{4,5},{5,4},{6,7},{7,6},{8,9},{9,8},{10,11... | collective-permute-start | bytes 2654216 | tf_op jit(solution)/shard_map/ppermute | solution.py:604
  5.0 21.9 %collective-permute-start = (bf16[2,384]{1,0:T(2,128)(2,1)S(1)}, bf16[2,384]{1,0:T(2,128)(2,1)S(1)}, u32[]{:S(2)}, u32[]{:S(2)}) collective-permute-start(bf16[2,384]{1,0:T(2,128)(2,1)S(1)} %pad_maximum_fusion.16), channel_id=1, source_target_pairs={{0,1},{1,0},{2,3},{3,2},{4,5},{5,4},{6,7},{7,6},{8,9},{9,8},{10,11... | collective-permute-start | bytes 4616 | tf_op jit(solution)/shard_map/ppermute | solution.py:604
  5.8 30.9 %all-to-all-start.1 = ((s32[4,2,2,256]{3,2,1,0:T(2,128)}), s32[4,2,2,256]{3,2,1,0:T(2,128)S(1)}, u32[]{:S(2)}, u32[]{:S(2)}) async-start(s32[4,2,2,256]{3,2,1,0:T(2,128)} %broadcast_in_dim.46), calls=%async_computation.1 | async-start | bytes 32768 | tf_op jit(solution)/shard_map/all_to_all | solution.py:975
  24.6 2.9 collective-permute-start.2
  36.7 34.3 %all-to-all-start.3 = ((bf16[4,9,128,128]{3,2,1,0:T(8,128)(2,1)}), bf16[4,9,128,128]{3,2,1,0:T(8,128)(2,1)S(1)}, u32[]{:S(2)}, u32[]{:S(2)}) async-start(bf16[4,9,128,128]{3,2,1,0:T(8,128)(2,1)} %shard_map.216), calls=%async_computation.3 | async-start | bytes 2359296 | tf_op jit(solution)/shard_map/all_to_all | solution.py:1027
  71.0 5.9 copy-start.17
  71.0 57.7 %all-to-all-start = ((bf16[4,9,128,128]{3,2,1,0:T(8,128)(2,1)}), bf16[4,9,128,128]{3,2,1,0:T(8,128)(2,1)}, u32[]{:S(2)}, u32[]{:S(2)}) async-start(bf16[4,9,128,128]{3,2,1,0:T(8,128)(2,1)} %shard_map.213), calls=%async_computation | async-start | bytes 2359296 | tf_op jit(solution)/shard_map/all_to_all | solution.py:1027
  75.3 3.9 copy-start.18
  77.0 3.9 copy-start.28
  77.0 3.8 copy-start.29
  77.0 51.7 %collective-permute-start.5 = (bf16[192,4096]{1,0:T(8,128)(2,1)S(1)}, bf16[192,4096]{1,0:T(8,128)(2,1)}, u32[]{:S(2)}, u32[]{:S(2)}) collective-permute-start(bf16[192,4096]{1,0:T(8,128)(2,1)S(1)} %constant_dynamic-slice_fusion.7), channel_id=1, source_target_pairs={{0,1},{1,0},{2,3},{3,2},{4,5},{5,4},{6,7},{7,6},{8,9},{9,8},{10,11... | collective-permute-start | bytes 4718600 | tf_op jit(solution)/shard_map/ppermute | solution.py:604
  78.6 40.6 %collective-permute-start.3 = (bf16[192,768]{1,0:T(8,128)(2,1)S(1)}, bf16[192,768]{1,0:T(8,128)(2,1)}, u32[]{:S(2)}, u32[]{:S(2)}) collective-permute-start(bf16[192,768]{1,0:T(8,128)(2,1)S(1)} %constant_dynamic-slice_fusion.8), channel_id=1, source_target_pairs={{0,1},{1,0},{2,3},{3,2},{4,5},{5,4},{6,7},{7,6},{8,9},{9,8},{10,11... | collective-permute-start | bytes 884744 | tf_op jit(solution)/shard_map/ppermute | solution.py:604
  79.2 44.5 %collective-permute-start.13 = (bf16[256,768]{1,0:T(8,128)(2,1)S(1)}, bf16[256,768]{1,0:T(8,128)(2,1)S(1)}, u32[]{:S(2)}, u32[]{:S(2)}) collective-permute-start(bf16[256,768]{1,0:T(8,128)(2,1)S(1)} %get-tuple-element.126), channel_id=1, source_target_pairs={{0,16},{8,24},{16,0},{24,8},{1,17},{9,25},{17,1},{25,9},{2,18},{10... | collective-permute-start | bytes 1179656 | tf_op jit(solution)/shard_map/ppermute | solution.py:604
  81.4 103.1 %collective-permute-start.15 = (f32[1,4,512]{2,1,0:T(4,128)}, f32[1,4,512]{2,1,0:T(4,128)}, u32[]{:S(2)}, u32[]{:S(2)}) collective-permute-start(f32[1,4,512]{2,1,0:T(4,128)} %bitcast.23), channel_id=1, source_target_pairs={{0,16},{8,24},{16,0},{24,8},{1,17},{9,25},{17,1},{25,9},{2,18},{10... | collective-permute-start | bytes 24584 | tf_op jit(solution)/shard_map/ppermute | solution.py:604
  81.9 112.8 %collective-permute-start.23 = (bf16[256,768]{1,0:T(8,128)(2,1)S(1)}, bf16[256,768]{1,0:T(8,128)(2,1)S(1)}, u32[]{:S(2)}, u32[]{:S(2)}) collective-permute-start(bf16[256,768]{1,0:T(8,128)(2,1)S(1)} %get-tuple-element.127), channel_id=1, source_target_pairs={{0,16},{8,24},{16,0},{24,8},{1,17},{9,25},{17,1},{25,9},{2,18},{10... | collective-permute-start | bytes 1179656 | tf_op jit(solution)/shard_map/ppermute | solution.py:604
  119.2 7.0 collective-permute-start.4
  123.7 73.5 %collective-permute-start.8 = (bf16[512,768]{1,0:T(8,128)(2,1)}, bf16[512,768]{1,0:T(8,128)(2,1)}, u32[]{:S(2)}, u32[]{:S(2)}) collective-permute-start(bf16[512,768]{1,0:T(8,128)(2,1)} %constant_dynamic-slice_fusion.5), channel_id=1, source_target_pairs={{0,1},{1,0},{2,3},{3,2},{4,5},{5,4},{6,7},{7,6},{8,9},{9,8},{10,11... | collective-permute-start | bytes 2359304 | tf_op jit(solution)/shard_map/ppermute | solution.py:604
  126.2 84.9 %collective-permute-start.14 = (bf16[512,768]{1,0:T(8,128)(2,1)}, bf16[512,768]{1,0:T(8,128)(2,1)}, u32[]{:S(2)}, u32[]{:S(2)}) collective-permute-start(bf16[512,768]{1,0:T(8,128)(2,1)} %pad_maximum_fusion.9), channel_id=1, source_target_pairs={{0,8},{8,0},{16,24},{24,16},{1,9},{9,1},{17,25},{25,17},{2,10},{10... | collective-permute-start | bytes 2359304 | tf_op jit(solution)/shard_map/ppermute | solution.py:604
  154.2 19.2 %all-to-all-start.4 = ((bf16[4,3,128,128]{3,2,1,0:T(8,128)(2,1)}), bf16[4,3,128,128]{3,2,1,0:T(8,128)(2,1)S(1)}, u32[]{:S(2)}, u32[]{:S(2)}) async-start(bf16[4,3,128,128]{3,2,1,0:T(8,128)(2,1)} %get-tuple-element.65.refs_3_), calls=%async_computation.4 | async-start | bytes 786432 | tf_op jit(solution)/shard_map/all_to_all | solution.py:1033
  174.1 16.8 %all-to-all-start.2 = ((bf16[4,3,128,128]{3,2,1,0:T(8,128)(2,1)}), bf16[4,3,128,128]{3,2,1,0:T(8,128)(2,1)S(1)}, u32[]{:S(2)}, u32[]{:S(2)}) async-start(bf16[4,3,128,128]{3,2,1,0:T(8,128)(2,1)} %get-tuple-element.62.refs_2_), calls=%async_computation.2 | async-start | bytes 786432 | tf_op jit(solution)/shard_map/all_to_all | solution.py:1033
  180.9 52.8 %collective-permute-start.6 = (bf16[192,4096]{1,0:T(8,128)(2,1)S(1)}, bf16[192,4096]{1,0:T(8,128)(2,1)}, u32[]{:S(2)}, u32[]{:S(2)}) collective-permute-start(bf16[192,4096]{1,0:T(8,128)(2,1)S(1)} %constant_dynamic-slice_fusion.6), channel_id=1, source_target_pairs={{0,1},{1,0},{2,3},{3,2},{4,5},{5,4},{6,7},{7,6},{8,9},{9,8},{10,11... | collective-permute-start | bytes 4718600 | tf_op jit(solution)/shard_map/ppermute | solution.py:604
  184.5 12.6 %collective-permute-start.21 = (bf16[256,768]{1,0:T(8,128)(2,1)}, bf16[256,768]{1,0:T(8,128)(2,1)}, u32[]{:S(2)}, u32[]{:S(2)}) collective-permute-start(bf16[256,768]{1,0:T(8,128)(2,1)} %get-tuple-element.66), channel_id=1, source_target_pairs={{0,16},{8,24},{16,0},{24,8},{1,17},{9,25},{17,1},{25,9},{2,18},{10... | collective-permute-start | bytes 1179656 | tf_op jit(solution)/shard_map/ppermute | solution.py:604
  194.7 11.4 %copy-start.12 = (bf16[256,768]{1,0:T(8,128)(2,1)S(1)}, bf16[256,768]{1,0:T(8,128)(2,1)}, u32[]{:S(2)}) copy-start(bf16[256,768]{1,0:T(8,128)(2,1)} %get-tuple-element.66) | copy-start | bytes 1179652
  194.7 11.4 %collective-permute-start.11 = (bf16[256,768]{1,0:T(8,128)(2,1)}, bf16[256,768]{1,0:T(8,128)(2,1)}, u32[]{:S(2)}, u32[]{:S(2)}) collective-permute-start(bf16[256,768]{1,0:T(8,128)(2,1)} %get-tuple-element.64), channel_id=1, source_target_pairs={{0,16},{8,24},{16,0},{24,8},{1,17},{9,25},{17,1},{25,9},{2,18},{10... | collective-permute-start | bytes 1179656 | tf_op jit(solution)/shard_map/ppermute | solution.py:604
  197.2 17.3 %collective-permute-start.24 = (bf16[512,768]{1,0:T(8,128)(2,1)}, bf16[512,768]{1,0:T(8,128)(2,1)}, u32[]{:S(2)}, u32[]{:S(2)}) collective-permute-start(bf16[512,768]{1,0:T(8,128)(2,1)} %pad_maximum_fusion.11), channel_id=1, source_target_pairs={{0,8},{8,0},{16,24},{24,16},{1,9},{9,1},{17,25},{25,17},{2,10},{10... | collective-permute-start | bytes 2359304 | tf_op jit(solution)/shard_map/ppermute | solution.py:604
  197.2 54.0 %collective-permute-start.17 = (bf16[192,4096]{1,0:T(8,128)(2,1)}, bf16[192,4096]{1,0:T(8,128)(2,1)}, u32[]{:S(2)}, u32[]{:S(2)}) collective-permute-start(bf16[192,4096]{1,0:T(8,128)(2,1)} %collective-permute-done.5.refs_5_.refs_8_), channel_id=1, source_target_pairs={{0,2},{2,0},{4,6},{6,4},{1,3},{3,1},{5,7},{7,5},{8,10},{10,8},{12,... | collective-permute-start | bytes 4718600 | tf_op jit(solution)/shard_map/ppermute | solution.py:604
  206.1 5.1 copy-start.25
  206.1 2.6 collective-permute-start.16
  208.7 24.9 %collective-permute-start.9 = (bf16[512,768]{1,0:T(8,128)(2,1)}, bf16[512,768]{1,0:T(8,128)(2,1)}, u32[]{:S(2)}, u32[]{:S(2)}) collective-permute-start(bf16[512,768]{1,0:T(8,128)(2,1)} %constant_dynamic-slice_fusion.4), channel_id=1, source_target_pairs={{0,1},{1,0},{2,3},{3,2},{4,5},{5,4},{6,7},{7,6},{8,9},{9,8},{10,11... | collective-permute-start | bytes 2359304 | tf_op jit(solution)/shard_map/ppermute | solution.py:604
  211.0 23.1 %collective-permute-start.12 = (bf16[512,768]{1,0:T(8,128)(2,1)}, bf16[512,768]{1,0:T(8,128)(2,1)}, u32[]{:S(2)}, u32[]{:S(2)}) collective-permute-start(bf16[512,768]{1,0:T(8,128)(2,1)} %get-tuple-element.132), channel_id=1, source_target_pairs={{0,8},{8,0},{16,24},{24,16},{1,9},{9,1},{17,25},{25,17},{2,10},{10... | collective-permute-start | bytes 2359304 | tf_op jit(solution)/shard_map/ppermute | solution.py:604
  214.5 36.7 %collective-permute-start.18 = (bf16[512,768]{1,0:T(8,128)(2,1)}, bf16[512,768]{1,0:T(8,128)(2,1)}, u32[]{:S(2)}, u32[]{:S(2)}) collective-permute-start(bf16[512,768]{1,0:T(8,128)(2,1)} %collective-permute-done.8.refs_11_), channel_id=1, source_target_pairs={{0,2},{2,0},{4,6},{6,4},{1,3},{3,1},{5,7},{7,5},{8,10},{10,8},{12,... | collective-permute-start | bytes 2359304 | tf_op jit(solution)/shard_map/ppermute | solution.py:604
  225.6 8.6 %copy-start.14 = (bf16[256,768]{1,0:T(8,128)(2,1)S(1)}, bf16[256,768]{1,0:T(8,128)(2,1)}, u32[]{:S(2)}) copy-start(bf16[256,768]{1,0:T(8,128)(2,1)} %get-tuple-element.64) | copy-start | bytes 1179652
  233.6 108.3 %collective-permute-start.10 = (bf16[512,768]{1,0:T(8,128)(2,1)}, bf16[512,768]{1,0:T(8,128)(2,1)}, u32[]{:S(2)}, u32[]{:S(2)}) collective-permute-start(bf16[512,768]{1,0:T(8,128)(2,1)} %collective-permute-done.9.refs_10_), channel_id=1, source_target_pairs={{0,8},{8,0},{16,24},{24,16},{1,9},{9,1},{17,25},{25,17},{2,10},{10... | collective-permute-start | bytes 2359304 | tf_op jit(solution)/shard_map/ppermute | solution.py:604
  233.6 108.3 %collective-permute-start.7 = (bf16[192,4096]{1,0:T(8,128)(2,1)}, bf16[192,4096]{1,0:T(8,128)(2,1)}, u32[]{:S(2)}, u32[]{:S(2)}) collective-permute-start(bf16[192,4096]{1,0:T(8,128)(2,1)} %collective-permute-done.6.refs_4_.refs_7_), channel_id=1, source_target_pairs={{0,8},{8,0},{16,24},{24,16},{1,9},{9,1},{17,25},{25,17},{2,10},{10... | collective-permute-start | bytes 4718600 | tf_op jit(solution)/shard_map/ppermute | solution.py:604
  234.1 60.0 %collective-permute-start.22 = (bf16[512,768]{1,0:T(8,128)(2,1)}, bf16[512,768]{1,0:T(8,128)(2,1)S(1)}, u32[]{:S(2)}, u32[]{:S(2)}) collective-permute-start(bf16[512,768]{1,0:T(8,128)(2,1)} %get-tuple-element.131), channel_id=1, source_target_pairs={{0,8},{8,0},{16,24},{24,16},{1,9},{9,1},{17,25},{25,17},{2,10},{10... | collective-permute-start | bytes 2359304 | tf_op jit(solution)/shard_map/ppermute | solution.py:604
  294.0 47.1 %collective-permute-start.27 = (bf16[512,768]{1,0:T(8,128)(2,1)S(1)}, bf16[512,768]{1,0:T(8,128)(2,1)S(1)}, u32[]{:S(2)}, u32[]{:S(2)}) collective-permute-start(bf16[512,768]{1,0:T(8,128)(2,1)S(1)} %slice.99), channel_id=1, source_target_pairs={{0,8},{8,0},{16,24},{24,16},{1,9},{9,1},{17,25},{25,17},{2,10},{10... | collective-permute-start | bytes 2359304 | tf_op jit(solution)/shard_map/ppermute | solution.py:604
  340.5 25.0 %collective-permute-start.29 = (bf16[512,768]{1,0:T(8,128)(2,1)S(1)}, bf16[512,768]{1,0:T(8,128)(2,1)}, u32[]{:S(2)}, u32[]{:S(2)}) collective-permute-start(bf16[512,768]{1,0:T(8,128)(2,1)S(1)} %slice.103), channel_id=1, source_target_pairs={{0,8},{8,0},{16,24},{24,16},{1,9},{9,1},{17,25},{25,17},{2,10},{10... | collective-permute-start | bytes 2359304 | tf_op jit(solution)/shard_map/ppermute | solution.py:604
  341.3 27.1 %collective-permute-start.28 = (bf16[256,768]{1,0:T(8,128)(2,1)S(1)}, bf16[256,768]{1,0:T(8,128)(2,1)}, u32[]{:S(2)}, u32[]{:S(2)}) collective-permute-start(bf16[256,768]{1,0:T(8,128)(2,1)S(1)} %slice.117), channel_id=1, source_target_pairs={{0,16},{8,24},{16,0},{24,8},{1,17},{9,25},{17,1},{25,9},{2,18},{10... | collective-permute-start | bytes 1179656 | tf_op jit(solution)/shard_map/ppermute | solution.py:604
  341.9 23.6 %copy-start.8 = (bf16[1024,768]{1,0:T(8,128)(2,1)S(1)}, bf16[1024,768]{1,0:T(8,128)(2,1)}, u32[]{:S(2)}) copy-start(bf16[1024,768]{1,0:T(8,128)(2,1)} %get-tuple-element.84) | copy-start | bytes 4718596
  366.9 11.1 %collective-permute-start.30 = (bf16[256,768]{1,0:T(8,128)(2,1)S(1)}, bf16[256,768]{1,0:T(8,128)(2,1)S(1)}, u32[]{:S(2)}, u32[]{:S(2)}) collective-permute-start(bf16[256,768]{1,0:T(8,128)(2,1)S(1)} %slice.119), channel_id=1, source_target_pairs={{0,16},{8,24},{16,0},{24,8},{1,17},{9,25},{17,1},{25,9},{2,18},{10... | collective-permute-start | bytes 1179656 | tf_op jit(solution)/shard_map/ppermute | solution.py:604
  373.9 15.2 %all-to-all-start.5 = ((bf16[4,3,128,128]{3,2,1,0:T(8,128)(2,1)}), bf16[4,3,128,128]{3,2,1,0:T(8,128)(2,1)S(1)}, u32[]{:S(2)}, u32[]{:S(2)}) async-start(bf16[4,3,128,128]{3,2,1,0:T(8,128)(2,1)} %get-tuple-element.81), calls=%async_computation.5 | async-start | bytes 786432 | tf_op jit(solution)/shard_map/all_to_all | solution.py:1075
  389.2 26.0 %all-to-all-start.7 = ((bf16[4,3,128,128]{3,2,1,0:T(8,128)(2,1)}), bf16[4,3,128,128]{3,2,1,0:T(8,128)(2,1)S(1)}, u32[]{:S(2)}, u32[]{:S(2)}) async-start(bf16[4,3,128,128]{3,2,1,0:T(8,128)(2,1)} %get-tuple-element.87), calls=%async_computation.7 | async-start | bytes 786432 | tf_op jit(solution)/shard_map/all_to_all | solution.py:1083
  415.1 5.0 copy-start.22
  415.1 48.2 %all-to-all-start.6 = ((bf16[4,3,128,128]{3,2,1,0:T(8,128)(2,1)}), bf16[4,3,128,128]{3,2,1,0:T(8,128)(2,1)S(1)}, u32[]{:S(2)}, u32[]{:S(2)}) async-start(bf16[4,3,128,128]{3,2,1,0:T(8,128)(2,1)} %get-tuple-element.83), calls=%async_computation.6 | async-start | bytes 786432 | tf_op jit(solution)/shard_map/all_to_all | solution.py:1079
  463.3 6.0 copy-start.7
  464.1 6.1 copy-start.6
  464.1 23.8 %all-to-all-start.8 = ((bf16[4,6,128,128]{3,2,1,0:T(8,128)(2,1)}), bf16[4,6,128,128]{3,2,1,0:T(8,128)(2,1)}, u32[]{:S(2)}, u32[]{:S(2)}) async-start(bf16[4,6,128,128]{3,2,1,0:T(8,128)(2,1)} %get-tuple-element.91), calls=%async_computation.8 | async-start | bytes 1572864 | tf_op jit(solution)/shard_map/all_to_all | solution.py:1087
  470.2 22.1 %collective-permute-start.25 = (bf16[512,768]{1,0:T(8,128)(2,1)}, bf16[512,768]{1,0:T(8,128)(2,1)}, u32[]{:S(2)}, u32[]{:S(2)}) collective-permute-start(bf16[512,768]{1,0:T(8,128)(2,1)} %slice.95), channel_id=1, source_target_pairs={{0,8},{8,0},{16,24},{24,16},{1,9},{9,1},{17,25},{25,17},{2,10},{10... | collective-permute-start | bytes 2359304 | tf_op jit(solution)/shard_map/ppermute | solution.py:604
  470.3 24.9 %collective-permute-start.19 = (bf16[512,768]{1,0:T(8,128)(2,1)S(1)}, bf16[512,768]{1,0:T(8,128)(2,1)}, u32[]{:S(2)}, u32[]{:S(2)}) collective-permute-start(bf16[512,768]{1,0:T(8,128)(2,1)S(1)} %slice.88), channel_id=1, source_target_pairs={{0,8},{8,0},{16,24},{24,16},{1,9},{9,1},{17,25},{25,17},{2,10},{10... | collective-permute-start | bytes 2359304 | tf_op jit(solution)/shard_map/ppermute | solution.py:604
  487.9 38.2 %all-to-all-start.9 = ((bf16[4,9,128,128]{3,2,1,0:T(8,128)(2,1)}), bf16[4,9,128,128]{3,2,1,0:T(8,128)(2,1)}, u32[]{:S(2)}, u32[]{:S(2)}) async-start(bf16[4,9,128,128]{3,2,1,0:T(8,128)(2,1)} %get-tuple-element.92), calls=%async_computation.9 | async-start | bytes 2359296 | tf_op jit(solution)/shard_map/all_to_all | solution.py:1088
  494.7 25.0 %collective-permute-start.26 = (bf16[256,768]{1,0:T(8,128)(2,1)}, bf16[256,768]{1,0:T(8,128)(2,1)S(1)}, u32[]{:S(2)}, u32[]{:S(2)}) collective-permute-start(bf16[256,768]{1,0:T(8,128)(2,1)} %slice.115), channel_id=1, source_target_pairs={{0,16},{8,24},{16,0},{24,8},{1,17},{9,25},{17,1},{25,9},{2,18},{10... | collective-permute-start | bytes 1179656 | tf_op jit(solution)/shard_map/ppermute | solution.py:604
  496.5 23.1 %collective-permute-start.20 = (bf16[256,768]{1,0:T(8,128)(2,1)S(1)}, bf16[256,768]{1,0:T(8,128)(2,1)S(1)}, u32[]{:S(2)}, u32[]{:S(2)}) collective-permute-start(bf16[256,768]{1,0:T(8,128)(2,1)S(1)} %slice.112), channel_id=1, source_target_pairs={{0,16},{8,24},{16,0},{24,8},{1,17},{9,25},{17,1},{25,9},{2,18},{10... | collective-permute-start | bytes 1179656 | tf_op jit(solution)/shard_map/ppermute | solution.py:604
  498.1 1.2 collective-permute-start.31
  499.4 14.1 %collective-permute-start.32 = (f32[1,768]{1,0:T(1,128)S(1)}, f32[1,768]{1,0:T(1,128)S(1)}, u32[]{:S(2)}, u32[]{:S(2)}) collective-permute-start(f32[1,768]{1,0:T(1,128)S(1)} %add.179), channel_id=1, source_target_pairs={{0,16},{8,24},{16,0},{24,8},{1,17},{9,25},{17,1},{25,9},{2,18},{10... | collective-permute-start | bytes 9224 | tf_op jit(solution)/shard_map/ppermute | solution.py:604
  513.4 3.9 collective-permute-start.33
  517.4 4.5 collective-permute-start.34
  521.9 3.6 collective-permute-start.35
  536.9 196.1 %copy-start.1 = (bf16[384,2304]{1,0:T(8,128)(2,1)S(1)}, bf16[384,2304]{1,0:T(8,128)(2,1)}, u32[]{:S(2)}) copy-start(bf16[384,2304]{1,0:T(8,128)(2,1)} %param.20) | copy-start | bytes 5308420
  733.0 3.9 copy-start.27
  733.0 4.4 copy-start.11
  (17 other events, 41.7 us)

commit v2 on v1

--- a/solution.py
+++ b/solution.py
@@ -75,12 +75,10 @@
     return jax.ShapeDtypeStruct(tuple(shape), dtype)
 
 
-def pre_kernel(x_ref, gain_ref, w_ref, cos_ref, sin_ref, out_ref, *, groups):
-    tokens = x_ref[0].astype(F32)
-    normed = (tokens * rms_scale(tokens) * gain_ref[...]).astype(BF)
+def project(tokens, gain, w_ref, cosines, sines, pay, groups):
+    normed = (tokens * rms_scale(tokens) * gain).astype(BF)
     width = tokens.shape[1]
     per = width // HEAD // groups
-    cosines, sines = cos_ref[...], sin_ref[...]
     for kind in range(3):
         joined = dot(normed, w_ref[:, kind * width : (kind + 1) * width])
         for pair in range(width // HALF):
@@ -91,26 +89,7 @@
                 tile = tile * 0.125
             for side, packed in enumerate(swap_heads(tile[:HALF], tile[HALF:])):
                 head = 2 * pair + side
-                out_ref[head // per, kind * per + head % per] = packed.astype(BF)
-
-
-def run_pre(x, micro, gain, w, cosines, sines, groups):
-    _, rows, width = x.shape
-    per = width // HEAD // groups
-    return call(
-        functools.partial(pre_kernel, groups=groups),
-        struct((groups, 3 * per, HALF, HALF), BF),
-        grid=(1,),
-        in_specs=[
-            pl.BlockSpec((1, rows, width), lambda _: (micro, 0, 0)),
-            full_spec(gain.shape),
-            full_spec(w.shape),
-            pl.BlockSpec((rows, HALF), lambda _: (micro, 0)),
-            pl.BlockSpec((rows, HALF), lambda _: (micro, 0)),
-        ],
-        out_specs=full_spec((groups, 3 * per, HALF, HALF)),
-        us=5,
-    )(x, gain, w, cosines, sines)
+                pay[head // per, kind * per + head % per] = packed.astype(BF)
 
 
 def unpack(ref, index, kind_head):
@@ -118,15 +97,15 @@
     return tile, pltpu.roll(tile.astype(F32), HEAD, 1).astype(BF)
 
 
-def fill_keys(recvs, ks, vs, heads):
-    for micro, recv in enumerate(recvs):
-        for src in range(recv.shape[0]):
-            base = (micro * recv.shape[0] + src) * TILE
-            for h in range(heads):
-                for store, kind in ((ks, 1), (vs, 2)):
-                    first, second = unpack(recv, src, kind * heads + h)
-                    store[h, base : base + HALF] = first
-                    store[h, base + HALF : base + TILE] = second
+def fill_keys(recv, micro, ks, vs, heads):
+    groups = recv.shape[0]
+    for src in range(groups):
+        base = (micro * groups + src) * TILE
+        for h in range(heads):
+            for store, kind in ((ks, 1), (vs, 2)):
+                first, second = unpack(recv, src, kind * heads + h)
+                store[h, base : base + HALF] = first
+                store[h, base + HALF : base + TILE] = second
 
 
 def masked_rows(ref, index, kind_head):
@@ -139,25 +118,18 @@
     return jnp.where(low_lanes(HALF), values[:HALF], pltpu.roll(values[HALF:], HEAD, 1))
 
 
-def attend_kernel(*refs, micro, heads, groups):
-    recvs = refs[: micro + 1]
-    key_tag, query_tag, out_ref, lse_ref, ks, vs, scores = refs[micro + 1 :]
-    step = pl.program_id(0)
-
-    @pl.when(step == 0)
-    def _():
-        fill_keys(recvs, ks, vs, heads)
-
+def attend_step(step, micro, heads, groups, recv, tags, out_ref, lse_ref, ks, vs, scores):
     count = groups * micro + jnp.minimum(step + 2, groups)
-    queries = [masked_rows(recvs[micro], step, h).astype(BF) for h in range(heads)]
-    tag = query_tag[...]
+    queries = [masked_rows(recv, step, h).astype(BF) for h in range(heads)]
+    tag = jnp.broadcast_to(tags[step, 0, micro], (8, TILE)).T[:, :1]
     same = lax.broadcasted_iota(jnp.int32, (TILE, TILE), 0) == lax.broadcasted_iota(
         jnp.int32, (TILE, TILE), 1
     )
 
     def first_pass(j, tops):
         keys = pl.ds(pl.multiple_of(j * TILE, TILE), TILE)
-        seen = (key_tag[j] <= tag) | (same & (j == groups * micro + step))
+        key_tag = tags[j % groups, 1, j // groups]
+        seen = (key_tag <= tag) | (same & (j == groups * micro + step))
         new = []
         for h in range(heads):
             part = jnp.where(seen, dot(queries[h], ks[h, keys, :], NT), MASKED)
@@ -191,46 +163,19 @@
     lse_ref[step] = logs.T[:8]
 
 
-def run_attend(recvs, key_tag, query_tag, groups):
-    micro = len(recvs) - 1
-    heads = recvs[0].shape[1] // 3
-    held = groups * (micro + 1) * TILE
-    return call(
-        functools.partial(attend_kernel, micro=micro, heads=heads, groups=groups),
-        (struct((groups, heads, HALF, HALF), BF), struct((groups, 8, TILE), F32)),
-        grid=(groups,),
-        in_specs=[full_spec(r.shape) for r in recvs]
-        + [full_spec(key_tag.shape), pl.BlockSpec((TILE, 1), lambda s: (micro * groups + s, 0))],
-        out_specs=(full_spec((groups, heads, HALF, HALF)), full_spec((groups, 8, TILE))),
-        scratch=[
-            pltpu.VMEM((heads, held, HALF), BF),
-            pltpu.VMEM((heads, held, HALF), BF),
-            pltpu.VMEM((heads, TILE, held), F32),
-        ],
-        us=15 + 11 * micro,
-    )(*recvs, key_tag, query_tag)
-
-
-def attend_back_kernel(*refs, micro, heads, groups):
-    recvs = refs[: micro + 1]
-    refs = refs[micro + 1 :]
-    grad_ref, out_ref, lse_ref, key_tag, query_tag = refs[:5]
-    refs = refs[5:]
-    if micro == 0:
-        pay_ref, early_k, early_v, ks, vs, dk, dv = refs
-    else:
-        early_k, early_v, pay_ref, pay0_ref, ks, vs, dk, dv = refs
-    step = pl.program_id(0)
-
-    @pl.when(step == 0)
-    def _():
-        fill_keys(recvs, ks, vs, heads)
+def back_start(recvs, ks, vs, dk, dv, early, heads, groups):
+    for micro, recv in enumerate(recvs):
+        fill_keys(recv, micro, ks, vs, heads)
+    if early is None:
         dk[...] = jnp.zeros_like(dk)
         dv[...] = jnp.zeros_like(dv)
-        if micro > 0:
-            dk[:, : groups * TILE] = early_k[...]
-            dv[:, : groups * TILE] = early_v[...]
-
+    else:
+        for total, part in zip((dk, dv), early):
+            total[:, : groups * TILE] = part[...]
+            total[:, groups * TILE :] = jnp.zeros_like(total[:, groups * TILE :])
+
+
+def back_step(step, micro, heads, groups, recvs, grad_ref, out_ref, lse_ref, key_tag, query_tag, pay_ref, ks, vs, dk, dv):
     count = groups * micro + jnp.minimum(step + 2, groups)
     queries = [masked_rows(recvs[micro], step, h).astype(BF) for h in range(heads)]
     grads_f = [masked_rows(grad_ref, step, h) for h in range(heads)]
@@ -270,41 +215,44 @@
     for h in range(heads):
         pay_ref[step, h] = pack_rows(totals[h]).astype(BF)
 
+
+def back_pack(dk, dv, pay_ref, src, first, base, heads):
+    rows = slice((base + src) * TILE, (base + src + 1) * TILE)
+    for h in range(heads):
+        pay_ref[src, first + h] = pack_rows(dk[h, rows]).astype(BF)
+        pay_ref[src, first + heads + h] = pack_rows(dv[h, rows]).astype(BF)
+
+
+def attend_back_kernel(*refs, heads, groups):
+    recv, grad_ref, out_ref, lse_ref, key_tag, query_tag, pay_ref, early_k, early_v, ks, vs, dk, dv = refs
+    step = pl.program_id(0)
+
+    @pl.when(step == 0)
+    def _():
+        back_start([recv], ks, vs, dk, dv, None, heads, groups)
+
+    back_step(step, 0, heads, groups, [recv], grad_ref, out_ref, lse_ref, key_tag, query_tag, pay_ref, ks, vs, dk, dv)
+
     @pl.when(step == groups - 1)
     def _():
-        if micro == 0:
-            early_k[...] = dk[...]
-            early_v[...] = dv[...]
-        else:
-            for src in range(groups):
-                for ref, base, first in ((pay0_ref, 0, 0), (pay_ref, groups, heads)):
-                    rows = slice((base + src) * TILE, (base + src + 1) * TILE)
-                    for h in range(heads):
-                        ref[src, first + h] = pack_rows(dk[h, rows]).astype(BF)
-                        ref[src, first + heads + h] = pack_rows(dv[h, rows]).astype(BF)
-
-
-def run_attend_back(recvs, grad, out, lse, key_tag, query_tag, early, groups):
-    micro = len(recvs) - 1
-    heads = recvs[0].shape[1] // 3
-    held = groups * (micro + 1) * TILE
-    pay = lambda n: struct((groups, n * heads, HALF, HALF), BF)
-    part = struct((heads, groups * TILE, HALF), F32)
-    args = [*recvs, grad, out, lse, key_tag, query_tag, *early]
-    outs = [pay(1), part, part] if micro == 0 else [pay(3), pay(2)]
+        early_k[...] = dk[...]
+        early_v[...] = dv[...]
+
+
+def run_attend_back(recv, grad, out, lse, key_tag, query_tag, groups):
+    heads = recv.shape[1] // 3
+    held = groups * TILE
+    part = struct((heads, held, HALF), F32)
+    args = [recv, grad, out, lse, key_tag, query_tag]
+    outs = [struct((groups, heads, HALF, HALF), BF), part, part]
     return call(
-        functools.partial(attend_back_kernel, micro=micro, heads=heads, groups=groups),
+        functools.partial(attend_back_kernel, heads=heads, groups=groups),
         tuple(outs),
         grid=(groups,),
         in_specs=[full_spec(a.shape) for a in args],
         out_specs=tuple(full_spec(o.shape) for o in outs),
-        scratch=[
-            pltpu.VMEM((heads, held, HALF), BF),
-            pltpu.VMEM((heads, held, HALF), BF),
-            pltpu.VMEM((heads, held, HALF), F32),
-            pltpu.VMEM((heads, held, HALF), F32),
-        ],
-        us=23 + 20 * micro,
+        scratch=[pltpu.VMEM((heads, held, HALF), BF)] * 2 + [pltpu.VMEM((heads, held, HALF), F32)] * 2,
+        us=23,
     )(*args)
 
 
@@ -315,30 +263,286 @@
     return jnp.concatenate(swap_heads(*tiles), 0)
 
 
-def post_kernel(o_ref, x_ref, w_ref, gain_ref, att_ref, res_ref, nf_ref, *, per):
+def remote(src, dst, sems, index, target, arrival=None):
+    return pltpu.make_async_remote_copy(
+        src_ref=src,
+        dst_ref=dst,
+        send_sem=sems[0].at[index],
+        recv_sem=sems[1].at[index if arrival is None else arrival],
+        device_id=target,
+        device_id_type=pl.DeviceIdType.MESH,
+    )
+
+
+def meet(barrier, targets):
+    for target in targets:
+        pl.semaphore_signal(barrier, inc=1, device_id=target, device_id_type=pl.DeviceIdType.MESH)
+    pl.semaphore_wait(barrier, len(targets))
+
+
+class Trade:
+    def __init__(self, src, dst, sems, local):
+        self.src, self.dst, self.sems, self.local = src, dst, sems, local
+        self.z = lax.axis_index("context")
+        self.groups = src.shape[0]
+
+    def wire(self, other, arrival):
+        return remote(self.src.at[other], self.dst.at[arrival], self.sems, other, {"context": other}, arrival)
+
+    def keep(self, index):
+        return pltpu.make_async_copy(self.src.at[index], self.dst.at[index], self.local)
+
+    def send(self, dest):
+        @pl.when(dest != self.z)
+        def _():
+            self.wire(dest, self.z).start()
+
+        @pl.when(dest == self.z)
+        def _():
+            self.keep(dest).start()
+
+    def await_from(self, other):
+        @pl.when(other != self.z)
+        def _():
+            self.wire(other, other).wait_recv()
+
+        @pl.when(other == self.z)
+        def _():
+            self.keep(other).wait()
+
+    def collect(self):
+        for other in range(self.groups):
+            self.await_from(other)
+
+    def release(self):
+        for other in range(self.groups):
+
+            @pl.when(other != self.z)
+            def _(other=other):
+                self.wire(other, self.z).wait_send()
+
+
+def front_kernel(*refs, heads, groups):
+    refs = list(refs)
+    take = lambda n: [refs.pop(0) for _ in range(n)]
+    x_ref, gains_in, cos_ref, sin_ref, tags_in, gates_in = take(6)
+    w_qkv, w_out, w_ein, w_eout, cot = take(5)
+    recv_out, mixed_out, lse_out, att_out, res_out = take(2), take(2), take(2), take(2), take(2)
+    rows_out, cot_out, gates_out, both_out, tags_out = take(2), take(2), take(1)[0], take(1)[0], take(1)[0]
+    qkv_out, wout_out, ein_out, eout_out, gains_out = take(5)
+    wq, wo, gains, tags, pay, recv, ks, vs, scores, mixed, got, lse, att, res, nf = take(15)
+    s_qkv, s_out, s_gain, s_exp, s_tag, s_gate, s_cot, s_pay, s_mix, s_row = [take(2) for _ in range(10)]
+    local, self_pay, self_mix, self_tag, stores = take(5)
+    e, z, d = lax.axis_index("expert"), lax.axis_index("context"), lax.axis_index("dp")
+    core, y = e % 2, e // 2 % 2
+    to_x, to_core, to_y = {"dp": 1 - d}, {"expert": e + 1 - 2 * core}, {"expert": e + 2 - 4 * y}
+    others = [{"context": (z + k) % groups} for k in range(1, groups)]
     width = x_ref.shape[2]
-    for pair in range(width // HALF):
-        att_ref[:, pair * HALF : (pair + 1) * HALF] = natural(o_ref, 0, pair, per).astype(BF)
-    residual = x_ref[0].astype(F32) + dot(att_ref[...], w_ref[...])
-    res_ref[...] = residual
-    nf_ref[...] = (residual * rms_scale(residual) * gain_ref[...]).astype(BF)
-
-
-def run_post(mixed, x, micro, w, gain):
+
+    loads = [
+        pltpu.make_async_copy(w_qkv, wq.at[d], local.at[0]),
+        pltpu.make_async_copy(w_out, wo.at[d], local.at[1]),
+        pltpu.make_async_copy(gains_in, gains.at[d], local.at[2]),
+    ]
+    for copy in loads:
+        copy.start()
+    meet(pltpu.get_barrier_semaphore(), [to_x, to_core, to_y, *others])
+
+    x_qkv = remote(w_qkv.at[core], wq.at[d, core], s_qkv, 0, to_x)
+    x_gain = remote(gains_in, gains.at[d], s_gain, 0, to_x)
+    x_out = remote(w_out.at[core], wo.at[d, core], s_out, 0, to_x)
+    x_exp = [remote(w_ein, ein_out, s_exp, 0, to_x), remote(w_eout, eout_out, s_exp, 1, to_x)]
+    for copy in (x_qkv, x_gain, x_out, *x_exp):
+        copy.start()
+    tag_trade = [
+        remote(tags_in, tags.at[z], s_tag, k, others[k]) for k in range(groups - 1)
+    ]
+    tag_own = pltpu.make_async_copy(tags_in, tags.at[z], self_tag.at[0])
+    tag_own.start()
+    for copy in tag_trade:
+        copy.start()
+    own_copies = [
+        pltpu.make_async_copy(gates_in, gates_out.at[0], stores.at[0]),
+        pltpu.make_async_copy(cot.at[0], cot_out[0].at[0], stores.at[1]),
+        pltpu.make_async_copy(cot.at[1], cot_out[1].at[0], stores.at[2]),
+    ]
+    for copy in own_copies:
+        copy.start()
+    y_gate = remote(gates_in, gates_out.at[1], s_gate, 0, to_y)
+    y_cot = [remote(cot.at[m], cot_out[m].at[1], s_cot, m, to_y) for m in range(MICRO)]
+    c_gate = [
+        remote(gates_in, gates_out.at[2], s_gate, 1, to_core),
+        remote(gates_out.at[1], gates_out.at[3], s_gate, 2, to_core),
+    ]
+    c_cot = [remote(cot.at[m], cot_out[m].at[2], s_cot, 2 + m, to_core) for m in range(MICRO)] + [
+        remote(cot_out[m].at[1], cot_out[m].at[3], s_cot, 4 + m, to_core) for m in range(MICRO)
+    ]
+    y_gate.start()
+    for copy in y_cot:
+        copy.start()
+
+    c_qkv = remote(wq.at[1 - d, core], wq.at[1 - d, core], s_qkv, 1, to_core)
+    c_out = remote(wo.at[1 - d, core], wo.at[1 - d, core], s_out, 1, to_core)
+    for copy in loads:
+        copy.wait()
+    x_qkv.wait_recv()
+    c_qkv.start()
+    x_gain.wait_recv()
+    c_qkv.wait_recv()
+    both = [jnp.concatenate([gains[0, k : k + 1], gains[1, k : k + 1]], 1) for k in range(2)]
+    w_full = wq.reshape(width, 3 * width)
+    trades, returns = [], []
+    for m in range(MICRO):
+        span = slice(m * TILE, (m + 1) * TILE)
+        project(x_ref[m].astype(F32), both[0], w_full, cos_ref[span, :], sin_ref[span, :], pay.at[m], groups)
+        trade = Trade(pay.at[m], recv.at[m], [s.at[m] for s in s_pay], self_pay.at[m])
+        for dest in range(groups):
+            trade.send(dest)
+        trades.append(trade)
+    c_gate[0].start()
+    for copy in c_cot[:MICRO]:
+        copy.start()
+    for k in range(groups - 1):
+        remote(tags_in, tags.at[(z + groups - 1 - k) % groups], s_tag, k, others[k]).wait_recv()
+    tag_own.wait()
+
+    def attend(m, first, last):
+        trade = Trade(mixed.at[m], got.at[m], [s.at[m] for s in s_mix], self_mix.at[m])
+
+        def one(step, carry):
+            attend_step(step, m, heads, groups, recv.at[m], tags, mixed.at[m], lse.at[m], ks, vs, scores)
+            trade.send(step)
+            return carry
+
+        lax.fori_loop(first, last, one, 0)
+        return trade
+
+    def post(m, trade):
+        trade.collect()
+        for pair in range(width // HALF):
+            att[m, :, pair * HALF : (pair + 1) * HALF] = natural(got.at[m], 0, pair, heads).astype(BF)
+        residual = x_ref[m].astype(F32) + dot(att[m], wo.reshape(width, width)[...])
+        res[m] = residual
+        nf[m] = (residual * rms_scale(residual) * both[1]).astype(BF)
+        remote(nf.at[m], rows_out[m].at[1], s_row, 3 * m, to_y).start()
+        remote(nf.at[m], rows_out[m].at[2], s_row, 3 * m + 1, to_core).start()
+
+    def forward_row(m):
+        remote(nf.at[m], rows_out[m].at[1], s_row, 3 * m, to_y).wait_recv()
+        remote(rows_out[m].at[1], rows_out[m].at[3], s_row, 3 * m + 2, to_core).start()
+
+    trades[0].collect()
+    fill_keys(recv.at[0], 0, ks, vs, heads)
+    back0 = attend(0, 0, groups)
+    x_out.wait_recv()
+    c_out.start()
+    y_gate.wait_recv()
+    c_gate[1].start()
+    for m in range(MICRO):
+        y_cot[m].wait_recv()
+        c_cot[MICRO + m].start()
+    trades[1].collect()
+    fill_keys(recv.at[1], 1, ks, vs, heads)
+    back1 = attend(1, 0, 2)
+    c_out.wait_recv()
+    post(0, back0)
+    back1 = attend(1, 2, groups)
+    forward_row(0)
+    post(1, back1)
+    keep = []
+    for m in range(MICRO):
+        keep += [
+            (recv.at[m], recv_out[m]),
+            (mixed.at[m], mixed_out[m]),
+            (lse.at[m], lse_out[m]),
+            (att.at[m], att_out[m]),
+            (res.at[m], res_out[m]),
+            (nf.at[m], rows_out[m].at[0]),
+            (nf.at[m], both_out.at[m]),
+        ]
+    keep += [(tags, tags_out), (wq, qkv_out), (wo, wout_out), (gains, gains_out)]
+    keep = [pltpu.make_async_copy(a, b, stores.at[3 + i]) for i, (a, b) in enumerate(keep)]
+    for copy in keep:
+        copy.start()
+    forward_row(1)
+    for copy in (*keep, *own_copies):
+        copy.wait()
+    for m in range(MICRO):
+        remote(nf.at[m], rows_out[m].at[2], s_row, 3 * m + 1, to_core).wait()
+        remote(rows_out[m].at[1], rows_out[m].at[3], s_row, 3 * m + 2, to_core).wait()
+        remote(nf.at[m], rows_out[m].at[1], s_row, 3 * m, to_y).wait_send()
+        trades[m].release()
+    back0.release()
+    back1.release()
+    for copy in (*x_exp, *c_gate, *c_cot):
+        copy.wait()
+    for copy in (x_qkv, x_gain, x_out, c_qkv, c_out, y_gate, *y_cot, *tag_trade):
+        copy.wait_send()
+
+
+def run_front(x, gains, cosines, sines, tags, gates, w_qkv, w_out, w_ein, w_eout, cot, groups):
     _, rows, width = x.shape
-    return call(
-        functools.partial(post_kernel, per=mixed.shape[1]),
-        (struct((rows, width), BF), struct((rows, width), F32), struct((rows, width), BF)),
-        grid=(1,),
-        in_specs=[
-            full_spec(mixed.shape),
-            pl.BlockSpec((1, rows, width), lambda _: (micro, 0, 0)),
-            full_spec(w.shape),
-            full_spec(gain.shape),
-        ],
-        out_specs=(full_spec((rows, width)),) * 3,
-        us=3,
-    )(mixed, x, w, gain)
+    heads = width // HEAD // groups
+    k = width // 4
+    w_qkv = w_qkv.reshape(2, k, 3 * width)
+    w_out = w_out.reshape(2, k, width)
+    vmem = pl.BlockSpec(memory_space=pltpu.VMEM)
+    anywhere = pl.BlockSpec(memory_space=pl.ANY)
+    packed = lambda n: (groups, n * heads, HALF, HALF)
+    held = MICRO * groups * TILE
+    twice = lambda *a: [struct(*a)] * 2
+    outs = (
+        twice(packed(3), BF)
+        + twice(packed(1), BF)
+        + twice((groups, 8, TILE), F32)
+        + twice((rows, width), BF)
+        + twice((rows, width), F32)
+        + twice((4, rows, width), BF)
+        + twice((4, rows, width), BF)
+        + [
+            struct((4, *gates.shape), F32),
+            struct((MICRO, rows, width), BF),
+            struct((groups, *tags.shape), jnp.int32),
+            struct((2, 2, k, 3 * width), BF),
+            struct((2, 2, k, width), BF),
+            struct(w_ein.shape, BF),
+            struct(w_eout.shape, BF),
+            struct((2, *gains.shape), F32),
+        ]
+    )
+    v = pltpu.VMEM
+    dma = lambda *n: pltpu.SemaphoreType.DMA(n)
+    scratch = [
+        v((2, 2, k, 3 * width), BF),
+        v((2, 2, k, width), BF),
+        v((2, *gains.shape), F32),
+        v((groups, *tags.shape), jnp.int32),
+        v((MICRO, *packed(3)), BF),
+        v((MICRO, *packed(3)), BF),
+        v((heads, held, HALF), BF),
+        v((heads, held, HALF), BF),
+        v((heads, TILE, held), F32),
+        v((MICRO, *packed(1)), BF),
+        v((MICRO, *packed(1)), BF),
+        v((MICRO, groups, 8, TILE), F32),
+        v((MICRO, rows, width), BF),
+        v((MICRO, rows, width), F32),
+        v((MICRO, rows, width), BF),
+    ]
+    for shape in ((2,), (2,), (1,), (2,), (groups - 1,), (3,), (6,), (MICRO, groups), (MICRO, groups), (6,)):
+        scratch += [dma(*shape), dma(*shape)]
+    scratch += [dma(3), dma(MICRO), dma(MICRO), dma(1), dma(3 + 7 * MICRO + 4)]
+    return pl.pallas_call(
+        functools.partial(front_kernel, heads=heads, groups=groups),
+        out_shape=tuple(outs),
+        in_specs=[vmem] * 6 + [anywhere] * 5,
+        out_specs=(anywhere,) * len(outs),
+        scratch_shapes=scratch,
+        compiler_params=pltpu.CompilerParams(
+            vmem_limit_bytes=VMEM_LIMIT, collective_id=3, has_side_effects=True
+        ),
+        cost_estimate=price(130),
+    )(x, gains, cosines, sines, tags, gates, w_qkv, w_out, w_ein, w_eout, cot)
 
 
 def ffn_kernel(*refs, tr, spans, counts, first, gated, opened, summed, closing, parts):
@@ -557,7 +761,7 @@
     )(*args)
 
 
-def fin_kernel(q0, kv0, d1, x_ref, gain_ref, w_ref, cos_ref, sin_ref, res0, res1, gin_ref, gw_ref, gj, *, per):
+def fin_kernel(q0, kv0, d1, x_ref, gain_ref, w_ref, cos_ref, sin_ref, res0, res1, gin_ref, gw0_ref, gw1_ref, gj, *, per):
     width = x_ref.shape[1]
     for micro, sources in enumerate((((q0, 0), (kv0, 0), (kv0, 1)), ((d1, 0), (d1, 1), (d1, 2)))):
         rows = slice(micro * TILE, (micro + 1) * TILE)
@@ -579,15 +783,16 @@
     gin_ref[:TILE] = res0[...] + back[:TILE]
     gin_ref[TILE:] = res1[...] + back[TILE:]
     turned = normed.T
-    for kind in range(3):
-        cols = slice(kind * width, (kind + 1) * width)
-        gw_ref[:, cols] = dot(turned, gj[:, cols]).astype(BF)
+    split = gw0_ref.shape[1]
+    gw0_ref[...] = dot(turned, gj[:, :split]).astype(BF)
+    gw1_ref[...] = dot(turned, gj[:, split:]).astype(BF)
 
 
 def run_fin(parts, x, gain, w, cosines, sines, gres):
     rows, width = x.shape
     args = (*parts, x, gain, w, cosines, sines, *gres)
-    outs = (struct((rows, width), F32), struct((width, 3 * width), BF))
+    half = struct((width, 3 * width // 2), BF)
+    outs = (struct((rows, width), F32), half, half)
     return call(
         functools.partial(fin_kernel, per=parts[0].shape[1]),
         outs,
@@ -608,16 +813,17 @@
     return [1 << b for b in range(size.bit_length() - 1)]
 
 
-def gather_xor(value, axis):
-    for mask in reversed(bits_of(lax.axis_size(axis))):
-        value = jnp.concatenate([value, exchange(value, axis, mask)], 0)
+def gather_rest(value):
+    for mask in bits_of(lax.axis_size("expert"))[2:]:
+        value = jnp.concatenate([value, exchange(value, "expert", mask)], 0)
     return value
 
 
-def scatter_xor(value, axis):
-    for mask in bits_of(lax.axis_size(axis)):
+def scatter_xor(value):
+    masks = bits_of(lax.axis_size("expert"))
+    for mask in (*reversed(masks[2:]), *masks[:2]):
         half = value.shape[0] // 2
-        got = exchange(value[half:], axis, mask)
+        got = exchange(value[half:], "expert", mask)
         value = (value[:half].astype(F32) + got.astype(F32)).astype(value.dtype)
     return value
 
@@ -642,34 +848,18 @@
     return part, exchange(part, axis, 1)
 
 
-def fetch_whole(shard):
-    part, other = fetch_parts(shard, "expert")
-    core = lax.axis_index("expert") % 2
-    return part, ordered(lax.axis_index("dp"), shard, ordered(core, part, other))
-
-
 PIECES = 4
-
-
-def remote(src, dst, sems, index, target):
-    return pltpu.make_async_remote_copy(
-        src_ref=src,
-        dst_ref=dst,
-        send_sem=sems[0].at[index],
-        recv_sem=sems[1].at[index],
-        device_id=target,
-        device_id_type=pl.DeviceIdType.MESH,
-    )
-
-
-def reduce_kernel(*refs, owned, common):
+AHEAD = 3
+
+
+def reduce_kernel(*refs, owned, common, extra, counts):
     refs = list(refs)
     take = lambda n: [refs.pop(0) for _ in range(n)]
-    own_in, com_in = take(owned), take(common)
-    own_out, com_out = take(owned), take(common)
+    own_in, com_in, extra_in = take(owned), take(common), take(counts[0])
+    own_out, com_out, extra_out = take(owned), take(common), take(counts[1])
     own_buf = [take(4) for _ in range(owned)]
     com_buf = [take(6) for _ in range(common)]
-    own_sems, com_sems = take(10), take(20)
+    own_sems, com_sems, extra_buf = take(10), take(20), take(counts[2])
     barrier = pltpu.get_barrier_semaphore()
     e, z, d = lax.axis_index("expert"), lax.axis_index("context"), lax.axis_index("dp")
     core, y = e % 2, e // 2 % 2
@@ -681,18 +871,10 @@
     to_y = {"expert": e + 2 - 4 * y}
     to_mate = {"context": mate}
     to_mid = {"context": 3 - z}
-    near = [to_x, to_core, to_y, to_mate]
-    for target in near:
-        pl.semaphore_signal(barrier, inc=1, device_id=target, device_id_type=pl.DeviceIdType.MESH)
-
-    @pl.when(inner)
-    def _():
-        pl.semaphore_signal(barrier, inc=1, device_id=to_mid, device_id_type=pl.DeviceIdType.MESH)
-        pl.semaphore_wait(barrier, 5)
-
-    @pl.when(outer)
-    def _():
-        pl.semaphore_wait(barrier, 4)
+    groups = lax.axis_size("context")
+    others = [{"context": (z + k) % groups} for k in range(1, groups)]
+    near = [to_x, to_core, to_y, *others]
+    meet(barrier, near)
 
     o_load, o_store = own_sems[:2]
     o_x, o_1, o_2, o_3 = [own_sems[2 + 2 * k : 4 + 2 * k] for k in range(4)]
@@ -731,8 +913,8 @@
         j, k = where(c)
         o_loading(c).wait()
         o_wire("x", c).wait_recv()
-        if c + 2 < chunks:
-            o_wire("x", c + 2).start()
+        if c + AHEAD < chunks:
+            o_wire("x", c + AHEAD).start()
         own_buf[j][0][k] = own_buf[j][0][k] + own_buf[j][1][k]
 
         @pl.when(outer)
@@ -856,9 +1038,9 @@
             c_loading(i, h).start()
     for c in range(chunks):
         o_loading(c).start()
-        if c < 2:
+        if c < AHEAD:
             o_wire("x", c).start()
-    events = []
+    events, closing = extra(extra_in, extra_out, extra_buf) if extra else ([], None)
     for c in range(chunks):
         for lag, step in ((1, o_first), (2.5, o_second), (3.5, o_third), (4.6, o_fourth)):
             events.append((c + lag, step, c))
@@ -868,6 +1050,8 @@
             events.append((base + lag, step, i))
     for _, step, index in sorted(events, key=lambda v: v[0]):
         step(index)
+    if closing:
+        closing()
     for c in range(chunks):
         o_wire("x", c).wait_send()
     for i in range(common):
@@ -897,7 +1081,7 @@
             c_wire("fore", i).wait_send()
 
 
-def run_reduce(expert_grads, shared_grads, collective_id, us):
+def run_reduce(expert_grads, shared_grads, collective_id, us, extra=None, extra_args=(), extra_outs=(), extra_scratch=()):
     own = [g.reshape(2, PIECES, g.shape[0] // (2 * PIECES), g.shape[1]) for g in expert_grads]
     com = []
     for g in shared_grads:
@@ -919,17 +1103,92 @@
     anywhere = pl.BlockSpec(memory_space=pl.ANY)
     outs = [struct(g.shape[1:], BF) for g in own] + [struct((2, 2, *g.shape[3:]), BF) for g in com]
     got = pl.pallas_call(
-        functools.partial(reduce_kernel, owned=len(own), common=n),
-        out_shape=tuple(outs),
-        in_specs=[anywhere] * (len(own) + n),
-        out_specs=(anywhere,) * len(outs),
-        scratch_shapes=scratch,
+        functools.partial(
+            reduce_kernel,
+            owned=len(own),
+            common=n,
+            extra=extra,
+            counts=(len(extra_args), len(extra_outs), len(extra_scratch)),
+        ),
+        out_shape=(*outs, *extra_outs),
+        in_specs=[anywhere] * (len(own) + n)
+        + [pl.BlockSpec(memory_space=pltpu.VMEM)] * len(extra_args),
+        out_specs=(anywhere,) * (len(outs) + len(extra_outs)),
+        scratch_shapes=[*scratch, *extra_scratch],
         compiler_params=pltpu.CompilerParams(
             vmem_limit_bytes=VMEM_LIMIT, collective_id=collective_id, has_side_effects=True
         ),
         cost_estimate=price(us),
-    )(*own, *com)
-    return [g.reshape(-1, g.shape[-1]).astype(F32) for g in got]
+    )(*own, *com, *extra_args)
+    return [g.reshape(-1, g.shape[-1]).astype(F32) for g in got[: len(outs)]], got[len(outs) :]
+
+
+def back_extra(ins, outs, bufs, *, heads, groups):
+    recv0, recv1, grad_ref, out_ref, lse_ref, key_tag, query_tag, early_k, early_v = ins
+    pay, pay0, ks, vs, dk, dv, s1, r1, s0, r0, local = bufs
+    z = lax.axis_index("context")
+    sets = ((pay, outs[0], (s1, r1), 0), (pay0, outs[1], (s0, r0), 1))
+
+    def send(index):
+        def _(dest):
+            src, out, sems, k = sets[index]
+
+            @pl.when(dest != z)
+            def _():
+                pltpu.make_async_remote_copy(
+                    src_ref=src.at[dest],
+                    dst_ref=out.at[z],
+                    send_sem=sems[0].at[dest],
+                    recv_sem=sems[1].at[z],
+                    device_id={"context": dest},
+                    device_id_type=pl.DeviceIdType.MESH,
+                ).start()
+
+            @pl.when(dest == z)
+            def _():
+                pltpu.make_async_copy(src.at[dest], out.at[dest], local.at[k]).start()
+
+        return _
+
+    def begin(_):
+        back_start([recv0, recv1], ks, vs, dk, dv, (early_k, early_v), heads, groups)
+
+    def step(s):
+        back_step(
+            s, 1, heads, groups, [recv0, recv1], grad_ref, out_ref, lse_ref, key_tag, query_tag, pay, ks, vs, dk, dv
+        )
+
+    def home(_):
+        for dest in range(groups):
+            back_pack(dk, dv, pay, dest, heads, groups, heads)
+            send(0)(dest)
+        for dest in range(groups):
+            back_pack(dk, dv, pay0, dest, 0, 0, heads)
+            send(1)(dest)
+
+    def closing():
+        for src, out, sems, k in sets:
+            for other in range(groups):
+
+                @pl.when(other != z)
+                def _(src=src, out=out, sems=sems, other=other):
+                    copy = pltpu.make_async_remote_copy(
+                        src_ref=src.at[other],
+                        dst_ref=out.at[other],
+                        send_sem=sems[0].at[other],
+                        recv_sem=sems[1].at[other],
+                        device_id={"context": other},
+                        device_id_type=pl.DeviceIdType.MESH,
+                    )
+                    copy.wait_send()
+                    copy.wait_recv()
+
+                @pl.when(other == z)
+                def _(src=src, out=out, k=k, other=other):
+                    pltpu.make_async_copy(src.at[other], out.at[other], local.at[k]).wait()
+
+    events = [(0.3, begin, 0)] + [(0.5 + 1.35 * s, step, s) for s in range(groups)] + [(0.5 + 1.35 * groups, home, 0)]
+    return events, closing
 
 
 def body(
@@ -971,38 +1230,64 @@
 
     blocks = block_ids[0] + 8 * jnp.arange(MICRO, dtype=jnp.int32)[:, None]
     key_tags = jnp.where(keep_flags[0] == 1, blocks, HIDDEN)
-    tags = jnp.broadcast_to(jnp.stack([blocks, key_tags])[None], (groups, 2, MICRO, rows))
-    tags = lax.all_to_all(tags, "context", 0, 0, tiled=True).transpose(1, 2, 0, 3)
-    query_row = tags[0].reshape(MICRO * groups, 1, rows)
-    key_row = tags[1].reshape(MICRO * groups, 1, rows)
-    query_col = tags[0].reshape(-1, 1)
-    key_col = tags[1].reshape(-1, 1)
-
-    gains = jnp.stack([norm_attn, norm_ffn])
-    both = ordered(lax.axis_index("dp"), gains[None], exchange(gains, "dp", 1)[None]).astype(F32)
-    gain_attn = both[:, 0].reshape(1, width)
-    gain_ffn = both[:, 1].reshape(1, width)
-    qkv_part, mat_qkv = fetch_whole(w_qkv)
-    out_part, mat_out = fetch_whole(w_attn_out)
-
-    ids = expert_ids[0].reshape(MICRO * rows, -1)
-    gates = gate_weights[0].reshape(MICRO * rows, -1)
+    tags = jnp.stack([blocks, key_tags])[:, :, None]
+
     per_expert = jnp.sum(
         jnp.where(
-            ids[None] == jnp.arange(experts, dtype=jnp.int32)[:, None, None], gates[None], 0.0
+            expert_ids[0][None] == jnp.arange(experts, dtype=jnp.int32)[:, None, None, None],
+            gate_weights[0][None],
+            0.0,
         ),
         -1,
     )
-    all_gates = gather_xor(per_expert[None], "expert")
-    gate = lax.dynamic_index_in_dim(all_gates, lax.axis_index("expert"), 1, False).reshape(-1, 1)
+    gains = jnp.stack([norm_attn, norm_ffn]).astype(F32)
+    (
+        *pairs,
+        gates_four,
+        nf_both,
+        all_tags,
+        mat_qkv,
+        mat_out,
+        ein_other,
+        eout_other,
+        gains,
+    ) = run_front(
+        x,
+        gains,
+        cosines,
+        sines,
+        tags,
+        per_expert,
+        w_qkv,
+        w_attn_out,
+        w_expert_in[0],
+        w_expert_out[0],
+        cotangent[0],
+        groups,
+    )
+    recvs, mixed, lses, att, res, rows_four, cot_four = [pairs[2 * i : 2 * i + 2] for i in range(7)]
+    mat_qkv = mat_qkv.reshape(width, -1)
+    mat_out = mat_out.reshape(width, width)
+    gain_attn = gains[:, 0].reshape(1, width)
+    gain_ffn = gains[:, 1].reshape(1, width)
+    all_tags = all_tags[:, :, :, 0].transpose(1, 2, 0, 3)
+    query_row = all_tags[0].reshape(MICRO * groups, 1, rows)
+    key_col = all_tags[1].reshape(-1, 1)
+    own_gates = lax.dynamic_index_in_dim(
+        gather_rest(gates_four), lax.axis_index("expert"), 1, False
+    )
+    gate = [own_gates[:, m].reshape(-1, 1) for m in range(MICRO)]
 
     core = lax.axis_index("expert") % 2
     dp = lax.axis_index("dp")
     k_half, f_half = width // 2, w_shared_out.shape[0]
-    ein_parts = (w_expert_in[0], *fetch_parts(after(w_expert_in[0], qkv_part), "context"))
-    eout_parts = (w_expert_out[0], *fetch_parts(after(w_expert_out[0], out_part), "context"))
-    sin_parts = (w_shared_in, *fetch_parts(after(w_shared_in, ein_parts[1]), "expert"))
-    sout_parts = (w_shared_out, *fetch_parts(after(w_shared_out, eout_parts[1]), "expert"))
+    ein_parts = (w_expert_in[0], ein_other)
+    eout_parts = (w_expert_out[0], eout_other)
+    sin_parts = (w_shared_in, *fetch_parts(after(w_shared_in, ein_other), "expert"))
+    sout_parts = (w_shared_out, *fetch_parts(after(w_shared_out, ein_other), "expert"))
+    expert_offs = jnp.stack(
+        [dp * k_half, (1 - dp) * k_half, dp * f_half // FB, (1 - dp) * f_half // FB]
+    )
 
     def offsets(bit):
         places = [2 * (1 - dp) + bit, 2 * (1 - dp) + 1 - bit]
@@ -1013,33 +1298,11 @@
             + [p * (f_half // 2) // FB for p in places]
         )
 
-    all_cot = [gather_xor(cotangent[0, m], "expert") for m in range(MICRO)]
-    gate = [
-        lax.dynamic_index_in_dim(
-            all_gates.reshape(experts, experts, MICRO, rows)[:, :, m], lax.axis_index("expert"), 1, False
-        ).reshape(-1, 1)
-        for m in range(MICRO)
-    ]
-
-    recvs, mixed, lses, att, res, nf = [], [], [], [], [], []
-    for micro in range(MICRO):
-        pay = run_pre(x, micro, gain_attn, mat_qkv, cosines, sines, groups)
-        recvs.append(lax.all_to_all(pay, "context", 0, 0, tiled=True))
-    for micro in range(MICRO):
-        out, lse = run_attend(recvs[: micro + 1], key_row, query_col, groups)
-        mixed.append(out)
-        lses.append(lse)
-    for micro in range(MICRO):
-        got = lax.all_to_all(mixed[micro], "context", 0, 0, tiled=True)
-        a, r, n = run_post(got, x, micro, mat_out, gain_ffn)
-        att.append(a)
-        res.append(r)
-        nf.append(n)
-
     capacity = 4 * rows // experts
 
     def expert_pass(m, grads):
-        hidden, grad, weight = gather_xor(nf[m], "expert"), all_cot[m], gate[m]
+        hidden = gather_rest(rows_four[m]).reshape(-1, width)
+        grad, weight = gather_rest(cot_four[m]).reshape(-1, width), gate[m]
         if capacity < rows:
             chosen = weight.reshape(-1, rows) > 0
             slots = jnp.cumsum(chosen.astype(jnp.int32), 1) - 1
@@ -1051,15 +1314,15 @@
             hidden, grad = squeeze(hidden), squeeze(grad)
             weight = jnp.sum(select.astype(F32) * weight.reshape(-1, 1, rows), -1).reshape(-1, 1)
         made, dx, *grads = run_ffn(
-            hidden, grad, weight, ein_parts, eout_parts, offsets(z % 2), grads=grads, us=38
+            hidden, grad, weight, ein_parts, eout_parts, expert_offs, grads=grads, us=41
         )
         if capacity < rows:
             made, dx = spread(made), spread(dx)
-        return scatter_xor(dx, "expert"), scatter_xor(made, "expert"), grads
+        return scatter_xor(dx), scatter_xor(made), grads
 
     dx0, routed0, g_expert = expert_pass(0, None)
     shared, dx_shared, *g_shared = run_ffn(
-        jnp.concatenate(nf, 0), cot, None, sin_parts, sout_parts, offsets(core), us=21
+        nf_both.reshape(-1, width), cot, None, sin_parts, sout_parts, offsets(core), us=21
     )
     dx1, routed1, g_expert = expert_pass(1, g_expert)
     output = jnp.stack(
@@ -1074,19 +1337,37 @@
     )
     grad0 = lax.all_to_all(pay0, "context", 0, 0, tiled=True)
     back_q0, early_k, early_v = run_attend_back(
-        recvs[:1], grad0, mixed[0], lses[0], key_col, query_row, (), groups
+        recvs[0], grad0, mixed[0], lses[0], key_col, query_row, groups
     )
     q0 = lax.all_to_all(back_q0, "context", 0, 0, tiled=True)
     gres1, pay1, gg1, g_out = run_mid(
         dx_shared, dx1, res[1], gain_ffn, cotangent[0], mat_out, att[1], groups, 1, (att[0], gbf0)
     )
     grad1 = lax.all_to_all(pay1, "context", 0, 0, tiled=True)
-    back1, back_kv0 = run_attend_back(
-        recvs, grad1, mixed[1], lses[1], key_col, query_row, (early_k, early_v), groups
-    )
-    kv0 = lax.all_to_all(back_kv0, "context", 0, 0, tiled=True)
-    d1 = lax.all_to_all(back1, "context", 0, 0, tiled=True)
-    grad_input, g_qkv = run_fin(
+    heads = width // HEAD // groups
+    pay = lambda n: (groups, n * heads, HALF, HALF)
+    held = MICRO * groups * TILE
+    reduced, (d1, kv0) = run_reduce(
+        g_expert,
+        [*g_shared, g_out],
+        1,
+        140,
+        functools.partial(back_extra, heads=heads, groups=groups),
+        (*recvs, grad1, mixed[1], lses[1], key_col, query_row, early_k, early_v),
+        (struct(pay(3), BF), struct(pay(2), BF)),
+        [
+            pltpu.VMEM(pay(3), BF),
+            pltpu.VMEM(pay(2), BF),
+            pltpu.VMEM((heads, held, HALF), BF),
+            pltpu.VMEM((heads, held, HALF), BF),
+            pltpu.VMEM((heads, held, HALF), F32),
+            pltpu.VMEM((heads, held, HALF), F32),
+        ]
+        + [pltpu.SemaphoreType.DMA((groups,))] * 4
+        + [pltpu.SemaphoreType.DMA((2,))],
+    )
+    e_gate, e_up, r_eout, r_gate, r_up, r_sout, r_out = reduced
+    grad_input, *g_qkv = run_fin(
         (q0, kv0, d1),
         x.reshape(MICRO * rows, width),
         gain_attn,
@@ -1102,9 +1383,8 @@
         for mask in bits_of(lax.axis_size(axis)):
             total = total + exchange(total, axis, mask)
     r_gain_ffn = pick(total[0], 2, dp)
-    e_gate, e_up, r_eout, r_gate, r_up, r_sout, r_out, r_qkv = run_reduce(
-        g_expert, [*g_shared, g_out, g_qkv], 1, 160
-    )
+    (r_qk, r_v), _ = run_reduce([], g_qkv, 2, 45)
+    r_qkv = jnp.concatenate([r_qk, r_v], 1)
     r_sin = jnp.concatenate([r_gate, r_up], 1)
     r_gain_attn = jnp.sum(w_qkv.astype(F32) * r_qkv, 1) / norm_attn.astype(F32)
     r_ein = jnp.concatenate([e_gate, e_up], 1)

time: 761 us -> 683 us (0.90)
  Pallas kernels: 445 us -> 572 us
  waiting for transfers between devices: 141 us -> 14.5 us
  starting transfers between devices: 75.2 us -> 28.8 us
  local copies, waits for them, and re-layouts: 38.2 us -> 22 us
  other arithmetic: 49.9 us -> 35.2 us
    pallas_call x9 -> x4, Pallas kernels: 318 us -> 445 us  [the longest x2 286 us: run_reduce(): pl.pallas_call(functools.partial(reduce_kernel, owned=len(own), common=n,...]
    ppermute x36 -> x17, waiting for transfers between devices: 89 us -> 14.5 us  [exchange(): return lax.ppermute(value, axis, [(i, i ^ mask) for i in range(size)])]
    all_to_all x7 -> x0, waiting for transfers between devices: 46.1 us -> none  [the longest x2 24.2 us: body(): recvs.append(lax.all_to_all(pay, 'context', 0, 0, tiled=True))]
    all_to_all x7 -> x0, starting transfers between devices: 34.4 us -> none  [the longest x2 10 us: body(): got = lax.all_to_all(mixed[micro], 'context', 0, 0, tiled=True)]
    concatenate x10 -> x0, other arithmetic: 17.8 us -> none  [the longest x7 12.2 us: gather_xor(): value = jnp.concatenate([value, exchange(value, axis, mask)], 0)]
    ppermute x36 -> x17, starting transfers between devices: 28.9 us -> 15.2 us  [exchange(): return lax.ppermute(value, axis, [(i, i ^ mask) for i in range(size)])]
  transfers between devices with their start and end apart: 46 -> 20, of which waited for: 14 -> 4; matrix products, arithmetic and copies ran while one was open for 9% -> 6% of each run, Pallas kernels for 32% -> 54%
where the time goes in v2:
time: 683 us; the launch traced here: 673 us
  Pallas kernels  572 us (84%)
  other arithmetic  35.2 us (5%)
  starting transfers between devices  28.8 us (4%)
  local copies, waits for them, and re-layouts  22 us (3%)
  waiting for transfers between devices  14.5 us (2%)
    pallas_call x2, Pallas kernels, run_reduce(): pl.pallas_call(functools.partial(reduce_kernel, owned=len(own), common=n,...  286 us
    pallas_call x1, Pallas kernels, run_front(): pl.pallas_call(functools.partial(front_kernel, heads=heads, groups=groups...  136 us
    pallas_call x3, Pallas kernels, run_ffn(): pl.pallas_call(functools.partial(ffn_kernel, tr=math.gcd(tr, rows), spans...  108 us
    pallas_call x1, Pallas kernels, run_attend_back(): call(functools.partial(attend_back_kernel, heads=heads, groups=groups), t...  22.5 us
    ppermute x17, starting transfers between devices, exchange(): return lax.ppermute(value, axis, [(i, i ^ mask) for i in range(size)])  15.2 us
    ppermute x17, waiting for transfers between devices, exchange(): return lax.ppermute(value, axis, [(i, i ^ mask) for i in range(size)])  14.5 us
  transfers between devices with their start and end apart: 20, of which 4 were waited for; matrix products, arithmetic and copies ran while one was open for 6% of the time, Pallas kernels for 54%

profile of v2, /device:TPU:0, one launch (start us, length us, event | category | flops | bytes accessed | tf_op | source)
XLA Modules:
  0.0 673.3 jit_solution(879783537202985186)
XLA Ops:
  0.8 0.8 compare_select_fusion
  2.2 0.7 select_reduce_fusion
  2.9 0.6 copy.44.refs_5_
  3.5 0.7 stack.55
  4.2 0.7 stack.56
  4.8 1.0 fusion.3
  6.4 1.3 pad_maximum_fusion
  7.7 136.2 %shard_map.213 = (bf16[4,9,128,128]{3,2,1,0:T(8,128)(2,1)}, bf16[4,9,128,128]{3,2,1,0:T(8,128)(2,1)}, bf16[4,3,128,128]{3,2,1,0:T(8,128)(2,1)}, bf16[4,3,128,128...) custom-call(bf16[2,256,768]{2,1,0:T(8,128)(2,1)} %bitcast.108, ...), custom_call_target="tpu_custom_call" | custom-call | flops 149500002304 | tf_op jit(solution)/shard_map/pallas_call | solution.py:535
  143.9 1.3 constant_dynamic-slice_fusion.1
  145.7 0.7 dynamic-slice_bitcast_fusion
  146.4 1.0 copy.45.refs_3_
  147.5 1.0 copy.46.refs_3_
  148.5 0.7 pad_add_fusion.1.refs_0_
  149.1 41.6 %shard_map.215 = (bf16[1024,768]{1,0:T(8,128)(2,1)}, bf16[1024,768]{1,0:T(8,128)(2,1)}, bf16[768,2048]{1,0:T(8,128)(2,1)}, bf16[768,2048]{1,0:T(8,128)(2,1)}, bf16[2048,768]{1,0:T(8,128)(2,1)}) custom-call(s32[4]{0:T(128)} %pad_add_fusion.1.refs_0_, bf16[1024,768]{1,0:T(8,128)(2,1)} %bitcast.122, bf16[1024,768]{1,0:T(8,128)(2,1)} %bitcast.123, ...), custom_call_target="tpu_custom_call" | custom-call | flops 47149998080 | tf_op jit(solution)/shard_map/pallas_call | solution.py:659
  190.8 42.8 %shard_map.216 = (bf16[1024,768]{1,0:T(8,128)(2,1)}, bf16[1024,768]{1,0:T(8,128)(2,1)}, bf16[768,2048]{1,0:T(8,128)(2,1)}, bf16[768,2048]{1,0:T(8,128)(2,1)}, bf16[2048,768]{1,0:T(8,128)(2,1)}) custom-call(s32[4]{0:T(128)} %pad_add_fusion.1.refs_0_, bf16[1024,768]{1,0:T(8,128)(2,1)} %bitcast.120, bf16[1024,768]{1,0:T(8,128)(2,1)} %bitcast.121, ...), custom_call_target="tpu_custom_call" | custom-call | flops 47149998080 | tf_op jit(solution)/shard_map/pallas_call | solution.py:659
  233.6 2.2 slice.92
  235.8 0.9 slice.85
  237.2 2.2 constant_dynamic-slice_fusion
  239.4 1.7 collective-permute-start.2
  241.1 0.9 slice.81
  242.1 0.9 slice.75
  243.0 0.7 stack.65.refs_0_
  244.9 1.3 add_convert_fusion
  246.2 1.6 collective-permute-start.11
  247.8 1.3 add_convert_fusion.1
  249.8 1.3 add_convert_fusion.2
  251.1 0.8 slice.101
  251.8 7.3 %collective-permute-done.2.refs_10_ = bf16[512,768]{1,0:T(8,128)(2,1)} collective-permute-done((bf16[512,768]{1,0:T(8,128)(2,1)}, bf16[512,768]{1,0:T(8,128)(2,1)}, u32[]{:S(2)}, u32[]{:S(2)}) %collective-permute-start.2) | collective-permute-done | bytes 786464 | tf_op jit(solution)/shard_map/ppermute | solution.py:809
  259.2 1.5 collective-permute-start.7
  260.9 0.8 slice.98
  262.2 0.9 add_convert_fusion.4.refs_1_
  263.0 3.6 collective-permute-done.9
  266.6 0.8 add_convert_fusion.5.refs_1_
  267.5 23.2 %shard_map.214 = (bf16[512,768]{1,0:T(8,128)(2,1)}, bf16[512,768]{1,0:T(8,128)(2,1)}, bf16[768,2048]{1,0:T(8,128)(2,1)}, bf16[768,2048]{1,0:T(8,128)(2,1)}, bf16[2048,768]{1,0:T(8,128)(2,1)}) custom-call(s32[6]{0:T(128)} %stack.65.refs_0_, bf16[512,768]{1,0:T(8,128)(2,1)} %bitcast.128, bf16[512,768]{1,0:T(8,128)(2,1)} %bitcast.105, ...), custom_call_target="tpu_custom_call" | custom-call | flops 24149999616 | tf_op jit(solution)/shard_map/pallas_call | solution.py:659
  290.7 3.6 shard_map.217
  294.4 4.6 shard_map.219
  299.0 0.8 add.148
  299.8 1.2 collective-permute-done.12
  301.6 1.5 collective-permute-start.13
  303.1 4.1 all-to-all-start
  307.3 1.3 add.150
  308.5 2.0 collective-permute-start.14
  310.5 0.6 fusion.5
  311.1 0.7 copy.47
  311.8 1.9 reshape_squeeze.32.refs_4_.refs_12_
  313.7 1.3 copy.48
  315.0 0.7 add.151
  315.7 3.8 collective-permute-start.15
  319.5 1.6 fusion.1
  321.5 0.9 maximum_bitcast_fusion.1
  322.4 2.3 collective-permute-done.16
  325.4 4.1 all-to-all-start.2
  329.5 22.5 %shard_map.218 = (bf16[4,3,128,128]{3,2,1,0:T(8,128)(2,1)}, f32[3,1024,128]{2,1,0:T(8,128)}, f32[3,1024,128]{2,1,0:T(8,128)}) custom-call(bf16[4,9,128,128]{3,2,1,0:T(8,128)(2,1)} %get-tuple-element.92.refs_0_.refs_7_, bf16[4,3,128,128]{3,2,1,0:T(8,128)(2,1)} %all-to-all-done.refs_1_, bf16[4,3,128,128]{3,2,1,0:T(8,128)(2,1)} %get-tuple-element.99.refs_2_, ...), custom_call_target="tpu_custom_call" | custom-call | flops 26449999872 | tf_op jit(solution)/shard_map/pallas_call | solution.py:248
  352.0 5.3 all-to-all-start.1
  357.3 226.7 %shard_map.220 = (bf16[4,96,2048]{2,1,0:T(8,128)(2,1)}, bf16[4,96,2048]{2,1,0:T(8,128)(2,1)}, bf16[4,256,768]{2,1,0:T(8,128)(2,1)}, bf16[2,2,96,2048]{3,2,1,0:T(...) custom-call(bf16[2,4,96,2048]{3,2,1,0:T(8,128)(2,1)} %bitcast.112, ...), custom_call_target="tpu_custom_call" | custom-call | flops 160999997440 | tf_op jit(solution)/shard_map/pallas_call | solution.py:1105
  584.0 3.4 bitcast_convert_fusion
  587.5 2.0 bitcast_convert_fusion.1
  589.5 1.1 bitcast_convert_fusion.2
  590.6 0.8 copy-done.3
  591.4 3.5 fusion
  594.8 3.5 maximum_convert_fusion
  598.3 10.6 %shard_map.221 = (f32[512,768]{1,0:T(8,128)}, bf16[768,1152]{1,0:T(8,128)(2,1)}, bf16[768,1152]{1,0:T(8,128)(2,1)}) custom-call(bf16[4,3,128,128]{3,2,1,0:T(8,128)(2,1)} %all-to-all-done.1.q0, bf16[4,6,128,128]{3,2,1,0:T(8,128)(2,1)} %get-tuple-element.119.kv0, bf16[4,9,128,128]{3,2,1,0:T(8,128)(2,1)} %get-tuple-element.120.d1, bf16[512,768]{1,0:T(8,128)(2,1)} %bitcast.109, ...), custom_call_target="tpu_custom_call" | custom-call | flops 12650000384 | tf_op jit(solution)/shard_map/pallas_call | solution.py:796
  608.9 59.7 %shard_map.222 = (bf16[2,2,96,1152]{3,2,1,0:T(8,128)(2,1)}, bf16[2,2,96,1152]{3,2,1,0:T(8,128)(2,1)}) custom-call(bf16[2,2,2,96,1152]{4,3,2,1,0:T(8,128)(2,1)} %bitcast.118, bf16[2,2,2,96,1152]{4,3,2,1,0:T(8,128)(2,1)} %bitcast.119), custom_call_target="tpu_custom_call" | custom-call | flops 51749998592 | tf_op jit(solution)/shard_map/pallas_call | solution.py:1105
  668.6 3.7 multiply_reduce_fusion
  (86 shorter events, 7.1 us)
Async XLA Ops:
  7.7 136.2 %copy-start.14 = (bf16[384,4096]{1,0:T(8,128)(2,1)S(1)}, bf16[384,4096]{1,0:T(8,128)(2,1)}, u32[]{:S(2)}) copy-start(bf16[384,4096]{1,0:T(8,128)(2,1)} %refs_6_.1) | copy-start | bytes 9437188
  145.2 99.6 %collective-permute-start = (bf16[192,4096]{1,0:T(8,128)(2,1)}, bf16[192,4096]{1,0:T(8,128)(2,1)}, u32[]{:S(2)}, u32[]{:S(2)}) collective-permute-start(bf16[192,4096]{1,0:T(8,128)(2,1)} %constant_dynamic-slice_fusion.1), channel_id=1, source_target_pairs={{0,1},{1,0},{2,3},{3,2},{4,5},{5,4},{6,7},{7,6},{8,9},{9,8},{10,11... | collective-permute-start | bytes 4718600 | tf_op jit(solution)/shard_map/ppermute | solution.py:809
  233.6 2.2 copy-start.8
  235.8 8.5 %collective-permute-start.10 = (bf16[512,768]{1,0:T(8,128)(2,1)}, bf16[512,768]{1,0:T(8,128)(2,1)}, u32[]{:S(2)}, u32[]{:S(2)}) collective-permute-start(bf16[512,768]{1,0:T(8,128)(2,1)} %slice.92), channel_id=1, source_target_pairs={{0,8},{8,0},{16,24},{24,16},{1,9},{9,1},{17,25},{25,17},{2,10},{10... | collective-permute-start | bytes 2359304 | tf_op jit(solution)/shard_map/ppermute | solution.py:809
  235.8 5.3 copy-start.6
  236.7 9.5 %collective-permute-start.8 = (bf16[512,768]{1,0:T(8,128)(2,1)}, bf16[512,768]{1,0:T(8,128)(2,1)}, u32[]{:S(2)}, u32[]{:S(2)}) collective-permute-start(bf16[512,768]{1,0:T(8,128)(2,1)} %slice.85), channel_id=1, source_target_pairs={{0,8},{8,0},{16,24},{24,16},{1,9},{9,1},{17,25},{25,17},{2,10},{10... | collective-permute-start | bytes 2359304 | tf_op jit(solution)/shard_map/ppermute | solution.py:809
  237.2 4.8 copy-start.5
  239.4 19.8 %collective-permute-start.2 = (bf16[512,768]{1,0:T(8,128)(2,1)}, bf16[512,768]{1,0:T(8,128)(2,1)}, u32[]{:S(2)}, u32[]{:S(2)}) collective-permute-start(bf16[512,768]{1,0:T(8,128)(2,1)} %constant_dynamic-slice_fusion), channel_id=1, source_target_pairs={{0,1},{1,0},{2,3},{3,2},{4,5},{5,4},{6,7},{7,6},{8,9},{9,8},{10,11... | collective-permute-start | bytes 2359304 | tf_op jit(solution)/shard_map/ppermute | solution.py:809
  241.1 2.6 copy-start.18
  242.0 2.8 copy-start.10
  242.0 7.1 %collective-permute-start.6 = (bf16[512,768]{1,0:T(8,128)(2,1)}, bf16[512,768]{1,0:T(8,128)(2,1)}, u32[]{:S(2)}, u32[]{:S(2)}) collective-permute-start(bf16[512,768]{1,0:T(8,128)(2,1)} %slice.81), channel_id=1, source_target_pairs={{0,8},{8,0},{16,24},{24,16},{1,9},{9,1},{17,25},{25,17},{2,10},{10... | collective-permute-start | bytes 2359304 | tf_op jit(solution)/shard_map/ppermute | solution.py:809
  244.3 3.6 copy-start.9
  244.3 16.4 %collective-permute-start.4 = (bf16[512,768]{1,0:T(8,128)(2,1)}, bf16[512,768]{1,0:T(8,128)(2,1)S(1)}, u32[]{:S(2)}, u32[]{:S(2)}) collective-permute-start(bf16[512,768]{1,0:T(8,128)(2,1)} %slice.75), channel_id=1, source_target_pairs={{0,8},{8,0},{16,24},{24,16},{1,9},{9,1},{17,25},{25,17},{2,10},{10... | collective-permute-start | bytes 2359304 | tf_op jit(solution)/shard_map/ppermute | solution.py:809
  244.8 22.7 %collective-permute-start.1 = (bf16[192,4096]{1,0:T(8,128)(2,1)}, bf16[192,4096]{1,0:T(8,128)(2,1)}, u32[]{:S(2)}, u32[]{:S(2)}) collective-permute-start(bf16[192,4096]{1,0:T(8,128)(2,1)} %collective-permute-done.refs_4_.refs_7_), channel_id=1, source_target_pairs={{0,8},{8,0},{16,24},{24,16},{1,9},{9,1},{17,25},{25,17},{2,10},{10... | collective-permute-start | bytes 4718600 | tf_op jit(solution)/shard_map/ppermute | solution.py:809
  246.2 3.5 copy-start.7
  246.2 15.4 %collective-permute-start.11 = (bf16[256,768]{1,0:T(8,128)(2,1)S(1)}, bf16[256,768]{1,0:T(8,128)(2,1)S(1)}, u32[]{:S(2)}, u32[]{:S(2)}) collective-permute-start(bf16[256,768]{1,0:T(8,128)(2,1)S(1)} %slice.107), channel_id=1, source_target_pairs={{0,16},{8,24},{16,0},{24,8},{1,17},{9,25},{17,1},{25,9},{2,18},{10... | collective-permute-start | bytes 1179656 | tf_op jit(solution)/shard_map/ppermute | solution.py:809
  249.2 17.5 %collective-permute-start.9 = (bf16[256,768]{1,0:T(8,128)(2,1)S(1)}, bf16[256,768]{1,0:T(8,128)(2,1)S(1)}, u32[]{:S(2)}, u32[]{:S(2)}) collective-permute-start(bf16[256,768]{1,0:T(8,128)(2,1)S(1)} %slice.103), channel_id=1, source_target_pairs={{0,16},{8,24},{16,0},{24,8},{1,17},{9,25},{17,1},{25,9},{2,18},{10... | collective-permute-start | bytes 1179656 | tf_op jit(solution)/shard_map/ppermute | solution.py:809
  259.2 60.3 %collective-permute-start.7 = (bf16[256,768]{1,0:T(8,128)(2,1)}, bf16[256,768]{1,0:T(8,128)(2,1)S(1)}, u32[]{:S(2)}, u32[]{:S(2)}) collective-permute-start(bf16[256,768]{1,0:T(8,128)(2,1)} %slice.101), channel_id=1, source_target_pairs={{0,16},{8,24},{16,0},{24,8},{1,17},{9,25},{17,1},{25,9},{2,18},{10... | collective-permute-start | bytes 1179656 | tf_op jit(solution)/shard_map/ppermute | solution.py:809
  260.7 6.8 %collective-permute-start.3 = (bf16[512,768]{1,0:T(8,128)(2,1)}, bf16[512,768]{1,0:T(8,128)(2,1)}, u32[]{:S(2)}, u32[]{:S(2)}) collective-permute-start(bf16[512,768]{1,0:T(8,128)(2,1)} %collective-permute-done.2.refs_10_), channel_id=1, source_target_pairs={{0,8},{8,0},{16,24},{24,16},{1,9},{9,1},{17,25},{25,17},{2,10},{10... | collective-permute-start | bytes 2359304 | tf_op jit(solution)/shard_map/ppermute | solution.py:809
  261.7 57.8 %collective-permute-start.5 = (bf16[256,768]{1,0:T(8,128)(2,1)}, bf16[256,768]{1,0:T(8,128)(2,1)}, u32[]{:S(2)}, u32[]{:S(2)}) collective-permute-start(bf16[256,768]{1,0:T(8,128)(2,1)} %slice.98), channel_id=1, source_target_pairs={{0,16},{8,24},{16,0},{24,8},{1,17},{9,25},{17,1},{25,9},{2,18},{10... | collective-permute-start | bytes 1179656 | tf_op jit(solution)/shard_map/ppermute | solution.py:809
  294.4 4.7 copy-start.20
  294.4 8.7 %copy-start.17 = (s32[4,2,2,1,256]{4,3,2,1,0:T(1,128)S(1)}, s32[4,2,2,1,256]{4,3,2,1,0:T(1,128)}, u32[]{:S(2)}) copy-start(s32[4,2,2,1,256]{4,3,2,1,0:T(1,128)} %get-tuple-element.101) | copy-start | bytes 49156
  299.0 20.5 %copy-start.12 = (f32[256,768]{1,0:T(8,128)S(1)}, f32[256,768]{1,0:T(8,128)}, u32[]{:S(2)}) copy-start(f32[256,768]{1,0:T(8,128)} %get-tuple-element.74.refs_2_) | copy-start | bytes 2359300
  299.0 20.5 %copy-start.13 = (f32[256,768]{1,0:T(8,128)S(1)}, f32[256,768]{1,0:T(8,128)}, u32[]{:S(2)}) copy-start(f32[256,768]{1,0:T(8,128)} %get-tuple-element.85.refs_2_) | copy-start | bytes 2359300
  299.8 1.2 collective-permute-start.12
  301.6 5.7 collective-permute-start.13
  303.1 22.3 %all-to-all-start = ((bf16[4,3,128,128]{3,2,1,0:T(8,128)(2,1)}), bf16[4,3,128,128]{3,2,1,0:T(8,128)(2,1)}, u32[]{:S(2)}, u32[]{:S(2)}) async-start(bf16[4,3,128,128]{3,2,1,0:T(8,128)(2,1)} %get-tuple-element.98), calls=%async_computation | async-start | bytes 786432 | tf_op jit(solution)/shard_map/all_to_all | solution.py:1338
  308.5 6.4 collective-permute-start.14
  315.7 5.4 collective-permute-start.15
  321.1 3.7 collective-permute-start.16
  325.4 26.6 %all-to-all-start.2 = ((bf16[4,3,128,128]{3,2,1,0:T(8,128)(2,1)}), bf16[4,3,128,128]{3,2,1,0:T(8,128)(2,1)S(1)}, u32[]{:S(2)}, u32[]{:S(2)}) async-start(bf16[4,3,128,128]{3,2,1,0:T(8,128)(2,1)} %get-tuple-element.114), calls=%async_computation.2 | async-start | bytes 786432 | tf_op jit(solution)/shard_map/all_to_all | solution.py:1346
  352.0 5.3 copy-start.16
  352.0 246.3 %all-to-all-start.1 = ((bf16[4,3,128,128]{3,2,1,0:T(8,128)(2,1)}), bf16[4,3,128,128]{3,2,1,0:T(8,128)(2,1)}, u32[]{:S(2)}, u32[]{:S(2)}) async-start(bf16[4,3,128,128]{3,2,1,0:T(8,128)(2,1)} %get-tuple-element.102), calls=%async_computation.1 | async-start | bytes 786432 | tf_op jit(solution)/shard_map/all_to_all | solution.py:1342
  584.0 3.4 copy-start.11
  587.4 2.0 copy-start.15
  587.4 3.1 copy-start.4
  589.5 1.9 copy-start.3
  591.4 3.5 copy-start.1
  591.4 3.5 copy-start.2
  608.9 59.7 %copy-start = (bf16[384,2304]{1,0:T(8,128)(2,1)S(1)}, bf16[384,2304]{1,0:T(8,128)(2,1)}, u32[]{:S(2)}) copy-start(bf16[384,2304]{1,0:T(8,128)(2,1)} %param.20) | copy-start | bytes 5308420
  668.6 3.7 copy-start.19

commit v3 on v2

v3 whole, which is shorter than its diff:
```python
import functools
import math

import jax
import jax.numpy as jnp
from jax import lax
from jax.experimental import pallas as pl
from jax.experimental.pallas import tpu as pltpu
from jax.sharding import PartitionSpec as P

HEAD = 64
MICRO = 2
TILE = 256
HALF = 128
EPSILON = 1e-05
ROPE_BASE = 10000.0
MASKED = -3e30
HIDDEN = 1 << 20
BF = jnp.bfloat16
F32 = jnp.float32
NT = (((1,), (1,)), ((), ()))
TN = (((0,), (0,)), ((), ()))
VMEM_LIMIT = 60 << 20
FB = 512


def dot(left, right, dims=(((1,), (0,)), ((), ()))):
    return lax.dot_general(left, right, dims, preferred_element_type=F32)


def rms_scale(values):
    return lax.rsqrt(jnp.mean(values * values, -1, keepdims=True) + EPSILON)


def low_lanes(rows):
    return lax.broadcasted_iota(jnp.int32, (rows, HALF), 1) < HEAD


def swap_heads(first, second):
    low = low_lanes(HALF)
    return (
        jnp.where(low, first, pltpu.roll(second, HEAD, 1)),
        jnp.where(low, pltpu.roll(first, HEAD, 1), second),
    )


def rotate(tile, cosines, sines):
    lane = lax.broadcasted_iota(jnp.int32, tile.shape, 1)
    partner = jnp.where(
        lane % HEAD < HEAD // 2,
        pltpu.roll(tile, HALF - HEAD // 2, 1),
        pltpu.roll(tile, HEAD // 2, 1),
    )
    return tile * cosines + partner * sines


def call(kernel, out_shape, *, grid=(), in_specs=None, out_specs=None, scratch=(), us=5):
    return pl.pallas_call(
        kernel,
        out_shape=out_shape,
        grid=grid,
        in_specs=in_specs,
        out_specs=out_specs,
        scratch_shapes=scratch,
        compiler_params=pltpu.CompilerParams(vmem_limit_bytes=VMEM_LIMIT),
        cost_estimate=price(us),
    )


def full_spec(shape):
    return pl.BlockSpec(tuple(shape), lambda *_: (0,) * len(shape))


def struct(shape, dtype):
    return jax.ShapeDtypeStruct(tuple(shape), dtype)


def project(tokens, gain, w_ref, cosines, sines, pay, groups):
    normed = (tokens * rms_scale(tokens) * gain).astype(BF)
    width = tokens.shape[1]
    per = width // HEAD // groups
    for kind in range(3):
        joined = dot(normed, w_ref[:, kind * width : (kind + 1) * width])
        for pair in range(width // HALF):
            tile = joined[:, pair * HALF : (pair + 1) * HALF]
            if kind < 2:
                tile = rotate(tile, cosines, sines)
            if kind == 0:
                tile = tile * 0.125
            for side, packed in enumerate(swap_heads(tile[:HALF], tile[HALF:])):
                head = 2 * pair + side
                pay[head // per, kind * per + head % per] = packed.astype(BF)


def unpack(ref, index, kind_head):
    tile = ref[index, kind_head]
    return tile, pltpu.roll(tile.astype(F32), HEAD, 1).astype(BF)


def fill_keys(recv, micro, ks, vs, heads):
    groups = recv.shape[0]
    for src in range(groups):
        base = (micro * groups + src) * TILE
        for h in range(heads):
            for store, kind in ((ks, 1), (vs, 2)):
                first, second = unpack(recv, src, kind * heads + h)
                store[h, base : base + HALF] = first
                store[h, base + HALF : base + TILE] = second


def masked_rows(ref, index, kind_head):
    tile = ref[index, kind_head].astype(F32)
    both = jnp.concatenate([tile, pltpu.roll(tile, HEAD, 1)], 0)
    return jnp.where(low_lanes(TILE), both, 0.0)


def pack_rows(values):
    return jnp.where(low_lanes(HALF), values[:HALF], pltpu.roll(values[HALF:], HEAD, 1))


def attend_step(step, micro, heads, groups, recv, tags, out_ref, lse_ref, ks, vs, scores):
    count = groups * micro + jnp.minimum(step + 2, groups)
    queries = [masked_rows(recv, step, h).astype(BF) for h in range(heads)]
    tag = jnp.broadcast_to(tags[step, 0, micro], (8, TILE)).T[:, :1]
    same = lax.broadcasted_iota(jnp.int32, (TILE, TILE), 0) == lax.broadcasted_iota(
        jnp.int32, (TILE, TILE), 1
    )

    def first_pass(j, tops):
        keys = pl.ds(pl.multiple_of(j * TILE, TILE), TILE)
        key_tag = tags[j % groups, 1, j // groups]
        seen = (key_tag <= tag) | (same & (j == groups * micro + step))
        new = []
        for h in range(heads):
            part = jnp.where(seen, dot(queries[h], ks[h, keys, :], NT), MASKED)
            scores[h, :, keys] = part
            new.append(jnp.maximum(tops[h], jnp.maximum(part[:, :HALF], part[:, HALF:])))
        return tuple(new)

    tops = lax.fori_loop(
        0, count, first_pass, (jnp.full((TILE, HALF), MASKED, F32),) * heads
    )
    tops = [jnp.max(top, 1, keepdims=True) for top in tops]

    def second_pass(j, carry):
        keys = pl.ds(pl.multiple_of(j * TILE, TILE), TILE)
        sums, totals = carry
        new_sums, new_totals = [], []
        for h in range(heads):
            expo = jnp.exp(scores[h, :, keys] - tops[h])
            new_sums.append(sums[h] + (expo[:, :HALF] + expo[:, HALF:]))
            new_totals.append(totals[h] + dot(expo.astype(BF), vs[h, keys, :]))
        return tuple(new_sums), tuple(new_totals)

    zero = (jnp.zeros((TILE, HALF), F32),) * heads
    sums, totals = lax.fori_loop(0, count, second_pass, (zero, zero))
    lane = lax.broadcasted_iota(jnp.int32, (TILE, HALF), 1)
    logs = jnp.zeros((TILE, HALF), F32)
    for h in range(heads):
        total = jnp.sum(sums[h], 1, keepdims=True)
        out_ref[step, h] = pack_rows(totals[h] / total).astype(BF)
        logs = jnp.where(lane == h, tops[h] + jnp.log(total), logs)
    lse_ref[step] = logs.T[:8]


def back_begin(micro, step, heads, recv, grad, out, qs, gs, deltas, acc):
    ones = jnp.ones((8, HALF), F32)
    for h in range(heads):
        grad_f = masked_rows(grad, step, h)
        qs[h] = masked_rows(recv, step, h).astype(BF)
        gs[h] = grad_f.astype(BF)
        deltas[h] = lax.dot_general(
            ones,
            grad_f * masked_rows(out, step, h),
            NT,
            precision=lax.Precision.HIGHEST,
            preferred_element_type=F32,
        )
    acc[...] = jnp.zeros_like(acc)


def back_tile(micro, step, j, heads, groups, lse, key_tag, query_tag, ks, vs, dk, dv, qs, gs, deltas, acc):
    keys = pl.ds(pl.multiple_of(j * TILE, TILE), TILE)
    same = lax.broadcasted_iota(jnp.int32, (TILE, TILE), 0) == lax.broadcasted_iota(
        jnp.int32, (TILE, TILE), 1
    )
    tag = query_tag[groups * micro + step]
    seen = (key_tag[keys, :] <= tag) | (same & (j == groups * micro + step))
    for h in range(heads):
        key, value = ks[h, keys, :], vs[h, keys, :]
        scores = dot(key, qs[h], NT)
        probs = jnp.where(seen, jnp.exp(scores - lse[step, h : h + 1, :]), 0.0)
        dv[h, keys, :] += dot(probs.astype(BF), gs[h])
        slope = (probs * (dot(value, gs[h], NT) - deltas[h, :1])).astype(BF)
        dk[h, keys, :] += dot(slope, qs[h])
        acc[h] += dot(slope, key, TN)


def back_pack(dk, dv, pay, src, base, heads):
    rows = slice((base + src) * TILE, (base + src + 1) * TILE)
    for h in range(heads):
        pay[src, heads + h] = pack_rows(dk[h, rows]).astype(BF)
        pay[src, 2 * heads + h] = pack_rows(dv[h, rows]).astype(BF)


def natural(ref, first_kind, pair, per):
    tiles = []
    for head in (2 * pair, 2 * pair + 1):
        tiles.append(ref[head // per, first_kind * per + head % per].astype(F32))
    return jnp.concatenate(swap_heads(*tiles), 0)


def remote(src, dst, sems, index, target, arrival=None):
    return pltpu.make_async_remote_copy(
        src_ref=src,
        dst_ref=dst,
        send_sem=sems[0].at[index],
        recv_sem=sems[1].at[index if arrival is None else arrival],
        device_id=target,
        device_id_type=pl.DeviceIdType.MESH,
    )


def meet(barrier, targets):
    for target in targets:
        pl.semaphore_signal(barrier, inc=1, device_id=target, device_id_type=pl.DeviceIdType.MESH)
    pl.semaphore_wait(barrier, len(targets))


class Trade:
    def __init__(self, src, dst, sems, local):
        self.src, self.dst, self.sems, self.local = src, dst, sems, local
        self.z = lax.axis_index("context")
        self.groups = src.shape[0]

    def wire(self, other, arrival):
        return remote(self.src.at[other], self.dst.at[arrival], self.sems, other, {"context": other}, arrival)

    def keep(self, index):
        return pltpu.make_async_copy(self.src.at[index], self.dst.at[index], self.local)

    def send(self, dest):
        @pl.when(dest != self.z)
        def _():
            self.wire(dest, self.z).start()

        @pl.when(dest == self.z)
        def _():
            self.keep(dest).start()

    def await_from(self, other):
        @pl.when(other != self.z)
        def _():
            self.wire(other, other).wait_recv()

        @pl.when(other == self.z)
        def _():
            self.keep(other).wait()

    def collect(self):
        for other in range(self.groups):
            self.await_from(other)

    def release(self):
        for other in range(self.groups):

            @pl.when(other != self.z)
            def _(other=other):
                self.wire(other, self.z).wait_send()


def front_kernel(*refs, heads, groups):
    refs = list(refs)
    take = lambda n: [refs.pop(0) for _ in range(n)]
    x_ref, gains_in, cos_ref, sin_ref, tags_in, gates_in = take(6)
    w_qkv, w_out, w_ein, w_eout, w_sin, w_sout, cot = take(7)
    recv_out, mixed_out, lse_out, att_out, res_out = take(2), take(2), take(2), take(2), take(2)
    rows_out, cot_out, gates_out, both_out, tags_out = take(2), take(2), take(1)[0], take(1)[0], take(1)[0]
    qkv_out, wout_out, ein_out, eout_out, sin_out, sout_out, gains_out = take(7)
    wq, wo, gains, tags, pay, recv, ks, vs, scores, mixed, got, lse, att, res, nf = take(15)
    s_qkv, s_out, s_gain, s_exp, s_tag, s_gate, s_cot, s_pay, s_mix, s_row = [take(2) for _ in range(10)]
    local, self_pay, self_mix, self_tag, stores = take(5)
    e, z, d = lax.axis_index("expert"), lax.axis_index("context"), lax.axis_index("dp")
    core, y = e % 2, e // 2 % 2
    to_x, to_core, to_y = {"dp": 1 - d}, {"expert": e + 1 - 2 * core}, {"expert": e + 2 - 4 * y}
    others = [{"context": (z + k) % groups} for k in range(1, groups)]
    width = x_ref.shape[2]

    loads = [
        pltpu.make_async_copy(w_qkv, wq.at[d], local.at[0]),
        pltpu.make_async_copy(w_out, wo.at[d], local.at[1]),
        pltpu.make_async_copy(gains_in, gains.at[d], local.at[2]),
    ]
    for copy in loads:
        copy.start()
    meet(pltpu.get_barrier_semaphore(), [to_x, to_core, to_y, *others])

    x_qkv = remote(w_qkv.at[core], wq.at[d, core], s_qkv, 0, to_x)
    x_gain = remote(gains_in, gains.at[d], s_gain, 0, to_x)
    x_out = remote(w_out.at[core], wo.at[d, core], s_out, 0, to_x)
    half = z % 2
    to_mate = {"context": z + 1 - 2 * half}
    x_exp = [
        remote(w_ein.at[half], ein_out.at[0], s_exp, 0, to_x),
        remote(w_eout, eout_out, s_exp, 1, to_x),
        remote(w_sin.at[core], sin_out.at[0], s_exp, 2, to_x),
        remote(w_sout.at[core], sout_out.at[0], s_exp, 3, to_x),
    ]
    n_exp = [
        remote(ein_out.at[0], ein_out.at[1], s_exp, 4, to_mate),
        remote(sin_out.at[0], sin_out.at[1], s_exp, 5, to_core),
        remote(sout_out.at[0], sout_out.at[1], s_exp, 6, to_core),
    ]
    for copy in (x_qkv, x_gain, x_out, *x_exp):
        copy.start()
    tag_trade = [
        remote(tags_in, tags.at[z], s_tag, k, others[k]) for k in range(groups - 1)
    ]
    tag_own = pltpu.make_async_copy(tags_in, tags.at[z], self_tag.at[0])
    tag_own.start()
    for copy in tag_trade:
        copy.start()
    own_copies = [
        pltpu.make_async_copy(gates_in, gates_out.at[0], stores.at[0]),
        pltpu.make_async_copy(cot.at[0], cot_out[0].at[0], stores.at[1]),
        pltpu.make_async_copy(cot.at[1], cot_out[1].at[0], stores.at[2]),
    ]
    for copy in own_copies:
        copy.start()
    y_gate = remote(gates_in, gates_out.at[1], s_gate, 0, to_y)
    y_cot = [remote(cot.at[m], cot_out[m].at[1], s_cot, m, to_y) for m in range(MICRO)]
    c_gate = [
        remote(gates_in, gates_out.at[2], s_gate, 1, to_core),
        remote(gates_out.at[1], gates_out.at[3], s_gate, 2, to_core),
    ]
    c_cot = [remote(cot.at[m], cot_out[m].at[2], s_cot, 2 + m, to_core) for m in range(MICRO)] + [
        remote(cot_out[m].at[1], cot_out[m].at[3], s_cot, 4 + m, to_core) for m in range(MICRO)
    ]
    y_gate.start()
    for copy in y_cot:
        copy.start()

    c_qkv = remote(wq.at[1 - d, core], wq.at[1 - d, core], s_qkv, 1, to_core)
    c_out = remote(wo.at[1 - d, core], wo.at[1 - d, core], s_out, 1, to_core)
    for copy in loads:
        copy.wait()
    x_qkv.wait_recv()
    c_qkv.start()
    x_gain.wait_recv()
    c_qkv.wait_recv()
    both = [jnp.concatenate([gains[0, k : k + 1], gains[1, k : k + 1]], 1) for k in range(2)]
    w_full = wq.reshape(width, 3 * width)
    trades, returns = [], []
    for m in range(MICRO):
        span = slice(m * TILE, (m + 1) * TILE)
        project(x_ref[m].astype(F32), both[0], w_full, cos_ref[span, :], sin_ref[span, :], pay.at[m], groups)
        trade = Trade(pay.at[m], recv.at[m], [s.at[m] for s in s_pay], self_pay.at[m])
        for dest in range(groups):
            trade.send(dest)
        trades.append(trade)
    c_gate[0].start()
    for copy in c_cot[:MICRO]:
        copy.start()
    for k in range(groups - 1):
        remote(tags_in, tags.at[(z + groups - 1 - k) % groups], s_tag, k, others[k]).wait_recv()
    tag_own.wait()

    def attend(m, first, last):
        trade = Trade(mixed.at[m], got.at[m], [s.at[m] for s in s_mix], self_mix.at[m])

        def one(step, carry):
            attend_step(step, m, heads, groups, recv.at[m], tags, mixed.at[m], lse.at[m], ks, vs, scores)
            trade.send(step)
            return carry

        lax.fori_loop(first, last, one, 0)
        return trade

    def post(m, trade):
        trade.collect()
        for pair in range(width // HALF):
            att[m, :, pair * HALF : (pair + 1) * HALF] = natural(got.at[m], 0, pair, heads).astype(BF)
        residual = x_ref[m].astype(F32) + dot(att[m], wo.reshape(width, width)[...])
        res[m] = residual
        nf[m] = (residual * rms_scale(residual) * both[1]).astype(BF)
        remote(nf.at[m], rows_out[m].at[1], s_row, 3 * m, to_y).start()
        remote(nf.at[m], rows_out[m].at[2], s_row, 3 * m + 1, to_core).start()

    def forward_row(m):
        remote(nf.at[m], rows_out[m].at[1], s_row, 3 * m, to_y).wait_recv()
        remote(rows_out[m].at[1], rows_out[m].at[3], s_row, 3 * m + 2, to_core).start()

    trades[0].collect()
    fill_keys(recv.at[0], 0, ks, vs, heads)
    back0 = attend(0, 0, groups)
    x_exp[0].wait_recv()
    n_exp[0].start()
    x_out.wait_recv()
    c_out.start()
    y_gate.wait_recv()
    c_gate[1].start()
    for m in range(MICRO):
        y_cot[m].wait_recv()
        c_cot[MICRO + m].start()
    trades[1].collect()
    fill_keys(recv.at[1], 1, ks, vs, heads)
    back1 = attend(1, 0, 2)
    c_out.wait_recv()
    post(0, back0)
    back1 = attend(1, 2, groups)
    forward_row(0)
    post(1, back1)
    keep = []
    for m in range(MICRO):
        keep += [
            (recv.at[m], recv_out[m]),
            (mixed.at[m], mixed_out[m]),
            (lse.at[m], lse_out[m]),
            (att.at[m], att_out[m]),
            (res.at[m], res_out[m]),
            (nf.at[m], rows_out[m].at[0]),
            (nf.at[m], both_out.at[m]),
        ]
    keep += [(tags, tags_out), (wq, qkv_out), (wo, wout_out), (gains, gains_out)]
    keep = [pltpu.make_async_copy(a, b, stores.at[3 + i]) for i, (a, b) in enumerate(keep)]
    for copy in keep:
        copy.start()
    forward_row(1)
    for k in (2, 3):
        x_exp[k].wait_recv()
        n_exp[k - 1].start()
    for copy in (*keep, *own_copies):
        copy.wait()
    for m in range(MICRO):
        remote(nf.at[m], rows_out[m].at[2], s_row, 3 * m + 1, to_core).wait()
        remote(rows_out[m].at[1], rows_out[m].at[3], s_row, 3 * m + 2, to_core).wait()
        remote(nf.at[m], rows_out[m].at[1], s_row, 3 * m, to_y).wait_send()
        trades[m].release()
    back0.release()
    back1.release()
    x_exp[1].wait_recv()
    for copy in (*n_exp, *c_gate, *c_cot):
        copy.wait()
    for copy in (*x_exp, x_qkv, x_gain, x_out, c_qkv, c_out, y_gate, *y_cot, *tag_trade):
        copy.wait_send()


def run_front(x, gains, cosines, sines, tags, gates, w_qkv, w_out, w_ein, w_eout, w_sin, w_sout, cot, groups):
    _, rows, width = x.shape
    heads = width // HEAD // groups
    k = width // 4
    w_qkv = w_qkv.reshape(2, k, 3 * width)
    w_out = w_out.reshape(2, k, width)
    w_ein, w_sin, w_sout = [w.reshape(2, -1, w.shape[1]) for w in (w_ein, w_sin, w_sout)]
    vmem = pl.BlockSpec(memory_space=pltpu.VMEM)
    anywhere = pl.BlockSpec(memory_space=pl.ANY)
    packed = lambda n: (groups, n * heads, HALF, HALF)
    held = MICRO * groups * TILE
    twice = lambda *a: [struct(*a)] * 2
    outs = (
        twice(packed(3), BF)
        + twice(packed(1), BF)
        + twice((groups, 8, TILE), F32)
        + twice((rows, width), BF)
        + twice((rows, width), F32)
        + twice((4, rows, width), BF)
        + twice((4, rows, width), BF)
        + [
            struct((4, *gates.shape), F32),
            struct((MICRO, rows, width), BF),
            struct((groups, *tags.shape), jnp.int32),
            struct((2, 2, k, 3 * width), BF),
            struct((2, 2, k, width), BF),
            struct(w_ein.shape, BF),
            struct(w_eout.shape, BF),
            struct(w_sin.shape, BF),
            struct(w_sout.shape, BF),
            struct((2, *gains.shape), F32),
        ]
    )
    v = pltpu.VMEM
    dma = lambda *n: pltpu.SemaphoreType.DMA(n)
    scratch = [
        v((2, 2, k, 3 * width), BF),
        v((2, 2, k, width), BF),
        v((2, *gains.shape), F32),
        v((groups, *tags.shape), jnp.int32),
        v((MICRO, *packed(3)), BF),
        v((MICRO, *packed(3)), BF),
        v((heads, held, HALF), BF),
        v((heads, held, HALF), BF),
        v((heads, TILE, held), F32),
        v((MICRO, *packed(1)), BF),
        v((MICRO, *packed(1)), BF),
        v((MICRO, groups, 8, TILE), F32),
        v((MICRO, rows, width), BF),
        v((MICRO, rows, width), F32),
        v((MICRO, rows, width), BF),
    ]
    for shape in ((2,), (2,), (1,), (7,), (groups - 1,), (3,), (6,), (MICRO, groups), (MICRO, groups), (6,)):
        scratch += [dma(*shape), dma(*shape)]
    scratch += [dma(3), dma(MICRO), dma(MICRO), dma(1), dma(3 + 7 * MICRO + 4)]
    return pl.pallas_call(
        functools.partial(front_kernel, heads=heads, groups=groups),
        out_shape=tuple(outs),
        in_specs=[vmem] * 6 + [anywhere] * 7,
        out_specs=(anywhere,) * len(outs),
        scratch_shapes=scratch,
        compiler_params=pltpu.CompilerParams(
            vmem_limit_bytes=VMEM_LIMIT, collective_id=3, has_side_effects=True
        ),
        cost_estimate=price(130),
    )(x, gains, cosines, sines, tags, gates, w_qkv, w_out, w_ein, w_eout, w_sin, w_sout, cot)


def ffn_kernel(*refs, tr, spans, counts, first, gated, opened, summed, closing):
    offs = refs[0]
    refs = list(refs[1:])
    take = lambda n: [refs.pop(0) for _ in range(n)]
    x_ref, dy_in = take(2)
    gate_ref = take(1)[0] if gated else None
    parts = len(spans)
    wg_parts, wu_parts, wo_parts = take(parts), take(parts), take(len(counts))
    y0, dx0 = take(2) if opened else (None, None)
    g0 = take(3) if summed else None
    y_ref, dx_ref, dwg_ref, dwu_ref, dwo_ref = take(5)
    xt, yacc, dxacc, hs, djg, dju, wg_ref, wu_ref, wo_ref = take(9)
    dy_ref = take(1)[0] if gated else dy_in
    f = pl.program_id(0)
    rows = x_ref.shape[0]

    @pl.when(f == 0)
    def _():
        xt[...] = x_ref[...].T
        if opened:
            yacc[...] = y0[...].astype(F32)
            dxacc[...] = dx0[...].astype(F32)
        else:
            yacc[...] = jnp.zeros_like(yacc)
            dxacc[...] = jnp.zeros_like(dxacc)
        if gated:
            dy_ref[...] = (dy_in[...].astype(F32) * gate_ref[...]).astype(BF)

    for index, span in enumerate(spans):
        place = pl.ds(pl.multiple_of(offs[index], HALF // 2), span)
        wg_ref[place, :] = wg_parts[index][...]
        wu_ref[place, :] = wu_parts[index][...]
    for index, count in enumerate(counts):
        begin = offs[parts + index]

        @pl.when((f + first >= begin) & (f + first < begin + count))
        def _(index=index):
            wo_ref[...] = wo_parts[index][...]

    wg, wu, wo = wg_ref[...], wu_ref[...], wo_ref[...]

    def tile(i, carry):
        r = pl.ds(pl.multiple_of(i * tr, tr), tr)
        x = x_ref[r, :]
        g = dot(x, wg)
        u = dot(x, wu)
        dh = dot(dy_ref[r, :], wo, NT)
        sig = 1.0 / (1.0 + jnp.exp(-g))
        act = g * sig
        h = (act * u).astype(BF)
        dg = (dh * u * (sig * (1.0 + g * (1.0 - sig)))).astype(BF)
        du = (dh * act).astype(BF)
        hs[r, :] = h
        djg[r, :] = dg
        dju[r, :] = du
        yacc[r, :] += dot(h, wo)
        dxacc[r, :] += dot(dg, wg, NT) + dot(du, wu, NT)
        return carry

    lax.fori_loop(0, rows // tr, tile, 0)
    grads = [dot(xt[...], djg[...]), dot(xt[...], dju[...]), dot(hs[...], dy_ref[...], TN)]
    for k, out in enumerate((dwg_ref, dwu_ref, dwo_ref)):
        value = grads[k]
        if summed:
            value = value + g0[k][...].astype(F32)
        out[...] = value.astype(BF)

    @pl.when(f == pl.num_programs(0) - 1)
    def _():
        made = yacc[...].astype(BF)
        if gated and closing:
            made = (made.astype(F32) * gate_ref[...]).astype(BF)
        y_ref[...] = made
        dx_ref[...] = dxacc[...].astype(BF)


def run_ffn(x, dy, gate, w_in, w_out, offsets, start=None, grads=None, span=None, closing=True, tr=512, fb=FB, us=10):
    rows, d = x.shape
    ff = sum(w.shape[0] for w in w_out)
    nf = ff // fb
    first, last = span or (0, nf)
    steps = last - first
    gated = gate is not None
    parts = len(w_in)
    spans = [w.shape[0] for w in w_in]
    counts = [w.shape[0] // fb for w in w_out]
    whole = lambda a: pl.BlockSpec(
        a.shape, lambda f, o: (0,) * a.ndim, pipeline_mode=pl.Buffered(1)
    )
    args = [x, dy] + ([gate] if gated else [])
    specs = [whole(a) for a in args]
    args += list(w_in) * 2 + list(w_out)
    specs += [pl.BlockSpec((n, fb), lambda f, o: (0, f + first)) for n in spans]
    specs += [pl.BlockSpec((n, fb), lambda f, o: (0, f + first + nf)) for n in spans]
    for i, c in enumerate(counts):
        specs.append(
            pl.BlockSpec(
                (fb, d), lambda f, o, i=i, c=c: (jnp.clip(f + first - o[parts + i], 0, c - 1), 0)
            )
        )
    if start is not None:
        args += list(start)
        specs += [whole(a) for a in start]
    wide = pl.BlockSpec((d, fb), lambda f, o: (0, f))
    tall = pl.BlockSpec((fb, d), lambda f, o: (f, 0))
    if grads is not None:
        args += list(grads)
        specs += [
            pl.BlockSpec((d, fb), lambda f, o: (0, f + first)),
            pl.BlockSpec((d, fb), lambda f, o: (0, f + first)),
            pl.BlockSpec((fb, d), lambda f, o: (f + first, 0)),
        ]
    full = pl.BlockSpec((rows, d), lambda f, o: (0, 0), pipeline_mode=pl.Buffered(1))
    return pl.pallas_call(
        functools.partial(
            ffn_kernel,
            tr=math.gcd(tr, rows),
            spans=spans,
            counts=counts,
            first=first,
            gated=gated,
            opened=start is not None,
            summed=grads is not None,
            closing=closing,
        ),
        out_shape=(
            struct((rows, d), BF),
            struct((rows, d), BF),
            struct((d, steps * fb), BF),
            struct((d, steps * fb), BF),
            struct((steps * fb, d), BF),
        ),
        grid_spec=pltpu.PrefetchScalarGridSpec(
            num_scalar_prefetch=1,
            grid=(steps,),
            in_specs=specs,
            out_specs=(full, full, wide, wide, tall),
            scratch_shapes=[
                pltpu.VMEM((d, rows), BF),
                pltpu.VMEM((rows, d), F32),
                pltpu.VMEM((rows, d), F32),
                pltpu.VMEM((rows, fb), BF),
                pltpu.VMEM((rows, fb), BF),
                pltpu.VMEM((rows, fb), BF),
                pltpu.VMEM((d, fb), BF),
                pltpu.VMEM((d, fb), BF),
                pltpu.VMEM((fb, d), BF),
            ]
            + ([pltpu.VMEM((rows, d), BF)] if gated else []),
        ),
        compiler_params=pltpu.CompilerParams(vmem_limit_bytes=VMEM_LIMIT),
        cost_estimate=price(us),
    )(offsets, *args)


def price(us):
    return pl.CostEstimate(flops=int(us * 1.15e9), bytes_accessed=0, transcendentals=0)


def norm_back(values, scale, gain, grad):
    gain_grad = jnp.sum(grad * values * scale, 0, keepdims=True)
    scaled = gain * grad
    grad_in = scale * scaled - values * (scale * scale * scale) * jnp.mean(
        scaled * values, -1, keepdims=True
    )
    return grad_in, gain_grad


def mid_core(grad, residual, gain, cot, w_ref, pay, gres_ref, gbf_ref, per):
    back, gain_grad = norm_back(residual, rms_scale(residual), gain, grad)
    total = cot.astype(F32) + back
    gres_ref[...] = total
    gbf_ref[...] = total.astype(BF)
    mixed = dot(gbf_ref[...], w_ref[...], NT)
    for pair in range(mixed.shape[1] // HALF):
        tile = mixed[:, pair * HALF : (pair + 1) * HALF]
        for side, packed in enumerate(swap_heads(tile[:HALF], tile[HALF:])):
            head = 2 * pair + side
            pay[head // per, head % per] = packed.astype(BF)
    return gain_grad


def mid_kernel(dxs, dxr, res_ref, gain_ref, cot_ref, w_ref, gres_ref, pay, gg_ref, gbf, *, per):
    grad = dxs[...].astype(F32) + dxr[...].astype(F32)
    gg_ref[...] = mid_core(grad, res_ref[...], gain_ref[...], cot_ref[0], w_ref, pay, gres_ref, gbf, per)


def run_mid(dxs, dxr, residual, gain, cot, w, groups):
    rows, width = residual.shape
    per = width // HEAD // groups
    args = (dxs, dxr, residual, gain, cot, w)
    specs = [full_spec(a.shape) for a in args]
    specs[0] = pl.BlockSpec((rows, width), lambda _: (0, 0))
    specs[4] = pl.BlockSpec((1, rows, width), lambda _: (0, 0, 0))
    outs = [
        struct((rows, width), F32),
        struct((groups, per, HALF, HALF), BF),
        struct((1, width), F32),
        struct((rows, width), BF),
    ]
    return call(
        functools.partial(mid_kernel, per=per),
        tuple(outs),
        grid=(1,),
        in_specs=specs,
        out_specs=tuple(full_spec(o.shape) for o in outs),
        us=4,
    )(*args)


def finish(d0, d1, x_ref, gain_ref, w_ref, cos_ref, sin_ref, gres, atts, gbfs, gin_ref, gq, gv, go, gj, per):
    width = x_ref.shape[2]
    for micro, ref in enumerate((d0, d1)):
        rows = slice(micro * TILE, (micro + 1) * TILE)
        cosines, sines = cos_ref[rows, :], sin_ref[rows, :]
        for kind in range(3):
            for pair in range(width // HALF):
                tile = natural(ref, kind, pair, per)
                if kind == 0:
                    tile = tile * 0.125
                if kind < 2:
                    tile = rotate(tile, cosines, -sines)
                gj[rows, kind * width + pair * HALF : kind * width + (pair + 1) * HALF] = tile.astype(BF)
    tokens = x_ref[...].reshape(MICRO * TILE, width).astype(F32)
    scale = rms_scale(tokens)
    gain = gain_ref[...]
    turned = (tokens * scale * gain).astype(BF).T
    split = gq.shape[-1]
    gq[...] = dot(turned, gj[:, :split]).astype(BF).reshape(gq.shape)
    gv[...] = dot(turned, gj[:, split:]).astype(BF).reshape(gv.shape)
    go[...] = (dot(atts[0][...], gbfs[0][...], TN) + dot(atts[1][...], gbfs[1][...], TN)).astype(BF).reshape(go.shape)
    yield
    first = dot(gj[...], w_ref[...], NT)
    back, _ = norm_back(tokens, scale, gain, first)
    for micro in range(MICRO):
        rows = slice(micro * TILE, (micro + 1) * TILE)
        gin_ref[rows, :] = gres[micro][...] + back[rows]


def exchange(value, axis, mask):
    size = lax.axis_size(axis)
    return lax.ppermute(value, axis, [(i, i ^ mask) for i in range(size)])


def bits_of(size):
    return [1 << b for b in range(size.bit_length() - 1)]


def gather_rest(value):
    for mask in bits_of(lax.axis_size("expert"))[2:]:
        value = jnp.concatenate([value, exchange(value, "expert", mask)], 0)
    return value


def scatter_xor(value):
    masks = bits_of(lax.axis_size("expert"))
    for mask in (*reversed(masks[2:]), *masks[:2]):
        half = value.shape[0] // 2
        got = exchange(value[half:], "expert", mask)
        value = (value[:half].astype(F32) + got.astype(F32)).astype(value.dtype)
    return value


def ordered(flag, mine, theirs):
    first = jnp.where(flag == 0, mine, theirs)
    second = jnp.where(flag == 0, theirs, mine)
    return jnp.concatenate([first, second], 0)


def pick(value, parts, index):
    size = value.shape[0] // parts
    return lax.dynamic_slice_in_dim(value, index * size, size, 0)


def after(value, token):
    return lax.optimization_barrier((value, token))[0]


PIECES = 4
EARLY = 6
AHEAD = 2
PLAN = {
    2: ("rs1",),
    4: ("a0", "A0",),
    5: ("a1", "rs2",),
    6: ("A1",),
    7: ("B0",),
    10: ("a2",),
    11: ("A2", "b0", "A3", "B1",),
    15: ("C0",),
    16: ("B2",),
    17: ("C1",),
    19: ("A4",),
    20: ("c0", "B3",),
    21: ("b1", "C2",),
    23: ("B4",),
    24: ("D0",),
    25: ("C3",),
    27: ("b2", "d0", "A5",),
    28: ("C4",),
    31: ("B5",),
    33: ("c1",),
    36: ("d1", "e0", "c2",),
    37: ("A6",),
    38: ("C5", "d2",),
    42: ("e1", "e2", "zhome", "f0", "A7", "A8", "f1", "f2", "g2", "D3", "D1", "D5", "A9", "D4", "g1", "g0", "D2", "h0", "A10", "A11", "h1", "h2",),
}
LAST_PLAN = (
    "A0", "A1", "A2", "B0", "A3", "a0", "A4", "B1", "a1", "C0",
    "B2", "C1", "zrest", "b0", "B3", "C2", "b1", "c0", "a2", "B4",
    "C3", "c1", "b2", "D1", "d0", "C4", "c2", "d1", "e0", "d2",
    "e1", "A5", "D2", "D4", "D0", "f0", "f1", "B5", "f2", "e2",
    "g0", "g1", "D3", "h1", "h0", "C5", "g2", "D5", "h2",
)


class Engine:
    def __init__(self, own, com, own_buf, com_buf, own_out, com_out, sems):
        self.own, self.com, self.own_buf, self.com_buf = own, com, own_buf, com_buf
        self.own_out, self.com_out = own_out, com_out
        e, z, d = lax.axis_index("expert"), lax.axis_index("context"), lax.axis_index("dp")
        groups = lax.axis_size("context")
        self.d, self.core, self.y = d, e % 2, e // 2 % 2
        self.outer = (z == 0) | (z == 3)
        self.inner = (z == 1) | (z == 2)
        self.to_x = {"dp": 1 - d}
        self.to_core = {"expert": e + 1 - 2 * self.core}
        self.to_y = {"expert": e + 2 - 4 * self.y}
        self.to_mate = {"context": z + 1 - 2 * (z % 2)}
        self.to_mid = {"context": 3 - z}
        self.others = [{"context": (z + k) % groups} for k in range(1, groups)]
        sems = list(sems)
        take = lambda n: [sems.pop(0) for _ in range(n)]
        self.o_load, self.o_store = take(2)
        self.o = {k: take(2) for k in "x123"}
        self.c_load, self.c_store = take(2)
        self.c = {k: take(2) for k in ("core", "y", "x", "1", "2", "3", "fore", "last")}

    @staticmethod
    def scratch(own_shapes, kinds, com_shapes):
        v, dma = pltpu.VMEM, lambda n: pltpu.SemaphoreType.DMA((max(n, 1),))
        tiny = (16, HALF)
        own_buf = []
        for s, kind in zip(own_shapes, kinds):
            own_buf += [v(s, BF), v(s if "x" in kind else tiny, BF)]
            own_buf += [v(s if "z" in kind else tiny, BF)] * 2
        com_buf = []
        for s in com_shapes:
            com_buf += [v((2, 2, *s), BF)] * 2 + [v((2, *s), BF)] + [v(s, BF)] * 3
        chunks, n = len(own_shapes), len(com_shapes)
        sems = [dma(chunks)] * 10 + [dma(2 * n), dma(n)] + [dma(2 * n)] * 4 + [dma(n)] * 12
        return own_buf, com_buf, sems

    def greet(self):
        meet(
            pltpu.get_barrier_semaphore(), [self.to_x, self.to_core, self.to_y, *self.others]
        )

    def o_wire(self, stage, c):
        total, r_x, r_1, r_2 = self.own_buf[c]
        src, k, _ = self.own[c]
        target = {"x": self.to_x, "1": self.to_mate, "2": self.to_mid, "3": self.to_mate}[stage]
        source = {"x": lambda: src.at[1 - self.d, k], "1": lambda: total, "2": lambda: total, "3": lambda: r_1}
        place = {"x": r_x, "1": r_1, "2": r_2, "3": self.own_out[c]}[stage]
        return remote(source[stage](), place, self.o[stage], c, target)

    def o_loading(self, c):
        src, k, kind = self.own[c]
        src = src.at[k] if kind == "z" else src.at[self.d, k]
        return pltpu.make_async_copy(src, self.own_buf[c][0], self.o_load.at[c])

    def o_storing(self, c):
        buf = self.own_buf[c][0 if self.own[c][2] == "x" else 2]
        return pltpu.make_async_copy(buf, self.own_out[c], self.o_store.at[c])

    def A(self, c):
        total, r_x = self.own_buf[c][:2]
        kind = self.own[c][2]
        self.o_loading(c).wait()
        if kind != "z":
            self.o_wire("x", c).wait_recv()
            if c + self.ahead < len(self.own):
                self.o_wire("x", c + self.ahead).start()
            total[...] = total[...] + r_x[...]
        if kind == "x":
            self.o_storing(c).start()
            return

        @pl.when(self.outer)
        def _():
            self.o_wire("1", c).start()

    def B(self, c):
        total, _, r_1, _ = self.own_buf[c]

        @pl.when(self.inner)
        def _():
            self.o_wire("1", c).wait_recv()
            total[...] = total[...] + r_1[...]
            self.o_wire("2", c).start()

    def C(self, c):
        total, _, r_1, r_2 = self.own_buf[c]

        @pl.when(self.inner)
        def _():
            self.o_wire("2", c).wait_recv()
            r_1[...] = total[...] + r_2[...]
            self.o_wire("3", c).start()
            self.o_storing(c).start()

    def D(self, c):
        @pl.when(self.outer)
        def _():
            self.o_wire("3", c).wait_recv()

    def c_loading(self, i, h):
        return pltpu.make_async_copy(
            self.com[i].at[h, self.core], self.com_buf[i][0].at[h], self.c_load.at[2 * i + h]
        )

    def c_storing(self, i):
        return pltpu.make_async_copy(
            self.com_buf[i][4], self.com_out[i].at[self.core, self.y], self.c_store.at[i]
        )

    def c_wire(self, stage, i, h=0):
        total, r_core, r_y, r_x, r_1, r_2 = self.com_buf[i]
        core, y, d = self.core, self.y, self.d
        out = self.com_out[i]
        if stage == "core":
            return remote(self.com[i].at[h, 1 - core], r_core.at[h], self.c["core"], 2 * i + h, self.to_core)
        if stage == "y":
            return remote(total.at[h, 1 - y], r_y.at[h], self.c["y"], 2 * i + h, self.to_y)
        if stage == "x":
            return remote(total.at[1 - d, y], r_x, self.c["x"], i, self.to_x)
        if stage == "1":
            return remote(total.at[d, y], r_1, self.c["1"], i, self.to_mate)
        if stage == "2":
            return remote(total.at[d, y], r_2, self.c["2"], i, self.to_mid)
        if stage == "3":
            return remote(r_1, out.at[core, y], self.c["3"], i, self.to_mate)
        if stage == "fore":
            return remote(r_1, out.at[core, y], self.c["fore"], i, self.to_y)
        if stage == "back":
            return remote(out.at[core, y], out.at[core, y], self.c["fore"], i, self.to_y)
        return remote(out.at[core], out.at[core], self.c["last"], i, self.to_core)

    def c_start(self, i):
        for h in range(2):
            self.c_wire("core", i, h).start()
            self.c_loading(i, h).start()

    def a(self, i):
        total, r_core = self.com_buf[i][:2]
        for h in range(2):
            self.c_loading(i, h).wait()
            self.c_wire("core", i, h).wait_recv()
        total[...] = total[...] + r_core[...]
        for h in range(2):
            self.c_wire("y", i, h).start()

    def b(self, i):
        total, r_y, y = self.com_buf[i][0], self.com_buf[i][2], self.y
        for h in range(2):
            self.c_wire("y", i, h).wait_recv()
            total[h, y] = total[h, y] + r_y[h]
        self.c_wire("x", i).start()

    def c_(self, i):
        total, r_x, y, d = self.com_buf[i][0], self.com_buf[i][3], self.y, self.d
        self.c_wire("x", i).wait_recv()
        total[d, y] = total[d, y] + r_x[...]

        @pl.when(self.outer)
        def _():
            self.c_wire("1", i).start()

    def d_(self, i):
        total, r_1, y, d = self.com_buf[i][0], self.com_buf[i][4], self.y, self.d

        @pl.when(self.inner)
        def _():
            self.c_wire("1", i).wait_recv()
            total[d, y] = total[d, y] + r_1[...]
            self.c_wire("2", i).start()

    def e(self, i):
        total, r_1, r_2 = self.com_buf[i][0], self.com_buf[i][4], self.com_buf[i][5]

        @pl.when(self.inner)
        def _():
            self.c_wire("2", i).wait_recv()
            r_1[...] = total[self.d, self.y] + r_2[...]
            self.c_wire("3", i).start()
            self.c_wire("fore", i).start()
            self.c_storing(i).start()

    def f(self, i):
        @pl.when(self.outer)
        def _():
            self.c_wire("3", i).wait_recv()
            self.c_wire("back", i).start()

    def g(self, i):
        @pl.when(self.inner)
        def _():
            self.c_storing(i).wait()

        self.c_wire("fore", i).wait_recv()
        self.c_wire("last", i).start()

    def h(self, i):
        self.c_wire("last", i).wait_recv()

    def start(self, ahead, com=True):
        self.ahead = ahead
        for c in range(min(ahead, len(self.own))):
            if self.own[c][2] != "z":
                self.o_wire("x", c).start()
        if com:
            for i in range(len(self.com)):
                self.c_start(i)
        for c in range(len(self.own)):
            self.o_loading(c).start()

    def run(self, name):
        kind, index = name[0], int(name[1:])
        {"c": self.c_, "d": self.d_}.get(kind, getattr(self, kind, None))(index)

    def close(self):
        chunks, common = range(len(self.own)), range(len(self.com))
        for c in chunks:
            if self.own[c][2] != "z":
                self.o_wire("x", c).wait_send()
            if self.own[c][2] == "x":
                self.o_storing(c).wait()
        chunks = [c for c in chunks if self.own[c][2] != "x"]
        for i in common:
            for h in range(2):
                self.c_wire("core", i, h).wait_send()
                self.c_wire("y", i, h).wait_send()
            self.c_wire("x", i).wait_send()
            self.c_wire("last", i).wait_send()

        @pl.when(self.outer)
        def _():
            for c in chunks:
                self.o_wire("1", c).wait_send()
            for i in common:
                self.c_wire("1", i).wait_send()
                self.c_wire("back", i).wait_send()

        @pl.when(self.inner)
        def _():
            for c in chunks:
                self.o_wire("2", c).wait_send()
                self.o_wire("3", c).wait_send()
                self.o_storing(c).wait()
            for i in common:
                self.c_wire("2", i).wait_send()
                self.c_wire("3", i).wait_send()
                self.c_wire("fore", i).wait_send()


class Arrays:
    def __init__(self, refs):
        self.refs = list(refs)

    def take(self, n):
        got, self.refs = self.refs[:n], self.refs[n:]
        return got

    def engine(self, own_at, sources, own_out, com, com_out):
        own_buf = [self.take(4) for _ in own_at]
        com_buf = [self.take(6) for _ in com]
        own = [(sources[j], k, kind) for j, k, kind in own_at]
        places = [own_out[j].at[k] for j, k, _ in own_at]
        return Engine(own, com, own_buf, com_buf, places, com_out, self.take(10 + 18))


def back_kernel(*refs, own_at, sources, common, heads, groups):
    refs = Arrays(refs)
    own_in, com_in = refs.take(sources), refs.take(common)
    recv0, recv1, grad0, out0, out1, lse0, lse1, key_tag, query_tag = refs.take(9)
    dxs, res_ref, gain_ref, cot_ref, w_ref, dx_made = refs.take(6)
    own_out, com_out = refs.take(sources), refs.take(common)
    d0_out, d1_out, gres_out, gbf_out, gg_out = refs.take(5)
    engine = refs.engine(own_at, own_in, own_out, com_in, com_out)
    dx, r_core, r_y, gres, gbf, gg, pay_o, grad1, pay0, pay1 = refs.take(10)
    ks, vs, dk, dv, qs, gs, deltas, acc = refs.take(8)
    s_dx, s_o, s_0, s_1 = [refs.take(2) for _ in range(4)]
    local, = refs.take(1)

    engine.greet()
    send_core = remote(dx_made.at[2:4], r_core, s_dx, 0, engine.to_core)
    send_core.start()
    own_dx = pltpu.make_async_copy(dx_made.at[0:2], dx, local.at[0])
    own_dx.start()
    engine.start(AHEAD)
    send_y = remote(dx.at[1], r_y, s_dx, 1, engine.to_y)
    trade_o = Trade(pay_o, grad1, s_o, local.at[1])
    homes = [Trade(pay0, d0_out, s_0, local.at[2]), Trade(pay1, d1_out, s_1, local.at[3])]
    results = [
        pltpu.make_async_copy(a, b, local.at[4 + i])
        for i, (a, b) in enumerate(((gres, gres_out), (gbf, gbf_out), (gg, gg_out)))
    ]

    def rs1():
        own_dx.wait()
        send_core.wait_recv()
        dx[...] = dx[...] + r_core[...]
        send_y.start()

    def rs2():
        send_y.wait_recv()
        grad = dxs[TILE:, :].astype(F32) + dx[0].astype(F32) + r_y[...].astype(F32)
        gg[...] = mid_core(grad, res_ref[...], gain_ref[...], cot_ref[1], w_ref, pay_o, gres, gbf, heads)
        for dest in range(groups):
            trade_o.send(dest)
        for copy in results:
            copy.start()

    def zhome():
        for base, pay, trade in ((groups, pay1, homes[1]), (0, pay0, homes[0])):
            for dest in range(groups):
                back_pack(dk, dv, pay, dest, base, heads)
                trade.send(dest)

    named = {"rs1": rs1, "rs2": rs2, "zhome": zhome, "zend": lambda: None}

    def events(slot):
        for name in PLAN.get(slot, ()):
            named[name]() if name in named else engine.run(name)

    for recv, micro in ((recv0, 0), (recv1, 1)):
        fill_keys(recv, micro, ks, vs, heads)
    dk[...] = jnp.zeros_like(dk)
    dv[...] = jnp.zeros_like(dv)
    first_of = (0, sum(min(s + 2, groups) for s in range(groups)))
    total = 2 * first_of[1] + groups * groups
    for micro, (recv, grad, out, lse, pay) in enumerate(
        ((recv0, grad0, out0, lse0, pay0), (recv1, grad1, out1, lse1, pay1))
    ):
        begin, end = first_of[micro], (first_of + (total,))[micro + 1]
        if micro:
            trade_o.collect()

        def step(s, carry, micro=micro, recv=recv, grad=grad, out=out, lse=lse, pay=pay, begin=begin, end=end):
            back_begin(micro, s, heads, recv, grad, out, qs, gs, deltas, acc)
            before = begin + s * (s + 3) // 2 + groups * micro * s

            def tile(j, carry):
                for slot in range(begin, end):
                    if slot in PLAN:

                        @pl.when(before + j == slot)
                        def _(slot=slot):
                            events(slot)

                back_tile(
                    micro, s, j, heads, groups, lse, key_tag, query_tag, ks, vs, dk, dv, qs, gs, deltas, acc
                )
                return carry

            lax.fori_loop(0, groups * micro + jnp.minimum(s + 2, groups), tile, 0)
            for h in range(heads):
                pay[s, h] = pack_rows(acc[h]).astype(BF)
            return carry

        lax.fori_loop(0, groups, step, 0)
    events(total)
    for trade in homes:
        trade.collect()
        trade.release()
    trade_o.release()
    send_core.wait_send()
    send_y.wait_send()
    for copy in results:
        copy.wait()
    engine.close()


def chunk_views(grads):
    return [g.reshape(2, PIECES, g.shape[0] // (2 * PIECES), g.shape[1]) for g in grads]


def shared_shape(shape):
    return (2, 2, 2, shape[0] // 8, shape[1])


def device_call(kernel, args, vmem_args, outs, scratch, collective_id, us, aliases=None):
    anywhere = pl.BlockSpec(memory_space=pl.ANY)
    return pl.pallas_call(
        kernel,
        out_shape=tuple(outs),
        in_specs=[pl.BlockSpec(memory_space=pltpu.VMEM) if v else anywhere for v in vmem_args],
        out_specs=(anywhere,) * len(outs),
        scratch_shapes=scratch,
        input_output_aliases=aliases or {},
        compiler_params=pltpu.CompilerParams(
            vmem_limit_bytes=VMEM_LIMIT, collective_id=collective_id, has_side_effects=True
        ),
        cost_estimate=price(us),
    )(*args)


def rest_sum(value):
    for mask in bits_of(lax.axis_size("expert"))[2:]:
        value = value + exchange(value, "expert", mask)
    return value


def run_back(expert_grads, own_at, shared_grads, attention, middle, dx_made, groups):
    own = chunk_views(expert_grads)
    com = [g.reshape(shared_shape(g.shape)) for g in shared_grads]
    heads = attention[0].shape[1] // 3
    rows, width = middle[1].shape
    args = [*own, *com, *attention, *middle, dx_made]
    own_shapes = [own[j].shape[2:] for j, _, _ in own_at]
    com_shapes = [g.shape[3:] for g in com]
    own_buf, com_buf, sems = Engine.scratch(own_shapes, [kind for *_, kind in own_at], com_shapes)
    held = MICRO * groups * TILE
    v, dma = pltpu.VMEM, lambda n: pltpu.SemaphoreType.DMA((n,))
    pay = lambda n: (groups, n * heads, HALF, HALF)
    outs = (
        [struct(g.shape[1:], BF) for g in own]
        + [struct((2, 2, *s), BF) for s in com_shapes]
        + [struct(pay(3), BF)] * 2
        + [struct((rows, width), F32), struct((rows, width), BF), struct((1, width), F32)]
    )
    scratch = [
        *own_buf,
        *com_buf,
        *sems,
        v((2, rows, width), BF),
        v((2, rows, width), BF),
        v((rows, width), BF),
        v((rows, width), F32),
        v((rows, width), BF),
        v((1, width), F32),
        v(pay(1), BF),
        v(pay(1), BF),
        v(pay(3), BF),
        v(pay(3), BF),
        v((heads, held, HALF), BF),
        v((heads, held, HALF), BF),
        v((heads, held, HALF), F32),
        v((heads, held, HALF), F32),
        v((heads, TILE, HALF), BF),
        v((heads, TILE, HALF), BF),
        v((heads, 8, TILE), F32),
        v((heads, TILE, HALF), F32),
        dma(2),
        dma(2),
        *[dma(groups)] * 6,
        dma(7),
    ]
    flags = [False] * (len(own) + len(com)) + [True] * (len(attention) + len(middle)) + [False]
    kernel = functools.partial(
        back_kernel, own_at=own_at, sources=len(own), common=len(com), heads=heads, groups=groups
    )
    got = device_call(kernel, args, flags, outs, scratch, 1, 165)
    n, m = len(own), len(com)
    return got[:n], [rest_sum(g.reshape(-1, g.shape[-1]).astype(F32)) for g in got[n : n + m]], got[n + m :]


def last_kernel(*refs, own_at, sources, per):
    refs = Arrays(refs)
    own_in = refs.take(sources)
    d0, d1, x_ref, gain_ref, w_ref, cos_ref, sin_ref = refs.take(7)
    gres, atts, gbfs, ggs = refs.take(2), refs.take(2), refs.take(2), refs.take(2)
    own_out, com_out = refs.take(sources), refs.take(3)
    gin_out, gg_out = refs.take(2)
    sources = [refs.refs.pop(len(own_at) * 4 + 3 * 6 + 28) for _ in range(3)]
    engine = refs.engine(own_at, own_in, own_out, sources, com_out)
    gj, gin, gg_sum, gg_got, g_send, g_recv, local = refs.take(7)
    engine.greet()
    engine.start(0, com=False)
    z = lax.axis_index("context")
    rounds = (engine.to_core, engine.to_y, engine.to_x, engine.to_mate, {"context": z + 2 - 4 * (z // 2)})
    wires = [
        remote(gg_sum.at[k], gg_got.at[k], (g_send, g_recv), k, target) for k, target in enumerate(rounds)
    ]
    gg_sum[0] = jnp.broadcast_to(ggs[0][...] + ggs[1][...], gg_sum.shape[1:])
    wires[0].start()
    work = finish(
        d0, d1, x_ref, gain_ref, w_ref, cos_ref, sin_ref, gres, atts, gbfs, gin, *sources, gj, per
    )
    store = pltpu.make_async_copy(gin, gin_out, local.at[0])
    next(work)
    for i in range(3):
        engine.c_start(i)
    turn = 0
    for index, name in enumerate(LAST_PLAN):
        if name == "zrest":
            for _ in work:
                pass
            store.start()
        else:
            engine.run(name)
        if index % 5 == 4 and turn < len(wires):
            wires[turn].wait_recv()
            gg_sum[turn + 1] = gg_sum[turn] + gg_got[turn]
            turn += 1
            if turn < len(wires):
                wires[turn].start()
    total = pltpu.make_async_copy(gg_sum.at[len(wires)], gg_out, local.at[1])
    total.start()
    store.wait()
    total.wait()
    for wire in wires:
        wire.wait_send()
    engine.close()


def run_last(sums, own_at, parts, groups):
    x, w = parts[2], parts[4]
    _, rows, width = x.shape
    args = [*sums, *parts]
    own_shapes = [sums[j].shape[1:] for j, _, _ in own_at]
    com = [shared_shape((width, 3 * width // 2))] * 2 + [shared_shape((width, width))]
    own_buf, com_buf, sems = Engine.scratch(own_shapes, [k for *_, k in own_at], [s[3:] for s in com])
    v = pltpu.VMEM
    outs = (
        [struct(g.shape, BF) for g in sums]
        + [struct((2, 2, *s[3:]), BF) for s in com]
        + [struct((MICRO * rows, width), F32), struct((8, width), F32)]
    )
    rounds = 5
    scratch = [
        *own_buf,
        *com_buf,
        *sems,
        *[v(s, BF) for s in com],
        v((MICRO * rows, 3 * width), BF),
        v((MICRO * rows, width), F32),
        v((rounds + 1, 8, width), F32),
        v((rounds, 8, width), F32),
        *[pltpu.SemaphoreType.DMA((rounds,))] * 2,
        pltpu.SemaphoreType.DMA((2,)),
    ]
    flags = [False] * len(sums) + [True] * len(parts)
    kernel = functools.partial(
        last_kernel, own_at=own_at, sources=len(sums), per=width // HEAD // groups
    )
    got = device_call(
        kernel, args, flags, outs, scratch, 2, 90, {i: i for i in range(len(sums))}
    )
    n = len(sums)
    return got[:n], [rest_sum(g.reshape(-1, g.shape[-1]).astype(F32)) for g in got[n : n + 3]], got[n + 3], got[n + 4]


def body(
    inputs,
    keep_flags,
    block_ids,
    expert_ids,
    gate_weights,
    norm_attn,
    w_qkv,
    w_attn_out,
    norm_ffn,
    w_shared_in,
    w_shared_out,
    w_expert_in,
    w_expert_out,
    cotangent,
):
    width = w_qkv.shape[1] // 3
    rows = inputs.shape[2]
    groups = lax.axis_size("context")
    experts = lax.axis_size("expert")
    z = lax.axis_index("context")
    seq_rows = rows * groups
    x = inputs[0]
    cot = cotangent[0].reshape(MICRO * rows, width)

    positions = (
        jnp.arange(MICRO, dtype=jnp.int32)[:, None] * seq_rows
        + z * rows
        + jnp.arange(rows, dtype=jnp.int32)[None, :]
    ).reshape(-1)
    half = HEAD // 2
    freq = jnp.exp(-math.log(ROPE_BASE) * jnp.arange(half, dtype=F32) * 2.0 / HEAD)
    angle = positions.astype(F32)[:, None] * freq[None, :]
    cos_t, sin_t = jnp.cos(angle), jnp.sin(angle)
    cosines = jnp.concatenate([cos_t] * 4, -1)
    sines = jnp.concatenate([-sin_t, sin_t, -sin_t, sin_t], -1)

    blocks = block_ids[0] + 8 * jnp.arange(MICRO, dtype=jnp.int32)[:, None]
    key_tags = jnp.where(keep_flags[0] == 1, blocks, HIDDEN)
    tags = jnp.stack([blocks, key_tags])[:, :, None]

    per_expert = jnp.sum(
        jnp.where(
            expert_ids[0][None] == jnp.arange(experts, dtype=jnp.int32)[:, None, None, None],
            gate_weights[0][None],
            0.0,
        ),
        -1,
    )
    gains = jnp.stack([norm_attn, norm_ffn]).astype(F32)
    (
        *pairs,
        gates_four,
        nf_both,
        all_tags,
        mat_qkv,
        mat_out,
        ein_parts,
        eout_other,
        sin_parts,
        sout_parts,
        gains,
    ) = run_front(
        x,
        gains,
        cosines,
        sines,
        tags,
        per_expert,
        w_qkv,
        w_attn_out,
        w_expert_in[0],
        w_expert_out[0],
        w_shared_in,
        w_shared_out,
        cotangent[0],
        groups,
    )
    recvs, mixed, lses, att, res, rows_four, cot_four = [pairs[2 * i : 2 * i + 2] for i in range(7)]
    mat_qkv = mat_qkv.reshape(width, -1)
    mat_out = mat_out.reshape(width, width)
    gain_attn = gains[:, 0].reshape(1, width)
    gain_ffn = gains[:, 1].reshape(1, width)
    all_tags = all_tags[:, :, :, 0].transpose(1, 2, 0, 3)
    query_row = all_tags[0].reshape(MICRO * groups, 1, rows)
    key_col = all_tags[1].reshape(-1, 1)
    own_gates = lax.dynamic_index_in_dim(
        gather_rest(gates_four), lax.axis_index("expert"), 1, False
    )
    gate = [own_gates[:, m].reshape(-1, 1) for m in range(MICRO)]

    core = lax.axis_index("expert") % 2
    dp = lax.axis_index("dp")
    k_half, f_half = width // 2, w_shared_out.shape[0]
    ein_parts = (w_expert_in[0], ein_parts[0], ein_parts[1])
    eout_parts = (w_expert_out[0], eout_other)
    sin_parts = (w_shared_in, sin_parts[0], sin_parts[1])
    sout_parts = (w_shared_out, sout_parts[0], sout_parts[1])
    places = lambda bit: [2 * (1 - dp) + bit, 2 * (1 - dp) + 1 - bit]
    row_offs = lambda bit: [dp * k_half] + [p * (k_half // 2) for p in places(bit)]
    chunk = f_half // FB
    expert_offs = jnp.stack(row_offs(z % 2) + [dp * chunk, (1 - dp) * chunk])
    shared_offs = jnp.stack(
        row_offs(core) + [dp * chunk] + [p * (chunk // 2) for p in places(core)]
    )

    capacity = 4 * rows // experts

    def expert_pass(m, grads, token=None):
        hidden = gather_rest(rows_four[m]).reshape(-1, width)
        if token is not None:
            hidden = after(hidden, token)
        grad, weight = gather_rest(cot_four[m]).reshape(-1, width), gate[m]
        if capacity < rows:
            chosen = weight.reshape(-1, rows) > 0
            slots = jnp.cumsum(chosen.astype(jnp.int32), 1) - 1
            select = (
                chosen[:, None] & (slots[:, None] == jnp.arange(capacity, dtype=jnp.int32)[:, None])
            ).astype(BF)
            squeeze = lambda v: jnp.einsum("bcr,brd->bcd", select, v.reshape(-1, rows, width)).reshape(-1, width)
            spread = lambda v: jnp.einsum("bcr,bcd->brd", select, v.reshape(-1, capacity, width)).reshape(-1, width)
            hidden, grad = squeeze(hidden), squeeze(grad)
            weight = jnp.sum(select.astype(F32) * weight.reshape(-1, 1, rows), -1).reshape(-1, 1)
        made, dx, *grads = run_ffn(
            hidden, grad, weight, ein_parts, eout_parts, expert_offs, grads=grads, us=41
        )
        if capacity < rows:
            made, dx = spread(made), spread(dx)
        return made, dx, *grads

    made0, dx0, *g_expert = expert_pass(0, None)
    dx0, routed0 = scatter_xor(dx0), scatter_xor(made0)
    shared, dx_shared, *g_shared = run_ffn(
        nf_both.reshape(-1, width), cot, None, sin_parts, sout_parts, shared_offs, us=23
    )
    gres0, pay0, gg0, gbf0 = run_mid(dx_shared, dx0, res[0], gain_ffn, cotangent[0], mat_out, groups)
    grad0 = lax.all_to_all(pay0, "context", 0, 0, tiled=True)
    made1, dx1, *g_expert = expert_pass(1, g_expert, (pay0, routed0))
    masks = bits_of(experts)
    for mask in reversed(masks[2:]):
        half = dx1.shape[0] // 2
        dx1 = (dx1[:half].astype(F32) + exchange(dx1[half:], "expert", mask).astype(F32)).astype(BF)

    spread = [(j, k) for j in range(3) for k in range(PIECES)]
    early = [(j, k, "xz" if i < EARLY else "x") for i, (j, k) in enumerate(spread)]
    first = spread[EARLY][0]
    late = [(j - first, k, "z") for j, k in spread[EARLY:]]
    attention = (*recvs, grad0, *mixed, *lses, key_col, query_row)
    own_sums, (r_gate, r_up, r_sout), (d0, d1, gres1, gbf1, gg1) = run_back(
        g_expert,
        early,
        g_shared,
        attention,
        (dx_shared, res[1], gain_ffn, cotangent[0], mat_out),
        dx1.reshape(4, rows, width),
        groups,
    )
    routed1 = scatter_xor(made1)
    output = jnp.stack(
        [
            (res[m] + shared[m * rows : (m + 1) * rows].astype(F32) + r.astype(F32)).astype(BF)
            for m, r in enumerate((routed0, routed1))
        ]
    )
    own_late, (r_qk, r_v, r_out), grad_input, gain_sum = run_last(
        own_sums[first:],
        late,
        (d0, d1, x, gain_attn, mat_qkv, cosines, sines, gres0, gres1, *att, gbf0, gbf1, gg0, gg1),
        groups,
    )
    r_gain_ffn = pick(rest_sum(gain_sum)[0], 2, dp)
    r_qkv = jnp.concatenate([r_qk, r_v], 1)
    r_sin = jnp.concatenate([r_gate, r_up], 1)
    r_gain_attn = jnp.sum(w_qkv.astype(F32) * r_qkv, 1) / norm_attn.astype(F32)
    e_gate, e_up, r_eout = [
        g.reshape(-1, g.shape[-1]).astype(F32) for g in (*own_sums[:first], *own_late)
    ]
    r_ein = jnp.concatenate([e_gate, e_up], 1)
    return (
        output[None],
        grad_input.reshape(1, MICRO, rows, width),
        r_gain_attn,
        r_qkv,
        r_out,
        r_gain_ffn,
        r_sin,
        r_sout,
        r_ein[None],
        r_eout[None],
    )


def solution(mesh):
    tokens = P(("expert", "dp"), None, "context", None)
    flags = P(("expert", "dp"), None, "context")
    placed = (
        tokens,
        flags,
        flags,
        tokens,
        tokens,
        P("dp"),
        P("dp", None),
        P("dp", None),
        P("dp"),
        P("dp", None),
        P("dp", None),
        P("expert", "dp", None),
        P("expert", "dp", None),
        tokens,
    )
    return jax.shard_map(
        body,
        mesh=mesh,
        in_specs=placed,
        out_specs=(
            tokens,
            tokens,
            P("dp"),
            P("dp", None),
            P("dp", None),
            P("dp"),
            P("dp", None),
            P("dp", None),
            P("expert", "dp", None),
            P("expert", "dp", None),
        ),
        check_vma=False,
    )
```

time: 683 us -> 629 us (0.921)
  Pallas kernels: 572 us -> 546 us
  starting transfers between devices: 28.8 us -> 8.16 us
    pallas_call x6 -> x3, Pallas kernels: 328 us -> 283 us  [the longest x2 279 us: device_call(): pl.pallas_call(kernel, out_shape=tuple(outs), in_specs=[pl.BlockSpec(memo...]
    pallas_call x1, Pallas kernels: 136 us -> 155 us  [run_front(): pl.pallas_call(functools.partial(front_kernel, heads=heads, groups=groups...]
    ppermute x17 -> x6, starting transfers between devices: 15.2 us -> 4.53 us  [exchange(): return lax.ppermute(value, axis, [(i, i ^ mask) for i in range(size)])]
    all_to_all x2 -> x0, starting transfers between devices: 9.4 us -> none  [the longest x1 5.32 us: body(): q0 = lax.all_to_all(back_q0, 'context', 0, 0, tiled=True)]
    squeeze x0 -> x3, local copies, waits for them, and re-layouts: none -> 6.97 us  [the longest x1 3.89 us: body(): ein_parts = (w_expert_in[0], ein_parts[0], ein_parts[1])]
    ppermute x17 -> x6, waiting for transfers between devices: 14.5 us -> 8.06 us  [exchange(): return lax.ppermute(value, axis, [(i, i ^ mask) for i in range(size)])]
  transfers between devices with their start and end apart: 20 -> 7, of which waited for: 4 -> 2; matrix products, arithmetic and copies ran while one was open for 6% -> 6% of each run, Pallas kernels for 54% -> 56%
where the time goes in v3:
time: 629 us; the launch traced here: 620 us
  Pallas kernels  546 us (87%)
  other arithmetic  28.7 us (5%)
  local copies, waits for them, and re-layouts  28.1 us (4%)
  starting transfers between devices  8.16 us (1%)
  waiting for transfers between devices  8.06 us (1%)
    pallas_call x2, Pallas kernels, device_call(): pl.pallas_call(kernel, out_shape=tuple(outs), in_specs=[pl.BlockSpec(memo...  279 us
    pallas_call x1, Pallas kernels, run_front(): pl.pallas_call(functools.partial(front_kernel, heads=heads, groups=groups...  155 us
    pallas_call x3, Pallas kernels, run_ffn(): pl.pallas_call(functools.partial(ffn_kernel, tr=math.gcd(tr, rows), spans...  108 us
  transfers between devices with their start and end apart: 7, of which 2 were waited for; matrix products, arithmetic and copies ran while one was open for 6% of the time, Pallas kernels for 56%

profile of v3, /device:TPU:0, one launch (start us, length us, event | category | flops | bytes accessed | tf_op | source)
XLA Modules:
  0.0 620.2 jit_solution(17867103517911528893)
XLA Ops:
  0.7 0.1 convert_bitcast_fusion
  0.8 0.8 compare_select_fusion
  1.6 0.6 broadcast_in_dim.38.refs_4_
  2.2 0.7 select_reduce_fusion
  2.9 0.6 copy.44.refs_5_
  3.5 0.7 stack.58
  4.2 0.7 stack.59
  4.8 1.0 fusion.3
  5.8 0.6 maximum_convert_fusion.2.refs_1_
  6.4 1.3 pad_maximum_fusion
  7.7 155.2 %shard_map.213 = (bf16[4,9,128,128]{3,2,1,0:T(8,128)(2,1)}, bf16[4,9,128,128]{3,2,1,0:T(8,128)(2,1)}, bf16[4,3,128,128]{3,2,1,0:T(8,128)(2,1)}, bf16[4,3,128,128...) custom-call(bf16[2,256,768]{2,1,0:T(8,128)(2,1)} %bitcast.123, ...), custom_call_target="tpu_custom_call" | custom-call | flops 149500002304 | tf_op jit(solution)/shard_map/pallas_call | solution.py:503
  163.0 0.7 dynamic-slice_bitcast_fusion
  163.7 1.0 copy.45.refs_3_
  164.7 3.9 slice_bitcast_fusion
  168.6 0.6 stack.72.refs_0_
  169.2 41.8 %shard_map.215 = (bf16[1024,768]{1,0:T(8,128)(2,1)}, bf16[1024,768]{1,0:T(8,128)(2,1)}, bf16[768,2048]{1,0:T(8,128)(2,1)}, bf16[768,2048]{1,0:T(8,128)(2,1)}, bf16[2048,768]{1,0:T(8,128)(2,1)}) custom-call(s32[5]{0:T(128)} %stack.72.refs_0_, bf16[1024,768]{1,0:T(8,128)(2,1)} %bitcast.136, bf16[1024,768]{1,0:T(8,128)(2,1)} %bitcast.137, ...), custom_call_target="tpu_custom_call" | custom-call | flops 47149998080 | tf_op jit(solution)/shard_map/pallas_call | solution.py:629
  211.1 2.2 slice.90
  213.3 0.4 collective-permute-start
  213.6 2.1 slice.95
  215.8 0.1 collective-permute-start.2
  215.9 1.8 slice_bitcast_fusion.2
  217.8 0.2 copy-done.6
  218.0 1.2 slice_bitcast_fusion.4
  219.2 0.6 stack.68.refs_0_
  219.9 23.2 %shard_map.214 = (bf16[512,768]{1,0:T(8,128)(2,1)}, bf16[512,768]{1,0:T(8,128)(2,1)}, bf16[768,2048]{1,0:T(8,128)(2,1)}, bf16[768,2048]{1,0:T(8,128)(2,1)}, bf16[2048,768]{1,0:T(8,128)(2,1)}) custom-call(s32[6]{0:T(128)} %stack.68.refs_0_, bf16[512,768]{1,0:T(8,128)(2,1)} %bitcast.140, bf16[512,768]{1,0:T(8,128)(2,1)} %bitcast.120, ...), custom_call_target="tpu_custom_call" | custom-call | flops 26449999872 | tf_op jit(solution)/shard_map/pallas_call | solution.py:629
  243.2 0.0 collective-permute-done.2
  243.2 1.3 add_convert_fusion.1
  244.5 0.0 copy-start.9
  244.5 1.6 collective-permute-start.3
  246.1 0.6 fusion.6
  246.7 1.0 copy.46.refs_3_
  247.8 1.9 reshape_squeeze.32.refs_13_
  249.6 0.6 copy.48
  250.2 0.0 collective-permute-done
  250.2 1.3 add_convert_fusion.2
  251.6 0.8 slice.110
  252.3 0.5 collective-permute-start.1
  252.8 3.8 collective-permute-done.3
  256.7 1.8 add_convert_fusion.5.dxr
  258.5 3.7 shard_map.216
  262.2 3.6 all-to-all-start
  265.9 0.9 fusion.1
  266.8 42.4 %shard_map.217 = (bf16[1024,768]{1,0:T(8,128)(2,1)}, bf16[1024,768]{1,0:T(8,128)(2,1)}, bf16[768,2048]{1,0:T(8,128)(2,1)}, bf16[768,2048]{1,0:T(8,128)(2,1)}, bf16[2048,768]{1,0:T(8,128)(2,1)}) custom-call(s32[5]{0:T(128)} %stack.72.refs_0_, bf16[1024,768]{1,0:T(8,128)(2,1)} %bitcast.133, bf16[1024,768]{1,0:T(8,128)(2,1)} %bitcast.134, ...), custom_call_target="tpu_custom_call" | custom-call | flops 47149998080 | tf_op jit(solution)/shard_map/pallas_call | solution.py:629
  309.2 2.1 slice.101
  311.3 0.0 collective-permute-start.4
  311.3 0.7 copy-done.20
  312.0 182.7 %shard_map.218 = (bf16[4,96,2048]{2,1,0:T(8,128)(2,1)}, bf16[4,96,2048]{2,1,0:T(8,128)(2,1)}, bf16[4,256,768]{2,1,0:T(8,128)(2,1)}, bf16[2,2,96,2048]{3,2,1,0:T(...) custom-call(bf16[2,4,96,2048]{3,2,1,0:T(8,128)(2,1)} %bitcast.130, ...), custom_call_target="tpu_custom_call" | custom-call | flops 189750001664 | tf_op jit(solution)/shard_map/pallas_call | solution.py:1209
  494.7 96.5 %shard_map.219 = (bf16[4,96,2048]{2,1,0:T(8,128)(2,1)}, bf16[4,256,768]{2,1,0:T(8,128)(2,1)}, bf16[2,2,96,1152]{3,2,1,0:T(8,128)(2,1)}, bf16[2,2,96,1152]{3,2,1,...) custom-call(bf16[4,96,2048]{2,1,0:T(8,128)(2,1)} %get-tuple-element., ...), custom_call_target="tpu_custom_call", output_to_operand_aliasing={{0}: (0, {}), {1}: (1, {})} | custom-call | flops 103499997184 | tf_op jit(solution)/shard_map/pallas_call | solution.py:1209
  591.3 3.5 bitcast_convert_fusion
  594.8 3.5 fusion
  598.3 2.2 multiply_reduce_fusion
  600.5 1.1 bitcast_convert_fusion.2
  601.7 0.7 copy-done.2
  602.4 3.5 maximum_convert_fusion
  605.8 1.5 add_convert_fusion
  607.4 1.9 collective-permute-start.5
  609.3 0.6 convert_divide_fusion
  609.9 0.7 slice.107
  610.6 0.6 dynamic-slice_reduce_fusion
  611.2 2.0 bitcast_convert_fusion.1
  613.2 4.2 collective-permute-done.5
  617.4 0.2 fusion.2
  617.6 0.9 maximum_bitcast_fusion.1
  618.6 1.1 copy.57
  (58 shorter events, 0.2 us)
Async XLA Ops:
  211.1 4.9 copy-start
  213.3 37.0 %collective-permute-start = (bf16[512,768]{1,0:T(8,128)(2,1)}, bf16[512,768]{1,0:T(8,128)(2,1)}, u32[]{:S(2)}, u32[]{:S(2)}) collective-permute-start(bf16[512,768]{1,0:T(8,128)(2,1)} %slice.90), channel_id=1, source_target_pairs={{0,8},{8,0},{16,24},{24,16},{1,9},{9,1},{17,25},{25,17},{2,10},{10... | collective-permute-start | bytes 2359304 | tf_op jit(solution)/shard_map/ppermute | solution.py:757
  215.8 27.4 %collective-permute-start.2 = (bf16[512,768]{1,0:T(8,128)(2,1)}, bf16[512,768]{1,0:T(8,128)(2,1)}, u32[]{:S(2)}, u32[]{:S(2)}) collective-permute-start(bf16[512,768]{1,0:T(8,128)(2,1)} %slice.95), channel_id=1, source_target_pairs={{0,8},{8,0},{16,24},{24,16},{1,9},{9,1},{17,25},{25,17},{2,10},{10... | collective-permute-start | bytes 2359304 | tf_op jit(solution)/shard_map/ppermute | solution.py:757
  215.9 2.0 copy-start.6
  219.9 23.3 %copy-start.21 = (s32[4,2,2,1,256]{4,3,2,1,0:T(1,128)S(1)}, s32[4,2,2,1,256]{4,3,2,1,0:T(1,128)}, u32[]{:S(2)}) copy-start(s32[4,2,2,1,256]{4,3,2,1,0:T(1,128)} %get-tuple-element.108) | copy-start | bytes 49156
  219.9 23.3 %copy-start.11 = (bf16[1024,768]{1,0:T(8,128)(2,1)S(1)}, bf16[1024,768]{1,0:T(8,128)(2,1)}, u32[]{:S(2)}) copy-start(bf16[1024,768]{1,0:T(8,128)(2,1)} %get-tuple-element.86) | copy-start | bytes 4718596
  243.2 3.0 copy-start.22
  244.5 5.7 copy-start.9
  244.5 12.1 %collective-permute-start.3 = (bf16[256,768]{1,0:T(8,128)(2,1)S(1)}, bf16[256,768]{1,0:T(8,128)(2,1)}, u32[]{:S(2)}, u32[]{:S(2)}) collective-permute-start(bf16[256,768]{1,0:T(8,128)(2,1)S(1)} %slice.112), channel_id=1, source_target_pairs={{0,16},{8,24},{16,0},{24,8},{1,17},{9,25},{17,1},{25,9},{2,18},{10... | collective-permute-start | bytes 1179656 | tf_op jit(solution)/shard_map/ppermute | solution.py:757
  252.3 13.5 %collective-permute-start.1 = (bf16[256,768]{1,0:T(8,128)(2,1)}, bf16[256,768]{1,0:T(8,128)(2,1)S(1)}, u32[]{:S(2)}, u32[]{:S(2)}) collective-permute-start(bf16[256,768]{1,0:T(8,128)(2,1)} %slice.110), channel_id=1, source_target_pairs={{0,16},{8,24},{16,0},{24,8},{1,17},{9,25},{17,1},{25,9},{2,18},{10... | collective-permute-start | bytes 1179656 | tf_op jit(solution)/shard_map/ppermute | solution.py:757
  258.5 7.3 %copy-start.15 = (bf16[512,768]{1,0:T(8,128)(2,1)S(1)}, bf16[512,768]{1,0:T(8,128)(2,1)}, u32[]{:S(2)}) copy-start(bf16[512,768]{1,0:T(8,128)(2,1)} %get-tuple-element.76) | copy-start | bytes 2359300
  258.5 7.4 %copy-start.18 = (f32[256,768]{1,0:T(8,128)S(1)}, f32[256,768]{1,0:T(8,128)}, u32[]{:S(2)}) copy-start(f32[256,768]{1,0:T(8,128)} %get-tuple-element.72.res_ref) | copy-start | bytes 2359300
  262.2 49.1 %all-to-all-start = ((bf16[4,3,128,128]{3,2,1,0:T(8,128)(2,1)}), bf16[4,3,128,128]{3,2,1,0:T(8,128)(2,1)S(1)}, u32[]{:S(2)}, u32[]{:S(2)}) async-start(bf16[4,3,128,128]{3,2,1,0:T(8,128)(2,1)} %get-tuple-element.89), calls=%async_computation | async-start | bytes 786432 | tf_op jit(solution)/shard_map/all_to_all | solution.py:1505
  311.3 294.6 %collective-permute-start.4 = (bf16[512,768]{1,0:T(8,128)(2,1)}, bf16[512,768]{1,0:T(8,128)(2,1)}, u32[]{:S(2)}, u32[]{:S(2)}) collective-permute-start(bf16[512,768]{1,0:T(8,128)(2,1)} %slice.101), channel_id=1, source_target_pairs={{0,8},{8,0},{16,24},{24,16},{1,9},{9,1},{17,25},{25,17},{2,10},{10... | collective-permute-start | bytes 2359304 | tf_op jit(solution)/shard_map/ppermute | solution.py:757
  311.3 0.7 copy-start.20
  591.3 3.5 copy-start.4
  591.3 3.5 copy-start.5
  594.8 3.5 copy-start.1
  594.8 3.5 copy-start.13
  594.8 3.5 copy-start.14
  598.3 2.3 copy-start.19
  598.3 3.4 copy-start.3
  600.5 1.8 copy-start.2
  602.4 3.5 copy-start.10
  605.8 3.4 copy-start.23
  605.8 5.4 copy-start.12
  607.4 10.1 %collective-permute-start.5 = (bf16[256,768]{1,0:T(8,128)(2,1)S(1)}, bf16[256,768]{1,0:T(8,128)(2,1)S(1)}, u32[]{:S(2)}, u32[]{:S(2)}) collective-permute-start(bf16[256,768]{1,0:T(8,128)(2,1)S(1)} %slice.115), channel_id=1, source_target_pairs={{0,16},{8,24},{16,0},{24,8},{1,17},{9,25},{17,1},{25,9},{2,18},{10... | collective-permute-start | bytes 1179656 | tf_op jit(solution)/shard_map/ppermute | solution.py:757
  611.2 6.2 %copy-start.16 = (bf16[512,768]{1,0:T(8,128)(2,1)S(1)}, bf16[512,768]{1,0:T(8,128)(2,1)}, u32[]{:S(2)}) copy-start(bf16[512,768]{1,0:T(8,128)(2,1)} %get-tuple-element.76) | copy-start | bytes 2359300
  611.2 6.2 %copy-start.17 = (f32[256,768]{1,0:T(8,128)S(1)}, f32[256,768]{1,0:T(8,128)}, u32[]{:S(2)}) copy-start(f32[256,768]{1,0:T(8,128)} %get-tuple-element.83.refs_16_) | copy-start | bytes 2359300
  613.2 4.4 copy-start.8
  613.2 5.4 copy-start.7

commit v4 on v3

--- a/solution.py
+++ b/solution.py
@@ -52,23 +52,6 @@
         pltpu.roll(tile, HEAD // 2, 1),
     )
     return tile * cosines + partner * sines
-
-
-def call(kernel, out_shape, *, grid=(), in_specs=None, out_specs=None, scratch=(), us=5):
-    return pl.pallas_call(
-        kernel,
-        out_shape=out_shape,
-        grid=grid,
-        in_specs=in_specs,
-        out_specs=out_specs,
-        scratch_shapes=scratch,
-        compiler_params=pltpu.CompilerParams(vmem_limit_bytes=VMEM_LIMIT),
-        cost_estimate=price(us),
-    )
-
-
-def full_spec(shape):
-    return pl.BlockSpec(tuple(shape), lambda *_: (0,) * len(shape))
 
 
 def struct(shape, dtype):
@@ -272,12 +255,12 @@
 def front_kernel(*refs, heads, groups):
     refs = list(refs)
     take = lambda n: [refs.pop(0) for _ in range(n)]
-    x_ref, gains_in, cos_ref, sin_ref, tags_in, gates_in = take(6)
+    x_ref, gains_in, tags_in, gates_in = take(4)
     w_qkv, w_out, w_ein, w_eout, w_sin, w_sout, cot = take(7)
     recv_out, mixed_out, lse_out, att_out, res_out = take(2), take(2), take(2), take(2), take(2)
     rows_out, cot_out, gates_out, both_out, tags_out = take(2), take(2), take(1)[0], take(1)[0], take(1)[0]
-    qkv_out, wout_out, ein_out, eout_out, sin_out, sout_out, gains_out = take(7)
-    wq, wo, gains, tags, pay, recv, ks, vs, scores, mixed, got, lse, att, res, nf = take(15)
+    qkv_out, wout_out, ein_out, eout_out, sin_out, sout_out, gains_out, table_out = take(8)
+    wq, wo, gains, tags, pay, recv, ks, vs, scores, mixed, got, lse, att, res, nf, table = take(16)
     s_qkv, s_out, s_gain, s_exp, s_tag, s_gate, s_cot, s_pay, s_mix, s_row = [take(2) for _ in range(10)]
     local, self_pay, self_mix, self_tag, stores = take(5)
     e, z, d = lax.axis_index("expert"), lax.axis_index("context"), lax.axis_index("dp")
@@ -301,17 +284,19 @@
     half = z % 2
     to_mate = {"context": z + 1 - 2 * half}
     x_exp = [
-        remote(w_ein.at[half], ein_out.at[0], s_exp, 0, to_x),
+        remote(w_ein.at[half], ein_out.at[half], s_exp, 0, to_x),
         remote(w_eout, eout_out, s_exp, 1, to_x),
-        remote(w_sin.at[core], sin_out.at[0], s_exp, 2, to_x),
-        remote(w_sout.at[core], sout_out.at[0], s_exp, 3, to_x),
+        remote(w_sin.at[core, y], sin_out.at[core, y], s_exp, 2, to_x),
+        remote(w_sout.at[core, y], sout_out.at[core, y], s_exp, 3, to_x),
     ]
     n_exp = [
-        remote(ein_out.at[0], ein_out.at[1], s_exp, 4, to_mate),
-        remote(sin_out.at[0], sin_out.at[1], s_exp, 5, to_core),
-        remote(sout_out.at[0], sout_out.at[1], s_exp, 6, to_core),
+        remote(ein_out.at[half], ein_out.at[half], s_exp, 4, to_mate),
+        remote(sin_out.at[core, y], sin_out.at[core, y], s_exp, 5, to_y),
+        remote(sout_out.at[core, y], sout_out.at[core, y], s_exp, 6, to_y),
+        remote(sin_out.at[core], sin_out.at[core], s_exp, 7, to_core),
+        remote(sout_out.at[core], sout_out.at[core], s_exp, 8, to_core),
     ]
-    for copy in (x_qkv, x_gain, x_out, *x_exp):
+    for copy in (x_qkv, x_gain, x_out, x_exp[0], x_exp[2], x_exp[3], x_exp[1]):
         copy.start()
     tag_trade = [
         remote(tags_in, tags.at[z], s_tag, k, others[k]) for k in range(groups - 1)
@@ -340,6 +325,14 @@
     for copy in y_cot:
         copy.start()
 
+    row = lax.broadcasted_iota(jnp.int32, (MICRO * TILE, HALF), 0)
+    lane = lax.broadcasted_iota(jnp.int32, (MICRO * TILE, HALF), 1)
+    place = row // TILE * (TILE * groups) + z * TILE + row % TILE
+    freq = jnp.exp((-math.log(ROPE_BASE) * 2.0 / HEAD) * (lane % (HEAD // 2)).astype(F32))
+    angle = place.astype(F32) * freq
+    table[0] = jnp.cos(angle)
+    table[1] = jnp.where(lane % HEAD < HEAD // 2, -jnp.sin(angle), jnp.sin(angle))
+
     c_qkv = remote(wq.at[1 - d, core], wq.at[1 - d, core], s_qkv, 1, to_core)
     c_out = remote(wo.at[1 - d, core], wo.at[1 - d, core], s_out, 1, to_core)
     for copy in loads:
@@ -353,7 +346,7 @@
     trades, returns = [], []
     for m in range(MICRO):
         span = slice(m * TILE, (m + 1) * TILE)
-        project(x_ref[m].astype(F32), both[0], w_full, cos_ref[span, :], sin_ref[span, :], pay.at[m], groups)
+        project(x_ref[m].astype(F32), both[0], w_full, table[0, span, :], table[1, span, :], pay.at[m], groups)
         trade = Trade(pay.at[m], recv.at[m], [s.at[m] for s in s_pay], self_pay.at[m])
         for dest in range(groups):
             trade.send(dest)
@@ -404,11 +397,17 @@
         c_cot[MICRO + m].start()
     trades[1].collect()
     fill_keys(recv.at[1], 1, ks, vs, heads)
+    for k in (2, 3):
+        x_exp[k].wait_recv()
+        n_exp[k - 1].start()
     back1 = attend(1, 0, 2)
     c_out.wait_recv()
     post(0, back0)
     back1 = attend(1, 2, groups)
     forward_row(0)
+    for k in (1, 2):
+        n_exp[k].wait_recv()
+        n_exp[k + 2].start()
     post(1, back1)
     keep = []
     for m in range(MICRO):
@@ -421,14 +420,11 @@
             (nf.at[m], rows_out[m].at[0]),
             (nf.at[m], both_out.at[m]),
         ]
-    keep += [(tags, tags_out), (wq, qkv_out), (wo, wout_out), (gains, gains_out)]
+    keep += [(tags, tags_out), (wq, qkv_out), (wo, wout_out), (gains, gains_out), (table, table_out)]
     keep = [pltpu.make_async_copy(a, b, stores.at[3 + i]) for i, (a, b) in enumerate(keep)]
     for copy in keep:
         copy.start()
     forward_row(1)
-    for k in (2, 3):
-        x_exp[k].wait_recv()
-        n_exp[k - 1].start()
     for copy in (*keep, *own_copies):
         copy.wait()
     for m in range(MICRO):
@@ -439,19 +435,24 @@
     back0.release()
     back1.release()
     x_exp[1].wait_recv()
-    for copy in (*n_exp, *c_gate, *c_cot):
+    for copy in n_exp:
+        copy.wait_send()
+    for copy in (n_exp[0], n_exp[3], n_exp[4]):
+        copy.wait_recv()
+    for copy in (*c_gate, *c_cot):
         copy.wait()
     for copy in (*x_exp, x_qkv, x_gain, x_out, c_qkv, c_out, y_gate, *y_cot, *tag_trade):
         copy.wait_send()
 
 
-def run_front(x, gains, cosines, sines, tags, gates, w_qkv, w_out, w_ein, w_eout, w_sin, w_sout, cot, groups):
+def run_front(x, gains, tags, gates, w_qkv, w_out, w_ein, w_eout, w_sin, w_sout, cot, groups):
     _, rows, width = x.shape
     heads = width // HEAD // groups
     k = width // 4
     w_qkv = w_qkv.reshape(2, k, 3 * width)
     w_out = w_out.reshape(2, k, width)
-    w_ein, w_sin, w_sout = [w.reshape(2, -1, w.shape[1]) for w in (w_ein, w_sin, w_sout)]
+    w_ein = w_ein.reshape(2, -1, w_ein.shape[1])
+    w_sin, w_sout = [w.reshape(2, 2, -1, w.shape[1]) for w in (w_sin, w_sout)]
     vmem = pl.BlockSpec(memory_space=pltpu.VMEM)
     anywhere = pl.BlockSpec(memory_space=pl.ANY)
     packed = lambda n: (groups, n * heads, HALF, HALF)
@@ -476,6 +477,7 @@
             struct(w_sin.shape, BF),
             struct(w_sout.shape, BF),
             struct((2, *gains.shape), F32),
+            struct((2, MICRO * rows, HALF), F32),
         ]
     )
     v = pltpu.VMEM
@@ -496,21 +498,22 @@
         v((MICRO, rows, width), BF),
         v((MICRO, rows, width), F32),
         v((MICRO, rows, width), BF),
+        v((2, MICRO * rows, HALF), F32),
     ]
-    for shape in ((2,), (2,), (1,), (7,), (groups - 1,), (3,), (6,), (MICRO, groups), (MICRO, groups), (6,)):
+    for shape in ((2,), (2,), (1,), (9,), (groups - 1,), (3,), (6,), (MICRO, groups), (MICRO, groups), (6,)):
         scratch += [dma(*shape), dma(*shape)]
-    scratch += [dma(3), dma(MICRO), dma(MICRO), dma(1), dma(3 + 7 * MICRO + 4)]
+    scratch += [dma(3), dma(MICRO), dma(MICRO), dma(1), dma(3 + 7 * MICRO + 5)]
     return pl.pallas_call(
         functools.partial(front_kernel, heads=heads, groups=groups),
         out_shape=tuple(outs),
-        in_specs=[vmem] * 6 + [anywhere] * 7,
+        in_specs=[vmem] * 4 + [anywhere] * 7,
         out_specs=(anywhere,) * len(outs),
         scratch_shapes=scratch,
         compiler_params=pltpu.CompilerParams(
             vmem_limit_bytes=VMEM_LIMIT, collective_id=3, has_side_effects=True
         ),
         cost_estimate=price(130),
-    )(x, gains, cosines, sines, tags, gates, w_qkv, w_out, w_ein, w_eout, w_sin, w_sout, cot)
+    )(x, gains, tags, gates, w_qkv, w_out, w_ein, w_eout, w_sin, w_sout, cot)
 
 
 def ffn_kernel(*refs, tr, spans, counts, first, gated, opened, summed, closing):
@@ -695,39 +698,11 @@
     return gain_grad
 
 
-def mid_kernel(dxs, dxr, res_ref, gain_ref, cot_ref, w_ref, gres_ref, pay, gg_ref, gbf, *, per):
-    grad = dxs[...].astype(F32) + dxr[...].astype(F32)
-    gg_ref[...] = mid_core(grad, res_ref[...], gain_ref[...], cot_ref[0], w_ref, pay, gres_ref, gbf, per)
-
-
-def run_mid(dxs, dxr, residual, gain, cot, w, groups):
-    rows, width = residual.shape
-    per = width // HEAD // groups
-    args = (dxs, dxr, residual, gain, cot, w)
-    specs = [full_spec(a.shape) for a in args]
-    specs[0] = pl.BlockSpec((rows, width), lambda _: (0, 0))
-    specs[4] = pl.BlockSpec((1, rows, width), lambda _: (0, 0, 0))
-    outs = [
-        struct((rows, width), F32),
-        struct((groups, per, HALF, HALF), BF),
-        struct((1, width), F32),
-        struct((rows, width), BF),
-    ]
-    return call(
-        functools.partial(mid_kernel, per=per),
-        tuple(outs),
-        grid=(1,),
-        in_specs=specs,
-        out_specs=tuple(full_spec(o.shape) for o in outs),
-        us=4,
-    )(*args)
-
-
-def finish(d0, d1, x_ref, gain_ref, w_ref, cos_ref, sin_ref, gres, atts, gbfs, gin_ref, gq, gv, go, gj, per):
+def finish(d0, d1, x_ref, gain_ref, w_ref, table, gres, atts, gbfs, gin_ref, gq, gv, go, gj, per):
     width = x_ref.shape[2]
     for micro, ref in enumerate((d0, d1)):
         rows = slice(micro * TILE, (micro + 1) * TILE)
-        cosines, sines = cos_ref[rows, :], sin_ref[rows, :]
+        cosines, sines = table[0, rows, :], table[1, rows, :]
         for kind in range(3):
             for pair in range(width // HALF):
                 tile = natural(ref, kind, pair, per)
@@ -743,13 +718,13 @@
     split = gq.shape[-1]
     gq[...] = dot(turned, gj[:, :split]).astype(BF).reshape(gq.shape)
     gv[...] = dot(turned, gj[:, split:]).astype(BF).reshape(gv.shape)
-    go[...] = (dot(atts[0][...], gbfs[0][...], TN) + dot(atts[1][...], gbfs[1][...], TN)).astype(BF).reshape(go.shape)
+    go[...] = (dot(atts[0][...], gbfs[0], TN) + dot(atts[1][...], gbfs[1], TN)).astype(BF).reshape(go.shape)
     yield
     first = dot(gj[...], w_ref[...], NT)
     back, _ = norm_back(tokens, scale, gain, first)
     for micro in range(MICRO):
         rows = slice(micro * TILE, (micro + 1) * TILE)
-        gin_ref[rows, :] = gres[micro][...] + back[rows]
+        gin_ref[rows, :] = gres[micro] + back[rows]
 
 
 def exchange(value, axis, mask):
@@ -767,9 +742,8 @@
     return value
 
 
-def scatter_xor(value):
-    masks = bits_of(lax.axis_size("expert"))
-    for mask in (*reversed(masks[2:]), *masks[:2]):
+def scatter_rest(value):
+    for mask in reversed(bits_of(lax.axis_size("expert"))[2:]):
         half = value.shape[0] // 2
         got = exchange(value[half:], "expert", mask)
         value = (value[:half].astype(F32) + got.astype(F32)).astype(value.dtype)
@@ -795,37 +769,33 @@
 EARLY = 6
 AHEAD = 2
 PLAN = {
-    2: ("rs1",),
-    4: ("a0", "A0",),
-    5: ("a1", "rs2",),
-    6: ("A1",),
-    7: ("B0",),
-    10: ("a2",),
-    11: ("A2", "b0", "A3", "B1",),
-    15: ("C0",),
-    16: ("B2",),
-    17: ("C1",),
-    19: ("A4",),
-    20: ("c0", "B3",),
-    21: ("b1", "C2",),
-    23: ("B4",),
-    24: ("D0",),
-    25: ("C3",),
-    27: ("b2", "d0", "A5",),
-    28: ("C4",),
-    31: ("B5",),
-    33: ("c1",),
-    36: ("d1", "e0", "c2",),
-    37: ("A6",),
-    38: ("C5", "d2",),
-    42: ("e1", "e2", "zhome", "f0", "A7", "A8", "f1", "f2", "g2", "D3", "D1", "D5", "A9", "D4", "g1", "g0", "D2", "h0", "A10", "A11", "h1", "h2",),
+    -1: ("rs1", "A0", "a0", "rs2", "B0", "A1", "a1", "a2", "A2", "rs3",),
+    3: ("A3", "B1",),
+    8: ("A4",),
+    9: ("b0",),
+    10: ("B2", "C0",),
+    11: ("A5",),
+    12: ("C1",),
+    14: ("B3",),
+    20: ("B4", "C2",),
+    23: ("b1", "B5",),
+    24: ("C3", "c0",),
+    25: ("b2",),
+    26: ("C4",),
+    27: ("d0",),
+    29: ("c1",),
+    32: ("d1", "C5",),
+    33: ("c2",),
+    36: ("d2", "e0",),
+    41: ("e1", "f0",),
+    42: ("D3", "e2", "zhome", "A7", "A9", "g0", "f2", "D5", "D4", "A6", "f1", "D1", "h0", "g2", "A11", "h2", "g1", "D2", "A8", "h1", "A10", "D0",),
 }
 LAST_PLAN = (
-    "A0", "A1", "A2", "B0", "A3", "a0", "A4", "B1", "a1", "C0",
-    "B2", "C1", "zrest", "b0", "B3", "C2", "b1", "c0", "a2", "B4",
-    "C3", "c1", "b2", "D1", "d0", "C4", "c2", "d1", "e0", "d2",
-    "e1", "A5", "D2", "D4", "D0", "f0", "f1", "B5", "f2", "e2",
-    "g0", "g1", "D3", "h1", "h0", "C5", "g2", "D5", "h2",
+    "A0", "A1", "A2", "A3", "B0", "B1", "a0", "C0", "A5", "a1",
+    "B2", "C1", "B3", "b0", "a2", "C2", "b1", "B5", "C3", "c0",
+    "b2", "d0", "c1", "C5", "c2", "D2", "d2", "D0", "e0", "A4",
+    "f0", "d1", "D5", "f1", "zrest", "B4", "g0", "f2", "e1", "e2",
+    "g1", "h0", "D3", "D1", "C4", "g2", "D4", "h1", "h2",
 )
 
 
@@ -1097,42 +1067,57 @@
 def back_kernel(*refs, own_at, sources, common, heads, groups):
     refs = Arrays(refs)
     own_in, com_in = refs.take(sources), refs.take(common)
-    recv0, recv1, grad0, out0, out1, lse0, lse1, key_tag, query_tag = refs.take(9)
-    dxs, res_ref, gain_ref, cot_ref, w_ref, dx_made = refs.take(6)
+    recv0, recv1, out0, out1, lse0, lse1, key_tag, query_tag = refs.take(8)
+    dxs, res0, res1, gain_ref, cot_ref, w_ref = refs.take(6)
+    dx_made = refs.take(MICRO)
     own_out, com_out = refs.take(sources), refs.take(common)
     d0_out, d1_out, gres_out, gbf_out, gg_out = refs.take(5)
     engine = refs.engine(own_at, own_in, own_out, com_in, com_out)
-    dx, r_core, r_y, gres, gbf, gg, pay_o, grad1, pay0, pay1 = refs.take(10)
+    dx, r_core, r_y, gres, gbf, gg, pay_o, back_o, pay0, pay1 = refs.take(10)
     ks, vs, dk, dv, qs, gs, deltas, acc = refs.take(8)
     s_dx, s_o, s_0, s_1 = [refs.take(2) for _ in range(4)]
     local, = refs.take(1)
 
     engine.greet()
-    send_core = remote(dx_made.at[2:4], r_core, s_dx, 0, engine.to_core)
-    send_core.start()
-    own_dx = pltpu.make_async_copy(dx_made.at[0:2], dx, local.at[0])
-    own_dx.start()
+    both = range(MICRO)
+    send_core = [remote(dx_made[m].at[2:4], r_core.at[m], s_dx, m, engine.to_core) for m in both]
+    own_dx = [pltpu.make_async_copy(dx_made[m].at[0:2], dx.at[m], local.at[m]) for m in both]
+    for m in both:
+        send_core[m].start()
+        own_dx[m].start()
     engine.start(AHEAD)
-    send_y = remote(dx.at[1], r_y, s_dx, 1, engine.to_y)
-    trade_o = Trade(pay_o, grad1, s_o, local.at[1])
-    homes = [Trade(pay0, d0_out, s_0, local.at[2]), Trade(pay1, d1_out, s_1, local.at[3])]
+    send_y = [remote(dx.at[m, 1], r_y.at[m], s_dx, MICRO + m, engine.to_y) for m in both]
+    trade_o = [
+        Trade(pay_o.at[m], back_o.at[m], [s.at[m] for s in s_o], local.at[2 + m]) for m in both
+    ]
+    homes = [Trade(pay0, d0_out, s_0, local.at[4]), Trade(pay1, d1_out, s_1, local.at[5])]
     results = [
-        pltpu.make_async_copy(a, b, local.at[4 + i])
+        pltpu.make_async_copy(a, b, local.at[6 + i])
         for i, (a, b) in enumerate(((gres, gres_out), (gbf, gbf_out), (gg, gg_out)))
     ]
 
     def rs1():
-        own_dx.wait()
-        send_core.wait_recv()
-        dx[...] = dx[...] + r_core[...]
-        send_y.start()
+        for m in both:
+            own_dx[m].wait()
+            send_core[m].wait_recv()
+            dx[m] = dx[m] + r_core[m]
+            send_y[m].start()
+
+    def middle(m, res_ref):
+        send_y[m].wait_recv()
+        grad = dxs[m * TILE : (m + 1) * TILE, :].astype(F32) + dx[m, 0].astype(F32) + r_y[m].astype(F32)
+        part = mid_core(
+            grad, res_ref[...], gain_ref[...], cot_ref[m], w_ref, pay_o.at[m], gres.at[m], gbf.at[m], heads
+        )
+        for dest in range(groups):
+            trade_o[m].send(dest)
+        return part
 
     def rs2():
-        send_y.wait_recv()
-        grad = dxs[TILE:, :].astype(F32) + dx[0].astype(F32) + r_y[...].astype(F32)
-        gg[...] = mid_core(grad, res_ref[...], gain_ref[...], cot_ref[1], w_ref, pay_o, gres, gbf, heads)
-        for dest in range(groups):
-            trade_o.send(dest)
+        gg[...] = middle(0, res0)
+
+    def rs3():
+        gg[...] = gg[...] + middle(1, res1)
         for copy in results:
             copy.start()
 
@@ -1142,7 +1127,7 @@
                 back_pack(dk, dv, pay, dest, base, heads)
                 trade.send(dest)
 
-    named = {"rs1": rs1, "rs2": rs2, "zhome": zhome, "zend": lambda: None}
+    named = {"rs1": rs1, "rs2": rs2, "rs3": rs3, "zhome": zhome}
 
     def events(slot):
         for name in PLAN.get(slot, ()):
@@ -1155,11 +1140,12 @@
     first_of = (0, sum(min(s + 2, groups) for s in range(groups)))
     total = 2 * first_of[1] + groups * groups
     for micro, (recv, grad, out, lse, pay) in enumerate(
-        ((recv0, grad0, out0, lse0, pay0), (recv1, grad1, out1, lse1, pay1))
+        ((recv0, back_o.at[0], out0, lse0, pay0), (recv1, back_o.at[1], out1, lse1, pay1))
     ):
         begin, end = first_of[micro], (first_of + (total,))[micro + 1]
-        if micro:
-            trade_o.collect()
+        if micro == 0:
+            events(-1)
+        trade_o[micro].collect()
 
         def step(s, carry, micro=micro, recv=recv, grad=grad, out=out, lse=lse, pay=pay, begin=begin, end=end):
             back_begin(micro, s, heads, recv, grad, out, qs, gs, deltas, acc)
@@ -1188,9 +1174,10 @@
     for trade in homes:
         trade.collect()
         trade.release()
-    trade_o.release()
-    send_core.wait_send()
-    send_y.wait_send()
+    for m in both:
+        trade_o[m].release()
+        send_core[m].wait_send()
+        send_y[m].wait_send()
     for copy in results:
         copy.wait()
     engine.close()
@@ -1231,7 +1218,7 @@
     com = [g.reshape(shared_shape(g.shape)) for g in shared_grads]
     heads = attention[0].shape[1] // 3
     rows, width = middle[1].shape
-    args = [*own, *com, *attention, *middle, dx_made]
+    args = [*own, *com, *attention, *middle, *dx_made]
     own_shapes = [own[j].shape[2:] for j, _, _ in own_at]
     com_shapes = [g.shape[3:] for g in com]
     own_buf, com_buf, sems = Engine.scratch(own_shapes, [kind for *_, kind in own_at], com_shapes)
@@ -1242,20 +1229,20 @@
         [struct(g.shape[1:], BF) for g in own]
         + [struct((2, 2, *s), BF) for s in com_shapes]
         + [struct(pay(3), BF)] * 2
-        + [struct((rows, width), F32), struct((rows, width), BF), struct((1, width), F32)]
+        + [struct((MICRO, rows, width), F32), struct((MICRO, rows, width), BF), struct((1, width), F32)]
     )
     scratch = [
         *own_buf,
         *com_buf,
         *sems,
-        v((2, rows, width), BF),
-        v((2, rows, width), BF),
-        v((rows, width), BF),
-        v((rows, width), F32),
-        v((rows, width), BF),
+        v((MICRO, 2, rows, width), BF),
+        v((MICRO, 2, rows, width), BF),
+        v((MICRO, rows, width), BF),
+        v((MICRO, rows, width), F32),
+        v((MICRO, rows, width), BF),
         v((1, width), F32),
-        v(pay(1), BF),
-        v(pay(1), BF),
+        v((MICRO, *pay(1)), BF),
+        v((MICRO, *pay(1)), BF),
         v(pay(3), BF),
         v(pay(3), BF),
         v((heads, held, HALF), BF),
@@ -1266,12 +1253,14 @@
         v((heads, TILE, HALF), BF),
         v((heads, 8, TILE), F32),
         v((heads, TILE, HALF), F32),
-        dma(2),
-        dma(2),
-        *[dma(groups)] * 6,
-        dma(7),
+        dma(2 * MICRO),
+        dma(2 * MICRO),
+        *[pltpu.SemaphoreType.DMA((MICRO, groups))] * 2,
+        *[dma(groups)] * 4,
+        dma(9),
     ]
-    flags = [False] * (len(own) + len(com)) + [True] * (len(attention) + len(middle)) + [False]
+    flags = [False] * (len(own) + len(com)) + [True] * (len(attention) + len(middle))
+    flags += [False] * len(dx_made)
     kernel = functools.partial(
         back_kernel, own_at=own_at, sources=len(own), common=len(com), heads=heads, groups=groups
     )
@@ -1283,13 +1272,13 @@
 def last_kernel(*refs, own_at, sources, per):
     refs = Arrays(refs)
     own_in = refs.take(sources)
-    d0, d1, x_ref, gain_ref, w_ref, cos_ref, sin_ref = refs.take(7)
-    gres, atts, gbfs, ggs = refs.take(2), refs.take(2), refs.take(2), refs.take(2)
+    d0, d1, x_ref, gain_ref, w_ref, table = refs.take(6)
+    (gres, gbfs, gg_in), atts, made = refs.take(3), refs.take(2), refs.take(MICRO)
     own_out, com_out = refs.take(sources), refs.take(3)
-    gin_out, gg_out = refs.take(2)
+    gin_out, gg_out, routed_out = refs.take(3)
     sources = [refs.refs.pop(len(own_at) * 4 + 3 * 6 + 28) for _ in range(3)]
     engine = refs.engine(own_at, own_in, own_out, sources, com_out)
-    gj, gin, gg_sum, gg_got, g_send, g_recv, local = refs.take(7)
+    gj, gin, gg_sum, gg_got, g_send, g_recv, local, row, row_core, row_y, m_send, m_recv = refs.take(12)
     engine.greet()
     engine.start(0, com=False)
     z = lax.axis_index("context")
@@ -1297,10 +1286,18 @@
     wires = [
         remote(gg_sum.at[k], gg_got.at[k], (g_send, g_recv), k, target) for k, target in enumerate(rounds)
     ]
-    gg_sum[0] = jnp.broadcast_to(ggs[0][...] + ggs[1][...], gg_sum.shape[1:])
+    gg_sum[0] = jnp.broadcast_to(gg_in[...], gg_sum.shape[1:])
     wires[0].start()
+    both = range(MICRO)
+    row_wires = [remote(made[m].at[2:4], row_core.at[m], (m_send, m_recv), m, engine.to_core) for m in both]
+    row_next = [remote(row.at[m, 1], row_y.at[m], (m_send, m_recv), MICRO + m, engine.to_y) for m in both]
+    row_own = [pltpu.make_async_copy(made[m].at[0:2], row.at[m], local.at[2 + m]) for m in both]
+    row_out = [pltpu.make_async_copy(row.at[m, 0], routed_out.at[m], local.at[2 + m]) for m in both]
+    for m in both:
+        row_wires[m].start()
+        row_own[m].start()
     work = finish(
-        d0, d1, x_ref, gain_ref, w_ref, cos_ref, sin_ref, gres, atts, gbfs, gin, *sources, gj, per
+        d0, d1, x_ref, gain_ref, w_ref, table, gres, atts, gbfs, gin, *sources, gj, per
     )
     store = pltpu.make_async_copy(gin, gin_out, local.at[0])
     next(work)
@@ -1314,6 +1311,17 @@
             store.start()
         else:
             engine.run(name)
+        if index == 12:
+            for m in both:
+                row_own[m].wait()
+                row_wires[m].wait_recv()
+                row[m] = row[m] + row_core[m]
+                row_next[m].start()
+        if index == 30:
+            for m in both:
+                row_next[m].wait_recv()
+                row[m, 0] = row[m, 0] + row_y[m]
+                row_out[m].start()
         if index % 5 == 4 and turn < len(wires):
             wires[turn].wait_recv()
             gg_sum[turn + 1] = gg_sum[turn] + gg_got[turn]
@@ -1324,15 +1332,17 @@
     total.start()
     store.wait()
     total.wait()
-    for wire in wires:
+    for wire in (*wires, *row_wires, *row_next):
         wire.wait_send()
+    for copy in row_out:
+        copy.wait()
     engine.close()
 
 
-def run_last(sums, own_at, parts, groups):
+def run_last(sums, own_at, parts, made, groups):
     x, w = parts[2], parts[4]
     _, rows, width = x.shape
-    args = [*sums, *parts]
+    args = [*sums, *parts, *made]
     own_shapes = [sums[j].shape[1:] for j, _, _ in own_at]
     com = [shared_shape((width, 3 * width // 2))] * 2 + [shared_shape((width, width))]
     own_buf, com_buf, sems = Engine.scratch(own_shapes, [k for *_, k in own_at], [s[3:] for s in com])
@@ -1340,7 +1350,7 @@
     outs = (
         [struct(g.shape, BF) for g in sums]
         + [struct((2, 2, *s[3:]), BF) for s in com]
-        + [struct((MICRO * rows, width), F32), struct((8, width), F32)]
+        + [struct((MICRO * rows, width), F32), struct((8, width), F32), struct((MICRO, rows, width), BF)]
     )
     rounds = 5
     scratch = [
@@ -1353,9 +1363,13 @@
         v((rounds + 1, 8, width), F32),
         v((rounds, 8, width), F32),
         *[pltpu.SemaphoreType.DMA((rounds,))] * 2,
-        pltpu.SemaphoreType.DMA((2,)),
+        pltpu.SemaphoreType.DMA((2 + MICRO,)),
+        v((MICRO, 2, rows, width), BF),
+        v((MICRO, 2, rows, width), BF),
+        v((MICRO, rows, width), BF),
+        *[pltpu.SemaphoreType.DMA((2 * MICRO,))] * 2,
     ]
-    flags = [False] * len(sums) + [True] * len(parts)
+    flags = [False] * len(sums) + [True] * len(parts) + [False] * len(made)
     kernel = functools.partial(
         last_kernel, own_at=own_at, sources=len(sums), per=width // HEAD // groups
     )
@@ -1363,7 +1377,7 @@
         kernel, args, flags, outs, scratch, 2, 90, {i: i for i in range(len(sums))}
     )
     n = len(sums)
-    return got[:n], [rest_sum(g.reshape(-1, g.shape[-1]).astype(F32)) for g in got[n : n + 3]], got[n + 3], got[n + 4]
+    return got[:n], [rest_sum(g.reshape(-1, g.shape[-1]).astype(F32)) for g in got[n : n + 3]], *got[n + 3 :]
 
 
 def body(
@@ -1391,18 +1405,6 @@
     x = inputs[0]
     cot = cotangent[0].reshape(MICRO * rows, width)
 
-    positions = (
-        jnp.arange(MICRO, dtype=jnp.int32)[:, None] * seq_rows
-        + z * rows
-        + jnp.arange(rows, dtype=jnp.int32)[None, :]
-    ).reshape(-1)
-    half = HEAD // 2
-    freq = jnp.exp(-math.log(ROPE_BASE) * jnp.arange(half, dtype=F32) * 2.0 / HEAD)
-    angle = positions.astype(F32)[:, None] * freq[None, :]
-    cos_t, sin_t = jnp.cos(angle), jnp.sin(angle)
-    cosines = jnp.concatenate([cos_t] * 4, -1)
-    sines = jnp.concatenate([-sin_t, sin_t, -sin_t, sin_t], -1)
-
     blocks = block_ids[0] + 8 * jnp.arange(MICRO, dtype=jnp.int32)[:, None]
     key_tags = jnp.where(keep_flags[0] == 1, blocks, HIDDEN)
     tags = jnp.stack([blocks, key_tags])[:, :, None]
@@ -1428,11 +1430,10 @@
         sin_parts,
         sout_parts,
         gains,
+        table,
     ) = run_front(
         x,
         gains,
-        cosines,
-        sines,
         tags,
         per_expert,
         w_qkv,
@@ -1460,17 +1461,13 @@
     core = lax.axis_index("expert") % 2
     dp = lax.axis_index("dp")
     k_half, f_half = width // 2, w_shared_out.shape[0]
-    ein_parts = (w_expert_in[0], ein_parts[0], ein_parts[1])
+    whole = lambda w: w.reshape(-1, w.shape[-1])
+    ein_parts = (w_expert_in[0], whole(ein_parts))
     eout_parts = (w_expert_out[0], eout_other)
-    sin_parts = (w_shared_in, sin_parts[0], sin_parts[1])
-    sout_parts = (w_shared_out, sout_parts[0], sout_parts[1])
-    places = lambda bit: [2 * (1 - dp) + bit, 2 * (1 - dp) + 1 - bit]
-    row_offs = lambda bit: [dp * k_half] + [p * (k_half // 2) for p in places(bit)]
+    sin_parts = (w_shared_in, whole(sin_parts))
+    sout_parts = (w_shared_out, whole(sout_parts))
     chunk = f_half // FB
-    expert_offs = jnp.stack(row_offs(z % 2) + [dp * chunk, (1 - dp) * chunk])
-    shared_offs = jnp.stack(
-        row_offs(core) + [dp * chunk] + [p * (chunk // 2) for p in places(core)]
-    )
+    offs = jnp.stack([dp * k_half, (1 - dp) * k_half, dp * chunk, (1 - dp) * chunk])
 
     capacity = 4 * rows // experts
 
@@ -1490,51 +1487,45 @@
             hidden, grad = squeeze(hidden), squeeze(grad)
             weight = jnp.sum(select.astype(F32) * weight.reshape(-1, 1, rows), -1).reshape(-1, 1)
         made, dx, *grads = run_ffn(
-            hidden, grad, weight, ein_parts, eout_parts, expert_offs, grads=grads, us=41
+            hidden, grad, weight, ein_parts, eout_parts, offs, grads=grads, us=41
         )
         if capacity < rows:
             made, dx = spread(made), spread(dx)
         return made, dx, *grads
 
     made0, dx0, *g_expert = expert_pass(0, None)
-    dx0, routed0 = scatter_xor(dx0), scatter_xor(made0)
     shared, dx_shared, *g_shared = run_ffn(
-        nf_both.reshape(-1, width), cot, None, sin_parts, sout_parts, shared_offs, us=23
-    )
-    gres0, pay0, gg0, gbf0 = run_mid(dx_shared, dx0, res[0], gain_ffn, cotangent[0], mat_out, groups)
-    grad0 = lax.all_to_all(pay0, "context", 0, 0, tiled=True)
-    made1, dx1, *g_expert = expert_pass(1, g_expert, (pay0, routed0))
-    masks = bits_of(experts)
-    for mask in reversed(masks[2:]):
-        half = dx1.shape[0] // 2
-        dx1 = (dx1[:half].astype(F32) + exchange(dx1[half:], "expert", mask).astype(F32)).astype(BF)
+        nf_both.reshape(-1, width), cot, None, sin_parts, sout_parts, offs, us=23
+    )
+    made1, dx1, *g_expert = expert_pass(1, g_expert, dx_shared)
+    dx0, dx1, made0, made1 = [scatter_rest(v).reshape(4, rows, width) for v in (dx0, dx1, made0, made1)]
 
     spread = [(j, k) for j in range(3) for k in range(PIECES)]
     early = [(j, k, "xz" if i < EARLY else "x") for i, (j, k) in enumerate(spread)]
     first = spread[EARLY][0]
     late = [(j - first, k, "z") for j, k in spread[EARLY:]]
-    attention = (*recvs, grad0, *mixed, *lses, key_col, query_row)
-    own_sums, (r_gate, r_up, r_sout), (d0, d1, gres1, gbf1, gg1) = run_back(
+    attention = (*recvs, *mixed, *lses, key_col, query_row)
+    own_sums, (r_gate, r_up, r_sout), (d0, d1, gres, gbf, gg) = run_back(
         g_expert,
         early,
         g_shared,
         attention,
-        (dx_shared, res[1], gain_ffn, cotangent[0], mat_out),
-        dx1.reshape(4, rows, width),
+        (dx_shared, *res, gain_ffn, cotangent[0], mat_out),
+        (dx0, dx1),
         groups,
     )
-    routed1 = scatter_xor(made1)
+    own_late, (r_qk, r_v, r_out), grad_input, gain_sum, routed = run_last(
+        own_sums[first:],
+        late,
+        (d0, d1, x, gain_attn, mat_qkv, table, gres, gbf, gg, *att),
+        (made0, made1),
+        groups,
+    )
     output = jnp.stack(
         [
-            (res[m] + shared[m * rows : (m + 1) * rows].astype(F32) + r.astype(F32)).astype(BF)
-            for m, r in enumerate((routed0, routed1))
+            (res[m] + shared[m * rows : (m + 1) * rows].astype(F32) + routed[m].astype(F32)).astype(BF)
+            for m in range(MICRO)
         ]
-    )
-    own_late, (r_qk, r_v, r_out), grad_input, gain_sum = run_last(
-        own_sums[first:],
-        late,
-        (d0, d1, x, gain_attn, mat_qkv, cosines, sines, gres0, gres1, *att, gbf0, gbf1, gg0, gg1),
-        groups,
     )
     r_gain_ffn = pick(rest_sum(gain_sum)[0], 2, dp)
     r_qkv = jnp.concatenate([r_qk, r_v], 1)

time: 629 us -> 578 us (0.919)
  local copies, waits for them, and re-layouts: 28.1 us -> 10.9 us
  Pallas kernels: 546 us -> 537 us
  other arithmetic: 28.7 us -> 20.2 us
  starting transfers between devices: 8.16 us -> 0 us
  waiting for transfers between devices: 8.06 us -> 0 us
    pallas_call x1, Pallas kernels: 155 us -> 140 us  [run_front(): pl.pallas_call(functools.partial(front_kernel, heads=heads, groups=groups...]
    pallas_call x2, Pallas kernels: 279 us -> 290 us  [device_call(): pl.pallas_call(kernel, out_shape=tuple(outs), in_specs=[pl.BlockSpec(memo...]
    ppermute x6 -> x0, waiting for transfers between devices: 8.06 us -> none  [exchange(): return lax.ppermute(value, axis, [(i, i ^ mask) for i in range(size)])]
    slice x6 -> x0, local copies, waits for them, and re-layouts: 7.24 us -> none  [scatter_xor(): got = exchange(value[half:], 'expert', mask)]
    squeeze x3 -> x0, local copies, waits for them, and re-layouts: 6.97 us -> none  [the longest x1 3.89 us: body(): ein_parts = (w_expert_in[0], ein_parts[0], ein_parts[1])]
  transfers between devices with their start and end apart: 7 -> 0, of which waited for: 2 -> 0; matrix products, arithmetic and copies ran while one was open for 6% -> 0% of each run, Pallas kernels for 56% -> 0%
where the time goes in v4:
time: 578 us; the launch traced here: 570 us
  Pallas kernels  537 us (93%)
  other arithmetic  20.2 us (3%)
  local copies, waits for them, and re-layouts  10.9 us (2%)
    pallas_call x2, Pallas kernels, device_call(): pl.pallas_call(kernel, out_shape=tuple(outs), in_specs=[pl.BlockSpec(memo...  290 us
    pallas_call x1, Pallas kernels, run_front(): pl.pallas_call(functools.partial(front_kernel, heads=heads, groups=groups...  140 us
    pallas_call x3, Pallas kernels, run_ffn(): pl.pallas_call(functools.partial(ffn_kernel, tr=math.gcd(tr, rows), spans...  107 us

profile of v4, /device:TPU:0, one launch (start us, length us, event | category | flops | bytes accessed | tf_op | source)
XLA Modules:
  0.0 569.5 jit_solution(12187873214958975248)
XLA Ops:
  0.7 0.8 compare_select_fusion
  1.4 0.6 broadcast_in_dim.34.refs_2_
  2.0 0.7 select_reduce_fusion
  2.7 0.6 copy.37.refs_3_
  3.4 0.7 stack.38
  4.0 0.7 stack.39
  4.7 0.6 maximum_convert_fusion.2.refs_1_
  5.3 139.5 %shard_map.213 = (bf16[4,9,128,128]{3,2,1,0:T(8,128)(2,1)}, bf16[4,9,128,128]{3,2,1,0:T(8,128)(2,1)}, bf16[4,3,128,128]{3,2,1,0:T(8,128)(2,1)}, bf16[4,3,128,128...) custom-call(bf16[2,256,768]{2,1,0:T(8,128)(2,1)} %bitcast.112, ...), custom_call_target="tpu_custom_call" | custom-call | flops 149500002304 | tf_op jit(solution)/shard_map/pallas_call | solution.py:506
  144.9 0.7 dynamic-slice_bitcast_fusion
  145.6 1.0 copy.38.refs_3_
  146.6 0.6 pad_add_fusion.1.refs_0_
  147.2 42.0 %shard_map.215 = (bf16[1024,768]{1,0:T(8,128)(2,1)}, bf16[1024,768]{1,0:T(8,128)(2,1)}, bf16[768,2048]{1,0:T(8,128)(2,1)}, bf16[768,2048]{1,0:T(8,128)(2,1)}, bf16[2048,768]{1,0:T(8,128)(2,1)}) custom-call(s32[4]{0:T(128)} %pad_add_fusion.1.refs_0_, bf16[1024,768]{1,0:T(8,128)(2,1)} %bitcast.132, bf16[1024,768]{1,0:T(8,128)(2,1)} %bitcast.133, ...), custom_call_target="tpu_custom_call" | custom-call | flops 47149998080 | tf_op jit(solution)/shard_map/pallas_call | solution.py:632
  189.2 22.8 %shard_map.214 = (bf16[512,768]{1,0:T(8,128)(2,1)}, bf16[512,768]{1,0:T(8,128)(2,1)}, bf16[768,2048]{1,0:T(8,128)(2,1)}, bf16[768,2048]{1,0:T(8,128)(2,1)}, bf16[2048,768]{1,0:T(8,128)(2,1)}) custom-call(s32[4]{0:T(128)} %pad_add_fusion.1.refs_0_, bf16[512,768]{1,0:T(8,128)(2,1)} %bitcast.138, bf16[512,768]{1,0:T(8,128)(2,1)} %bitcast.110, ...), custom_call_target="tpu_custom_call" | custom-call | flops 26449999872 | tf_op jit(solution)/shard_map/pallas_call | solution.py:632
  212.0 1.0 copy.39.refs_3_
  213.0 0.0 copy-start.14
  213.0 0.0 copy-start.15
  213.0 42.7 %shard_map.216 = (bf16[1024,768]{1,0:T(8,128)(2,1)}, bf16[1024,768]{1,0:T(8,128)(2,1)}, bf16[768,2048]{1,0:T(8,128)(2,1)}, bf16[768,2048]{1,0:T(8,128)(2,1)}, bf16[2048,768]{1,0:T(8,128)(2,1)}) custom-call(s32[4]{0:T(128)} %pad_add_fusion.1.refs_0_, bf16[1024,768]{1,0:T(8,128)(2,1)} %bitcast.129, bf16[1024,768]{1,0:T(8,128)(2,1)} %bitcast.130, ...), custom_call_target="tpu_custom_call" | custom-call | flops 47149998080 | tf_op jit(solution)/shard_map/pallas_call | solution.py:632
  255.7 0.0 copy-done.14
  255.8 1.9 reshape_squeeze.32.refs_12_
  257.6 0.6 copy.41
  258.2 0.0 copy-done.15
  258.2 0.6 fusion.7
  258.8 183.0 %shard_map.217 = (bf16[4,96,2048]{2,1,0:T(8,128)(2,1)}, bf16[4,96,2048]{2,1,0:T(8,128)(2,1)}, bf16[4,256,768]{2,1,0:T(8,128)(2,1)}, bf16[2,2,96,2048]{3,2,1,0:T(...) custom-call(bf16[2,4,96,2048]{3,2,1,0:T(8,128)(2,1)} %bitcast.125, ...), custom_call_target="tpu_custom_call" | custom-call | flops 189750001664 | tf_op jit(solution)/shard_map/pallas_call | solution.py:1196
  441.9 0.0 copy-start.3
  441.9 107.0 %shard_map.218 = (bf16[4,96,2048]{2,1,0:T(8,128)(2,1)}, bf16[4,256,768]{2,1,0:T(8,128)(2,1)}, bf16[2,2,96,1152]{3,2,1,0:T(8,128)(2,1)}, bf16[2,2,96,1152]{3,2,1,...) custom-call(bf16[4,96,2048]{2,1,0:T(8,128)(2,1)} %get-tuple-element., ...), custom_call_target="tpu_custom_call", output_to_operand_aliasing={{0}: (0, {}), {1}: (1, {})} | custom-call | flops 103499997184 | tf_op jit(solution)/shard_map/pallas_call | solution.py:1196
  548.9 0.0 copy-done.3
  548.9 0.0 copy-start.1
  548.9 0.0 copy-start.2
  548.9 5.0 fusion
  553.9 0.0 copy-done.1
  553.9 0.0 copy-done.2
  553.9 0.0 copy-start
  553.9 0.0 copy-start.7
  553.9 0.0 copy-start.8
  554.0 3.5 maximum_convert_fusion
  557.4 0.0 copy-done
  557.4 0.0 copy-done.7
  557.4 0.0 copy-done.8
  557.4 0.0 copy-start.16
  557.4 0.0 copy-start.6
  557.5 2.2 multiply_reduce_fusion
  559.7 0.0 copy-start.9
  559.7 0.0 copy-start.10
  559.7 0.0 copy-start.11
  559.7 0.0 copy-start.12
  559.7 0.0 copy-done.16
  559.7 0.6 convert_divide_fusion
  560.3 0.0 copy-done.6
  560.3 1.9 bitcast_convert_fusion
  562.2 0.0 copy-done.9
  562.2 0.0 copy-done.10
  562.2 0.0 copy-done.11
  562.2 0.0 copy-done.12
  562.2 0.0 copy-start.5
  562.2 0.2 fusion.3
  562.5 0.9 maximum_bitcast_fusion.1
  563.4 0.0 copy-done.13
  563.4 1.1 bitcast_convert_fusion.2
  564.6 0.7 slice.43
  565.3 0.6 dynamic-slice_reduce_fusion
  565.9 0.0 copy-done.5
  565.9 2.0 bitcast_convert_fusion.1
  567.9 0.0 copy-done.4
  567.9 1.1 copy.49
  (8 shorter events, 0.0 us)
Async XLA Ops:
  213.0 42.7 %copy-start.14 = (s32[4,2,2,1,256]{4,3,2,1,0:T(1,128)S(1)}, s32[4,2,2,1,256]{4,3,2,1,0:T(1,128)}, u32[]{:S(2)}) copy-start(s32[4,2,2,1,256]{4,3,2,1,0:T(1,128)} %get-tuple-element.99) | copy-start | bytes 49156
  213.0 45.2 %copy-start.15 = (f32[2,2,384]{2,1,0:T(2,128)S(1)}, f32[2,2,384]{2,1,0:T(2,128)}, u32[]{:S(2)}) copy-start(f32[2,2,384]{2,1,0:T(2,128)} %get-tuple-element.101) | copy-start | bytes 18436
  441.9 107.0 %copy-start.3 = (bf16[4,96,2048]{2,1,0:T(8,128)(2,1)S(1)}, bf16[4,96,2048]{2,1,0:T(8,128)(2,1)}, u32[]{:S(2)}) copy-start(bf16[4,96,2048]{2,1,0:T(8,128)(2,1)} %get-tuple-element.127) | copy-start | bytes 4718596
  548.9 5.1 copy-start.1
  548.9 5.0 copy-start.2
  553.9 3.5 copy-start
  553.9 3.5 copy-start.7
  553.9 3.5 copy-start.8
  557.4 2.3 copy-start.16
  557.4 2.9 copy-start.6
  559.7 2.5 copy-start.9
  559.7 2.5 copy-start.10
  559.7 2.5 copy-start.11
  559.7 2.5 copy-start.12
  562.2 1.2 copy-start.13
  562.2 3.7 copy-start.5
  563.4 4.5 copy-start.4

commit v5 on v4

--- a/solution.py
+++ b/solution.py
@@ -91,6 +91,14 @@
                 store[h, base + HALF : base + TILE] = second
 
 
+def column(row):
+    return jnp.broadcast_to(row, (8, row.shape[1])).T[:, :1]
+
+
+def gain_row(gains, which):
+    return jnp.concatenate([gains[0, which : which + 1], gains[1, which : which + 1]], 1)
+
+
 def masked_rows(ref, index, kind_head):
     tile = ref[index, kind_head].astype(F32)
     both = jnp.concatenate([tile, pltpu.roll(tile, HEAD, 1)], 0)
@@ -104,7 +112,7 @@
 def attend_step(step, micro, heads, groups, recv, tags, out_ref, lse_ref, ks, vs, scores):
     count = groups * micro + jnp.minimum(step + 2, groups)
     queries = [masked_rows(recv, step, h).astype(BF) for h in range(heads)]
-    tag = jnp.broadcast_to(tags[step, 0, micro], (8, TILE)).T[:, :1]
+    tag = column(tags[step, 0, micro])
     same = lax.broadcasted_iota(jnp.int32, (TILE, TILE), 0) == lax.broadcasted_iota(
         jnp.int32, (TILE, TILE), 1
     )
@@ -162,13 +170,13 @@
     acc[...] = jnp.zeros_like(acc)
 
 
-def back_tile(micro, step, j, heads, groups, lse, key_tag, query_tag, ks, vs, dk, dv, qs, gs, deltas, acc):
+def back_tile(micro, step, j, heads, groups, lse, tags, ks, vs, dk, dv, qs, gs, deltas, acc):
     keys = pl.ds(pl.multiple_of(j * TILE, TILE), TILE)
     same = lax.broadcasted_iota(jnp.int32, (TILE, TILE), 0) == lax.broadcasted_iota(
         jnp.int32, (TILE, TILE), 1
     )
-    tag = query_tag[groups * micro + step]
-    seen = (key_tag[keys, :] <= tag) | (same & (j == groups * micro + step))
+    key_tag = column(tags[j % groups, 1, j // groups])
+    seen = (key_tag <= tags[step, 0, micro]) | (same & (j == groups * micro + step))
     for h in range(heads):
         key, value = ks[h, keys, :], vs[h, keys, :]
         scores = dot(key, qs[h], NT)
@@ -210,6 +218,14 @@
     pl.semaphore_wait(barrier, len(targets))
 
 
+def project_out(got, tokens, w_ref, gain, att, res, nf, heads):
+    for pair in range(tokens.shape[1] // HALF):
+        att[:, pair * HALF : (pair + 1) * HALF] = natural(got, 0, pair, heads).astype(BF)
+    residual = tokens.astype(F32) + dot(att[...], w_ref[...])
+    res[...] = residual
+    nf[...] = (residual * rms_scale(residual) * gain).astype(BF)
+
+
 class Trade:
     def __init__(self, src, dst, sems, local):
         self.src, self.dst, self.sems, self.local = src, dst, sems, local
@@ -255,14 +271,14 @@
 def front_kernel(*refs, heads, groups):
     refs = list(refs)
     take = lambda n: [refs.pop(0) for _ in range(n)]
-    x_ref, gains_in, tags_in, gates_in = take(4)
+    x_ref, gains_in, blocks, keeps, gates_in = take(5)
     w_qkv, w_out, w_ein, w_eout, w_sin, w_sout, cot = take(7)
-    recv_out, mixed_out, lse_out, att_out, res_out = take(2), take(2), take(2), take(2), take(2)
-    rows_out, cot_out, gates_out, both_out, tags_out = take(2), take(2), take(1)[0], take(1)[0], take(1)[0]
+    recv_out, mixed_out, lse_out, cot_out = take(2), take(2), take(2), take(2)
+    att_out, res_out, rows_out, got_out, gates_out, tags_out = take(6)
     qkv_out, wout_out, ein_out, eout_out, sin_out, sout_out, gains_out, table_out = take(8)
     wq, wo, gains, tags, pay, recv, ks, vs, scores, mixed, got, lse, att, res, nf, table = take(16)
     s_qkv, s_out, s_gain, s_exp, s_tag, s_gate, s_cot, s_pay, s_mix, s_row = [take(2) for _ in range(10)]
-    local, self_pay, self_mix, self_tag, stores = take(5)
+    local, self_pay, self_mix, stores = take(4)
     e, z, d = lax.axis_index("expert"), lax.axis_index("context"), lax.axis_index("dp")
     core, y = e % 2, e // 2 % 2
     to_x, to_core, to_y = {"dp": 1 - d}, {"expert": e + 1 - 2 * core}, {"expert": e + 2 - 4 * y}
@@ -298,11 +314,11 @@
     ]
     for copy in (x_qkv, x_gain, x_out, x_exp[0], x_exp[2], x_exp[3], x_exp[1]):
         copy.start()
-    tag_trade = [
-        remote(tags_in, tags.at[z], s_tag, k, others[k]) for k in range(groups - 1)
-    ]
-    tag_own = pltpu.make_async_copy(tags_in, tags.at[z], self_tag.at[0])
-    tag_own.start()
+    for m in range(MICRO):
+        block = blocks[0, m : m + 1, :] + 8 * m
+        tags[z, 0, m] = block
+        tags[z, 1, m] = jnp.where(keeps[0, m : m + 1, :] == 1, block, HIDDEN)
+    tag_trade = [remote(tags.at[z], tags.at[z], s_tag, k, others[k]) for k in range(groups - 1)]
     for copy in tag_trade:
         copy.start()
     own_copies = [
@@ -341,7 +357,7 @@
     c_qkv.start()
     x_gain.wait_recv()
     c_qkv.wait_recv()
-    both = [jnp.concatenate([gains[0, k : k + 1], gains[1, k : k + 1]], 1) for k in range(2)]
+    both = [gain_row(gains, k) for k in range(2)]
     w_full = wq.reshape(width, 3 * width)
     trades, returns = [], []
     for m in range(MICRO):
@@ -355,8 +371,8 @@
     for copy in c_cot[:MICRO]:
         copy.start()
     for k in range(groups - 1):
-        remote(tags_in, tags.at[(z + groups - 1 - k) % groups], s_tag, k, others[k]).wait_recv()
-    tag_own.wait()
+        source = (z + groups - 1 - k) % groups
+        remote(tags.at[z], tags.at[source], s_tag, k, others[k]).wait_recv()
 
     def attend(m, first, last):
         trade = Trade(mixed.at[m], got.at[m], [s.at[m] for s in s_mix], self_mix.at[m])
@@ -369,19 +385,9 @@
         lax.fori_loop(first, last, one, 0)
         return trade
 
-    def post(m, trade):
-        trade.collect()
-        for pair in range(width // HALF):
-            att[m, :, pair * HALF : (pair + 1) * HALF] = natural(got.at[m], 0, pair, heads).astype(BF)
-        residual = x_ref[m].astype(F32) + dot(att[m], wo.reshape(width, width)[...])
-        res[m] = residual
-        nf[m] = (residual * rms_scale(residual) * both[1]).astype(BF)
-        remote(nf.at[m], rows_out[m].at[1], s_row, 3 * m, to_y).start()
-        remote(nf.at[m], rows_out[m].at[2], s_row, 3 * m + 1, to_core).start()
-
-    def forward_row(m):
-        remote(nf.at[m], rows_out[m].at[1], s_row, 3 * m, to_y).wait_recv()
-        remote(rows_out[m].at[1], rows_out[m].at[3], s_row, 3 * m + 2, to_core).start()
+    row_y = remote(nf, rows_out.at[1], s_row, 0, to_y)
+    row_core = remote(nf, rows_out.at[2], s_row, 1, to_core)
+    row_next = remote(rows_out.at[1], rows_out.at[3], s_row, 2, to_core)
 
     trades[0].collect()
     fill_keys(recv.at[0], 0, ks, vs, heads)
@@ -402,36 +408,34 @@
         n_exp[k - 1].start()
     back1 = attend(1, 0, 2)
     c_out.wait_recv()
-    post(0, back0)
+    back0.collect()
+    project_out(got.at[0], x_ref[0], wo.reshape(width, width), both[1], att, res, nf, heads)
+    row_y.start()
+    row_core.start()
     back1 = attend(1, 2, groups)
-    forward_row(0)
+    row_y.wait_recv()
+    row_next.start()
     for k in (1, 2):
         n_exp[k].wait_recv()
         n_exp[k + 2].start()
-    post(1, back1)
     keep = []
     for m in range(MICRO):
-        keep += [
-            (recv.at[m], recv_out[m]),
-            (mixed.at[m], mixed_out[m]),
-            (lse.at[m], lse_out[m]),
-            (att.at[m], att_out[m]),
-            (res.at[m], res_out[m]),
-            (nf.at[m], rows_out[m].at[0]),
-            (nf.at[m], both_out.at[m]),
-        ]
+        keep += [(recv.at[m], recv_out[m]), (mixed.at[m], mixed_out[m]), (lse.at[m], lse_out[m])]
+    keep += [(att, att_out), (res, res_out), (nf, rows_out.at[0])]
     keep += [(tags, tags_out), (wq, qkv_out), (wo, wout_out), (gains, gains_out), (table, table_out)]
     keep = [pltpu.make_async_copy(a, b, stores.at[3 + i]) for i, (a, b) in enumerate(keep)]
     for copy in keep:
         copy.start()
-    forward_row(1)
-    for copy in (*keep, *own_copies):
+    back1.collect()
+    got_copy = pltpu.make_async_copy(got.at[1], got_out, stores.at[3 + len(keep)])
+    got_copy.start()
+    for copy in (*keep, got_copy, *own_copies):
         copy.wait()
     for m in range(MICRO):
-        remote(nf.at[m], rows_out[m].at[2], s_row, 3 * m + 1, to_core).wait()
-        remote(rows_out[m].at[1], rows_out[m].at[3], s_row, 3 * m + 2, to_core).wait()
-        remote(nf.at[m], rows_out[m].at[1], s_row, 3 * m, to_y).wait_send()
         trades[m].release()
+    row_y.wait_send()
+    row_core.wait()
+    row_next.wait()
     back0.release()
     back1.release()
     x_exp[1].wait_recv()
@@ -445,10 +449,11 @@
         copy.wait_send()
 
 
-def run_front(x, gains, tags, gates, w_qkv, w_out, w_ein, w_eout, w_sin, w_sout, cot, groups):
+def run_front(x, gains, blocks, keeps, gates, w_qkv, w_out, w_ein, w_eout, w_sin, w_sout, cot, groups):
     _, rows, width = x.shape
     heads = width // HEAD // groups
     k = width // 4
+    tags = (groups, 2, MICRO, 1, rows)
     w_qkv = w_qkv.reshape(2, k, 3 * width)
     w_out = w_out.reshape(2, k, width)
     w_ein = w_ein.reshape(2, -1, w_ein.shape[1])
@@ -462,14 +467,14 @@
         twice(packed(3), BF)
         + twice(packed(1), BF)
         + twice((groups, 8, TILE), F32)
-        + twice((rows, width), BF)
-        + twice((rows, width), F32)
-        + twice((4, rows, width), BF)
         + twice((4, rows, width), BF)
         + [
+            struct((rows, width), BF),
+            struct((rows, width), F32),
+            struct((4, rows, width), BF),
+            struct(packed(1), BF),
             struct((4, *gates.shape), F32),
-            struct((MICRO, rows, width), BF),
-            struct((groups, *tags.shape), jnp.int32),
+            struct(tags, jnp.int32),
             struct((2, 2, k, 3 * width), BF),
             struct((2, 2, k, width), BF),
             struct(w_ein.shape, BF),
@@ -486,7 +491,7 @@
         v((2, 2, k, 3 * width), BF),
         v((2, 2, k, width), BF),
         v((2, *gains.shape), F32),
-        v((groups, *tags.shape), jnp.int32),
+        v(tags, jnp.int32),
         v((MICRO, *packed(3)), BF),
         v((MICRO, *packed(3)), BF),
         v((heads, held, HALF), BF),
@@ -495,63 +500,72 @@
         v((MICRO, *packed(1)), BF),
         v((MICRO, *packed(1)), BF),
         v((MICRO, groups, 8, TILE), F32),
-        v((MICRO, rows, width), BF),
-        v((MICRO, rows, width), F32),
-        v((MICRO, rows, width), BF),
+        v((rows, width), BF),
+        v((rows, width), F32),
+        v((rows, width), BF),
         v((2, MICRO * rows, HALF), F32),
     ]
-    for shape in ((2,), (2,), (1,), (9,), (groups - 1,), (3,), (6,), (MICRO, groups), (MICRO, groups), (6,)):
+    for shape in ((2,), (2,), (1,), (9,), (groups - 1,), (3,), (6,), (MICRO, groups), (MICRO, groups), (3,)):
         scratch += [dma(*shape), dma(*shape)]
-    scratch += [dma(3), dma(MICRO), dma(MICRO), dma(1), dma(3 + 7 * MICRO + 5)]
+    scratch += [dma(3), dma(MICRO), dma(MICRO), dma(3 + 3 * MICRO + 9)]
     return pl.pallas_call(
         functools.partial(front_kernel, heads=heads, groups=groups),
         out_shape=tuple(outs),
-        in_specs=[vmem] * 4 + [anywhere] * 7,
+        in_specs=[vmem] * 5 + [anywhere] * 7,
         out_specs=(anywhere,) * len(outs),
         scratch_shapes=scratch,
         compiler_params=pltpu.CompilerParams(
             vmem_limit_bytes=VMEM_LIMIT, collective_id=3, has_side_effects=True
         ),
         cost_estimate=price(130),
-    )(x, gains, tags, gates, w_qkv, w_out, w_ein, w_eout, w_sin, w_sout, cot)
-
-
-def ffn_kernel(*refs, tr, spans, counts, first, gated, opened, summed, closing):
-    offs = refs[0]
-    refs = list(refs[1:])
+    )(x, gains, blocks, keeps, gates, w_qkv, w_out, w_ein, w_eout, w_sin, w_sout, cot)
+
+
+def ffn_kernel(*refs, tr, halves, gated, micro, summed, guest, guest_counts):
+    refs = list(refs)
     take = lambda n: [refs.pop(0) for _ in range(n)]
     x_ref, dy_in = take(2)
-    gate_ref = take(1)[0] if gated else None
-    parts = len(spans)
-    wg_parts, wu_parts, wo_parts = take(parts), take(parts), take(len(counts))
-    y0, dx0 = take(2) if opened else (None, None)
+    gate_in = take(1)[0] if gated else None
+    wg_parts, wu_parts, wo_parts = take(2), take(2), take(2)
     g0 = take(3) if summed else None
+    guest_in = take(guest_counts[0])
     y_ref, dx_ref, dwg_ref, dwu_ref, dwo_ref = take(5)
+    guest_out = take(guest_counts[1])
     xt, yacc, dxacc, hs, djg, dju, wg_ref, wu_ref, wo_ref = take(9)
-    dy_ref = take(1)[0] if gated else dy_in
+    dy_ref, gate_ref = take(2) if gated else (dy_in, None)
     f = pl.program_id(0)
+    last = pl.num_programs(0) - 1
     rows = x_ref.shape[0]
+    span = wg_parts[0].shape[0]
+    dp = lax.axis_index("dp")
+    visits = guest(guest_in, guest_out, refs) if guest else {}
 
     @pl.when(f == 0)
     def _():
+        if 0 in visits:
+            visits[0]()
         xt[...] = x_ref[...].T
-        if opened:
-            yacc[...] = y0[...].astype(F32)
-            dxacc[...] = dx0[...].astype(F32)
-        else:
-            yacc[...] = jnp.zeros_like(yacc)
-            dxacc[...] = jnp.zeros_like(dxacc)
+        yacc[...] = jnp.zeros_like(yacc)
+        dxacc[...] = jnp.zeros_like(dxacc)
         if gated:
+            if micro is None:
+                gate_ref[...] = gate_in[...]
+            else:
+                for block in range(gate_in.shape[0]):
+                    row = gate_in[block, lax.axis_index("expert"), micro : micro + 1, :]
+                    gate_ref[block * TILE : (block + 1) * TILE, :] = column(row)
             dy_ref[...] = (dy_in[...].astype(F32) * gate_ref[...]).astype(BF)
 
-    for index, span in enumerate(spans):
-        place = pl.ds(pl.multiple_of(offs[index], HALF // 2), span)
+    for step, visit in visits.items():
+        if step not in (0, "end"):
+            pl.when(f == step)(visit)
+
+    for index, part in enumerate((dp, 1 - dp)):
+        place = pl.ds(pl.multiple_of(part * span, HALF // 2), span)
         wg_ref[place, :] = wg_parts[index][...]
         wu_ref[place, :] = wu_parts[index][...]
-    for index, count in enumerate(counts):
-        begin = offs[parts + index]
-
-        @pl.when((f + first >= begin) & (f + first < begin + count))
+
+        @pl.when(f // halves == part)
         def _(index=index):
             wo_ref[...] = wo_parts[index][...]
 
@@ -583,92 +597,128 @@
             value = value + g0[k][...].astype(F32)
         out[...] = value.astype(BF)
 
-    @pl.when(f == pl.num_programs(0) - 1)
+    @pl.when(f == last)
     def _():
         made = yacc[...].astype(BF)
-        if gated and closing:
+        if gated:
             made = (made.astype(F32) * gate_ref[...]).astype(BF)
         y_ref[...] = made
         dx_ref[...] = dxacc[...].astype(BF)
-
-
-def run_ffn(x, dy, gate, w_in, w_out, offsets, start=None, grads=None, span=None, closing=True, tr=512, fb=FB, us=10):
+        if "end" in visits:
+            visits["end"]()
+
+
+def run_ffn(x, dy, gate, w_in, w_out, grads=None, tr=512, fb=FB, us=10, guest=None):
     rows, d = x.shape
     ff = sum(w.shape[0] for w in w_out)
     nf = ff // fb
-    first, last = span or (0, nf)
-    steps = last - first
+    halves = nf // 2
     gated = gate is not None
-    parts = len(w_in)
-    spans = [w.shape[0] for w in w_in]
-    counts = [w.shape[0] // fb for w in w_out]
-    whole = lambda a: pl.BlockSpec(
-        a.shape, lambda f, o: (0,) * a.ndim, pipeline_mode=pl.Buffered(1)
-    )
+    gate, micro = gate if isinstance(gate, tuple) else (gate, None)
+    whole = lambda a: pl.BlockSpec(a.shape, lambda f: (0,) * a.ndim, pipeline_mode=pl.Buffered(1))
     args = [x, dy] + ([gate] if gated else [])
     specs = [whole(a) for a in args]
     args += list(w_in) * 2 + list(w_out)
-    specs += [pl.BlockSpec((n, fb), lambda f, o: (0, f + first)) for n in spans]
-    specs += [pl.BlockSpec((n, fb), lambda f, o: (0, f + first + nf)) for n in spans]
-    for i, c in enumerate(counts):
-        specs.append(
-            pl.BlockSpec(
-                (fb, d), lambda f, o, i=i, c=c: (jnp.clip(f + first - o[parts + i], 0, c - 1), 0)
-            )
-        )
-    if start is not None:
-        args += list(start)
-        specs += [whole(a) for a in start]
-    wide = pl.BlockSpec((d, fb), lambda f, o: (0, f))
-    tall = pl.BlockSpec((fb, d), lambda f, o: (f, 0))
+    span = w_in[0].shape[0]
+    specs += [pl.BlockSpec((span, fb), lambda f: (0, f))] * 2
+    specs += [pl.BlockSpec((span, fb), lambda f: (0, f + nf))] * 2
+    specs += [pl.BlockSpec((fb, d), lambda f: (f % halves, 0))] * 2
+    wide = pl.BlockSpec((d, fb), lambda f: (0, f))
+    tall = pl.BlockSpec((fb, d), lambda f: (f, 0))
     if grads is not None:
         args += list(grads)
-        specs += [
-            pl.BlockSpec((d, fb), lambda f, o: (0, f + first)),
-            pl.BlockSpec((d, fb), lambda f, o: (0, f + first)),
-            pl.BlockSpec((fb, d), lambda f, o: (f + first, 0)),
-        ]
-    full = pl.BlockSpec((rows, d), lambda f, o: (0, 0), pipeline_mode=pl.Buffered(1))
+        specs += [wide, wide, tall]
+    full = pl.BlockSpec((rows, d), lambda f: (0, 0), pipeline_mode=pl.Buffered(1))
+    outs = [
+        struct((rows, d), BF),
+        struct((rows, d), BF),
+        struct((d, ff), BF),
+        struct((d, ff), BF),
+        struct((ff, d), BF),
+    ]
+    out_specs = [full, full, wide, wide, tall]
+    scratch = [
+        pltpu.VMEM((d, rows), BF),
+        pltpu.VMEM((rows, d), F32),
+        pltpu.VMEM((rows, d), F32),
+        pltpu.VMEM((rows, fb), BF),
+        pltpu.VMEM((rows, fb), BF),
+        pltpu.VMEM((rows, fb), BF),
+        pltpu.VMEM((d, fb), BF),
+        pltpu.VMEM((d, fb), BF),
+        pltpu.VMEM((fb, d), BF),
+    ] + ([pltpu.VMEM((rows, d), BF), pltpu.VMEM((rows, 1), F32)] if gated else [])
+    anywhere = pl.BlockSpec(memory_space=pl.ANY)
+    counts, visit, params = (0, 0), None, {}
+    if guest is not None:
+        visit, guest_args, guest_outs, guest_scratch, collective_id = guest
+        args += [a for a, _ in guest_args]
+        specs += [whole(a) if near else anywhere for a, near in guest_args]
+        outs += guest_outs
+        out_specs += [anywhere] * len(guest_outs)
+        scratch += guest_scratch
+        counts = (len(guest_args), len(guest_outs))
+        params = {"collective_id": collective_id, "has_side_effects": True}
     return pl.pallas_call(
         functools.partial(
             ffn_kernel,
             tr=math.gcd(tr, rows),
-            spans=spans,
-            counts=counts,
-            first=first,
+            halves=halves,
             gated=gated,
-            opened=start is not None,
+            micro=micro,
             summed=grads is not None,
-            closing=closing,
+            guest=visit,
+            guest_counts=counts,
         ),
-        out_shape=(
-            struct((rows, d), BF),
-            struct((rows, d), BF),
-            struct((d, steps * fb), BF),
-            struct((d, steps * fb), BF),
-            struct((steps * fb, d), BF),
-        ),
-        grid_spec=pltpu.PrefetchScalarGridSpec(
-            num_scalar_prefetch=1,
-            grid=(steps,),
-            in_specs=specs,
-            out_specs=(full, full, wide, wide, tall),
-            scratch_shapes=[
-                pltpu.VMEM((d, rows), BF),
-                pltpu.VMEM((rows, d), F32),
-                pltpu.VMEM((rows, d), F32),
-                pltpu.VMEM((rows, fb), BF),
-                pltpu.VMEM((rows, fb), BF),
-                pltpu.VMEM((rows, fb), BF),
-                pltpu.VMEM((d, fb), BF),
-                pltpu.VMEM((d, fb), BF),
-                pltpu.VMEM((fb, d), BF),
-            ]
-            + ([pltpu.VMEM((rows, d), BF)] if gated else []),
-        ),
-        compiler_params=pltpu.CompilerParams(vmem_limit_bytes=VMEM_LIMIT),
+        out_shape=tuple(outs),
+        grid=(nf,),
+        in_specs=specs,
+        out_specs=tuple(out_specs),
+        scratch_shapes=scratch,
+        compiler_params=pltpu.CompilerParams(vmem_limit_bytes=VMEM_LIMIT, **params),
         cost_estimate=price(us),
-    )(offsets, *args)
+    )(*args)
+
+
+def rows_guest(ins, outs, bufs, *, heads):
+    got, x_ref, w_ref, gain_ref, first_rows = ins
+    att_out, res_out, rows_out, both_out = outs
+    att, res, nf, sends, recvs, stores = bufs
+    e = lax.axis_index("expert")
+    core, y = e % 2, e // 2 % 2
+    to_core, to_y = {"expert": e + 1 - 2 * core}, {"expert": e + 2 - 4 * y}
+    wires = [
+        remote(nf, rows_out.at[1], (sends, recvs), 0, to_y),
+        remote(nf, rows_out.at[2], (sends, recvs), 1, to_core),
+        remote(rows_out.at[1], rows_out.at[3], (sends, recvs), 2, to_core),
+    ]
+    keep = [
+        (att, att_out),
+        (res, res_out),
+        (nf, rows_out.at[0]),
+        (nf, both_out.at[1]),
+        (first_rows.at[0], both_out.at[0]),
+    ]
+    keep = [pltpu.make_async_copy(a, b, stores.at[i]) for i, (a, b) in enumerate(keep)]
+
+    def begin():
+        meet(pltpu.get_barrier_semaphore(), [to_core, to_y])
+        project_out(got, x_ref[1], w_ref, gain_row(gain_ref, 1), att, res, nf, heads)
+        for copy in (wires[0], wires[1], *keep):
+            copy.start()
+
+    def later():
+        wires[0].wait_recv()
+        wires[2].start()
+
+    def end():
+        wires[0].wait_send()
+        wires[1].wait()
+        wires[2].wait()
+        for copy in keep:
+            copy.wait()
+
+    return {0: begin, 2: later, "end": end}
 
 
 def price(us):
@@ -713,7 +763,7 @@
                 gj[rows, kind * width + pair * HALF : kind * width + (pair + 1) * HALF] = tile.astype(BF)
     tokens = x_ref[...].reshape(MICRO * TILE, width).astype(F32)
     scale = rms_scale(tokens)
-    gain = gain_ref[...]
+    gain = gain_row(gain_ref, 0)
     turned = (tokens * scale * gain).astype(BF).T
     split = gq.shape[-1]
     gq[...] = dot(turned, gj[:, :split]).astype(BF).reshape(gq.shape)
@@ -766,41 +816,55 @@
 
 
 PIECES = 4
-EARLY = 6
+FLIPPED = (1,)
+EARLY = 7
 AHEAD = 2
 PLAN = {
-    -1: ("rs1", "A0", "a0", "rs2", "B0", "A1", "a1", "a2", "A2", "rs3",),
-    3: ("A3", "B1",),
-    8: ("A4",),
-    9: ("b0",),
-    10: ("B2", "C0",),
-    11: ("A5",),
-    12: ("C1",),
-    14: ("B3",),
-    20: ("B4", "C2",),
-    23: ("b1", "B5",),
-    24: ("C3", "c0",),
-    25: ("b2",),
-    26: ("C4",),
-    27: ("d0",),
-    29: ("c1",),
-    32: ("d1", "C5",),
-    33: ("c2",),
-    36: ("d2", "e0",),
-    41: ("e1", "f0",),
-    42: ("D3", "e2", "zhome", "A7", "A9", "g0", "f2", "D5", "D4", "A6", "f1", "D1", "h0", "g2", "A11", "h2", "g1", "D2", "A8", "h1", "A10", "D0",),
+    -1: ("rs1", "a0", "A0", "a1", "rs2", "A1", "a2", "B0", "rs3",),
+    1: ("A2",),
+    3: ("B1",),
+    4: ("C0",),
+    5: ("b1",),
+    6: ("b0",),
+    7: ("A3",),
+    8: ("B2",),
+    9: ("b2", "A4",),
+    10: ("B3",),
+    11: ("C1",),
+    12: ("c0",),
+    13: ("C2",),
+    14: ("c1",),
+    15: ("B4",),
+    16: ("A5",),
+    17: ("d0",),
+    18: ("c2",),
+    19: ("C3",),
+    21: ("d1",),
+    23: ("C4",),
+    24: ("D3",),
+    25: ("A6",),
+    26: ("e0",),
+    27: ("B5",),
+    28: ("e1",),
+    31: ("d2",),
+    34: ("f1",),
+    35: ("C5",),
+    37: ("B6",),
+    38: ("e2",),
+    42: ("f0", "zhome", "C6", "D2", "A7", "g0", "A8", "D5", "f2", "g1", "A9", "D4", "g2", "h0", "h2", "h1", "A11", "D1", "A10", "D6", "D0",),
 }
 LAST_PLAN = (
-    "A0", "A1", "A2", "A3", "B0", "B1", "a0", "C0", "A5", "a1",
-    "B2", "C1", "B3", "b0", "a2", "C2", "b1", "B5", "C3", "c0",
-    "b2", "d0", "c1", "C5", "c2", "D2", "d2", "D0", "e0", "A4",
-    "f0", "d1", "D5", "f1", "zrest", "B4", "g0", "f2", "e1", "e2",
-    "g1", "h0", "D3", "D1", "C4", "g2", "D4", "h1", "h2",
+    "A0", "A1", "A2", "A3", "B0", "a0", "B1", "C0", "a1", "a2",
+    "b0", "B2", "C1", "b2", "D0", "B3", "b1", "C2", "c0", "c2",
+    "d0", "c1", "A4", "C3", "f0", "d2", "d1", "e0", "B4", "f1",
+    "g0", "e1", "f2", "e2", "D3", "zrest", "C4", "D2", "g1", "g2",
+    "D1", "h0", "D4", "h1", "h2",
 )
 
 
 class Engine:
     def __init__(self, own, com, own_buf, com_buf, own_out, com_out, sems):
+        self.flip = [i in FLIPPED for i in range(len(com))]
         self.own, self.com, self.own_buf, self.com_buf = own, com, own_buf, com_buf
         self.own_out, self.com_out = own_out, com_out
         e, z, d = lax.axis_index("expert"), lax.axis_index("context"), lax.axis_index("dp")
@@ -915,6 +979,10 @@
         out = self.com_out[i]
         if stage == "core":
             return remote(self.com[i].at[h, 1 - core], r_core.at[h], self.c["core"], 2 * i + h, self.to_core)
+        if stage == "y" and self.flip[i]:
+            return remote(total.at[1 - d, h], r_y.at[h], self.c["y"], 2 * i + h, self.to_x)
+        if stage == "x" and self.flip[i]:
+            return remote(total.at[d, 1 - y], r_x, self.c["x"], i, self.to_y)
         if stage == "y":
             return remote(total.at[h, 1 - y], r_y.at[h], self.c["y"], 2 * i + h, self.to_y)
         if stage == "x":
@@ -949,7 +1017,10 @@
         total, r_y, y = self.com_buf[i][0], self.com_buf[i][2], self.y
         for h in range(2):
             self.c_wire("y", i, h).wait_recv()
-            total[h, y] = total[h, y] + r_y[h]
+            if self.flip[i]:
+                total[self.d, h] = total[self.d, h] + r_y[h]
+            else:
+                total[h, y] = total[h, y] + r_y[h]
         self.c_wire("x", i).start()
 
     def c_(self, i):
@@ -1067,7 +1138,7 @@
 def back_kernel(*refs, own_at, sources, common, heads, groups):
     refs = Arrays(refs)
     own_in, com_in = refs.take(sources), refs.take(common)
-    recv0, recv1, out0, out1, lse0, lse1, key_tag, query_tag = refs.take(8)
+    recv0, recv1, out0, out1, lse0, lse1, tags = refs.take(7)
     dxs, res0, res1, gain_ref, cot_ref, w_ref = refs.take(6)
     dx_made = refs.take(MICRO)
     own_out, com_out = refs.take(sources), refs.take(common)
@@ -1107,7 +1178,7 @@
         send_y[m].wait_recv()
         grad = dxs[m * TILE : (m + 1) * TILE, :].astype(F32) + dx[m, 0].astype(F32) + r_y[m].astype(F32)
         part = mid_core(
-            grad, res_ref[...], gain_ref[...], cot_ref[m], w_ref, pay_o.at[m], gres.at[m], gbf.at[m], heads
+            grad, res_ref[...], gain_row(gain_ref, 1), cot_ref[m], w_ref, pay_o.at[m], gres.at[m], gbf.at[m], heads
         )
         for dest in range(groups):
             trade_o[m].send(dest)
@@ -1160,7 +1231,7 @@
                             events(slot)
 
                 back_tile(
-                    micro, s, j, heads, groups, lse, key_tag, query_tag, ks, vs, dk, dv, qs, gs, deltas, acc
+                    micro, s, j, heads, groups, lse, tags, ks, vs, dk, dv, qs, gs, deltas, acc
                 )
                 return carry
 
@@ -1405,10 +1476,6 @@
     x = inputs[0]
     cot = cotangent[0].reshape(MICRO * rows, width)
 
-    blocks = block_ids[0] + 8 * jnp.arange(MICRO, dtype=jnp.int32)[:, None]
-    key_tags = jnp.where(keep_flags[0] == 1, blocks, HIDDEN)
-    tags = jnp.stack([blocks, key_tags])[:, :, None]
-
     per_expert = jnp.sum(
         jnp.where(
             expert_ids[0][None] == jnp.arange(experts, dtype=jnp.int32)[:, None, None, None],
@@ -1420,8 +1487,11 @@
     gains = jnp.stack([norm_attn, norm_ffn]).astype(F32)
     (
         *pairs,
+        att0,
+        res0,
+        rows0,
+        got1,
         gates_four,
-        nf_both,
         all_tags,
         mat_qkv,
         mat_out,
@@ -1434,7 +1504,8 @@
     ) = run_front(
         x,
         gains,
-        tags,
+        block_ids,
+        keep_flags,
         per_expert,
         w_qkv,
         w_attn_out,
@@ -1445,39 +1516,29 @@
         cotangent[0],
         groups,
     )
-    recvs, mixed, lses, att, res, rows_four, cot_four = [pairs[2 * i : 2 * i + 2] for i in range(7)]
+    recvs, mixed, lses, cot_four = [pairs[2 * i : 2 * i + 2] for i in range(4)]
     mat_qkv = mat_qkv.reshape(width, -1)
     mat_out = mat_out.reshape(width, width)
-    gain_attn = gains[:, 0].reshape(1, width)
-    gain_ffn = gains[:, 1].reshape(1, width)
-    all_tags = all_tags[:, :, :, 0].transpose(1, 2, 0, 3)
-    query_row = all_tags[0].reshape(MICRO * groups, 1, rows)
-    key_col = all_tags[1].reshape(-1, 1)
-    own_gates = lax.dynamic_index_in_dim(
-        gather_rest(gates_four), lax.axis_index("expert"), 1, False
-    )
-    gate = [own_gates[:, m].reshape(-1, 1) for m in range(MICRO)]
-
     core = lax.axis_index("expert") % 2
     dp = lax.axis_index("dp")
-    k_half, f_half = width // 2, w_shared_out.shape[0]
     whole = lambda w: w.reshape(-1, w.shape[-1])
     ein_parts = (w_expert_in[0], whole(ein_parts))
     eout_parts = (w_expert_out[0], eout_other)
     sin_parts = (w_shared_in, whole(sin_parts))
     sout_parts = (w_shared_out, whole(sout_parts))
-    chunk = f_half // FB
-    offs = jnp.stack([dp * k_half, (1 - dp) * k_half, dp * chunk, (1 - dp) * chunk])
 
     capacity = 4 * rows // experts
 
-    def expert_pass(m, grads, token=None):
-        hidden = gather_rest(rows_four[m]).reshape(-1, width)
+    def expert_pass(m, four, grads, guest=None, token=None):
+        hidden = gather_rest(four).reshape(-1, width)
         if token is not None:
             hidden = after(hidden, token)
-        grad, weight = gather_rest(cot_four[m]).reshape(-1, width), gate[m]
+        grad, weight = gather_rest(cot_four[m]).reshape(-1, width), (gates_four, m)
         if capacity < rows:
-            chosen = weight.reshape(-1, rows) > 0
+            weight = lax.dynamic_index_in_dim(
+                gather_rest(gates_four)[:, :, m], lax.axis_index("expert"), 1, False
+            )
+            chosen = weight > 0
             slots = jnp.cumsum(chosen.astype(jnp.int32), 1) - 1
             select = (
                 chosen[:, None] & (slots[:, None] == jnp.arange(capacity, dtype=jnp.int32)[:, None])
@@ -1486,38 +1547,53 @@
             spread = lambda v: jnp.einsum("bcr,bcd->brd", select, v.reshape(-1, capacity, width)).reshape(-1, width)
             hidden, grad = squeeze(hidden), squeeze(grad)
             weight = jnp.sum(select.astype(F32) * weight.reshape(-1, 1, rows), -1).reshape(-1, 1)
-        made, dx, *grads = run_ffn(
-            hidden, grad, weight, ein_parts, eout_parts, offs, grads=grads, us=41
+        made, dx, *rest = run_ffn(
+            hidden, grad, weight, ein_parts, eout_parts, grads=grads, us=42, guest=guest
         )
         if capacity < rows:
             made, dx = spread(made), spread(dx)
-        return made, dx, *grads
-
-    made0, dx0, *g_expert = expert_pass(0, None)
+        return made, dx, rest[:3], rest[3:]
+
+    heads = width // HEAD // groups
+    buf, dma = pltpu.VMEM, pltpu.SemaphoreType.DMA
+    guest = (
+        functools.partial(rows_guest, heads=heads),
+        ((got1, True), (x, True), (mat_out, True), (gains, True), (rows0, False)),
+        [
+            struct((rows, width), BF),
+            struct((rows, width), F32),
+            struct((4, rows, width), BF),
+            struct((MICRO, rows, width), BF),
+        ],
+        [buf((rows, width), BF), buf((rows, width), F32), buf((rows, width), BF), dma((3,)), dma((3,)), dma((5,))],
+        4,
+    )
+    made0, dx0, g_expert, (att1, res1, rows1, nf_both) = expert_pass(0, rows0, None, guest)
+    att, res = (att0, att1), (res0, res1)
     shared, dx_shared, *g_shared = run_ffn(
-        nf_both.reshape(-1, width), cot, None, sin_parts, sout_parts, offs, us=23
-    )
-    made1, dx1, *g_expert = expert_pass(1, g_expert, dx_shared)
+        nf_both.reshape(-1, width), cot, None, sin_parts, sout_parts, us=23
+    )
+    made1, dx1, g_expert, _ = expert_pass(1, rows1, g_expert, None, dx_shared)
     dx0, dx1, made0, made1 = [scatter_rest(v).reshape(4, rows, width) for v in (dx0, dx1, made0, made1)]
 
     spread = [(j, k) for j in range(3) for k in range(PIECES)]
     early = [(j, k, "xz" if i < EARLY else "x") for i, (j, k) in enumerate(spread)]
     first = spread[EARLY][0]
     late = [(j - first, k, "z") for j, k in spread[EARLY:]]
-    attention = (*recvs, *mixed, *lses, key_col, query_row)
+    attention = (*recvs, *mixed, *lses, all_tags)
     own_sums, (r_gate, r_up, r_sout), (d0, d1, gres, gbf, gg) = run_back(
         g_expert,
         early,
         g_shared,
         attention,
-        (dx_shared, *res, gain_ffn, cotangent[0], mat_out),
+        (dx_shared, *res, gains, cotangent[0], mat_out),
         (dx0, dx1),
         groups,
     )
     own_late, (r_qk, r_v, r_out), grad_input, gain_sum, routed = run_last(
         own_sums[first:],
         late,
-        (d0, d1, x, gain_attn, mat_qkv, table, gres, gbf, gg, *att),
+        (d0, d1, x, gains, mat_qkv, table, gres, gbf, gg, *att),
         (made0, made1),
         groups,
     )

time: 578 us -> 552 us (0.955)
  Pallas kernels: 537 us -> 520 us
  local copies, waits for them, and re-layouts: 10.9 us -> 4.51 us
    pallas_call x1, Pallas kernels: 140 us -> 128 us  [run_front(): pl.pallas_call(functools.partial(front_kernel, heads=heads, groups=groups...]
    pallas_call x2, Pallas kernels: 290 us -> 284 us  [device_call(): pl.pallas_call(kernel, out_shape=tuple(outs), in_specs=[pl.BlockSpec(memo...]
where the time goes in v5:
time: 552 us; the launch traced here: 545 us
  Pallas kernels  520 us (94%)
  other arithmetic  18.9 us (3%)
    pallas_call x2, Pallas kernels, device_call(): pl.pallas_call(kernel, out_shape=tuple(outs), in_specs=[pl.BlockSpec(memo...  284 us
    pallas_call x1, Pallas kernels, run_front(): pl.pallas_call(functools.partial(front_kernel, heads=heads, groups=groups...  128 us
    pallas_call x3, Pallas kernels, run_ffn(): pl.pallas_call(functools.partial(ffn_kernel, tr=math.gcd(tr, rows), halve...  109 us

profile of v5, /device:TPU:0, one launch (start us, length us, event | category | flops | bytes accessed | tf_op | source)
XLA Modules:
  0.0 544.6 jit_solution(109776394813458111)
XLA Ops:
  0.6 0.7 select_reduce_fusion
  1.4 0.6 copy.28.refs_4_
  2.0 0.7 stack.18
  2.6 0.7 stack.19
  3.3 0.6 maximum_convert_fusion.2.refs_1_
  3.9 127.6 %shard_map.213 = (bf16[4,9,128,128]{3,2,1,0:T(8,128)(2,1)}, bf16[4,9,128,128]{3,2,1,0:T(8,128)(2,1)}, bf16[4,3,128,128]{3,2,1,0:T(8,128)(2,1)}, bf16[4,3,128,128...) custom-call(bf16[2,256,768]{2,1,0:T(8,128)(2,1)} %bitcast.90, ...), custom_call_target="tpu_custom_call" | custom-call | flops 149500002304 | tf_op jit(solution)/shard_map/pallas_call | solution.py:511
  131.5 44.4 %shard_map.214 = (bf16[1024,768]{1,0:T(8,128)(2,1)}, bf16[1024,768]{1,0:T(8,128)(2,1)}, bf16[768,2048]{1,0:T(8,128)(2,1)}, bf16[768,2048]{1,0:T(8,128)(2,1)}, bf...) custom-call(bf16[1024,768]{1,0:T(8,128)(2,1)} %bitcast.114, ...), custom_call_target="tpu_custom_call" | custom-call | flops 48299999232 | tf_op jit(solution)/shard_map/pallas_call | solution.py:662
  175.9 22.1 %shard_map.215 = (bf16[512,768]{1,0:T(8,128)(2,1)}, bf16[512,768]{1,0:T(8,128)(2,1)}, bf16[768,2048]{1,0:T(8,128)(2,1)}, bf16[768,2048]{1,0:T(8,128)(2,1)}, bf16[2048,768]{1,0:T(8,128)(2,1)}) custom-call(bf16[512,768]{1,0:T(8,128)(2,1)} %bitcast.118, bf16[512,768]{1,0:T(8,128)(2,1)} %bitcast.88, bf16[384,4096]{1,0:T(8,128)(2,1)} %refs_4_.1, ...), custom_call_target="tpu_custom_call" | custom-call | flops 26449999872 | tf_op jit(solution)/shard_map/pallas_call | solution.py:662
  198.0 42.2 %shard_map.216 = (bf16[1024,768]{1,0:T(8,128)(2,1)}, bf16[1024,768]{1,0:T(8,128)(2,1)}, bf16[768,2048]{1,0:T(8,128)(2,1)}, bf16[768,2048]{1,0:T(8,128)(2,1)}, bf16[2048,768]{1,0:T(8,128)(2,1)}) custom-call(bf16[1024,768]{1,0:T(8,128)(2,1)} %bitcast.115, bf16[1024,768]{1,0:T(8,128)(2,1)} %bitcast.110, f32[4,4,2,256]{3,2,1,0:T(2,128)} %get-tuple-element.74.refs_2_, ...), custom_call_target="tpu_custom_call" | custom-call | flops 48299999232 | tf_op jit(solution)/shard_map/pallas_call | solution.py:662
  240.2 194.0 %shard_map.217 = (bf16[4,96,2048]{2,1,0:T(8,128)(2,1)}, bf16[4,96,2048]{2,1,0:T(8,128)(2,1)}, bf16[4,256,768]{2,1,0:T(8,128)(2,1)}, bf16[2,2,96,2048]{3,2,1,0:T(...) custom-call(bf16[2,4,96,2048]{3,2,1,0:T(8,128)(2,1)} %bitcast.104, ...), custom_call_target="tpu_custom_call" | custom-call | flops 189750001664 | tf_op jit(solution)/shard_map/pallas_call | solution.py:1267
  434.2 0.0 copy-start.3
  434.2 89.7 %shard_map.218 = (bf16[4,96,2048]{2,1,0:T(8,128)(2,1)}, bf16[4,256,768]{2,1,0:T(8,128)(2,1)}, bf16[2,2,96,1152]{3,2,1,0:T(8,128)(2,1)}, bf16[2,2,96,1152]{3,2,1,...) custom-call(bf16[4,96,2048]{2,1,0:T(8,128)(2,1)} %get-tuple-element., ...), custom_call_target="tpu_custom_call", output_to_operand_aliasing={{0}: (0, {}), {1}: (1, {})} | custom-call | flops 103499997184 | tf_op jit(solution)/shard_map/pallas_call | solution.py:1267
  523.9 0.0 copy-done.3
  523.9 0.0 copy-start.1
  524.0 0.0 copy-start.2
  524.0 5.0 fusion
  529.0 0.0 copy-done.1
  529.0 0.0 copy-done.2
  529.0 0.0 copy-start
  529.0 0.0 copy-start.7
  529.0 0.0 copy-start.8
  529.0 3.5 maximum_convert_fusion
  532.5 0.0 copy-done
  532.5 0.0 copy-done.7
  532.5 0.0 copy-done.8
  532.5 0.0 copy-start.14
  532.5 0.0 copy-start.6
  532.5 2.2 multiply_reduce_fusion
  534.8 0.0 copy-start.9
  534.8 0.0 copy-start.10
  534.8 0.0 copy-start.11
  534.8 0.0 copy-start.12
  534.8 0.0 copy-done.14
  534.8 0.6 convert_divide_fusion
  535.4 0.0 copy-done.6
  535.4 1.9 bitcast_convert_fusion
  537.3 0.0 copy-start.13
  537.3 0.0 copy-done.9
  537.3 0.0 copy-done.10
  537.3 0.0 copy-done.11
  537.3 0.0 copy-done.12
  537.3 0.0 copy-start.5
  537.3 0.2 fusion.3
  537.6 0.9 maximum_bitcast_fusion.1
  538.5 0.0 copy-done.13
  538.5 0.0 copy-start.4
  538.5 1.1 bitcast_convert_fusion.2
  539.6 0.7 slice.19
  540.4 0.6 dynamic-slice_reduce_fusion
  541.0 0.0 copy-done.5
  541.0 2.0 bitcast_convert_fusion.1
  543.0 0.0 copy-done.4
  543.0 1.1 copy.32
Async XLA Ops:
  434.2 89.7 %copy-start.3 = (bf16[4,96,2048]{2,1,0:T(8,128)(2,1)S(1)}, bf16[4,96,2048]{2,1,0:T(8,128)(2,1)}, u32[]{:S(2)}) copy-start(bf16[4,96,2048]{2,1,0:T(8,128)(2,1)} %get-tuple-element.129) | copy-start | bytes 4718596
  523.9 5.1 copy-start.1
  524.0 5.0 copy-start.2
  529.0 3.5 copy-start
  529.0 3.5 copy-start.7
  529.0 3.5 copy-start.8
  532.5 2.3 copy-start.14
  532.5 2.9 copy-start.6
  534.8 2.5 copy-start.9
  534.8 2.5 copy-start.10
  534.8 2.5 copy-start.11
  534.8 2.5 copy-start.12
  537.3 1.2 copy-start.13
  537.3 3.7 copy-start.5
  538.5 4.5 copy-start.4

commit v6 on v5

--- a/solution.py
+++ b/solution.py
@@ -721,6 +721,56 @@
     return {0: begin, 2: later, "end": end}
 
 
+def halves_guest(ins, outs, bufs):
+    n = len(ins)
+    totals, cores, gots = bufs[:n], bufs[n : 2 * n], bufs[2 * n : 3 * n]
+    loads, sends, recvs, stores = bufs[3 * n :]
+    e, d = lax.axis_index("expert"), lax.axis_index("dp")
+    core, y = e % 2, e // 2 % 2
+    to_x, to_core, to_y = {"dp": 1 - d}, {"expert": e + 1 - 2 * core}, {"expert": e + 2 - 4 * y}
+    both = [(i, h) for i in range(n) for h in range(2)]
+    sems = (sends, recvs)
+    load = {(i, h): pltpu.make_async_copy(ins[i].at[h, core], totals[i].at[h], loads.at[2 * i + h]) for i, h in both}
+    first = {(i, h): remote(ins[i].at[h, 1 - core], cores[i].at[h], sems, 2 * i + h, to_core) for i, h in both}
+
+    def half(i, h):
+        if i in FLIPPED:
+            return remote(totals[i].at[1 - d, h], gots[i].at[h], sems, 2 * n + 2 * i + h, to_x)
+        return remote(totals[i].at[h, 1 - y], gots[i].at[h], sems, 2 * n + 2 * i + h, to_y)
+
+    store = [pltpu.make_async_copy(gots[i], outs[i], stores.at[i]) for i in range(n)]
+
+    def begin():
+        meet(pltpu.get_barrier_semaphore(), [to_x, to_core, to_y])
+        for key in both:
+            first[key].start()
+            load[key].start()
+
+    def later():
+        for i in range(n):
+            for h in range(2):
+                load[i, h].wait()
+                first[i, h].wait_recv()
+            totals[i][...] = totals[i][...] + cores[i][...]
+            for h in range(2):
+                half(i, h).start()
+
+    def end():
+        for i, h in both:
+            half(i, h).wait_recv()
+            mine = totals[i][d, h] if i in FLIPPED else totals[i][h, y]
+            gots[i][h] = mine + gots[i][h]
+        for copy in store:
+            copy.start()
+        for key in both:
+            first[key].wait_send()
+            half(*key).wait_send()
+        for copy in store:
+            copy.wait()
+
+    return {0: begin, 1: later, "end": end}
+
+
 def price(us):
     return pl.CostEstimate(flops=int(us * 1.15e9), bytes_accessed=0, transcendentals=0)
 
@@ -820,38 +870,28 @@
 EARLY = 7
 AHEAD = 2
 PLAN = {
-    -1: ("rs1", "a0", "A0", "a1", "rs2", "A1", "a2", "B0", "rs3",),
-    1: ("A2",),
-    3: ("B1",),
-    4: ("C0",),
-    5: ("b1",),
-    6: ("b0",),
-    7: ("A3",),
-    8: ("B2",),
-    9: ("b2", "A4",),
-    10: ("B3",),
-    11: ("C1",),
-    12: ("c0",),
-    13: ("C2",),
-    14: ("c1",),
-    15: ("B4",),
+    -1: ("b0", "b1", "b2", "A0", "rs1", "c1", "A1", "B0", "rs2", "c0", "d1", "c2", "C0", "rs3", "B1", "A2",),
+    4: ("e1",),
+    6: ("A3",),
+    7: ("d0",),
+    9: ("A4",),
+    12: ("d2",),
+    15: ("C1",),
     16: ("A5",),
-    17: ("d0",),
-    18: ("c2",),
-    19: ("C3",),
-    21: ("d1",),
-    23: ("C4",),
-    24: ("D3",),
-    25: ("A6",),
-    26: ("e0",),
-    27: ("B5",),
-    28: ("e1",),
-    31: ("d2",),
-    34: ("f1",),
-    35: ("C5",),
+    18: ("B2",),
+    19: ("e0",),
+    20: ("B3",),
+    21: ("e2",),
+    24: ("A6", "f2",),
+    25: ("C2",),
+    27: ("B4",),
+    28: ("f1",),
+    29: ("C3",),
+    32: ("B5",),
+    34: ("C4",),
     37: ("B6",),
-    38: ("e2",),
-    42: ("f0", "zhome", "C6", "D2", "A7", "g0", "A8", "D5", "f2", "g1", "A9", "D4", "g2", "h0", "h2", "h1", "A11", "D1", "A10", "D6", "D0",),
+    39: ("C5", "f0",),
+    42: ("zhome", "A7", "g1", "D5", "A8", "D3", "g2", "D2", "A10", "g0", "h1", "C6", "A9", "h2", "D1", "h0", "A11", "D0", "D4", "D6",),
 }
 LAST_PLAN = (
     "A0", "A1", "A2", "A3", "B0", "a0", "B1", "C0", "a1", "a2",
@@ -863,7 +903,8 @@
 
 
 class Engine:
-    def __init__(self, own, com, own_buf, com_buf, own_out, com_out, sems):
+    def __init__(self, own, com, own_buf, com_buf, own_out, com_out, sems, halved=False):
+        self.halved = halved
         self.flip = [i in FLIPPED for i in range(len(com))]
         self.own, self.com, self.own_buf, self.com_buf = own, com, own_buf, com_buf
         self.own_out, self.com_out = own_out, com_out
@@ -886,7 +927,7 @@
         self.c = {k: take(2) for k in ("core", "y", "x", "1", "2", "3", "fore", "last")}
 
     @staticmethod
-    def scratch(own_shapes, kinds, com_shapes):
+    def scratch(own_shapes, kinds, com_shapes, halved=False):
         v, dma = pltpu.VMEM, lambda n: pltpu.SemaphoreType.DMA((max(n, 1),))
         tiny = (16, HALF)
         own_buf = []
@@ -895,7 +936,11 @@
             own_buf += [v(s if "z" in kind else tiny, BF)] * 2
         com_buf = []
         for s in com_shapes:
-            com_buf += [v((2, 2, *s), BF)] * 2 + [v((2, *s), BF)] + [v(s, BF)] * 3
+            tiny = (16, HALF)
+            if halved:
+                com_buf += [v((2, *s), BF), v(tiny, BF), v(tiny, BF)] + [v(s, BF)] * 3
+            else:
+                com_buf += [v((2, 2, *s), BF)] * 2 + [v((2, *s), BF)] + [v(s, BF)] * 3
         chunks, n = len(own_shapes), len(com_shapes)
         sems = [dma(chunks)] * 10 + [dma(2 * n), dma(n)] + [dma(2 * n)] * 4 + [dma(n)] * 12
         return own_buf, com_buf, sems
@@ -963,7 +1008,15 @@
         def _():
             self.o_wire("3", c).wait_recv()
 
+    def slot(self, i):
+        total = self.com_buf[i][0]
+        if self.halved:
+            return total.at[self.y if self.flip[i] else self.d]
+        return total.at[self.d, self.y]
+
     def c_loading(self, i, h):
+        if self.halved:
+            return pltpu.make_async_copy(self.com[i], self.com_buf[i][0], self.c_load.at[2 * i])
         return pltpu.make_async_copy(
             self.com[i].at[h, self.core], self.com_buf[i][0].at[h], self.c_load.at[2 * i + h]
         )
@@ -981,6 +1034,9 @@
             return remote(self.com[i].at[h, 1 - core], r_core.at[h], self.c["core"], 2 * i + h, self.to_core)
         if stage == "y" and self.flip[i]:
             return remote(total.at[1 - d, h], r_y.at[h], self.c["y"], 2 * i + h, self.to_x)
+        if stage == "x" and self.halved:
+            other, target = (1 - y, self.to_y) if self.flip[i] else (1 - d, self.to_x)
+            return remote(total.at[other], r_x, self.c["x"], i, target)
         if stage == "x" and self.flip[i]:
             return remote(total.at[d, 1 - y], r_x, self.c["x"], i, self.to_y)
         if stage == "y":
@@ -988,9 +1044,9 @@
         if stage == "x":
             return remote(total.at[1 - d, y], r_x, self.c["x"], i, self.to_x)
         if stage == "1":
-            return remote(total.at[d, y], r_1, self.c["1"], i, self.to_mate)
+            return remote(self.slot(i), r_1, self.c["1"], i, self.to_mate)
         if stage == "2":
-            return remote(total.at[d, y], r_2, self.c["2"], i, self.to_mid)
+            return remote(self.slot(i), r_2, self.c["2"], i, self.to_mid)
         if stage == "3":
             return remote(r_1, out.at[core, y], self.c["3"], i, self.to_mate)
         if stage == "fore":
@@ -1000,6 +1056,9 @@
         return remote(out.at[core], out.at[core], self.c["last"], i, self.to_core)
 
     def c_start(self, i):
+        if self.halved:
+            self.c_loading(i, 0).start()
+            return
         for h in range(2):
             self.c_wire("core", i, h).start()
             self.c_loading(i, h).start()
@@ -1015,6 +1074,10 @@
 
     def b(self, i):
         total, r_y, y = self.com_buf[i][0], self.com_buf[i][2], self.y
+        if self.halved:
+            self.c_loading(i, 0).wait()
+            self.c_wire("x", i).start()
+            return
         for h in range(2):
             self.c_wire("y", i, h).wait_recv()
             if self.flip[i]:
@@ -1024,30 +1087,30 @@
         self.c_wire("x", i).start()
 
     def c_(self, i):
-        total, r_x, y, d = self.com_buf[i][0], self.com_buf[i][3], self.y, self.d
+        total, r_x = self.slot(i), self.com_buf[i][3]
         self.c_wire("x", i).wait_recv()
-        total[d, y] = total[d, y] + r_x[...]
+        total[...] = total[...] + r_x[...]
 
         @pl.when(self.outer)
         def _():
             self.c_wire("1", i).start()
 
     def d_(self, i):
-        total, r_1, y, d = self.com_buf[i][0], self.com_buf[i][4], self.y, self.d
+        total, r_1 = self.slot(i), self.com_buf[i][4]
 
         @pl.when(self.inner)
         def _():
             self.c_wire("1", i).wait_recv()
-            total[d, y] = total[d, y] + r_1[...]
+            total[...] = total[...] + r_1[...]
             self.c_wire("2", i).start()
 
     def e(self, i):
-        total, r_1, r_2 = self.com_buf[i][0], self.com_buf[i][4], self.com_buf[i][5]
+        total, r_1, r_2 = self.slot(i), self.com_buf[i][4], self.com_buf[i][5]
 
         @pl.when(self.inner)
         def _():
             self.c_wire("2", i).wait_recv()
-            r_1[...] = total[self.d, self.y] + r_2[...]
+            r_1[...] = total[...] + r_2[...]
             self.c_wire("3", i).start()
             self.c_wire("fore", i).start()
             self.c_storing(i).start()
@@ -1093,7 +1156,7 @@
                 self.o_storing(c).wait()
         chunks = [c for c in chunks if self.own[c][2] != "x"]
         for i in common:
-            for h in range(2):
+            for h in range(0 if self.halved else 2):
                 self.c_wire("core", i, h).wait_send()
                 self.c_wire("y", i, h).wait_send()
             self.c_wire("x", i).wait_send()
@@ -1127,12 +1190,12 @@
         got, self.refs = self.refs[:n], self.refs[n:]
         return got
 
-    def engine(self, own_at, sources, own_out, com, com_out):
+    def engine(self, own_at, sources, own_out, com, com_out, halved=False):
         own_buf = [self.take(4) for _ in own_at]
         com_buf = [self.take(6) for _ in com]
         own = [(sources[j], k, kind) for j, k, kind in own_at]
         places = [own_out[j].at[k] for j, k, _ in own_at]
-        return Engine(own, com, own_buf, com_buf, places, com_out, self.take(10 + 18))
+        return Engine(own, com, own_buf, com_buf, places, com_out, self.take(10 + 18), halved)
 
 
 def back_kernel(*refs, own_at, sources, common, heads, groups):
@@ -1143,7 +1206,7 @@
     dx_made = refs.take(MICRO)
     own_out, com_out = refs.take(sources), refs.take(common)
     d0_out, d1_out, gres_out, gbf_out, gg_out = refs.take(5)
-    engine = refs.engine(own_at, own_in, own_out, com_in, com_out)
+    engine = refs.engine(own_at, own_in, own_out, com_in, com_out, True)
     dx, r_core, r_y, gres, gbf, gg, pay_o, back_o, pay0, pay1 = refs.take(10)
     ks, vs, dk, dv, qs, gs, deltas, acc = refs.take(8)
     s_dx, s_o, s_0, s_1 = [refs.take(2) for _ in range(4)]
@@ -1286,13 +1349,13 @@
 
 def run_back(expert_grads, own_at, shared_grads, attention, middle, dx_made, groups):
     own = chunk_views(expert_grads)
-    com = [g.reshape(shared_shape(g.shape)) for g in shared_grads]
+    com = shared_grads
     heads = attention[0].shape[1] // 3
     rows, width = middle[1].shape
     args = [*own, *com, *attention, *middle, *dx_made]
     own_shapes = [own[j].shape[2:] for j, _, _ in own_at]
-    com_shapes = [g.shape[3:] for g in com]
-    own_buf, com_buf, sems = Engine.scratch(own_shapes, [kind for *_, kind in own_at], com_shapes)
+    com_shapes = [g.shape[1:] for g in com]
+    own_buf, com_buf, sems = Engine.scratch(own_shapes, [kind for *_, kind in own_at], com_shapes, True)
     held = MICRO * groups * TILE
     v, dma = pltpu.VMEM, lambda n: pltpu.SemaphoreType.DMA((n,))
     pay = lambda n: (groups, n * heads, HALF, HALF)
@@ -1548,7 +1611,7 @@
             hidden, grad = squeeze(hidden), squeeze(grad)
             weight = jnp.sum(select.astype(F32) * weight.reshape(-1, 1, rows), -1).reshape(-1, 1)
         made, dx, *rest = run_ffn(
-            hidden, grad, weight, ein_parts, eout_parts, grads=grads, us=42, guest=guest
+            hidden, grad, weight, ein_parts, eout_parts, grads=grads, us=42, guest=guest, fb=FB // (1 + m)
         )
         if capacity < rows:
             made, dx = spread(made), spread(dx)
@@ -1573,7 +1636,18 @@
     shared, dx_shared, *g_shared = run_ffn(
         nf_both.reshape(-1, width), cot, None, sin_parts, sout_parts, us=23
     )
-    made1, dx1, g_expert, _ = expert_pass(1, rows1, g_expert, None, dx_shared)
+    g_shared = [g.reshape(shared_shape(g.shape)) for g in g_shared]
+    shapes = [g.shape[3:] for g in g_shared]
+    guest = (
+        halves_guest,
+        [(g, False) for g in g_shared],
+        [struct((2, *sh), BF) for sh in shapes],
+        [buf((2, 2, *sh), BF) for sh in shapes] * 2
+        + [buf((2, *sh), BF) for sh in shapes]
+        + [dma((6,)), dma((12,)), dma((12,)), dma((3,))],
+        5,
+    )
+    made1, dx1, g_expert, g_shared = expert_pass(1, rows1, g_expert, guest)
     dx0, dx1, made0, made1 = [scatter_rest(v).reshape(4, rows, width) for v in (dx0, dx1, made0, made1)]
 
     spread = [(j, k) for j in range(3) for k in range(PIECES)]

time: 552 us -> 548 us (level)
    pallas_call x2, Pallas kernels: 284 us -> 271 us  [device_call(): pl.pallas_call(kernel, out_shape=tuple(outs), in_specs=[pl.BlockSpec(memo...]
    pallas_call x3, Pallas kernels: 109 us -> 117 us  [run_ffn(): pl.pallas_call(functools.partial(ffn_kernel, tr=math.gcd(tr, rows), halve...]
where the time goes in v6:
time: 548 us; the launch traced here: 540 us
  Pallas kernels  516 us (94%)
  other arithmetic  18.9 us (3%)
    pallas_call x2, Pallas kernels, device_call(): pl.pallas_call(kernel, out_shape=tuple(outs), in_specs=[pl.BlockSpec(memo...  271 us
    pallas_call x1, Pallas kernels, run_front(): pl.pallas_call(functools.partial(front_kernel, heads=heads, groups=groups...  128 us
    pallas_call x3, Pallas kernels, run_ffn(): pl.pallas_call(functools.partial(ffn_kernel, tr=math.gcd(tr, rows), halve...  117 us

profile of v6, /device:TPU:0, one launch (start us, length us, event | category | flops | bytes accessed | tf_op | source)
XLA Modules:
  0.0 540.1 jit_solution(17122725204107427237)
XLA Ops:
  0.6 0.7 select_reduce_fusion
  1.4 0.6 copy.28.refs_4_
  2.0 0.7 stack.18
  2.7 0.7 stack.19
  3.3 0.6 maximum_convert_fusion.2.refs_1_
  3.9 127.6 %shard_map.213 = (bf16[4,9,128,128]{3,2,1,0:T(8,128)(2,1)}, bf16[4,9,128,128]{3,2,1,0:T(8,128)(2,1)}, bf16[4,3,128,128]{3,2,1,0:T(8,128)(2,1)}, bf16[4,3,128,128...) custom-call(bf16[2,256,768]{2,1,0:T(8,128)(2,1)} %bitcast.90, ...), custom_call_target="tpu_custom_call" | custom-call | flops 149500002304 | tf_op jit(solution)/shard_map/pallas_call | solution.py:511
  131.5 44.3 %shard_map.214 = (bf16[1024,768]{1,0:T(8,128)(2,1)}, bf16[1024,768]{1,0:T(8,128)(2,1)}, bf16[768,2048]{1,0:T(8,128)(2,1)}, bf16[768,2048]{1,0:T(8,128)(2,1)}, bf...) custom-call(bf16[1024,768]{1,0:T(8,128)(2,1)} %bitcast.114, ...), custom_call_target="tpu_custom_call" | custom-call | flops 48299999232 | tf_op jit(solution)/shard_map/pallas_call | solution.py:662
  175.8 22.1 %shard_map.215 = (bf16[512,768]{1,0:T(8,128)(2,1)}, bf16[512,768]{1,0:T(8,128)(2,1)}, bf16[768,2048]{1,0:T(8,128)(2,1)}, bf16[768,2048]{1,0:T(8,128)(2,1)}, bf16[2048,768]{1,0:T(8,128)(2,1)}) custom-call(bf16[512,768]{1,0:T(8,128)(2,1)} %bitcast.118, bf16[512,768]{1,0:T(8,128)(2,1)} %bitcast.88, bf16[384,4096]{1,0:T(8,128)(2,1)} %refs_4_.1, ...), custom_call_target="tpu_custom_call" | custom-call | flops 26449999872 | tf_op jit(solution)/shard_map/pallas_call | solution.py:662
  197.9 50.8 %shard_map.216 = (bf16[1024,768]{1,0:T(8,128)(2,1)}, bf16[1024,768]{1,0:T(8,128)(2,1)}, bf16[768,2048]{1,0:T(8,128)(2,1)}, bf16[768,2048]{1,0:T(8,128)(2,1)}, bf...) custom-call(bf16[1024,768]{1,0:T(8,128)(2,1)} %bitcast.115, ...), custom_call_target="tpu_custom_call" | custom-call | flops 48299999232 | tf_op jit(solution)/shard_map/pallas_call | solution.py:662
  248.7 181.7 %shard_map.217 = (bf16[4,96,2048]{2,1,0:T(8,128)(2,1)}, bf16[4,96,2048]{2,1,0:T(8,128)(2,1)}, bf16[4,256,768]{2,1,0:T(8,128)(2,1)}, bf16[2,2,96,2048]{3,2,1,0:T(...) custom-call(bf16[2,4,96,2048]{3,2,1,0:T(8,128)(2,1)} %bitcast.99, ...), custom_call_target="tpu_custom_call" | custom-call | flops 189750001664 | tf_op jit(solution)/shard_map/pallas_call | solution.py:1330
  430.4 0.0 copy-start.3
  430.4 89.3 %shard_map.218 = (bf16[4,96,2048]{2,1,0:T(8,128)(2,1)}, bf16[4,256,768]{2,1,0:T(8,128)(2,1)}, bf16[2,2,96,1152]{3,2,1,0:T(8,128)(2,1)}, bf16[2,2,96,1152]{3,2,1,...) custom-call(bf16[4,96,2048]{2,1,0:T(8,128)(2,1)} %get-tuple-element., ...), custom_call_target="tpu_custom_call", output_to_operand_aliasing={{0}: (0, {}), {1}: (1, {})} | custom-call | flops 103499997184 | tf_op jit(solution)/shard_map/pallas_call | solution.py:1330
  519.7 0.0 copy-done.3
  519.7 0.0 copy-start.1
  519.7 0.0 copy-start.2
  519.7 5.0 fusion
  524.8 0.0 copy-done.1
  524.8 0.0 copy-done.2
  524.8 0.0 copy-start
  524.8 0.0 copy-start.7
  524.8 0.0 copy-start.8
  524.8 3.5 maximum_convert_fusion
  528.3 0.0 copy-done
  528.3 0.0 copy-done.7
  528.3 0.0 copy-done.8
  528.3 0.0 copy-start.14
  528.3 0.0 copy-start.6
  528.3 2.2 multiply_reduce_fusion
  530.5 0.0 copy-start.9
  530.5 0.0 copy-start.10
  530.5 0.0 copy-start.11
  530.5 0.0 copy-start.12
  530.5 0.0 copy-done.14
  530.6 0.6 convert_divide_fusion
  531.1 0.0 copy-done.6
  531.1 1.9 bitcast_convert_fusion
  533.0 0.0 copy-start.13
  533.0 0.0 copy-done.9
  533.0 0.0 copy-done.10
  533.0 0.0 copy-done.11
  533.1 0.0 copy-done.12
  533.1 0.0 copy-start.5
  533.1 0.2 fusion.3
  533.3 0.9 maximum_bitcast_fusion.1
  534.3 0.0 copy-done.13
  534.3 0.0 copy-start.4
  534.3 1.1 bitcast_convert_fusion.2
  535.4 0.7 slice.19
  536.1 0.6 dynamic-slice_reduce_fusion
  536.7 0.0 copy-done.5
  536.8 2.0 bitcast_convert_fusion.1
  538.8 0.0 copy-done.4
  538.8 1.1 copy.32
Async XLA Ops:
  430.4 89.3 %copy-start.3 = (bf16[4,96,2048]{2,1,0:T(8,128)(2,1)S(1)}, bf16[4,96,2048]{2,1,0:T(8,128)(2,1)}, u32[]{:S(2)}) copy-start(bf16[4,96,2048]{2,1,0:T(8,128)(2,1)} %get-tuple-element.133) | copy-start | bytes 4718596
  519.7 5.1 copy-start.1
  519.7 5.0 copy-start.2
  524.8 3.5 copy-start
  524.8 3.5 copy-start.7
  524.8 3.5 copy-start.8
  528.3 2.3 copy-start.14
  528.3 2.9 copy-start.6
  530.5 2.5 copy-start.9
  530.5 2.5 copy-start.10
  530.5 2.5 copy-start.11
  530.5 2.5 copy-start.12
  533.0 1.2 copy-start.13
  533.1 3.7 copy-start.5
  534.3 4.5 copy-start.4

commit v7 on v6

--- a/solution.py
+++ b/solution.py
@@ -1445,13 +1445,13 @@
             store.start()
         else:
             engine.run(name)
-        if index == 12:
+        if name == "a2":
             for m in both:
                 row_own[m].wait()
                 row_wires[m].wait_recv()
                 row[m] = row[m] + row_core[m]
                 row_next[m].start()
-        if index == 30:
+        if index == len(LAST_PLAN) - 9:
             for m in both:
                 row_next[m].wait_recv()
                 row[m, 0] = row[m, 0] + row_y[m]
@@ -1611,7 +1611,7 @@
             hidden, grad = squeeze(hidden), squeeze(grad)
             weight = jnp.sum(select.astype(F32) * weight.reshape(-1, 1, rows), -1).reshape(-1, 1)
         made, dx, *rest = run_ffn(
-            hidden, grad, weight, ein_parts, eout_parts, grads=grads, us=42, guest=guest, fb=FB // (1 + m)
+            hidden, grad, weight, ein_parts, eout_parts, grads=grads, us=42, guest=guest, fb=FB // (1 + m), tr=512 * (1 + m)
         )
         if capacity < rows:
             made, dx = spread(made), spread(dx)

time: 548 us -> 548 us (level)
  no operation moved by 1% of the time
where the time goes in v7:
time: 548 us; the launch traced here: 540 us
  Pallas kernels  516 us (94%)
  other arithmetic  18.9 us (3%)
    pallas_call x2, Pallas kernels, device_call(): pl.pallas_call(kernel, out_shape=tuple(outs), in_specs=[pl.BlockSpec(memo...  272 us
    pallas_call x1, Pallas kernels, run_front(): pl.pallas_call(functools.partial(front_kernel, heads=heads, groups=groups...  128 us
    pallas_call x3, Pallas kernels, run_ffn(): pl.pallas_call(functools.partial(ffn_kernel, tr=math.gcd(tr, rows), halve...  117 us

profile of v7, /device:TPU:0, one launch (start us, length us, event | category | flops | bytes accessed | tf_op | source)
XLA Modules:
  0.0 540.5 jit_solution(3560206406301305479)
XLA Ops:
  0.6 0.7 select_reduce_fusion
  1.4 0.6 copy.28.refs_4_
  2.0 0.7 stack.18
  2.7 0.7 stack.19
  3.3 0.6 maximum_convert_fusion.2.refs_1_
  3.9 127.6 %shard_map.213 = (bf16[4,9,128,128]{3,2,1,0:T(8,128)(2,1)}, bf16[4,9,128,128]{3,2,1,0:T(8,128)(2,1)}, bf16[4,3,128,128]{3,2,1,0:T(8,128)(2,1)}, bf16[4,3,128,128...) custom-call(bf16[2,256,768]{2,1,0:T(8,128)(2,1)} %bitcast.90, ...), custom_call_target="tpu_custom_call" | custom-call | flops 149500002304 | tf_op jit(solution)/shard_map/pallas_call | solution.py:511
  131.5 44.5 %shard_map.214 = (bf16[1024,768]{1,0:T(8,128)(2,1)}, bf16[1024,768]{1,0:T(8,128)(2,1)}, bf16[768,2048]{1,0:T(8,128)(2,1)}, bf16[768,2048]{1,0:T(8,128)(2,1)}, bf...) custom-call(bf16[1024,768]{1,0:T(8,128)(2,1)} %bitcast.114, ...), custom_call_target="tpu_custom_call" | custom-call | flops 48299999232 | tf_op jit(solution)/shard_map/pallas_call | solution.py:662
  175.9 22.1 %shard_map.215 = (bf16[512,768]{1,0:T(8,128)(2,1)}, bf16[512,768]{1,0:T(8,128)(2,1)}, bf16[768,2048]{1,0:T(8,128)(2,1)}, bf16[768,2048]{1,0:T(8,128)(2,1)}, bf16[2048,768]{1,0:T(8,128)(2,1)}) custom-call(bf16[512,768]{1,0:T(8,128)(2,1)} %bitcast.118, bf16[512,768]{1,0:T(8,128)(2,1)} %bitcast.88, bf16[384,4096]{1,0:T(8,128)(2,1)} %refs_4_.1, ...), custom_call_target="tpu_custom_call" | custom-call | flops 26449999872 | tf_op jit(solution)/shard_map/pallas_call | solution.py:662
  198.0 50.1 %shard_map.216 = (bf16[1024,768]{1,0:T(8,128)(2,1)}, bf16[1024,768]{1,0:T(8,128)(2,1)}, bf16[768,2048]{1,0:T(8,128)(2,1)}, bf16[768,2048]{1,0:T(8,128)(2,1)}, bf...) custom-call(bf16[1024,768]{1,0:T(8,128)(2,1)} %bitcast.115, ...), custom_call_target="tpu_custom_call" | custom-call | flops 48299999232 | tf_op jit(solution)/shard_map/pallas_call | solution.py:662
  248.1 181.7 %shard_map.217 = (bf16[4,96,2048]{2,1,0:T(8,128)(2,1)}, bf16[4,96,2048]{2,1,0:T(8,128)(2,1)}, bf16[4,256,768]{2,1,0:T(8,128)(2,1)}, bf16[2,2,96,2048]{3,2,1,0:T(...) custom-call(bf16[2,4,96,2048]{3,2,1,0:T(8,128)(2,1)} %bitcast.99, ...), custom_call_target="tpu_custom_call" | custom-call | flops 189750001664 | tf_op jit(solution)/shard_map/pallas_call | solution.py:1330
  429.8 0.0 copy-start.3
  429.8 90.0 %shard_map.218 = (bf16[4,96,2048]{2,1,0:T(8,128)(2,1)}, bf16[4,256,768]{2,1,0:T(8,128)(2,1)}, bf16[2,2,96,1152]{3,2,1,0:T(8,128)(2,1)}, bf16[2,2,96,1152]{3,2,1,...) custom-call(bf16[4,96,2048]{2,1,0:T(8,128)(2,1)} %get-tuple-element., ...), custom_call_target="tpu_custom_call", output_to_operand_aliasing={{0}: (0, {}), {1}: (1, {})} | custom-call | flops 103499997184 | tf_op jit(solution)/shard_map/pallas_call | solution.py:1330
  519.8 0.0 copy-done.3
  519.9 0.0 copy-start.1
  519.9 0.0 copy-start.2
  519.9 5.0 fusion
  524.9 0.0 copy-done.1
  524.9 0.0 copy-done.2
  524.9 0.0 copy-start
  524.9 0.0 copy-start.7
  524.9 0.0 copy-start.8
  524.9 3.5 maximum_convert_fusion
  528.4 0.0 copy-done
  528.4 0.0 copy-done.7
  528.4 0.0 copy-done.8
  528.4 0.0 copy-start.14
  528.4 0.0 copy-start.6
  528.4 2.2 multiply_reduce_fusion
  530.7 0.0 copy-start.9
  530.7 0.0 copy-start.10
  530.7 0.0 copy-start.11
  530.7 0.0 copy-start.12
  530.7 0.0 copy-done.14
  530.7 0.6 convert_divide_fusion
  531.3 0.0 copy-done.6
  531.3 1.9 bitcast_convert_fusion
  533.2 0.0 copy-start.13
  533.2 0.0 copy-done.9
  533.2 0.0 copy-done.10
  533.2 0.0 copy-done.11
  533.2 0.0 copy-done.12
  533.2 0.0 copy-start.5
  533.2 0.2 fusion.3
  533.5 0.9 maximum_bitcast_fusion.1
  534.4 0.0 copy-done.13
  534.4 0.0 copy-start.4
  534.4 1.1 bitcast_convert_fusion.2
  535.6 0.7 slice.19
  536.3 0.6 dynamic-slice_reduce_fusion
  536.9 0.0 copy-done.5
  536.9 2.0 bitcast_convert_fusion.1
  538.9 0.0 copy-done.4
  538.9 1.1 copy.32
Async XLA Ops:
  429.8 90.0 %copy-start.3 = (bf16[4,96,2048]{2,1,0:T(8,128)(2,1)S(1)}, bf16[4,96,2048]{2,1,0:T(8,128)(2,1)}, u32[]{:S(2)}) copy-start(bf16[4,96,2048]{2,1,0:T(8,128)(2,1)} %get-tuple-element.133) | copy-start | bytes 4718596
  519.9 5.1 copy-start.1
  519.9 5.0 copy-start.2
  524.9 3.5 copy-start
  524.9 3.5 copy-start.7
  524.9 3.5 copy-start.8
  528.4 2.3 copy-start.14
  528.4 2.9 copy-start.6
  530.7 2.5 copy-start.9
  530.7 2.5 copy-start.10
  530.7 2.5 copy-start.11
  530.7 2.5 copy-start.12
  533.2 1.2 copy-start.13
  533.2 3.7 copy-start.5
  534.4 4.5 copy-start.4
